TPU v7x, 32 devices: a whole 2x2x4 slice. The times are simulated.
32 devices in a mesh: fsdp: 8 (over z, y), rep: 4 (over x, core).
Axes of the slice: x: 2, y: 2, z: 4, core: 2. Of those that a mesh axis runs over, the one named last changes fastest.
Arguments:
- tokens: float32 [16384, 768], P(('fsdp', 'rep')), may hold values from -6 to 6
- mask_bits: int32 [16384], P(('fsdp', 'rep')), may hold values from 0 to 1, as said below
- timesteps: int32 [128], P(('fsdp', 'rep')), may hold values from 0 to 999
- cotangent: float32 [16384, 768], P(('fsdp', 'rep')), may hold values from -6 to 6
- w_qkv: float32 [768, 2304], P(('fsdp', 'rep')), may hold values from -0.21875 to 0.21875
- w_out: float32 [768, 768], P(('fsdp', 'rep')), may hold values from -0.625 to 0.625
- w_up: float32 [768, 3072], P(('fsdp', 'rep')), may hold values from -0.21875 to 0.21875
- w_down: float32 [3072, 768], P(('fsdp', 'rep')), may hold values from -0.109375 to 0.109375
- time_table: float32 [768, 1000], P(('fsdp', 'rep')), may hold values from -6 to 6
- b_query: float32 [768], P(('fsdp', 'rep')), may hold values from -3 to 3
- b_value: float32 [768], P(('fsdp', 'rep')), may hold values from -3 to 3
- b_out: float32 [768], P(('fsdp', 'rep')), may hold values from -3 to 3
- b_up: float32 [3072], P(('fsdp', 'rep')), may hold values from -3 to 3
- b_down: float32 [768], P(('fsdp', 'rep')), may hold values from -3 to 3
- gain_attn: float32 [768], P(('fsdp', 'rep')), may hold values from 0.5 to 1.5
- shift_attn: float32 [768], P(('fsdp', 'rep')), may hold values from -2 to 2
- gain_mlp: float32 [768], P(('fsdp', 'rep')), may hold values from 0.5 to 1.5
- shift_mlp: float32 [768], P(('fsdp', 'rep')), may hold values from -2 to 2
- mask_vector: float32 [768], P(('fsdp', 'rep')), may hold values from -5 to 5
Outputs:
- output: float32 [16384, 768], P(('fsdp', 'rep'))
- grad_tokens: float32 [16384, 768], P(('fsdp', 'rep'))
- grad_w_qkv: float32 [768, 2304], P(('fsdp', 'rep'))
- grad_w_out: float32 [768, 768], P(('fsdp', 'rep'))
- grad_w_up: float32 [768, 3072], P(('fsdp', 'rep'))
- grad_w_down: float32 [3072, 768], P(('fsdp', 'rep'))
- grad_time_table: float32 [768, 1000], P(('fsdp', 'rep'))
- grad_b_query: float32 [768], P(('fsdp', 'rep'))
- grad_b_value: float32 [768], P(('fsdp', 'rep'))
- grad_b_out: float32 [768], P(('fsdp', 'rep'))
- grad_b_up: float32 [3072], P(('fsdp', 'rep'))
- grad_b_down: float32 [768], P(('fsdp', 'rep'))
- grad_gain_attn: float32 [768], P(('fsdp', 'rep'))
- grad_shift_attn: float32 [768], P(('fsdp', 'rep'))
- grad_gain_mlp: float32 [768], P(('fsdp', 'rep'))
- grad_shift_mlp: float32 [768], P(('fsdp', 'rep'))
- grad_mask_vector: float32 [768], P(('fsdp', 'rep'))
Inputs may be any that keep to these rules, and one draw needn't show every extreme that they name: `mask_bits`: 1 marks an absorbed token; the number of absorbed tokens of a sequence varies widely, from none to all 128.
All inputs are finite; a program needn't handle non-finite values.
Results may differ from a plain program's by a relative error of at most 0.019.
Values may be sent and summed in bfloat16 or wider, within the bound.
No kernel may reach another device: no remote copies, remote signals or barrier semaphores. Data moves between devices by JAX's collectives and lax.ppermute only.
A program may use at most 192 MiB of HBM per device.

v0:
```python
import functools
import math

import jax
import jax.numpy as jnp
from jax import lax
from jax.experimental import pallas as pl
from jax.experimental.pallas import tpu as pltpu
from jax.sharding import PartitionSpec as P

HDIM = 64
EPSILON = 1e-05
AXES = ("fsdp", "rep")
BF = jnp.bfloat16
F32 = jnp.float32
LANES = 128
VMEM_BYTES = 32 << 20
GELU_OUTER = math.sqrt(2.0 / math.pi)
GELU_INNER = 0.044715


def layer_norm(values, gain, shift):
    center = values - jnp.mean(values, -1, keepdims=True)
    spread = jnp.mean(center * center, -1, keepdims=True)
    return center * lax.rsqrt(spread + EPSILON) * gain + shift


def contract(left, right, left_dim, right_dim):
    dims = (((left_dim,), (right_dim,)), ((), ()))
    return lax.dot_general(left, right, dims, preferred_element_type=F32)


def product(left, right):
    return contract(left, right, 1, 0)


def left_product(left, right):
    return contract(left, right, 0, 0)


def right_product(left, right):
    return contract(left, right, 1, 1)


def column_sums(values):
    return jnp.sum(values.astype(F32), 0)


def pick(array, index, axis):
    return lax.dynamic_index_in_dim(array, index, axis, keepdims=False)


def paired(bit, mine, other, axis):
    return jnp.stack([jnp.where(bit == 0, mine, other), jnp.where(bit == 0, other, mine)], axis)


def after(value, *others):
    return lax.optimization_barrier((value, others))[0]


def lane_masks(factor):
    lane = lax.broadcasted_iota(jnp.int32, (1, LANES), 1)
    return [jnp.where((lane < HDIM) == (head == 0), factor, 0.0).astype(BF) for head in (0, 1)]


def softmax(scores):
    powers = jnp.exp(scores - jnp.max(scores, -1, keepdims=True))
    return powers * (1.0 / jnp.sum(powers, -1, keepdims=True))


def attention_kernel(length, scale, rows_ref, query_ref, key_ref, value_ref, bias_ref, qkv_ref, context_ref):
    rows = rows_ref[...]
    for index, weight in enumerate((query_ref, key_ref, value_ref)):
        qkv_ref[index] = (product(rows, weight[...]) + bias_ref[index : index + 1, :]).astype(BF)
    ones, scaled = lane_masks(1.0), lane_masks(scale)

    for sequence in range(rows.shape[0] // length):
        span = slice(sequence * length, (sequence + 1) * length)
        queries, key_rows, value_rows = [qkv_ref[index, span, :] for index in range(3)]
        total = 0.0
        for head in (0, 1):
            probs = softmax(right_product(queries * scaled[head], key_rows)).astype(BF)
            total = total + product(probs, value_rows * ones[head])
        context_ref[span, :] = total.astype(BF)


def attention(rows, weight, bias, length):
    tokens, width = rows.shape
    half = bias.shape[1]
    pairs = half // LANES

    def weight_spec(index):
        return pl.BlockSpec((width, LANES), lambda pair: (0, index * pairs + pair))

    return pl.pallas_call(
        functools.partial(attention_kernel, length, 1.0 / math.sqrt(HDIM)),
        grid=(pairs,),
        in_specs=[
            pl.BlockSpec((tokens, width), lambda pair: (0, 0)),
            weight_spec(0),
            weight_spec(1),
            weight_spec(2),
            pl.BlockSpec((3, LANES), lambda pair: (0, pair)),
        ],
        out_specs=[
            pl.BlockSpec((3, tokens, LANES), lambda pair: (0, 0, pair)),
            pl.BlockSpec((tokens, LANES), lambda pair: (0, pair)),
        ],
        out_shape=[
            jax.ShapeDtypeStruct((3, tokens, half), BF),
            jax.ShapeDtypeStruct((tokens, half), BF),
        ],
        compiler_params=pltpu.CompilerParams(vmem_limit_bytes=VMEM_BYTES),
        cost_estimate=pl.CostEstimate(
            flops=6 * tokens * width * half,
            bytes_accessed=2 * tokens * width + 6 * width * half + 8 * tokens * half,
            transcendentals=2 * tokens * length * pairs,
        ),
        name="attention",
    )(rows, weight, weight, weight, bias)


def attention_back_kernel(length, scale, qkv_ref, grad_ref, rows_ref, grads_ref, weight_ref, sums_ref):
    ones, scaled = lane_masks(1.0), lane_masks(scale)

    for sequence in range(grad_ref.shape[0] // length):
        span = slice(sequence * length, (sequence + 1) * length)
        queries, key_rows, value_rows = [qkv_ref[index, span, :] for index in range(3)]
        grad = grad_ref[span, :]
        grad_queries, grad_keys, grad_values = 0.0, 0.0, 0.0
        for head in (0, 1):
            probs = softmax(right_product(queries * scaled[head], key_rows))
            grad_head = grad * ones[head]
            grad_probs = right_product(grad_head, value_rows)
            grad_scores = probs * (grad_probs - jnp.sum(grad_probs * probs, -1, keepdims=True))
            grad_scores = grad_scores.astype(BF)
            grad_values = grad_values + left_product(probs.astype(BF), grad_head)
            grad_queries = grad_queries + product(grad_scores, key_rows * ones[head])
            grad_keys = grad_keys + left_product(grad_scores, queries * ones[head])
        grads_ref[0, span, :] = (grad_queries * scale).astype(BF)
        grads_ref[1, span, :] = (grad_keys * scale).astype(BF)
        grads_ref[2, span, :] = grad_values.astype(BF)

    rows = rows_ref[...]
    for index in range(3):
        grads = grads_ref[index]
        weight_ref[index] = product(rows, grads).astype(weight_ref.dtype)
        sums_ref[index : index + 1, :] = jnp.sum(grads.astype(F32), 0, keepdims=True)


def attention_back(qkv, grad, rows_across, length, dtype):
    _, tokens, half = qkv.shape
    width = rows_across.shape[0]
    pairs = half // LANES
    return pl.pallas_call(
        functools.partial(attention_back_kernel, length, 1.0 / math.sqrt(HDIM)),
        grid=(pairs,),
        in_specs=[
            pl.BlockSpec((3, tokens, LANES), lambda pair: (0, 0, pair)),
            pl.BlockSpec((tokens, LANES), lambda pair: (0, pair)),
            pl.BlockSpec((width, tokens), lambda pair: (0, 0)),
        ],
        out_specs=[
            pl.BlockSpec((3, tokens, LANES), lambda pair: (0, 0, pair)),
            pl.BlockSpec((3, width, LANES), lambda pair: (0, 0, pair)),
            pl.BlockSpec((3, LANES), lambda pair: (0, pair)),
        ],
        out_shape=[
            jax.ShapeDtypeStruct((3, tokens, half), BF),
            jax.ShapeDtypeStruct((3, width, half), dtype),
            jax.ShapeDtypeStruct((3, half), F32),
        ],
        compiler_params=pltpu.CompilerParams(vmem_limit_bytes=VMEM_BYTES),
        cost_estimate=pl.CostEstimate(
            flops=6 * tokens * width * half,
            bytes_accessed=2 * tokens * width + 12 * width * half + 14 * tokens * half,
            transcendentals=2 * tokens * length * pairs,
        ),
        name="attention_back",
    )(qkv, grad, rows_across)


def feed_kernel(rows_ref, weight_ref, bias_ref, hidden_ref, slope_ref, pre_ref):
    pre_ref[...] = product(rows_ref[...], weight_ref[...])
    step = 32

    def chunk(index, carry):
        span = pl.ds(pl.multiple_of(index * step, step), step)
        pre = pre_ref[span, :] + bias_ref[...]
        square = pre * pre
        bend = jnp.tanh(GELU_OUTER * (pre + GELU_INNER * (square * pre)))
        share = 0.5 * (1.0 + bend)
        hidden_ref[span, :] = (pre * share).astype(BF)
        inner = (0.5 * GELU_OUTER) * pre * (1.0 + (3.0 * GELU_INNER) * square)
        slope_ref[span, :] = share + inner * (1.0 - bend * bend)
        return carry

    lax.fori_loop(0, rows_ref.shape[0] // step, chunk, 0, unroll=2)


def feed(rows, weight, bias, block=512):
    tokens, width = rows.shape
    columns = weight.shape[1]
    block = math.gcd(block, columns)
    out = pl.BlockSpec((tokens, block), lambda step: (0, step))
    return pl.pallas_call(
        feed_kernel,
        grid=(columns // block,),
        in_specs=[
            pl.BlockSpec((tokens, width), lambda step: (0, 0)),
            pl.BlockSpec((width, block), lambda step: (0, step)),
            pl.BlockSpec((1, block), lambda step: (0, step)),
        ],
        out_specs=[out, out],
        out_shape=[
            jax.ShapeDtypeStruct((tokens, columns), BF),
            jax.ShapeDtypeStruct((tokens, columns), F32),
        ],
        scratch_shapes=[pltpu.VMEM((tokens, block), F32)],
        compiler_params=pltpu.CompilerParams(vmem_limit_bytes=VMEM_BYTES),
        cost_estimate=pl.CostEstimate(
            flops=2 * tokens * width * columns,
            bytes_accessed=2 * tokens * width + 2 * width * columns + 6 * tokens * columns,
            transcendentals=tokens * columns,
        ),
        name="feed",
    )(rows, weight, bias)


def feed_back_kernel(grad_ref, weight_ref, slope_ref, rows_ref, pre_ref, sum_ref, up_ref):
    grad = (right_product(grad_ref[...], weight_ref[...]) * slope_ref[...]).astype(BF)
    pre_ref[...] = grad
    sum_ref[...] = jnp.sum(grad.astype(F32), 0, keepdims=True)
    up_ref[...] = product(rows_ref[...], grad).astype(up_ref.dtype)


def feed_back(grad, weight, slope, rows_across, dtype, block=512):
    tokens, width = grad.shape
    columns = weight.shape[0]
    block = math.gcd(block, columns)
    out = pl.BlockSpec((tokens, block), lambda step: (0, step))
    return pl.pallas_call(
        feed_back_kernel,
        grid=(columns // block,),
        in_specs=[
            pl.BlockSpec((tokens, width), lambda step: (0, 0)),
            pl.BlockSpec((block, width), lambda step: (step, 0)),
            out,
            pl.BlockSpec((width, tokens), lambda step: (0, 0)),
        ],
        out_specs=[
            out,
            pl.BlockSpec((1, block), lambda step: (0, step)),
            pl.BlockSpec((width, block), lambda step: (0, step)),
        ],
        out_shape=[
            jax.ShapeDtypeStruct((tokens, columns), BF),
            jax.ShapeDtypeStruct((1, columns), F32),
            jax.ShapeDtypeStruct((width, columns), dtype),
        ],
        compiler_params=pltpu.CompilerParams(vmem_limit_bytes=VMEM_BYTES),
        cost_estimate=pl.CostEstimate(
            flops=4 * tokens * width * columns,
            bytes_accessed=4 * tokens * width + 6 * width * columns + 6 * tokens * columns,
            transcendentals=0,
        ),
        name="feed_back",
    )(grad, weight, slope, rows_across)


class Tree:
    def __init__(self):
        fsdp, rep = lax.axis_index("fsdp"), lax.axis_index("rep")
        self.z, self.y, self.x, self.core = fsdp // 2, fsdp % 2, rep // 2, rep % 2

    def to_core(self, value):
        return lax.ppermute(value, "rep", [(i, i ^ 1) for i in range(4)])

    def to_x(self, value):
        return lax.ppermute(value, "rep", [(i, i ^ 2) for i in range(4)])

    def to_y(self, value):
        return lax.ppermute(value, "fsdp", [(i, i ^ 1) for i in range(8)])

    def to_z(self, value, step):
        return lax.ppermute(value, "fsdp", [(i, i ^ (2 * step)) for i in range(8)])


class Gather:
    def __init__(self, tree, first, second):
        self.tree, self.cut = tree, first.shape[0]
        self.own = jnp.concatenate([first, second], 0)

    @staticmethod
    def columns(tree, shard):
        mine = pick(shard, tree.core, 1)
        got = tree.to_core(pick(shard, 1 - tree.core, 1))
        return Gather(tree, jnp.where(tree.core == 0, mine, got), jnp.where(tree.core == 0, got, mine))

    @staticmethod
    def rows(tree, shard):
        cut = shard.shape[0] // 2
        return Gather(tree, shard[:cut], shard[cut:])

    def along_z(self, *wait):
        tree = self.tree
        own = after(self.own, *wait)
        held = [own] + [tree.to_z(own, step) for step in (1, 2, 3)]
        low, high = tree.z % 2 == 1, tree.z // 2 == 1

        def chosen(rows):
            out = []
            for place in range(4):
                near = [jnp.where(low, held[(place ^ 1) ^ h], held[place ^ h]) for h in (0, 2)]
                out.append(jnp.where(high, near[1], near[0])[rows])
            return jnp.stack(out)

        self.first, self.second = chosen(slice(0, self.cut)), chosen(slice(self.cut, None))
        return self.first, self.second

    def one(self, *wait):
        tree = self.tree
        first, second = after((self.first, self.second), *wait)
        self.first = paired(tree.x, first, tree.to_x(first), 1)
        self.second = paired(tree.y, second, tree.to_y(second), 1)
        return self.first, self.second

    def two(self, *wait):
        tree = self.tree
        first, second = after((self.first, self.second), *wait)
        first = paired(tree.y, first, tree.to_y(first), 1)
        second = paired(tree.x, second, tree.to_x(second), 2)
        half = jnp.concatenate([first, second], 3)
        self.half = half.reshape(-1, half.shape[-1])
        return self.half

    def halves(self):
        return self.half, self.tree.to_core(self.half)


class Reduce:
    def __init__(self, tree, rows):
        self.tree, self.rows = tree, rows
        self.mine, self.got = [], []

    def add(self, mine, other):
        sent = other.astype(BF)
        got = self.tree.to_core(sent)
        self.mine.append(mine)
        self.got.append(got)
        return got

    def one(self):
        tree = self.tree
        shaped = [
            [array.reshape(4, 2, 2, self.rows, -1) for array in (mine, got)] for mine, got in zip(self.mine, self.got)
        ]

        def stage(rows, index, axis):
            sums = [
                pick(mine[:, :, :, rows], index, axis).astype(F32) + pick(got[:, :, :, rows], index, axis).astype(F32)
                for mine, got in shaped
            ]
            return jnp.concatenate(sums, -1)

        upper, lower = slice(0, self.rows // 2), slice(self.rows // 2, None)
        self.first_kept = stage(upper, tree.x, 2)
        self.second_kept = stage(lower, tree.y, 1)
        self.sent = (stage(upper, 1 - tree.x, 2).astype(BF), stage(lower, 1 - tree.y, 1).astype(BF))
        self.got = (tree.to_x(self.sent[0]), tree.to_y(self.sent[1]))

    def two(self):
        tree = self.tree
        first, second = self.first_kept + self.got[0], self.second_kept + self.got[1]
        self.first_kept, self.second_kept = pick(first, tree.y, 1), pick(second, tree.x, 1)
        self.sent = (pick(first, 1 - tree.y, 1).astype(BF), pick(second, 1 - tree.x, 1).astype(BF))
        self.got = (tree.to_y(self.sent[0]), tree.to_x(self.sent[1]))

    def along_z(self):
        tree = self.tree
        both = jnp.concatenate([self.first_kept + self.got[0], self.second_kept + self.got[1]], 1)
        self.first_kept = pick(both, tree.z, 0)
        self.sent = tuple(pick(both, tree.z ^ step, 0).astype(BF) for step in (1, 2, 3))
        self.got = tuple(tree.to_z(sent, step) for sent, step in zip(self.sent, (1, 2, 3)))

    def sums(self):
        return self.first_kept + self.got[0] + self.got[1] + self.got[2]

    def columns(self):
        tree, total = self.tree, self.sums()
        first, second = total[: self.rows // 2], total[self.rows // 2 :]
        keep = jnp.where(tree.core == 0, first, second)
        got = tree.to_core(jnp.where(tree.core == 0, second, first))
        return paired(tree.core, keep, got, 1)


class Whole:
    core = 0

    def __init__(self, rows=None):
        self.mine, self.other = [], []
        self.got, self.sent = (), ()

    @staticmethod
    def columns_of(shard):
        out = Whole()
        whole = lax.all_gather(shard, AXES, axis=0, tiled=True)
        out.half, out.rest = whole[:, 0], whole[:, 1]
        return out

    @staticmethod
    def rows_of(shard):
        out = Whole()
        whole = lax.all_gather(shard, AXES, axis=0)
        whole = whole.reshape(-1, 2, *shard.shape)
        out.half, out.rest = [whole[:, i].reshape(-1, shard.shape[1]) for i in range(2)]
        return out

    def along_z(self, *wait):
        return ()

    def one(self, *wait):
        return ()

    def two(self, *wait):
        return self.half

    def halves(self):
        return self.half, self.rest

    def add(self, mine, other):
        self.mine.append(mine.astype(BF))
        self.other.append(other.astype(BF))
        return mine

    def columns(self):
        parts = [jnp.concatenate(item, 1) for item in (self.mine, self.other)]
        return lax.psum_scatter(jnp.stack(parts, 1), AXES, scatter_dimension=0, tiled=True).astype(F32)

    def sums(self):
        count = lax.axis_size(AXES)
        mine, other = [item[0].reshape(count // 2, -1, item[0].shape[1]) for item in (self.mine, self.other)]
        sums = jnp.stack([mine, other], 1).reshape(-1, mine.shape[-1])
        return lax.psum_scatter(sums, AXES, scatter_dimension=0, tiled=True).astype(F32)


def body(
    fast,
    tokens,
    mask_bits,
    timesteps,
    cotangent,
    w_qkv,
    w_out,
    w_up,
    w_down,
    time_table,
    b_query,
    b_value,
    b_out,
    b_up,
    b_down,
    gain_attn,
    shift_attn,
    gain_mlp,
    shift_mlp,
    mask_vector,
):
    tree = Tree() if fast else Whole()
    gather_columns = functools.partial(Gather.columns, tree) if fast else Whole.columns_of
    gather_rows = functools.partial(Gather.rows, tree) if fast else Whole.rows_of
    reduction = functools.partial(Reduce, tree) if fast else Whole
    core = tree.core
    count = lax.axis_size(AXES)
    chips = count // 2
    place = lax.axis_index(AXES)
    width = tokens.shape[1]
    part = width // count
    hidden_width = w_up.shape[1]
    hidden_part = hidden_width // count
    seq_count = timesteps.shape[0]
    seq_length = tokens.shape[0] // seq_count
    row_count = tokens.shape[0]
    half = width // 2
    table_cols = time_table.shape[1]
    absorbed = (mask_bits == 1)[:, None]
    absorbed_float = mask_bits.astype(F32)[:, None]
    sides = (core, 1 - core)

    small = [b_query, b_value, b_out, b_down, gain_attn, shift_attn, gain_mlp, shift_mlp, mask_vector]
    fixed = len(small)
    up_cols = hidden_part // part
    seq_cols = -(-2 * seq_count // part)
    steps = jnp.concatenate([timesteps // 256, timesteps % 256]).astype(F32)
    steps = jnp.pad(steps, (0, seq_cols * part - 2 * seq_count)).reshape(seq_cols, part)
    small = jnp.concatenate([jnp.stack(small), b_up.reshape(up_cols, part), steps], 0)
    small_cols = small.shape[0]
    all_cols = -(-(table_cols + small_cols) // (2 * LANES)) * (2 * LANES)
    table_half = all_cols // 2
    small = jnp.pad(small, ((0, all_cols - table_cols - small_cols), (0, 0)))
    table = jnp.concatenate([time_table, small.T], 1).astype(BF).reshape(part, 2, table_half)

    qkv = w_qkv.astype(BF).reshape(part, 3, 2, half)
    shard = [qkv[:, 0], qkv[:, 1], qkv[:, 2], w_out.astype(BF).reshape(part, 2, half), table]
    attn_w = gather_columns(jnp.concatenate(shard, 2))
    up_w = gather_columns(
        w_up.astype(BF)
        .reshape(part, chips, 2, hidden_part)
        .transpose(0, 2, 1, 3)
        .reshape(part, 2, hidden_width // 2)
    )
    down_w = gather_rows(w_down.astype(BF))
    attn_z = attn_w.along_z()
    up_z = up_w.along_z(attn_z)
    attn_one = attn_w.one()
    down_z = down_w.along_z(up_z)
    attn_w.two()
    up_one = up_w.one(attn_w.half)
    attn_w = attn_w.halves()
    out_w = jnp.concatenate(
        [
            jnp.where(core == 0, *[w[:, 3 * half : 4 * half] for w in pair])
            for pair in (attn_w, attn_w[::-1])
        ],
        1,
    )

    chosen = jnp.concatenate([timesteps, table_cols + jnp.arange(small_cols, dtype=jnp.int32)])
    rows = 0.0
    for side, weight in zip(sides, attn_w):
        columns = lax.broadcasted_iota(jnp.int32, (seq_count + small_cols, table_half), 1) + side * table_half
        rows = rows + right_product((chosen[:, None] == columns).astype(BF), weight[:, 4 * half :])
    table_rows = rows[:seq_count]
    rows = rows[seq_count:]
    bias_query, bias_value, bias_out, bias_down, gain_one, shift_one, gain_two, shift_two, mask_row = [
        rows[i] for i in range(fixed)
    ]
    bias_up = rows[fixed : fixed + up_cols].reshape(up_cols, chips, 2, part).transpose(2, 1, 0, 3)
    bias_up = bias_up.reshape(2, 1, hidden_width // 2)
    bias_up = [pick(bias_up, side, 0) for side in sides]
    steps = rows[fixed + up_cols :].reshape(seq_cols, count, part).transpose(1, 0, 2).reshape(count, -1)
    steps = steps.astype(jnp.int32)
    steps = (steps[:, :seq_count] * 256 + steps[:, seq_count : 2 * seq_count]).reshape(-1)
    bias_qkv = jnp.stack([bias_query, jnp.zeros_like(bias_query), bias_value]).reshape(3, 2, half)
    bias_qkv = [pick(bias_qkv, side, 1) for side in sides]

    start = jnp.where(absorbed, mask_row[None, :], tokens)
    start = (start.reshape(seq_count, seq_length, width) + table_rows[:, None, :]).reshape(row_count, width)
    normed_one = layer_norm(start, gain_one, shift_one).astype(BF)
    across_one = normed_one.T
    qkv_mine, context_mine = attention(normed_one, attn_w[0], bias_qkv[0], seq_length)
    up_half = up_w.two(context_mine)
    qkv_other, context_other = attention(after(normed_one, up_one), attn_w[1], bias_qkv[1], seq_length)
    context = jnp.concatenate(
        [
            jnp.where(core == 0, context_mine, context_other),
            jnp.where(core == 0, context_other, context_mine),
        ],
        1,
    )
    middle = start + (product(context, out_w) + bias_out)
    down_one = down_w.one(up_half, context_other)
    up_w = up_w.halves()
    normed_two = layer_norm(middle, gain_two, shift_two).astype(BF)
    across_two = normed_two.T
    down_w.two(normed_two)
    hidden, slope = [None, None], [None, None]
    hidden[0], slope[0] = feed(normed_two, up_w[0], bias_up[0])
    hidden[1], slope[1] = feed(after(normed_two, down_one), up_w[1], bias_up[1])
    down_w = down_w.halves()

    grad_output = cotangent * absorbed_float
    grad_branch = grad_output.astype(BF)
    down_sum = reduction(hidden_part)
    down_got = down_sum.add(left_product(hidden[0], grad_branch), left_product(hidden[1], grad_branch))
    grad_b_down = column_sums(grad_branch)
    up_sum = reduction(2 * part)
    grad_pre, grad_b_up, grad_up = [None, None], [None, None], [None, None]
    grad_pre[1], grad_b_up[1], grad_up[1] = feed_back(grad_branch, down_w[1], slope[1], across_two, BF)
    if fast:
        down_sum.one()
    grad_pre[0], grad_b_up[0], grad_up[0] = feed_back(
        after(grad_branch, down_sum.sent), down_w[0], slope[0], across_two, F32
    )
    up_sum.add(grad_up[0], grad_up[1])
    if fast:
        down_sum.two()
    grad_pre = after(grad_pre, down_sum.sent)
    grad_normed_two = right_product(grad_pre[0], up_w[0]) + right_product(grad_pre[1], up_w[1])
    _, norm_pull = jax.vjp(layer_norm, middle, gain_two, shift_two)
    back_middle, grad_gain_mlp, grad_shift_mlp = norm_pull(grad_normed_two)
    grad_middle = grad_output + back_middle

    grad_attn = grad_middle.astype(BF)
    grad_halves = [lax.dynamic_slice_in_dim(grad_attn, side * half, half, 1) for side in sides]
    attn_sum = reduction(2 * part)
    grad_out = [left_product(context, item) for item in grad_halves]
    grad_b_out = column_sums(grad_attn)
    grad_context = right_product(grad_attn, out_w).astype(BF)
    grad_context = [lax.dynamic_slice_in_dim(grad_context, side * half, half, 1) for side in sides]
    if fast:
        down_sum.along_z()
        up_sum.one()
    grads = [None, None]
    grads[1] = attention_back(
        qkv_other, after(grad_context[1], down_sum.sent, up_sum.sent), across_one, seq_length, BF
    )
    if fast:
        up_sum.two()
    grads[0] = attention_back(
        qkv_mine, after(grad_context[0], down_sum.got, up_sum.sent), across_one, seq_length, F32
    )
    grad_qkv, grad_weights, sums = zip(*grads)
    for index in range(3):
        attn_sum.add(grad_weights[0][index], grad_weights[1][index])
    attn_sum.add(grad_out[0], grad_out[1])
    if fast:
        up_sum.along_z()
    grad_qkv = after(grad_qkv, up_sum.sent)
    grad_normed_one = sum(
        right_product(grad_qkv[i][j], attn_w[i][:, j * half : (j + 1) * half]) for i in range(2) for j in range(3)
    )
    _, norm_pull = jax.vjp(layer_norm, start, gain_one, shift_one)
    back_start, grad_gain_attn, grad_shift_attn = norm_pull(grad_normed_one)
    grad_start = grad_middle + back_start
    grad_tokens = jnp.where(absorbed, 0.0, grad_start)
    grad_mask_vector = jnp.sum(grad_start * absorbed_float, 0)
    seq_sums = jnp.sum(grad_start.reshape(seq_count, seq_length, width), 1)

    grad_b_up = paired(core, *[item.reshape(chips, hidden_part) for item in grad_b_up], 1)
    grad_b_up = grad_b_up.reshape(count, up_cols, part).transpose(1, 0, 2).reshape(up_cols, width)
    grad_b_qkv = paired(core, sums[0], sums[1], 1).reshape(3, width)
    small = jnp.stack(
        [
            grad_b_qkv[0],
            grad_b_qkv[2],
            grad_b_out,
            grad_b_down,
            grad_gain_attn,
            grad_shift_attn,
            grad_gain_mlp,
            grad_shift_mlp,
            grad_mask_vector,
        ]
    )
    seqs = count * seq_count
    small = jnp.concatenate([small, grad_b_up], 0)
    blocks = jnp.pad(small, ((0, seqs + LANES - small.shape[0]), (0, 0)))
    blocks = lax.dynamic_update_slice(blocks, seq_sums, (LANES + place * seq_count, 0)).T
    blocks = [blocks[:, :LANES], blocks[:, LANES:]]
    if fast:
        attn_sum.add(jnp.where(core == 0, *blocks), jnp.where(core == 0, *blocks[::-1]))
        attn_sum.one()
        attn_sum.two()
        attn_sum.along_z()
        attn_grad = attn_sum.columns()
        small, seq_sums = attn_grad[:, 0, 4 * half :], attn_grad[:, 1, 4 * half :]
    else:
        attn_grad = attn_sum.columns()
        small, seq_sums = [
            lax.psum_scatter(item.astype(BF), AXES, scatter_dimension=0, tiled=True).astype(F32) for item in blocks
        ]
    small = small[:, : fixed + up_cols].T
    grad_b_up = small[fixed:].reshape(hidden_part)
    onehot = (steps[:, None] == lax.broadcasted_iota(jnp.int32, (seqs, table_cols), 1)).astype(F32)
    grad_time_table = jnp.dot(seq_sums, onehot, precision=lax.Precision.HIGHEST)
    grad_w_qkv = attn_grad[:, :, : 3 * half].reshape(part, 2, 3, half).transpose(0, 2, 1, 3).reshape(part, 3 * width)
    grad_w_out = attn_grad[:, :, 3 * half : 4 * half].reshape(part, width)
    grad_w_up = up_sum.columns().reshape(part, 2, chips, hidden_part).transpose(0, 2, 1, 3)
    grad_w_up = grad_w_up.reshape(part, hidden_width)
    output = middle + (product(hidden[0], down_w[0]) + product(hidden[1], down_w[1]) + bias_down)
    return (
        output,
        grad_tokens,
        grad_w_qkv,
        grad_w_out,
        grad_w_up,
        down_sum.sums(),
        grad_time_table,
        small[0],
        small[1],
        small[2],
        grad_b_up,
        small[3],
        small[4],
        small[5],
        small[6],
        small[7],
        small[8],
    )


def solution(mesh):
    matrix, vector = P(AXES, None), P(AXES)
    fast = dict(mesh.shape) == {"fsdp": 8, "rep": 4}
    return jax.shard_map(
        functools.partial(body, fast),
        mesh=mesh,
        in_specs=(matrix, vector, vector) + (matrix,) * 6 + (vector,) * 10,
        out_specs=(matrix,) * 7 + (vector,) * 10,
        check_vma=False,
    )
```

profile of v0, /device:TPU:0, one launch (start us, length us, event | category | flops | bytes accessed | tf_op | source)
XLA Modules:
  0.0 379.6 jit_solution(323247017699969375)
XLA Ops:
  9.8 3.1 collective-permute-start.3
  15.5 6.0 %collective-permute-done.3 = bf16[48,2048]{1,0:T(8,128)(2,1)S(1)} collective-permute-done((bf16[48,2048]{1,0:T(8,128)(2,1)S(1)}, bf16[48,2048]{1,0:T(8,128)(2,1)S(1)}, u32[]{:S(2)}, u32[]{:S(2)}) %collective-permute-start.3) | collective-permute-done | bytes 196640 | tf_op jit(solution)/shard_map/ppermute | solution.py:286
  21.5 8.5 %collective-permute-done.2 = bf16[48,2048]{1,0:T(8,128)(2,1)S(1)} collective-permute-done((bf16[48,2048]{1,0:T(8,128)(2,1)S(1)}, bf16[48,2048]{1,0:T(8,128)(2,1)S(1)}, u32[]{:S(2)}, u32[]{:S(2)}) %collective-permute-start.2) | collective-permute-done | bytes 196640 | tf_op jit(solution)/shard_map/ppermute | solution.py:286
  30.3 3.6 collective-permute-start.12
  40.1 7.0 %collective-permute-done.11 = bf16[48,1536]{1,0:T(8,128)(2,1)S(1)} collective-permute-done((bf16[48,1536]{1,0:T(8,128)(2,1)S(1)}, bf16[48,1536]{1,0:T(8,128)(2,1)S(1)}, u32[]{:S(2)}, u32[]{:S(2)}) %collective-permute-start.11) | collective-permute-done | bytes 147488 | tf_op jit(solution)/shard_map/ppermute | solution.py:286
  56.1 8.4 %collective-permute-done.6 = bf16[4,2,24,2048]{3,2,0,1:T(8,128)(2,1)S(1)} collective-permute-done((bf16[4,2,24,2048]{3,2,0,1:T(8,128)(2,1)S(1)}, bf16[4,2,24,2048]{3,2,0,1:T(8,128)(2,1)S(1)}, u32[]{:S(2)}, u32[]{:S(2)}) %collective-permute-start.6) | collective-permute-done | bytes 786464 | tf_op jit(solution)/shard_map/ppermute | solution.py:283
  77.7 7.1 %collective-permute-done.13 = bf16[4,24,1536]{2,1,0:T(8,128)(2,1)S(1)} collective-permute-done((bf16[4,24,1536]{2,1,0:T(8,128)(2,1)S(1)}, bf16[4,24,1536]{2,1,0:T(8,128)(2,1)S(1)}, u32[]{:S(2)}, u32[]{:S(2)}) %collective-permute-start.13) | collective-permute-done | bytes 294944 | tf_op jit(solution)/shard_map/ppermute | solution.py:280
  101.6 7.6 %attention.2 = (bf16[3,512,384]{2,1,0:T(8,128)(2,1)S(1)}, bf16[512,384]{1,0:T(8,128)(2,1)S(1)}) custom-call(bf16[512,768]{1,0:T(8,128)(2,1)S(1)} %copy-done.1, bf16[768,2048]{1,0:T(8,128)(2,1)S(1)} %bitcast.590, bf16[768,2048]{1,0:T(8,128)(2,1)S(1)} %bitcast.591, bf16[768,2048]{1,0:T(8,128)(2,1)S(1)} %bitcast.592, f32[3,384]{1,0:T(4,128)S(1)} %get-tuple-element.388.bias_ref), custom_call_target="tpu_custom_call" | custom-call | flops 905969664 | bytes 4128768 | tf_op jit(solution)/shard_map/attention/pallas_call | solution.py:95
  112.1 8.3 %attention.3 = (bf16[3,512,384]{2,1,0:T(8,128)(2,1)S(1)}, bf16[512,384]{1,0:T(8,128)(2,1)S(1)}) custom-call(bf16[512,768]{1,0:T(8,128)(2,1)S(1)} %copy-done, bf16[768,2048]{1,0:T(8,128)(2,1)} %collective-permute-done.8.query_ref.key_ref.value_ref, bf16[768,2048]{1,0:T(8,128)(2,1)} %collective-permute-done.8.query_ref.key_ref.value_ref, ...), custom_call_target="tpu_custom_call" | custom-call | flops 905969664 | bytes 4128768 | tf_op jit(solution)/shard_map/attention/pallas_call | solution.py:95
  131.2 3.9 %collective-permute-done.20 = bf16[4,48,768]{2,1,0:T(8,128)(2,1)S(1)} collective-permute-done((bf16[4,48,768]{2,1,0:T(8,128)(2,1)S(1)}, bf16[4,48,768]{2,1,0:T(8,128)(2,1)S(1)}, u32[]{:S(2)}, u32[]{:S(2)}) %collective-permute-start.20) | collective-permute-done | bytes 294944 | tf_op jit(solution)/shard_map/ppermute | solution.py:280
  165.2 5.6 %feed.3 = (bf16[512,1536]{1,0:T(8,128)(2,1)S(1)}, f32[512,1536]{1,0:T(8,128)S(1)}) custom-call(bf16[512,768]{1,0:T(8,128)(2,1)S(1)} %copy-done.5, bf16[768,1536]{1,0:T(8,128)(2,1)} %collective-permute-done.24.weight_ref, f32[1,1536]{1,0:T(1,128)S(1)} %get-tuple-element.386.bias_ref), custom_call_target="tpu_custom_call" | custom-call | flops 1207959552 | bytes 7864320 | tf_op jit(solution)/shard_map/feed/pallas_call | solution.py:206
  174.2 5.3 %feed.2 = (bf16[512,1536]{1,0:T(8,128)(2,1)S(1)}, f32[512,1536]{1,0:T(8,128)S(1)}) custom-call(bf16[512,768]{1,0:T(8,128)(2,1)S(1)} %copy-done.3, bf16[768,1536]{1,0:T(8,128)(2,1)} %bitcast.56.weight_ref, f32[1,1536]{1,0:T(1,128)S(1)} %get-tuple-element.387.bias_ref), custom_call_target="tpu_custom_call" | custom-call | flops 1207959552 | bytes 7864320 | tf_op jit(solution)/shard_map/feed/pallas_call | solution.py:206
  184.8 3.2 fusion.187
  188.0 5.8 %feed_back.3 = (bf16[512,1536]{1,0:T(8,128)(2,1)S(1)}, f32[1,1536]{1,0:T(1,128)S(1)}, bf16[768,1536]{1,0:T(8,128)(2,1)}) custom-call(bf16[512,768]{1,0:T(8,128)(2,1)S(1)} %copy-done.2, bf16[1536,768]{1,0:T(8,128)(2,1)} %collective-permute-done.25.weight_ref, f32[512,1536]{1,0:T(8,128)S(1)} %get-tuple-element.83.slope_ref, bf16[768,512]{1,0:T(8,128)(2,1)S(1)} %copy-done.7), custom_call_target="tpu_custom_call" | custom-call | flops 2415919104 | bytes 13369344 | tf_op jit(solution)/shard_map/feed_back/pallas_call | solution.py:242
  195.0 4.3 %add_add_fusion.5 = f32[512,768]{0,1:T(8,128)} fusion(f32[512,768]{0,1:T(8,128)S(1)} %copy-done.25, f32[512,768]{0,1:T(8,128)S(1)} %fusion.187, bf16[512,1536]{1,0:T(8,128)(2,1)S(1)} %get-tuple-element.79, bf16[1536,768]{1,0:T(8,128)(2,1)} %collective-permute-done.25.weight_ref, f32[768]{0:T(1024)S(1)} %copy-done.98), kind=kOutput, calls=%fused_computation.41 | convolution fusion | flops 1209139200 | bytes 8653824 | tf_op jit(solution)/shard_map/dot_general | solution.py:30
  216.3 5.1 %feed_back.2 = (bf16[512,1536]{1,0:T(8,128)(2,1)S(1)}, f32[1,1536]{1,0:T(1,128)S(1)}, f32[768,1536]{1,0:T(8,128)S(1)}) custom-call(bf16[512,768]{1,0:T(8,128)(2,1)S(1)} %copy-done.4, bf16[1536,768]{1,0:T(8,128)(2,1)} %bitcast.76.weight_ref, f32[512,1536]{1,0:T(8,128)S(1)} %copy-done.14, bf16[768,512]{1,0:T(8,128)(2,1)S(1)} %copy-done.8), custom_call_target="tpu_custom_call" | custom-call | flops 2415919104 | bytes 13369344 | tf_op jit(solution)/shard_map/feed_back/pallas_call | solution.py:242
  239.0 3.2 fusion.189
  242.3 3.5 multiply_reduce_fusion.1
  261.2 9.3 %attention_back.3 = (bf16[3,512,384]{2,1,0:T(8,128)(2,1)S(1)}, bf16[3,768,384]{2,1,0:T(8,128)(2,1)S(1)}, f32[3,384]{1,0:T(4,128)S(1)}) custom-call(bf16[3,512,384]{2,1,0:T(8,128)(2,1)S(1)} %copy-done.12, bf16[512,384]{1,0:T(8,128)(2,1)S(1)} %get-tuple-element.93.grad_ref, bf16[768,512]{1,0:T(8,128)(2,1)S(1)} %copy-done.6), custom_call_target="tpu_custom_call" | custom-call | flops 905969664 | bytes 7077888 | tf_op jit(solution)/shard_map/attention_back/pallas_call | solution.py:155
  275.1 11.9 %collective-permute-done.35 = bf16[4,2,24,1536]{3,2,0,1:T(8,128)(2,1)S(1)} collective-permute-done((bf16[4,2,24,1536]{3,2,0,1:T(8,128)(2,1)S(1)}, bf16[4,2,24,1536]{3,2,0,1:T(8,128)(2,1)S(1)}, u32[]{:S(2)}, u32[]{:S(2)}) %collective-permute-start.35) | collective-permute-done | bytes 589856 | tf_op jit(solution)/shard_map/ppermute | solution.py:280
  288.9 9.6 %attention_back.2 = (bf16[3,512,384]{2,1,0:T(8,128)(2,1)S(1)}, f32[3,768,384]{2,1,0:T(8,128)S(1)}, f32[3,384]{1,0:T(4,128)S(1)}) custom-call(bf16[3,512,384]{2,1,0:T(8,128)(2,1)S(1)} %copy-done.10, bf16[512,384]{1,0:T(8,128)(2,1)S(1)} %get-tuple-element.90.grad_ref, bf16[768,512]{1,0:T(8,128)(2,1)S(1)} %copy-done.6), custom_call_target="tpu_custom_call" | custom-call | flops 905969664 | bytes 7077888 | tf_op jit(solution)/shard_map/attention_back/pallas_call | solution.py:155
  335.7 12.1 %collective-permute-done.44 = bf16[4,2,24,1664]{3,2,1,0:T(8,128)(2,1)S(1)} collective-permute-done((bf16[4,2,24,1664]{3,2,1,0:T(8,128)(2,1)}, bf16[4,2,24,1664]{3,2,1,0:T(8,128)(2,1)S(1)}, u32[]{:S(2)}, u32[]{:S(2)}) %collective-permute-start.44) | collective-permute-done | bytes 639008 | tf_op jit(solution)/shard_map/ppermute | solution.py:280
  351.8 5.5 %collective-permute-done.45 = bf16[4,24,1664]{2,1,0:T(8,128)(2,1)S(1)} collective-permute-done((bf16[4,24,1664]{2,1,0:T(8,128)(2,1)S(1)}, bf16[4,24,1664]{2,1,0:T(8,128)(2,1)S(1)}, u32[]{:S(2)}, u32[]{:S(2)}) %collective-permute-start.45) | collective-permute-done | bytes 319520 | tf_op jit(solution)/shard_map/ppermute | solution.py:283
  364.7 8.1 %collective-permute-done.49 = bf16[48,1664]{1,0:T(8,128)(2,1)S(1)} collective-permute-done((bf16[48,1664]{1,0:T(8,128)(2,1)S(1)}, bf16[48,1664]{1,0:T(8,128)(2,1)S(1)}, u32[]{:S(2)}, u32[]{:S(2)}) %collective-permute-start.49) | collective-permute-done | bytes 159776 | tf_op jit(solution)/shard_map/ppermute | solution.py:286
  (592 shorter events, 220.3 us)
Async XLA Ops:
  12.9 17.1 %collective-permute-start.2 = (bf16[48,2048]{1,0:T(8,128)(2,1)S(1)}, bf16[48,2048]{1,0:T(8,128)(2,1)S(1)}, u32[]{:S(2)}, u32[]{:S(2)}) collective-permute-start(bf16[48,2048]{1,0:T(8,128)(2,1)S(1)} %pad_maximum_fusion.19), channel_id=1, source_target_pairs={{0,16},{4,20},{8,24},{12,28},{16,0},{20,4},{24,8},{28,12},{1,17},{... | collective-permute-start | bytes 589832 | tf_op jit(solution)/shard_map/ppermute | solution.py:286
  47.8 16.7 %collective-permute-start.6 = (bf16[4,2,24,2048]{3,2,0,1:T(8,128)(2,1)S(1)}, bf16[4,2,24,2048]{3,2,0,1:T(8,128)(2,1)S(1)}, u32[]{:S(2)}, u32[]{:S(2)}) collective-permute-start(bf16[4,2,24,2048]{3,2,0,1:T(8,128)(2,1)S(1)} %pad_maximum_fusion.1), channel_id=1, source_target_pairs={{0,4},{4,0},{8,12},{12,8},{16,20},{20,16},{24,28},{28,24},{1,5},{5... | collective-permute-start | bytes 2359304 | tf_op jit(solution)/shard_map/ppermute | solution.py:283
  51.5 21.8 %collective-permute-start.19 = (bf16[96,768]{1,0:T(8,128)(2,1)}, bf16[96,768]{1,0:T(8,128)(2,1)}, u32[]{:S(2)}, u32[]{:S(2)}) collective-permute-start(bf16[96,768]{1,0:T(8,128)(2,1)} %convert_element_type.366), channel_id=1, source_target_pairs={{0,8},{4,12},{8,0},{12,4},{16,24},{20,28},{24,16},{28,20},{1,9},{5... | collective-permute-start | bytes 442376 | tf_op jit(solution)/shard_map/ppermute | solution.py:286
  53.7 19.7 %collective-permute-start.18 = (bf16[96,768]{1,0:T(8,128)(2,1)}, bf16[96,768]{1,0:T(8,128)(2,1)}, u32[]{:S(2)}, u32[]{:S(2)}) collective-permute-start(bf16[96,768]{1,0:T(8,128)(2,1)} %convert_element_type.366), channel_id=1, source_target_pairs={{0,16},{4,20},{8,24},{12,28},{16,0},{20,4},{24,8},{28,12},{1,17},{... | collective-permute-start | bytes 442376 | tf_op jit(solution)/shard_map/ppermute | solution.py:286
  54.6 18.7 %collective-permute-start.17 = (bf16[96,768]{1,0:T(8,128)(2,1)}, bf16[96,768]{1,0:T(8,128)(2,1)}, u32[]{:S(2)}, u32[]{:S(2)}) collective-permute-start(bf16[96,768]{1,0:T(8,128)(2,1)} %convert_element_type.366), channel_id=1, source_target_pairs={{0,24},{4,28},{8,16},{12,20},{16,8},{20,12},{24,0},{28,4},{1,25},{... | collective-permute-start | bytes 442376 | tf_op jit(solution)/shard_map/ppermute | solution.py:286
  67.2 19.7 %collective-permute-start.8 = (bf16[768,2048]{1,0:T(8,128)(2,1)S(1)}, bf16[768,2048]{1,0:T(8,128)(2,1)}, u32[]{:S(2)}, u32[]{:S(2)}) collective-permute-start(bf16[768,2048]{1,0:T(8,128)(2,1)S(1)} %bitcast.588), channel_id=1, source_target_pairs={{0,1},{1,0},{2,3},{3,2},{4,5},{5,4},{6,7},{7,6},{8,9},{9,8},{10,11... | collective-permute-start | bytes 9437192 | tf_op jit(solution)/shard_map/ppermute | solution.py:277
  129.7 34.3 %collective-permute-start.24 = (bf16[768,1536]{1,0:T(8,128)(2,1)}, bf16[768,1536]{1,0:T(8,128)(2,1)}, u32[]{:S(2)}, u32[]{:S(2)}) collective-permute-start(bf16[768,1536]{1,0:T(8,128)(2,1)} %bitcast.56.weight_ref), channel_id=1, source_target_pairs={{0,1},{1,0},{2,3},{3,2},{4,5},{5,4},{6,7},{7,6},{8,9},{9,8},{10,11... | collective-permute-start | bytes 7077896 | tf_op jit(solution)/shard_map/ppermute | solution.py:277
  161.7 26.3 %collective-permute-start.25 = (bf16[1536,768]{1,0:T(8,128)(2,1)}, bf16[1536,768]{1,0:T(8,128)(2,1)}, u32[]{:S(2)}, u32[]{:S(2)}) collective-permute-start(bf16[1536,768]{1,0:T(8,128)(2,1)} %bitcast.76.weight_ref), channel_id=1, source_target_pairs={{0,1},{1,0},{2,3},{3,2},{4,5},{5,4},{6,7},{7,6},{8,9},{9,8},{10,11... | collective-permute-start | bytes 7077896 | tf_op jit(solution)/shard_map/ppermute | solution.py:277
  173.6 28.7 %collective-permute-start.26 = (bf16[1536,768]{1,0:T(8,128)(2,1)}, bf16[1536,768]{1,0:T(8,128)(2,1)}, u32[]{:S(2)}, u32[]{:S(2)}) collective-permute-start(bf16[1536,768]{1,0:T(8,128)(2,1)} %convolution_convert_fusion), channel_id=1, source_target_pairs={{0,1},{1,0},{2,3},{3,2},{4,5},{5,4},{6,7},{7,6},{8,9},{9,8},{10,11... | collective-permute-start | bytes 7077896 | tf_op jit(solution)/shard_map/ppermute | solution.py:277
  195.0 56.8 %collective-permute-start.34 = (bf16[768,1536]{1,0:T(8,128)(2,1)}, bf16[768,1536]{1,0:T(8,128)(2,1)}, u32[]{:S(2)}, u32[]{:S(2)}) collective-permute-start(bf16[768,1536]{1,0:T(8,128)(2,1)} %get-tuple-element.89), channel_id=1, source_target_pairs={{0,1},{1,0},{2,3},{3,2},{4,5},{5,4},{6,7},{7,6},{8,9},{9,8},{10,11... | collective-permute-start | bytes 7077896 | tf_op jit(solution)/shard_map/ppermute | solution.py:277
  207.5 25.6 %collective-permute-start.28 = (bf16[4,2,48,768]{3,2,0,1:T(8,128)(2,1)}, bf16[4,2,48,768]{3,2,0,1:T(8,128)(2,1)}, u32[]{:S(2)}, u32[]{:S(2)}) collective-permute-start(bf16[4,2,48,768]{3,2,0,1:T(8,128)(2,1)} %fusion.16), channel_id=1, source_target_pairs={{0,4},{4,0},{8,12},{12,8},{16,20},{20,16},{24,28},{28,24},{1,5},{5... | collective-permute-start | bytes 1769480 | tf_op jit(solution)/shard_map/ppermute | solution.py:283
  208.9 27.0 %collective-permute-start.27 = (bf16[4,2,48,768]{3,2,0,1:T(8,128)(2,1)}, bf16[4,2,48,768]{3,2,0,1:T(8,128)(2,1)}, u32[]{:S(2)}, u32[]{:S(2)}) collective-permute-start(bf16[4,2,48,768]{3,2,0,1:T(8,128)(2,1)} %fusion.15), channel_id=1, source_target_pairs={{0,2},{1,3},{2,0},{3,1},{4,6},{5,7},{6,4},{7,5},{8,10},{9,11},{10,... | collective-permute-start | bytes 1769480 | tf_op jit(solution)/shard_map/ppermute | solution.py:280
  234.7 20.2 %collective-permute-start.30 = (bf16[4,48,768]{2,1,0:T(8,128)(2,1)S(1)}, bf16[4,48,768]{2,1,0:T(8,128)(2,1)S(1)}, u32[]{:S(2)}, u32[]{:S(2)}) collective-permute-start(bf16[4,48,768]{2,1,0:T(8,128)(2,1)S(1)} %fusion.63), channel_id=1, source_target_pairs={{0,2},{1,3},{2,0},{3,1},{4,6},{5,7},{6,4},{7,5},{8,10},{9,11},{10,... | collective-permute-start | bytes 884744 | tf_op jit(solution)/shard_map/ppermute | solution.py:280
  237.4 17.8 %collective-permute-start.29 = (bf16[4,48,768]{2,1,0:T(8,128)(2,1)S(1)}, bf16[4,48,768]{2,1,0:T(8,128)(2,1)S(1)}, u32[]{:S(2)}, u32[]{:S(2)}) collective-permute-start(bf16[4,48,768]{2,1,0:T(8,128)(2,1)S(1)} %fusion.62), channel_id=1, source_target_pairs={{0,4},{4,0},{8,12},{12,8},{16,20},{20,16},{24,28},{28,24},{1,5},{5... | collective-permute-start | bytes 884744 | tf_op jit(solution)/shard_map/ppermute | solution.py:283
  250.0 23.4 %collective-permute-start.42 = (bf16[768,384]{1,0:T(8,128)(2,1)S(1)}, bf16[768,384]{1,0:T(8,128)(2,1)S(1)}, u32[]{:S(2)}, u32[]{:S(2)}) collective-permute-start(bf16[768,384]{1,0:T(8,128)(2,1)S(1)} %convolution_convert_fusion.2), channel_id=1, source_target_pairs={{0,1},{1,0},{2,3},{3,2},{4,5},{5,4},{6,7},{7,6},{8,9},{9,8},{10,11... | collective-permute-start | bytes 1769480 | tf_op jit(solution)/shard_map/ppermute | solution.py:277
  254.3 19.6 %collective-permute-start.36 = (bf16[4,2,24,1536]{3,2,1,0:T(8,128)(2,1)S(1)}, bf16[4,2,24,1536]{3,2,1,0:T(8,128)(2,1)S(1)}, u32[]{:S(2)}, u32[]{:S(2)}) collective-permute-start(bf16[4,2,24,1536]{3,2,1,0:T(8,128)(2,1)S(1)} %fusion.14), channel_id=1, source_target_pairs={{0,4},{4,0},{8,12},{12,8},{16,20},{20,16},{24,28},{28,24},{1,5},{5... | collective-permute-start | bytes 1769480 | tf_op jit(solution)/shard_map/ppermute | solution.py:283
  271.9 27.8 %collective-permute-start.41 = (bf16[768,384]{1,0:T(8,128)(2,1)S(1)}, bf16[768,384]{1,0:T(8,128)(2,1)S(1)}, u32[]{:S(2)}, u32[]{:S(2)}) collective-permute-start(bf16[768,384]{1,0:T(8,128)(2,1)S(1)} %get-tuple-element.259), channel_id=1, source_target_pairs={{0,1},{1,0},{2,3},{3,2},{4,5},{5,4},{6,7},{7,6},{8,9},{9,8},{10,11... | collective-permute-start | bytes 1769480 | tf_op jit(solution)/shard_map/ppermute | solution.py:277
  272.5 27.3 %collective-permute-start.40 = (bf16[768,384]{1,0:T(8,128)(2,1)S(1)}, bf16[768,384]{1,0:T(8,128)(2,1)S(1)}, u32[]{:S(2)}, u32[]{:S(2)}) collective-permute-start(bf16[768,384]{1,0:T(8,128)(2,1)S(1)} %get-tuple-element.260), channel_id=1, source_target_pairs={{0,1},{1,0},{2,3},{3,2},{4,5},{5,4},{6,7},{7,6},{8,9},{9,8},{10,11... | collective-permute-start | bytes 1769480 | tf_op jit(solution)/shard_map/ppermute | solution.py:277
  273.4 25.4 %collective-permute-start.39 = (bf16[768,384]{1,0:T(8,128)(2,1)S(1)}, bf16[768,384]{1,0:T(8,128)(2,1)S(1)}, u32[]{:S(2)}, u32[]{:S(2)}) collective-permute-start(bf16[768,384]{1,0:T(8,128)(2,1)S(1)} %get-tuple-element.261), channel_id=1, source_target_pairs={{0,1},{1,0},{2,3},{3,2},{4,5},{5,4},{6,7},{7,6},{8,9},{9,8},{10,11... | collective-permute-start | bytes 1769480 | tf_op jit(solution)/shard_map/ppermute | solution.py:277
  274.2 28.8 %collective-permute-start.38 = (bf16[4,24,1536]{2,1,0:T(8,128)(2,1)S(1)}, bf16[4,24,1536]{2,1,0:T(8,128)(2,1)S(1)}, u32[]{:S(2)}, u32[]{:S(2)}) collective-permute-start(bf16[4,24,1536]{2,1,0:T(8,128)(2,1)S(1)} %fusion.65), channel_id=1, source_target_pairs={{0,2},{1,3},{2,0},{3,1},{4,6},{5,7},{6,4},{7,5},{8,10},{9,11},{10,... | collective-permute-start | bytes 884744 | tf_op jit(solution)/shard_map/ppermute | solution.py:280
  304.1 28.1 %collective-permute-start.54 = (bf16[48,1536]{1,0:T(8,128)(2,1)}, bf16[48,1536]{1,0:T(8,128)(2,1)}, u32[]{:S(2)}, u32[]{:S(2)}) collective-permute-start(bf16[48,1536]{1,0:T(8,128)(2,1)} %get-tuple-element.277), channel_id=1, source_target_pairs={{0,24},{4,28},{8,16},{12,20},{16,8},{20,12},{24,0},{28,4},{1,25},{... | collective-permute-start | bytes 442376 | tf_op jit(solution)/shard_map/ppermute | solution.py:286
  306.5 25.8 %collective-permute-start.52 = (bf16[48,1536]{1,0:T(8,128)(2,1)}, bf16[48,1536]{1,0:T(8,128)(2,1)}, u32[]{:S(2)}, u32[]{:S(2)}) collective-permute-start(bf16[48,1536]{1,0:T(8,128)(2,1)} %get-tuple-element.278), channel_id=1, source_target_pairs={{0,8},{4,12},{8,0},{12,4},{16,24},{20,28},{24,16},{28,20},{1,9},{5... | collective-permute-start | bytes 442376 | tf_op jit(solution)/shard_map/ppermute | solution.py:286
  307.6 24.6 %collective-permute-start.53 = (bf16[48,1536]{1,0:T(8,128)(2,1)}, bf16[48,1536]{1,0:T(8,128)(2,1)}, u32[]{:S(2)}, u32[]{:S(2)}) collective-permute-start(bf16[48,1536]{1,0:T(8,128)(2,1)} %get-tuple-element.279), channel_id=1, source_target_pairs={{0,16},{4,20},{8,24},{12,28},{16,0},{20,4},{24,8},{28,12},{1,17},{... | collective-permute-start | bytes 442376 | tf_op jit(solution)/shard_map/ppermute | solution.py:286
  334.1 16.8 %collective-permute-start.46 = (bf16[4,2,24,1664]{3,2,1,0:T(8,128)(2,1)}, bf16[4,2,24,1664]{3,2,1,0:T(8,128)(2,1)S(1)}, u32[]{:S(2)}, u32[]{:S(2)}) collective-permute-start(bf16[4,2,24,1664]{3,2,1,0:T(8,128)(2,1)} %constant_dynamic-update-slice_fusion.6), channel_id=1, source_target_pairs={{0,4},{4,0},{8,12},{12,8},{16,20},{20,16},{24,28},{28,24},{1,5},{5... | collective-permute-start | bytes 1916936 | tf_op jit(solution)/shard_map/ppermute | solution.py:283
  (144 other events, 678.6 us)
where the time goes:
time: 386 us; the launch traced here: 380 us
  waiting for transfers between devices  92 us (24%)
  local copies, waits for them, and re-layouts  84.9 us (22%)
  starting transfers between devices  59.2 us (15%)
  Pallas kernels  56.7 us (15%)
  other arithmetic  51.9 us (13%)
  matrix products  31.7 us (8%)
    ppermute x12, waiting for transfers between devices, to_x(): return lax.ppermute(value, 'rep', [(i, i ^ 2) for i in range(4)])  39.8 us
    ppermute x18, waiting for transfers between devices, to_z(): return lax.ppermute(value, 'fsdp', [(i, i ^ 2 * step) for i in range(8)])  31.3 us
    ppermute x18, starting transfers between devices, to_z(): return lax.ppermute(value, 'fsdp', [(i, i ^ 2 * step) for i in range(8)])  30.9 us
    dot_general x18, matrix products, contract(): return lax.dot_general(left, right, dims, preferred_element_type=F32)  30.7 us
    unnamed x233, local copies, waits for them, and re-layouts  23.8 us
    ppermute x12, waiting for transfers between devices, to_y(): return lax.ppermute(value, 'fsdp', [(i, i ^ 1) for i in range(8)])  19.3 us
    pallas_call x2, Pallas kernels, attention_back(): pl.pallas_call(functools.partial(attention_back_kernel, length, 1.0 / mat...  19 us
    pallas_call x2, Pallas kernels, attention(): pl.pallas_call(functools.partial(attention_kernel, length, 1.0 / math.sqr...  15.9 us
  transfers between devices with their start and end apart: 56, of which 20 were waited for; matrix products, arithmetic and copies ran while one was open for 35% of the time, Pallas kernels for 13%

commit v1 on v0

--- a/solution.py
+++ b/solution.py
@@ -19,12 +19,6 @@
 GELU_INNER = 0.044715
 
 
-def layer_norm(values, gain, shift):
-    center = values - jnp.mean(values, -1, keepdims=True)
-    spread = jnp.mean(center * center, -1, keepdims=True)
-    return center * lax.rsqrt(spread + EPSILON) * gain + shift
-
-
 def contract(left, right, left_dim, right_dim):
     dims = (((left_dim,), (right_dim,)), ((), ()))
     return lax.dot_general(left, right, dims, preferred_element_type=F32)
@@ -40,10 +34,6 @@
 
 def right_product(left, right):
     return contract(left, right, 1, 1)
-
-
-def column_sums(values):
-    return jnp.sum(values.astype(F32), 0)
 
 
 def pick(array, index, axis):
@@ -100,7 +90,7 @@
             weight_spec(0),
             weight_spec(1),
             weight_spec(2),
-            pl.BlockSpec((3, LANES), lambda pair: (0, pair)),
+            pl.BlockSpec((8, LANES), lambda pair: (0, pair)),
         ],
         out_specs=[
             pl.BlockSpec((3, tokens, LANES), lambda pair: (0, 0, pair)),
@@ -180,13 +170,13 @@
     )(qkv, grad, rows_across)
 
 
-def feed_kernel(rows_ref, weight_ref, bias_ref, hidden_ref, slope_ref, pre_ref):
+def feed_kernel(side, rows_ref, weight_ref, bias_ref, hidden_ref, slope_ref, pre_ref):
     pre_ref[...] = product(rows_ref[...], weight_ref[...])
     step = 32
 
     def chunk(index, carry):
         span = pl.ds(pl.multiple_of(index * step, step), step)
-        pre = pre_ref[span, :] + bias_ref[...]
+        pre = pre_ref[span, :] + bias_ref[side : side + 1, :]
         square = pre * pre
         bend = jnp.tanh(GELU_OUTER * (pre + GELU_INNER * (square * pre)))
         share = 0.5 * (1.0 + bend)
@@ -198,18 +188,18 @@
     lax.fori_loop(0, rows_ref.shape[0] // step, chunk, 0, unroll=2)
 
 
-def feed(rows, weight, bias, block=512):
+def feed(rows, weight, bias, side, block=512):
     tokens, width = rows.shape
     columns = weight.shape[1]
     block = math.gcd(block, columns)
     out = pl.BlockSpec((tokens, block), lambda step: (0, step))
     return pl.pallas_call(
-        feed_kernel,
+        functools.partial(feed_kernel, side),
         grid=(columns // block,),
         in_specs=[
             pl.BlockSpec((tokens, width), lambda step: (0, 0)),
             pl.BlockSpec((width, block), lambda step: (0, step)),
-            pl.BlockSpec((1, block), lambda step: (0, step)),
+            pl.BlockSpec((8, block), lambda step: (0, step)),
         ],
         out_specs=[out, out],
         out_shape=[
@@ -266,6 +256,363 @@
         ),
         name="feed_back",
     )(grad, weight, slope, rows_across)
+
+
+def chosen_side(core, mine, other):
+    return jnp.where(core == 0, mine, other), jnp.where(core == 0, other, mine)
+
+
+def normalized(values):
+    center = values - jnp.mean(values, -1, keepdims=True)
+    rate = lax.rsqrt(jnp.mean(center * center, -1, keepdims=True) + EPSILON)
+    return center * rate, rate
+
+
+def start_kernel(
+    fixed, up_cols, table_cols, seq_count, parts,
+    place_ref, tokens_ref, mask_ref, table_mine_ref, table_other_ref,
+    rows_ref, start_ref, normed_ref, across_ref, bias_mine_ref, bias_other_ref, bias_up_ref,
+):
+    core = place_ref[0]
+    step = pl.program_id(0)
+    width = tokens_ref.shape[1]
+    half = width // 2
+    chips, part, hidden_part = parts
+
+    @pl.when(step == 0)
+    def _():
+        count, columns = rows_ref.shape[0], table_mine_ref.shape[1]
+        row = lax.broadcasted_iota(jnp.int32, (count, columns), 0)
+        wanted = table_cols + row - seq_count
+        for index in range(seq_count):
+            wanted = jnp.where(row == index, place_ref[2 + index], wanted)
+        column = lax.broadcasted_iota(jnp.int32, (count, columns), 1)
+        rows = 0.0
+        for side, table in ((core, table_mine_ref), (1 - core, table_other_ref)):
+            hit = jnp.where(wanted == column + side * columns, 1.0, 0.0).astype(BF)
+            rows = rows + right_product(hit, table[...])
+        rows_ref[...] = rows
+        for ref, side in ((bias_mine_ref, core), (bias_other_ref, 1 - core)):
+            ref[...] = jnp.zeros_like(ref)
+            for index in (0, 1):
+                line = rows_ref[seq_count + index : seq_count + index + 1, :]
+                ref[2 * index : 2 * index + 1, :] = jnp.where(side == 0, line[:, :half], line[:, half:])
+        for chip in range(chips):
+            for index in range(up_cols):
+                line = rows_ref[seq_count + fixed + index : seq_count + fixed + index + 1, :]
+                pair = [line[:, (2 * chip + i) * part : (2 * chip + i + 1) * part] for i in range(2)]
+                where = slice(chip * hidden_part + index * part, chip * hidden_part + (index + 1) * part)
+                bias_up_ref[0:1, where], bias_up_ref[1:2, where] = chosen_side(core, *pair)
+
+    small = seq_count
+    mask = mask_ref[...]
+    start = jnp.where(mask > 0.0, rows_ref[small + 8 : small + 9, :], tokens_ref[...])
+    start = start + rows_ref[pl.ds(step, 1), :]
+    start_ref[...] = start
+    normed, _ = normalized(start)
+    normed = normed * rows_ref[small + 4 : small + 5, :] + rows_ref[small + 5 : small + 6, :]
+    normed_ref[...] = normed.astype(BF)
+    across_ref[...] = normed.T.astype(BF)
+
+
+def start_rows(place, tokens, mask, weights, fixed, up_cols, table_cols, small_cols, chips, hidden_part):
+    count, width = tokens.shape
+    seq_count = place.shape[0] - 2
+    length = count // seq_count
+    half = width // 2
+    row_count = -(-(seq_count + small_cols) // 8) * 8
+    table_half = weights[0].shape[1] - 4 * half
+    tables = 4 * half // table_half
+    table_spec = pl.BlockSpec((width, table_half), lambda step: (0, tables))
+    rows_spec = pl.BlockSpec((length, width), lambda step: (step, 0))
+
+    def fixed_spec(*shape):
+        return pl.BlockSpec(shape, lambda step: (0,) * len(shape))
+
+    return pl.pallas_call(
+        functools.partial(
+            start_kernel, fixed, up_cols, table_cols, seq_count, (chips, width // (2 * chips), hidden_part)
+        ),
+        grid=(seq_count,),
+        in_specs=[
+            pl.BlockSpec(memory_space=pltpu.SMEM),
+            rows_spec,
+            pl.BlockSpec((length, 1), lambda step: (step, 0)),
+            table_spec,
+            table_spec,
+        ],
+        out_specs=[
+            fixed_spec(row_count, width),
+            rows_spec,
+            rows_spec,
+            pl.BlockSpec((width, length), lambda step: (0, step)),
+            fixed_spec(8, half),
+            fixed_spec(8, half),
+            fixed_spec(8, chips * hidden_part),
+        ],
+        out_shape=[
+            jax.ShapeDtypeStruct((row_count, width), F32),
+            jax.ShapeDtypeStruct((count, width), F32),
+            jax.ShapeDtypeStruct((count, width), BF),
+            jax.ShapeDtypeStruct((width, count), BF),
+            jax.ShapeDtypeStruct((8, half), F32),
+            jax.ShapeDtypeStruct((8, half), F32),
+            jax.ShapeDtypeStruct((8, chips * hidden_part), F32),
+        ],
+        compiler_params=pltpu.CompilerParams(vmem_limit_bytes=VMEM_BYTES),
+        cost_estimate=pl.CostEstimate(
+            flops=4 * row_count * width * table_half, bytes_accessed=14 * count * width, transcendentals=0
+        ),
+        name="start_rows",
+    )(place, tokens, mask, *weights)
+
+
+def middle_kernel(
+    small, place_ref, context_mine_ref, context_other_ref, out_mine_ref, out_other_ref, start_ref, rows_ref,
+    middle_ref, normed_ref, across_ref,
+):
+    core = place_ref[0]
+    half = context_mine_ref.shape[1]
+    contexts = chosen_side(core, context_mine_ref[...], context_other_ref[...])
+    outs = chosen_side(core, out_mine_ref[...], out_other_ref[...])
+    for index, out in enumerate(outs):
+        span = slice(index * half, (index + 1) * half)
+        total = product(contexts[0], out[:half]) + product(contexts[1], out[half:])
+        middle_ref[:, span] = start_ref[:, span] + (total + rows_ref[small + 2 : small + 3, span])
+    normed, _ = normalized(middle_ref[...])
+    normed = normed * rows_ref[small + 6 : small + 7, :] + rows_ref[small + 7 : small + 8, :]
+    normed_ref[...] = normed.astype(BF)
+    across_ref[...] = normed.T.astype(BF)
+
+
+def middle_rows(place, contexts, weights, start, rows, block=256):
+    count, width = start.shape
+    half = width // 2
+    small = place.shape[0] - 2
+    block = math.gcd(block, count)
+    out_spec = pl.BlockSpec((width, half), lambda step: (0, 3))
+    rows_spec = pl.BlockSpec((block, width), lambda step: (step, 0))
+    half_spec = pl.BlockSpec((block, half), lambda step: (step, 0))
+    return pl.pallas_call(
+        functools.partial(middle_kernel, small),
+        grid=(count // block,),
+        in_specs=[
+            pl.BlockSpec(memory_space=pltpu.SMEM),
+            half_spec,
+            half_spec,
+            out_spec,
+            out_spec,
+            rows_spec,
+            pl.BlockSpec(rows.shape, lambda step: (0, 0)),
+        ],
+        out_specs=[rows_spec, rows_spec, pl.BlockSpec((width, block), lambda step: (0, step))],
+        out_shape=[
+            jax.ShapeDtypeStruct((count, width), F32),
+            jax.ShapeDtypeStruct((count, width), BF),
+            jax.ShapeDtypeStruct((width, count), BF),
+        ],
+        compiler_params=pltpu.CompilerParams(vmem_limit_bytes=VMEM_BYTES),
+        cost_estimate=pl.CostEstimate(
+            flops=2 * count * width * width, bytes_accessed=14 * count * width + 2 * width * width, transcendentals=0
+        ),
+        name="middle_rows",
+    )(place, *contexts, *weights, start, rows)
+
+
+def norm_back(values, gain, grad):
+    unit, rate = normalized(values)
+    scaled = grad * gain
+    back = scaled - jnp.mean(scaled, -1, keepdims=True) - unit * jnp.mean(scaled * unit, -1, keepdims=True)
+    return rate * back, grad * unit
+
+
+def middle_back_kernel(
+    small, place_ref, pre_mine_ref, pre_other_ref, up_mine_ref, up_other_ref, middle_ref, cotangent_ref, mask_ref,
+    rows_ref, context_mine_ref, context_other_ref, out_mine_ref, out_other_ref,
+    grad_ref, context_grad_mine_ref, context_grad_other_ref, out_grad_mine_ref, out_grad_other_ref, sums_ref,
+    normed_ref, total_ref,
+):
+    core = place_ref[0]
+    step = pl.program_id(0)
+    half = context_mine_ref.shape[1]
+
+    @pl.when(step == 0)
+    def _():
+        sums_ref[...] = jnp.zeros_like(sums_ref)
+        total_ref[...] = jnp.zeros_like(total_ref)
+
+    normed_ref[...] = right_product(pre_mine_ref[...], up_mine_ref[...]) + right_product(
+        pre_other_ref[...], up_other_ref[...]
+    )
+    grad = normed_ref[...]
+    direct = cotangent_ref[...] * mask_ref[...]
+    back, shares = norm_back(middle_ref[...], rows_ref[small + 6 : small + 7, :], grad)
+    back = direct + back
+    grad_ref[...] = back
+    low = back.astype(BF)
+    for index, item in enumerate((low.astype(F32), direct.astype(BF).astype(F32), shares, grad)):
+        sums_ref[index : index + 1, :] += jnp.sum(item, 0, keepdims=True)
+    lows = (low[:, :half], low[:, half:])
+    contexts = chosen_side(core, context_mine_ref[...], context_other_ref[...])
+    outs = chosen_side(core, out_mine_ref[...], out_other_ref[...])
+    context_grads = [
+        (right_product(lows[0], outs[0][span]) + right_product(lows[1], outs[1][span])).astype(BF)
+        for span in (slice(0, half), slice(half, None))
+    ]
+    context_grad_mine_ref[...], context_grad_other_ref[...] = chosen_side(core, *context_grads)
+    for index, item in enumerate(chosen_side(core, *lows)):
+        for side, context in enumerate(contexts):
+            total_ref[index, side * half : (side + 1) * half, :] += left_product(context, item)
+
+    @pl.when(step == pl.num_programs(0) - 1)
+    def _():
+        out_grad_mine_ref[...] = total_ref[0]
+        out_grad_other_ref[...] = total_ref[1].astype(BF)
+
+
+def middle_back(place, grads, ups, middle, cotangent, mask, rows, contexts, weights, block=256):
+    count, width = middle.shape
+    half = width // 2
+    hidden_half = ups[0].shape[1]
+    small = place.shape[0] - 2
+    block = math.gcd(block, count)
+
+    def over_rows(columns):
+        return pl.BlockSpec((block, columns), lambda step: (step, 0))
+
+    def whole(*shape):
+        return pl.BlockSpec(shape, lambda step: (0,) * len(shape))
+
+    out_spec = pl.BlockSpec((width, half), lambda step: (0, 3))
+    return pl.pallas_call(
+        functools.partial(middle_back_kernel, small),
+        grid=(count // block,),
+        in_specs=[
+            pl.BlockSpec(memory_space=pltpu.SMEM),
+            over_rows(hidden_half),
+            over_rows(hidden_half),
+            whole(width, hidden_half),
+            whole(width, hidden_half),
+            over_rows(width),
+            over_rows(width),
+            over_rows(1),
+            whole(*rows.shape),
+            over_rows(half),
+            over_rows(half),
+            out_spec,
+            out_spec,
+        ],
+        out_specs=[
+            over_rows(width),
+            over_rows(half),
+            over_rows(half),
+            whole(width, half),
+            whole(width, half),
+            whole(8, width),
+        ],
+        out_shape=[
+            jax.ShapeDtypeStruct((count, width), F32),
+            jax.ShapeDtypeStruct((count, half), BF),
+            jax.ShapeDtypeStruct((count, half), BF),
+            jax.ShapeDtypeStruct((width, half), F32),
+            jax.ShapeDtypeStruct((width, half), BF),
+            jax.ShapeDtypeStruct((8, width), F32),
+        ],
+        scratch_shapes=[pltpu.VMEM((block, width), F32), pltpu.VMEM((2, width, half), F32)],
+        compiler_params=pltpu.CompilerParams(vmem_limit_bytes=VMEM_BYTES),
+        cost_estimate=pl.CostEstimate(
+            flops=4 * count * width * (hidden_half + width),
+            bytes_accessed=4 * count * hidden_half + 4 * width * hidden_half + 16 * count * width,
+            transcendentals=0,
+        ),
+        name="middle_back",
+    )(place, *grads, *ups, middle, cotangent, mask, rows, *contexts, *weights)
+
+
+def start_back_kernel(
+    small, length, place_ref, grads_mine_ref, grads_other_ref, weight_mine_ref, weight_other_ref, start_ref, middle_ref,
+    mask_ref, rows_ref, sums_ref, sums_mine_ref, sums_other_ref,
+    tokens_ref, blocks_ref, lines_ref,
+):
+    core, place = place_ref[0], place_ref[1]
+    step = pl.program_id(0)
+    width = start_ref.shape[1]
+    half = width // 2
+    seqs = start_ref.shape[0] // length
+
+    @pl.when(step == 0)
+    def _():
+        lines_ref[...] = jnp.zeros_like(lines_ref)
+        for index, row in ((0, 0), (1, 2)):
+            pair = (sums_mine_ref[row : row + 1, :], sums_other_ref[row : row + 1, :])
+            lines_ref[index : index + 1, :half], lines_ref[index : index + 1, half:] = chosen_side(core, *pair)
+        lines_ref[2:4, :] = sums_ref[0:2, :]
+        lines_ref[6:8, :] = sums_ref[2:4, :]
+
+    grad = 0.0
+    for grads, weight in ((grads_mine_ref, weight_mine_ref), (grads_other_ref, weight_other_ref)):
+        for index in range(3):
+            grad = grad + right_product(grads[index], weight[:, index * half : (index + 1) * half])
+    back, shares = norm_back(start_ref[...], rows_ref[small + 4 : small + 5, :], grad)
+    back = middle_ref[...] + back
+    mask = mask_ref[...]
+    tokens_ref[...] = jnp.where(mask > 0.0, 0.0, back)
+    for index, item in ((4, shares), (5, grad), (8, back * mask)):
+        lines_ref[index : index + 1, :] += jnp.sum(item, 0, keepdims=True)
+    for index in range(seqs):
+        line = LANES + place * small + step * seqs + index
+        lines_ref[pl.ds(line, 1), :] = jnp.sum(back[index * length : (index + 1) * length], 0, keepdims=True)
+
+    @pl.when(step == pl.num_programs(0) - 1)
+    def _():
+        blocks_ref[...] = lines_ref[...].T
+
+
+def start_back(place, grads, weights, start, middle, mask, rows, sums, side_sums, seqs, length, block=256):
+    count, width = start.shape
+    half = width // 2
+    small = place.shape[0] - 2
+    block = math.gcd(block, count)
+    lines = LANES + -(-seqs // LANES) * LANES
+
+    def over_rows(columns):
+        return pl.BlockSpec((block, columns), lambda step: (step, 0))
+
+    def whole(*shape):
+        return pl.BlockSpec(shape, lambda step: (0,) * len(shape))
+
+    grads_spec = pl.BlockSpec((3, block, half), lambda step: (0, step, 0))
+    return pl.pallas_call(
+        functools.partial(start_back_kernel, small, length),
+        grid=(count // block,),
+        in_specs=[
+            pl.BlockSpec(memory_space=pltpu.SMEM),
+            grads_spec,
+            grads_spec,
+            whole(width, 3 * half),
+            whole(width, 3 * half),
+            over_rows(width),
+            over_rows(width),
+            over_rows(1),
+            whole(*rows.shape),
+            whole(*sums.shape),
+            whole(*side_sums[0].shape),
+            whole(*side_sums[1].shape),
+        ],
+        out_specs=[over_rows(width), whole(width, lines)],
+        out_shape=[
+            jax.ShapeDtypeStruct((count, width), F32),
+            jax.ShapeDtypeStruct((width, lines), F32),
+        ],
+        scratch_shapes=[pltpu.VMEM((lines, width), F32)],
+        compiler_params=pltpu.CompilerParams(vmem_limit_bytes=VMEM_BYTES),
+        cost_estimate=pl.CostEstimate(
+            flops=4 * count * width * 3 * half,
+            bytes_accessed=12 * count * half + 12 * width * half + 12 * count * width,
+            transcendentals=0,
+        ),
+        name="start_back",
+    )(place, *grads, *weights, start, middle, mask, rows, sums, *side_sums)
 
 
 class Tree:
@@ -480,12 +827,9 @@
     hidden_part = hidden_width // count
     seq_count = timesteps.shape[0]
     seq_length = tokens.shape[0] // seq_count
-    row_count = tokens.shape[0]
     half = width // 2
     table_cols = time_table.shape[1]
-    absorbed = (mask_bits == 1)[:, None]
-    absorbed_float = mask_bits.astype(F32)[:, None]
-    sides = (core, 1 - core)
+    absorbed = mask_bits.astype(F32)[:, None]
 
     small = [b_query, b_value, b_out, b_down, gain_attn, shift_attn, gain_mlp, shift_mlp, mask_vector]
     fixed = len(small)
@@ -517,63 +861,30 @@
     attn_w.two()
     up_one = up_w.one(attn_w.half)
     attn_w = attn_w.halves()
-    out_w = jnp.concatenate(
-        [
-            jnp.where(core == 0, *[w[:, 3 * half : 4 * half] for w in pair])
-            for pair in (attn_w, attn_w[::-1])
-        ],
-        1,
+    place = jnp.concatenate([jnp.stack([jnp.int32(core), place]), timesteps])
+    rows, start, normed_one, across_one, bias_mine, bias_other, bias_up = start_rows(
+        place, tokens, absorbed, attn_w, fixed, up_cols, table_cols, small_cols, chips, hidden_part
     )
-
-    chosen = jnp.concatenate([timesteps, table_cols + jnp.arange(small_cols, dtype=jnp.int32)])
-    rows = 0.0
-    for side, weight in zip(sides, attn_w):
-        columns = lax.broadcasted_iota(jnp.int32, (seq_count + small_cols, table_half), 1) + side * table_half
-        rows = rows + right_product((chosen[:, None] == columns).astype(BF), weight[:, 4 * half :])
-    table_rows = rows[:seq_count]
-    rows = rows[seq_count:]
-    bias_query, bias_value, bias_out, bias_down, gain_one, shift_one, gain_two, shift_two, mask_row = [
-        rows[i] for i in range(fixed)
-    ]
-    bias_up = rows[fixed : fixed + up_cols].reshape(up_cols, chips, 2, part).transpose(2, 1, 0, 3)
-    bias_up = bias_up.reshape(2, 1, hidden_width // 2)
-    bias_up = [pick(bias_up, side, 0) for side in sides]
-    steps = rows[fixed + up_cols :].reshape(seq_cols, count, part).transpose(1, 0, 2).reshape(count, -1)
-    steps = steps.astype(jnp.int32)
+    steps = rows[seq_count + fixed + up_cols : seq_count + small_cols]
+    steps = steps.reshape(seq_cols, count, part).transpose(1, 0, 2).reshape(count, -1).astype(jnp.int32)
     steps = (steps[:, :seq_count] * 256 + steps[:, seq_count : 2 * seq_count]).reshape(-1)
-    bias_qkv = jnp.stack([bias_query, jnp.zeros_like(bias_query), bias_value]).reshape(3, 2, half)
-    bias_qkv = [pick(bias_qkv, side, 1) for side in sides]
-
-    start = jnp.where(absorbed, mask_row[None, :], tokens)
-    start = (start.reshape(seq_count, seq_length, width) + table_rows[:, None, :]).reshape(row_count, width)
-    normed_one = layer_norm(start, gain_one, shift_one).astype(BF)
-    across_one = normed_one.T
-    qkv_mine, context_mine = attention(normed_one, attn_w[0], bias_qkv[0], seq_length)
+
+    qkv_mine, context_mine = attention(normed_one, attn_w[0], bias_mine, seq_length)
     up_half = up_w.two(context_mine)
-    qkv_other, context_other = attention(after(normed_one, up_one), attn_w[1], bias_qkv[1], seq_length)
-    context = jnp.concatenate(
-        [
-            jnp.where(core == 0, context_mine, context_other),
-            jnp.where(core == 0, context_other, context_mine),
-        ],
-        1,
-    )
-    middle = start + (product(context, out_w) + bias_out)
+    qkv_other, context_other = attention(after(normed_one, up_one), attn_w[1], bias_other, seq_length)
+    contexts = (context_mine, context_other)
+    middle, normed_two, across_two = middle_rows(place, contexts, attn_w, start, rows)
     down_one = down_w.one(up_half, context_other)
     up_w = up_w.halves()
-    normed_two = layer_norm(middle, gain_two, shift_two).astype(BF)
-    across_two = normed_two.T
     down_w.two(normed_two)
     hidden, slope = [None, None], [None, None]
-    hidden[0], slope[0] = feed(normed_two, up_w[0], bias_up[0])
-    hidden[1], slope[1] = feed(after(normed_two, down_one), up_w[1], bias_up[1])
+    hidden[0], slope[0] = feed(normed_two, up_w[0], bias_up, 0)
+    hidden[1], slope[1] = feed(after(normed_two, down_one), up_w[1], bias_up, 1)
     down_w = down_w.halves()
 
-    grad_output = cotangent * absorbed_float
-    grad_branch = grad_output.astype(BF)
+    grad_branch = (cotangent * absorbed).astype(BF)
     down_sum = reduction(hidden_part)
     down_got = down_sum.add(left_product(hidden[0], grad_branch), left_product(hidden[1], grad_branch))
-    grad_b_down = column_sums(grad_branch)
     up_sum = reduction(2 * part)
     grad_pre, grad_b_up, grad_up = [None, None], [None, None], [None, None]
     grad_pre[1], grad_b_up[1], grad_up[1] = feed_back(grad_branch, down_w[1], slope[1], across_two, BF)
@@ -586,18 +897,11 @@
     if fast:
         down_sum.two()
     grad_pre = after(grad_pre, down_sum.sent)
-    grad_normed_two = right_product(grad_pre[0], up_w[0]) + right_product(grad_pre[1], up_w[1])
-    _, norm_pull = jax.vjp(layer_norm, middle, gain_two, shift_two)
-    back_middle, grad_gain_mlp, grad_shift_mlp = norm_pull(grad_normed_two)
-    grad_middle = grad_output + back_middle
-
-    grad_attn = grad_middle.astype(BF)
-    grad_halves = [lax.dynamic_slice_in_dim(grad_attn, side * half, half, 1) for side in sides]
+    grad_middle, *grad_context, grad_out_mine, grad_out_other, middle_sums = middle_back(
+        place, grad_pre, up_w, middle, cotangent, absorbed, rows, contexts, attn_w
+    )
+
     attn_sum = reduction(2 * part)
-    grad_out = [left_product(context, item) for item in grad_halves]
-    grad_b_out = column_sums(grad_attn)
-    grad_context = right_product(grad_attn, out_w).astype(BF)
-    grad_context = [lax.dynamic_slice_in_dim(grad_context, side * half, half, 1) for side in sides]
     if fast:
         down_sum.along_z()
         up_sum.one()
@@ -613,41 +917,19 @@
     grad_qkv, grad_weights, sums = zip(*grads)
     for index in range(3):
         attn_sum.add(grad_weights[0][index], grad_weights[1][index])
-    attn_sum.add(grad_out[0], grad_out[1])
+    attn_sum.add(grad_out_mine, grad_out_other)
     if fast:
         up_sum.along_z()
     grad_qkv = after(grad_qkv, up_sum.sent)
-    grad_normed_one = sum(
-        right_product(grad_qkv[i][j], attn_w[i][:, j * half : (j + 1) * half]) for i in range(2) for j in range(3)
+    seqs = count * seq_count
+    grad_tokens, blocks = start_back(
+        place, grad_qkv, attn_w, start, grad_middle, absorbed, rows, middle_sums, sums, seqs, seq_length
     )
-    _, norm_pull = jax.vjp(layer_norm, start, gain_one, shift_one)
-    back_start, grad_gain_attn, grad_shift_attn = norm_pull(grad_normed_one)
-    grad_start = grad_middle + back_start
-    grad_tokens = jnp.where(absorbed, 0.0, grad_start)
-    grad_mask_vector = jnp.sum(grad_start * absorbed_float, 0)
-    seq_sums = jnp.sum(grad_start.reshape(seq_count, seq_length, width), 1)
-
-    grad_b_up = paired(core, *[item.reshape(chips, hidden_part) for item in grad_b_up], 1)
-    grad_b_up = grad_b_up.reshape(count, up_cols, part).transpose(1, 0, 2).reshape(up_cols, width)
-    grad_b_qkv = paired(core, sums[0], sums[1], 1).reshape(3, width)
-    small = jnp.stack(
-        [
-            grad_b_qkv[0],
-            grad_b_qkv[2],
-            grad_b_out,
-            grad_b_down,
-            grad_gain_attn,
-            grad_shift_attn,
-            grad_gain_mlp,
-            grad_shift_mlp,
-            grad_mask_vector,
-        ]
-    )
-    seqs = count * seq_count
-    small = jnp.concatenate([small, grad_b_up], 0)
-    blocks = jnp.pad(small, ((0, seqs + LANES - small.shape[0]), (0, 0)))
-    blocks = lax.dynamic_update_slice(blocks, seq_sums, (LANES + place * seq_count, 0)).T
-    blocks = [blocks[:, :LANES], blocks[:, LANES:]]
+
+    grad_b_up = paired(core, *[item.reshape(chips, hidden_part) for item in grad_b_up], 1).reshape(count, hidden_part)
+    grad_b_up = jnp.pad(grad_b_up[:, None], ((0, 0), (0, part - 1), (LANES - hidden_part, 0)))
+    grad_b_up = grad_b_up.reshape(width, LANES)
+    blocks = [blocks[:, :LANES] + grad_b_up, blocks[:, LANES:]]
     if fast:
         attn_sum.add(jnp.where(core == 0, *blocks), jnp.where(core == 0, *blocks[::-1]))
         attn_sum.one()
@@ -660,15 +942,15 @@
         small, seq_sums = [
             lax.psum_scatter(item.astype(BF), AXES, scatter_dimension=0, tiled=True).astype(F32) for item in blocks
         ]
-    small = small[:, : fixed + up_cols].T
-    grad_b_up = small[fixed:].reshape(hidden_part)
+    grad_b_up = small[0, LANES - hidden_part :]
+    small = small[:, :fixed].T
     onehot = (steps[:, None] == lax.broadcasted_iota(jnp.int32, (seqs, table_cols), 1)).astype(F32)
     grad_time_table = jnp.dot(seq_sums, onehot, precision=lax.Precision.HIGHEST)
     grad_w_qkv = attn_grad[:, :, : 3 * half].reshape(part, 2, 3, half).transpose(0, 2, 1, 3).reshape(part, 3 * width)
     grad_w_out = attn_grad[:, :, 3 * half : 4 * half].reshape(part, width)
     grad_w_up = up_sum.columns().reshape(part, 2, chips, hidden_part).transpose(0, 2, 1, 3)
     grad_w_up = grad_w_up.reshape(part, hidden_width)
-    output = middle + (product(hidden[0], down_w[0]) + product(hidden[1], down_w[1]) + bias_down)
+    output = middle + (product(hidden[0], down_w[0]) + product(hidden[1], down_w[1]) + rows[seq_count + 3])
     return (
         output,
         grad_tokens,

time: 386 us -> 331 us (0.86)
  local copies, waits for them, and re-layouts: 84.9 us -> 25.7 us
  waiting for transfers between devices: 92 us -> 121 us
  other arithmetic: 51.9 us -> 23.4 us
  Pallas kernels: 56.7 us -> 80.9 us
  matrix products: 31.7 us -> 11.6 us
    pallas_call x2 -> x6, Pallas kernels: 10.9 us -> 35.7 us  [the longest x2 11 us: feed(): pl.pallas_call(functools.partial(feed_kernel, side), grid=(columns // blo...]
    ppermute x12, waiting for transfers between devices: 19.3 us -> 41.5 us  [to_y(): return lax.ppermute(value, 'fsdp', [(i, i ^ 1) for i in range(8)])]
    unnamed x233 -> x107, local copies, waits for them, and re-layouts: 23.8 us -> 2.83 us
    dot_general x18 -> x4, matrix products: 30.7 us -> 10.7 us  [contract(): return lax.dot_general(left, right, dims, preferred_element_type=F32)]
    ppermute x18, waiting for transfers between devices: 31.3 us -> 43.3 us  [to_z(): return lax.ppermute(value, 'fsdp', [(i, i ^ 2 * step) for i in range(8)])]
    reshape x11 -> x0, local copies, waits for them, and re-layouts: 10.6 us -> none  [the longest x2 3 us: body(): rows[fixed:fixed + up_cols].reshape(up_cols, chips, 2, part)]
    convert_element_type x4 -> x1, local copies, waits for them, and re-layouts: 7.66 us -> 0.08 us  [body(): steps.reshape(seq_cols, count, part).transpose(1, 0, 2).reshape(count, -1)]
    optimization_barrier x3 -> x0, local copies, waits for them, and re-layouts: 6.91 us -> none  [after(): return lax.optimization_barrier((value, others))[0]]
  transfers between devices with their start and end apart: 56 -> 56, of which waited for: 20 -> 25; matrix products, arithmetic and copies ran while one was open for 35% -> 15% of each run, Pallas kernels for 13% -> 21%
where the time goes in v1:
time: 331 us; the launch traced here: 327 us
  waiting for transfers between devices  121 us (37%)
  Pallas kernels  80.9 us (24%)
  starting transfers between devices  61.7 us (19%)
  local copies, waits for them, and re-layouts  25.7 us (8%)
  other arithmetic  23.4 us (7%)
  matrix products  11.6 us (4%)
    ppermute x18, waiting for transfers between devices, to_z(): return lax.ppermute(value, 'fsdp', [(i, i ^ 2 * step) for i in range(8)])  43.3 us
    ppermute x12, waiting for transfers between devices, to_y(): return lax.ppermute(value, 'fsdp', [(i, i ^ 1) for i in range(8)])  41.5 us
    ppermute x12, waiting for transfers between devices, to_x(): return lax.ppermute(value, 'rep', [(i, i ^ 2) for i in range(4)])  33.6 us
    ppermute x18, starting transfers between devices, to_z(): return lax.ppermute(value, 'fsdp', [(i, i ^ 2 * step) for i in range(8)])  31.9 us
    pallas_call x2, Pallas kernels, attention_back(): pl.pallas_call(functools.partial(attention_back_kernel, length, 1.0 / mat...  18.6 us
    pallas_call x2, Pallas kernels, attention(): pl.pallas_call(functools.partial(attention_kernel, length, 1.0 / math.sqr...  16 us
    ppermute x12, starting transfers between devices, to_x(): return lax.ppermute(value, 'rep', [(i, i ^ 2) for i in range(4)])  14.3 us
    ppermute x12, starting transfers between devices, to_y(): return lax.ppermute(value, 'fsdp', [(i, i ^ 1) for i in range(8)])  13.4 us
  transfers between devices with their start and end apart: 56, of which 25 were waited for; matrix products, arithmetic and copies ran while one was open for 15% of the time, Pallas kernels for 21%

profile of v1, /device:TPU:0, one launch (start us, length us, event | category | flops | bytes accessed | tf_op | source)
XLA Modules:
  0.0 326.9 jit_solution(5923725809906606821)
XLA Ops:
  11.2 6.5 %collective-permute-done.3 = bf16[48,2048]{1,0:T(8,128)(2,1)S(1)} collective-permute-done((bf16[48,2048]{1,0:T(8,128)(2,1)S(1)}, bf16[48,2048]{1,0:T(8,128)(2,1)S(1)}, u32[]{:S(2)}, u32[]{:S(2)}) %collective-permute-start.3) | collective-permute-done | bytes 196640 | tf_op jit(solution)/shard_map/ppermute | solution.py:633
  17.7 8.0 %collective-permute-done.2 = bf16[48,2048]{1,0:T(8,128)(2,1)S(1)} collective-permute-done((bf16[48,2048]{1,0:T(8,128)(2,1)S(1)}, bf16[48,2048]{1,0:T(8,128)(2,1)S(1)}, u32[]{:S(2)}, u32[]{:S(2)}) %collective-permute-start.2) | collective-permute-done | bytes 196640 | tf_op jit(solution)/shard_map/ppermute | solution.py:633
  26.1 3.9 %collective-permute-start.12 = (bf16[48,1536]{1,0:T(8,128)(2,1)S(1)}, bf16[48,1536]{1,0:T(8,128)(2,1)S(1)}, u32[]{:S(2)}, u32[]{:S(2)}) collective-permute-start(bf16[48,1536]{1,0:T(8,128)(2,1)S(1)} %pad_maximum_fusion.14), channel_id=1, source_target_pairs={{0,8},{4,12},{8,0},{12,4},{16,24},{20,28},{24,16},{28,20},{1,9},{5... | collective-permute-start | bytes 442376 | tf_op jit(solution)/shard_map/ppermute | solution.py:633
  36.2 7.4 %collective-permute-done.11 = bf16[48,1536]{1,0:T(8,128)(2,1)S(1)} collective-permute-done((bf16[48,1536]{1,0:T(8,128)(2,1)S(1)}, bf16[48,1536]{1,0:T(8,128)(2,1)S(1)}, u32[]{:S(2)}, u32[]{:S(2)}) %collective-permute-start.11) | collective-permute-done | bytes 147488 | tf_op jit(solution)/shard_map/ppermute | solution.py:633
  47.1 14.1 %collective-permute-done.6 = bf16[4,2,24,2048]{3,2,0,1:T(8,128)(2,1)S(1)} collective-permute-done((bf16[4,2,24,2048]{3,2,0,1:T(8,128)(2,1)S(1)}, bf16[4,2,24,2048]{3,2,0,1:T(8,128)(2,1)S(1)}, u32[]{:S(2)}, u32[]{:S(2)}) %collective-permute-start.6) | collective-permute-done | bytes 786464 | tf_op jit(solution)/shard_map/ppermute | solution.py:630
  71.0 4.5 %collective-permute-done.19 = bf16[96,768]{1,0:T(8,128)(2,1)} collective-permute-done((bf16[96,768]{1,0:T(8,128)(2,1)}, bf16[96,768]{1,0:T(8,128)(2,1)}, u32[]{:S(2)}, u32[]{:S(2)}) %collective-permute-start.19) | collective-permute-done | bytes 147488 | tf_op jit(solution)/shard_map/ppermute | solution.py:633
  75.5 6.6 %collective-permute-done.18 = bf16[96,768]{1,0:T(8,128)(2,1)} collective-permute-done((bf16[96,768]{1,0:T(8,128)(2,1)}, bf16[96,768]{1,0:T(8,128)(2,1)}, u32[]{:S(2)}, u32[]{:S(2)}) %collective-permute-start.18) | collective-permute-done | bytes 147488 | tf_op jit(solution)/shard_map/ppermute | solution.py:633
  85.2 6.5 %collective-permute-done.13 = bf16[4,24,1536]{2,1,0:T(8,128)(2,1)S(1)} collective-permute-done((bf16[4,24,1536]{2,1,0:T(8,128)(2,1)}, bf16[4,24,1536]{2,1,0:T(8,128)(2,1)S(1)}, u32[]{:S(2)}, u32[]{:S(2)}) %collective-permute-start.13) | collective-permute-done | bytes 294944 | tf_op jit(solution)/shard_map/ppermute | solution.py:627
  97.2 7.7 %attention.2 = (bf16[3,512,384]{2,1,0:T(8,128)(2,1)S(1)}, bf16[512,384]{1,0:T(8,128)(2,1)S(1)}) custom-call(bf16[512,768]{1,0:T(8,128)(2,1)S(1)} %get-tuple-element.88.rows_ref, bf16[768,2048]{1,0:T(8,128)(2,1)S(1)} %bitcast.572, bf16[768,2048]{1,0:T(8,128)(2,1)S(1)} %bitcast.573, bf16[768,2048]{1,0:T(8,128)(2,1)S(1)} %bitcast.574, ...), custom_call_target="tpu_custom_call" | custom-call | flops 905969664 | bytes 4128768 | tf_op jit(solution)/shard_map/attention/pallas_call | solution.py:85
  107.1 8.3 %attention.3 = (bf16[3,512,384]{2,1,0:T(8,128)(2,1)S(1)}, bf16[512,384]{1,0:T(8,128)(2,1)S(1)}) custom-call(bf16[512,768]{1,0:T(8,128)(2,1)S(1)} %get-tuple-element.88.rows_ref, bf16[768,2048]{1,0:T(8,128)(2,1)} %collective-permute-done.8.table_other_ref.query_ref.key_ref.value_ref.out_other_ref.weight_other_ref, ...), custom_call_target="tpu_custom_call" | custom-call | flops 905969664 | bytes 4128768 | tf_op jit(solution)/shard_map/attention/pallas_call | solution.py:85
  132.9 12.5 %collective-permute-done.22 = bf16[4,2,48,768]{3,2,0,1:T(8,128)(2,1)} collective-permute-done((bf16[4,2,48,768]{3,2,0,1:T(8,128)(2,1)}, bf16[4,2,48,768]{3,2,0,1:T(8,128)(2,1)}, u32[]{:S(2)}, u32[]{:S(2)}) %collective-permute-start.22) | collective-permute-done | bytes 589856 | tf_op jit(solution)/shard_map/ppermute | solution.py:630
  154.2 5.4 %feed.3 = (bf16[512,1536]{1,0:T(8,128)(2,1)S(1)}, f32[512,1536]{1,0:T(8,128)S(1)}) custom-call(bf16[512,768]{1,0:T(8,128)(2,1)S(1)} %copy-done.26, bf16[768,1536]{1,0:T(8,128)(2,1)} %collective-permute-done.24.weight_ref.up_other_ref, f32[8,1536]{1,0:T(8,128)S(1)} %get-tuple-element.97.bias_ref), custom_call_target="tpu_custom_call" | custom-call | flops 1207959552 | bytes 7864320 | tf_op jit(solution)/shard_map/feed/pallas_call | solution.py:196
  161.1 5.6 %feed.2 = (bf16[512,1536]{1,0:T(8,128)(2,1)S(1)}, f32[512,1536]{1,0:T(8,128)S(1)}) custom-call(bf16[512,768]{1,0:T(8,128)(2,1)S(1)} %copy-done.26, bf16[768,1536]{1,0:T(8,128)(2,1)} %bitcast.56.weight_ref.up_mine_ref, f32[8,1536]{1,0:T(8,128)S(1)} %get-tuple-element.97.bias_ref), custom_call_target="tpu_custom_call" | custom-call | flops 1207959552 | bytes 7864320 | tf_op jit(solution)/shard_map/feed/pallas_call | solution.py:196
  171.0 5.8 %feed_back.3 = (bf16[512,1536]{1,0:T(8,128)(2,1)S(1)}, f32[1,1536]{1,0:T(1,128)S(1)}, bf16[768,1536]{1,0:T(8,128)(2,1)}) custom-call(bf16[512,768]{1,0:T(8,128)(2,1)S(1)} %copy-done.4, bf16[1536,768]{1,0:T(8,128)(2,1)} %collective-permute-done.25.weight_ref, f32[512,1536]{1,0:T(8,128)S(1)} %get-tuple-element.111.slope_ref, bf16[768,512]{1,0:T(8,128)(2,1)S(1)} %copy-done.24), custom_call_target="tpu_custom_call" | custom-call | flops 2415919104 | bytes 13369344 | tf_op jit(solution)/shard_map/feed_back/pallas_call | solution.py:232
  180.9 4.2 %add_add_fusion = f32[512,768]{1,0:T(8,128)} fusion(f32[512,768]{1,0:T(8,128)S(1)} %copy-done.7, f32[512,768]{1,0:T(8,128)S(1)} %fusion.134, f32[768]{0:T(1024)S(1)} %slice_reduce_fusion.9, bf16[512,1536]{1,0:T(8,128)(2,1)S(1)} %get-tuple-element.98, bf16[1536,768]{1,0:T(8,128)(2,1)} %bitcast.74.weight_ref), kind=kOutput, calls=%fused_computation.29 | convolution fusion | flops 1209139200 | bytes 8653824 | tf_op jit(solution)/shard_map/dot_general | solution.py:24
  189.9 4.9 %feed_back.2 = (bf16[512,1536]{1,0:T(8,128)(2,1)S(1)}, f32[1,1536]{1,0:T(1,128)S(1)}, f32[768,1536]{1,0:T(8,128)S(1)}) custom-call(bf16[512,768]{1,0:T(8,128)(2,1)S(1)} %copy-done.4, bf16[1536,768]{1,0:T(8,128)(2,1)} %bitcast.74.weight_ref, f32[512,1536]{1,0:T(8,128)S(1)} %get-tuple-element.108.slope_ref, bf16[768,512]{1,0:T(8,128)(2,1)S(1)} %copy-done.24), custom_call_target="tpu_custom_call" | custom-call | flops 2415919104 | bytes 13369344 | tf_op jit(solution)/shard_map/feed_back/pallas_call | solution.py:232
  208.7 10.6 %middle_back.1 = (f32[512,768]{1,0:T(8,128)S(1)}, bf16[512,384]{1,0:T(8,128)(2,1)S(1)}, bf16[512,384]{1,0:T(8,128)(2,1)S(1)}, f32[768,384]{1,0:T(8,128)S(1)}, bf...) custom-call(s32[6]{0:T(128)S(1)} %pad_add_fusion.place_ref, bf16[512,1536]{1,0:T(8,128)(2,1)S(1)} %copy-done.12, ...), custom_call_target="tpu_custom_call" | custom-call | flops 3623878656 | bytes 14155776 | tf_op jit(solution)/shard_map/middle_back/pallas_call | solution.py:487
  228.0 9.4 %attention_back.3 = (bf16[3,512,384]{2,1,0:T(8,128)(2,1)S(1)}, bf16[3,768,384]{2,1,0:T(8,128)(2,1)S(1)}, f32[3,384]{1,0:T(4,128)S(1)}) custom-call(bf16[3,512,384]{2,1,0:T(8,128)(2,1)S(1)} %copy-done.20, bf16[512,384]{1,0:T(8,128)(2,1)S(1)} %get-tuple-element.123.grad_ref, bf16[768,512]{1,0:T(8,128)(2,1)S(1)} %copy-done.22), custom_call_target="tpu_custom_call" | custom-call | flops 905969664 | bytes 7077888 | tf_op jit(solution)/shard_map/attention_back/pallas_call | solution.py:145
  243.2 10.6 %collective-permute-done.35 = bf16[4,2,24,1536]{3,2,0,1:T(8,128)(2,1)S(1)} collective-permute-done((bf16[4,2,24,1536]{3,2,0,1:T(8,128)(2,1)S(1)}, bf16[4,2,24,1536]{3,2,0,1:T(8,128)(2,1)S(1)}, u32[]{:S(2)}, u32[]{:S(2)}) %collective-permute-start.35) | collective-permute-done | bytes 589856 | tf_op jit(solution)/shard_map/ppermute | solution.py:627
  255.4 9.2 %attention_back.2 = (bf16[3,512,384]{2,1,0:T(8,128)(2,1)S(1)}, f32[3,768,384]{2,1,0:T(8,128)S(1)}, f32[3,384]{1,0:T(4,128)S(1)}) custom-call(bf16[3,512,384]{2,1,0:T(8,128)(2,1)S(1)} %copy-done.18, bf16[512,384]{1,0:T(8,128)(2,1)S(1)} %get-tuple-element.118.grad_ref, bf16[768,512]{1,0:T(8,128)(2,1)S(1)} %copy-done.22), custom_call_target="tpu_custom_call" | custom-call | flops 905969664 | bytes 7077888 | tf_op jit(solution)/shard_map/attention_back/pallas_call | solution.py:145
  270.9 7.0 %start_back.1 = (f32[512,768]{1,0:T(8,128)}, f32[768,256]{1,0:T(8,128)S(1)}) custom-call(s32[6]{0:T(128)S(1)} %pad_add_fusion.place_ref, bf16[3,512,384]{2,1,0:T(8,128)(2,1)S(1)} %get-tuple-element.125.grads_mine_ref, bf16[3,512,384]{2,1,0:T(8,128)(2,1)S(1)} %get-tuple-element.126.grads_other_ref, bf16[768,2048]{1,0:T(8,128)(2,1)S(1)} %bitcast.577, ...), custom_call_target="tpu_custom_call" | custom-call | flops 1811939328 | bytes 10616832 | tf_op jit(solution)/shard_map/start_back/pallas_call | solution.py:585
  282.1 13.9 %collective-permute-done.44 = bf16[4,2,24,1664]{3,2,1,0:T(8,128)(2,1)S(1)} collective-permute-done((bf16[4,2,24,1664]{3,2,1,0:T(8,128)(2,1)S(1)}, bf16[4,2,24,1664]{3,2,1,0:T(8,128)(2,1)S(1)}, u32[]{:S(2)}, u32[]{:S(2)}) %collective-permute-start.44) | collective-permute-done | bytes 639008 | tf_op jit(solution)/shard_map/ppermute | solution.py:627
  298.8 6.2 %collective-permute-done.45 = bf16[4,24,1664]{2,1,0:T(8,128)(2,1)S(1)} collective-permute-done((bf16[4,24,1664]{2,1,0:T(8,128)(2,1)S(1)}, bf16[4,24,1664]{2,1,0:T(8,128)(2,1)S(1)}, u32[]{:S(2)}, u32[]{:S(2)}) %collective-permute-start.45) | collective-permute-done | bytes 319520 | tf_op jit(solution)/shard_map/ppermute | solution.py:630
  312.1 8.0 %collective-permute-done.49 = bf16[48,1664]{1,0:T(8,128)(2,1)S(1)} collective-permute-done((bf16[48,1664]{1,0:T(8,128)(2,1)S(1)}, bf16[48,1664]{1,0:T(8,128)(2,1)S(1)}, u32[]{:S(2)}, u32[]{:S(2)}) %collective-permute-start.49) | collective-permute-done | bytes 159776 | tf_op jit(solution)/shard_map/ppermute | solution.py:633
  (394 shorter events, 137.6 us)
Async XLA Ops:
  8.6 17.1 %collective-permute-start.2 = (bf16[48,2048]{1,0:T(8,128)(2,1)S(1)}, bf16[48,2048]{1,0:T(8,128)(2,1)S(1)}, u32[]{:S(2)}, u32[]{:S(2)}) collective-permute-start(bf16[48,2048]{1,0:T(8,128)(2,1)S(1)} %pad_maximum_fusion.13), channel_id=1, source_target_pairs={{0,16},{4,20},{8,24},{12,28},{16,0},{20,4},{24,8},{28,12},{1,17},{... | collective-permute-start | bytes 589832 | tf_op jit(solution)/shard_map/ppermute | solution.py:633
  11.2 14.5 %collective-permute-start.1 = (bf16[48,2048]{1,0:T(8,128)(2,1)S(1)}, bf16[48,2048]{1,0:T(8,128)(2,1)S(1)}, u32[]{:S(2)}, u32[]{:S(2)}) collective-permute-start(bf16[48,2048]{1,0:T(8,128)(2,1)S(1)} %pad_maximum_fusion.13), channel_id=1, source_target_pairs={{0,24},{4,28},{8,16},{12,20},{16,8},{20,12},{24,0},{28,4},{1,25},{... | collective-permute-start | bytes 589832 | tf_op jit(solution)/shard_map/ppermute | solution.py:633
  44.2 17.0 %collective-permute-start.6 = (bf16[4,2,24,2048]{3,2,0,1:T(8,128)(2,1)S(1)}, bf16[4,2,24,2048]{3,2,0,1:T(8,128)(2,1)S(1)}, u32[]{:S(2)}, u32[]{:S(2)}) collective-permute-start(bf16[4,2,24,2048]{3,2,0,1:T(8,128)(2,1)S(1)} %pad_maximum_fusion.1), channel_id=1, source_target_pairs={{0,4},{4,0},{8,12},{12,8},{16,20},{20,16},{24,28},{28,24},{1,5},{5... | collective-permute-start | bytes 2359304 | tf_op jit(solution)/shard_map/ppermute | solution.py:630
  45.8 16.7 %collective-permute-start.7 = (bf16[4,2,24,2048]{3,2,0,1:T(8,128)(2,1)S(1)}, bf16[4,2,24,2048]{3,2,0,1:T(8,128)(2,1)S(1)}, u32[]{:S(2)}, u32[]{:S(2)}) collective-permute-start(bf16[4,2,24,2048]{3,2,0,1:T(8,128)(2,1)S(1)} %pad_maximum_fusion.2), channel_id=1, source_target_pairs={{0,2},{1,3},{2,0},{3,1},{4,6},{5,7},{6,4},{7,5},{8,10},{9,11},{10,... | collective-permute-start | bytes 2359304 | tf_op jit(solution)/shard_map/ppermute | solution.py:627
  63.3 29.7 %collective-permute-start.8 = (bf16[768,2048]{1,0:T(8,128)(2,1)S(1)}, bf16[768,2048]{1,0:T(8,128)(2,1)}, u32[]{:S(2)}, u32[]{:S(2)}) collective-permute-start(bf16[768,2048]{1,0:T(8,128)(2,1)S(1)} %bitcast.570), channel_id=1, source_target_pairs={{0,1},{1,0},{2,3},{3,2},{4,5},{5,4},{6,7},{7,6},{8,9},{9,8},{10,11... | collective-permute-start | bytes 9437192 | tf_op jit(solution)/shard_map/ppermute | solution.py:624
  127.3 25.7 %collective-permute-start.24 = (bf16[768,1536]{1,0:T(8,128)(2,1)}, bf16[768,1536]{1,0:T(8,128)(2,1)}, u32[]{:S(2)}, u32[]{:S(2)}) collective-permute-start(bf16[768,1536]{1,0:T(8,128)(2,1)} %bitcast.56.weight_ref.up_mine_ref), channel_id=1, source_target_pairs={{0,1},{1,0},{2,3},{3,2},{4,5},{5,4},{6,7},{7,6},{8,9},{9,8},{10,11... | collective-permute-start | bytes 7077896 | tf_op jit(solution)/shard_map/ppermute | solution.py:624
  149.8 21.2 %collective-permute-start.25 = (bf16[1536,768]{1,0:T(8,128)(2,1)}, bf16[1536,768]{1,0:T(8,128)(2,1)}, u32[]{:S(2)}, u32[]{:S(2)}) collective-permute-start(bf16[1536,768]{1,0:T(8,128)(2,1)} %bitcast.74.weight_ref), channel_id=1, source_target_pairs={{0,1},{1,0},{2,3},{3,2},{4,5},{5,4},{6,7},{7,6},{8,9},{9,8},{10,11... | collective-permute-start | bytes 7077896 | tf_op jit(solution)/shard_map/ppermute | solution.py:624
  161.1 24.0 %collective-permute-start.26 = (bf16[1536,768]{1,0:T(8,128)(2,1)S(1)}, bf16[1536,768]{1,0:T(8,128)(2,1)S(1)}, u32[]{:S(2)}, u32[]{:S(2)}) collective-permute-start(bf16[1536,768]{1,0:T(8,128)(2,1)S(1)} %convolution_convert_fusion), channel_id=1, source_target_pairs={{0,1},{1,0},{2,3},{3,2},{4,5},{5,4},{6,7},{7,6},{8,9},{9,8},{10,11... | collective-permute-start | bytes 7077896 | tf_op jit(solution)/shard_map/ppermute | solution.py:624
  176.8 42.7 %collective-permute-start.34 = (bf16[768,1536]{1,0:T(8,128)(2,1)}, bf16[768,1536]{1,0:T(8,128)(2,1)}, u32[]{:S(2)}, u32[]{:S(2)}) collective-permute-start(bf16[768,1536]{1,0:T(8,128)(2,1)} %get-tuple-element.117), channel_id=1, source_target_pairs={{0,1},{1,0},{2,3},{3,2},{4,5},{5,4},{6,7},{7,6},{8,9},{9,8},{10,11... | collective-permute-start | bytes 7077896 | tf_op jit(solution)/shard_map/ppermute | solution.py:624
  188.1 15.6 %collective-permute-start.28 = (bf16[4,2,48,768]{3,2,0,1:T(8,128)(2,1)}, bf16[4,2,48,768]{3,2,0,1:T(8,128)(2,1)}, u32[]{:S(2)}, u32[]{:S(2)}) collective-permute-start(bf16[4,2,48,768]{3,2,0,1:T(8,128)(2,1)} %fusion.13), channel_id=1, source_target_pairs={{0,4},{4,0},{8,12},{12,8},{16,20},{20,16},{24,28},{28,24},{1,5},{5... | collective-permute-start | bytes 1769480 | tf_op jit(solution)/shard_map/ppermute | solution.py:630
  189.6 16.0 %collective-permute-start.27 = (bf16[4,2,48,768]{3,2,0,1:T(8,128)(2,1)}, bf16[4,2,48,768]{3,2,0,1:T(8,128)(2,1)}, u32[]{:S(2)}, u32[]{:S(2)}) collective-permute-start(bf16[4,2,48,768]{3,2,0,1:T(8,128)(2,1)} %fusion.12), channel_id=1, source_target_pairs={{0,2},{1,3},{2,0},{3,1},{4,6},{5,7},{6,4},{7,5},{8,10},{9,11},{10,... | collective-permute-start | bytes 1769480 | tf_op jit(solution)/shard_map/ppermute | solution.py:627
  205.3 17.0 %collective-permute-start.30 = (bf16[4,48,768]{2,1,0:T(8,128)(2,1)S(1)}, bf16[4,48,768]{2,1,0:T(8,128)(2,1)S(1)}, u32[]{:S(2)}, u32[]{:S(2)}) collective-permute-start(bf16[4,48,768]{2,1,0:T(8,128)(2,1)S(1)} %fusion.31), channel_id=1, source_target_pairs={{0,2},{1,3},{2,0},{3,1},{4,6},{5,7},{6,4},{7,5},{8,10},{9,11},{10,... | collective-permute-start | bytes 884744 | tf_op jit(solution)/shard_map/ppermute | solution.py:627
  207.1 15.3 %collective-permute-start.29 = (bf16[4,48,768]{2,1,0:T(8,128)(2,1)S(1)}, bf16[4,48,768]{2,1,0:T(8,128)(2,1)S(1)}, u32[]{:S(2)}, u32[]{:S(2)}) collective-permute-start(bf16[4,48,768]{2,1,0:T(8,128)(2,1)S(1)} %fusion.30), channel_id=1, source_target_pairs={{0,4},{4,0},{8,12},{12,8},{16,20},{20,16},{24,28},{28,24},{1,5},{5... | collective-permute-start | bytes 884744 | tf_op jit(solution)/shard_map/ppermute | solution.py:630
  219.3 21.4 %collective-permute-start.42 = (bf16[768,384]{1,0:T(8,128)(2,1)S(1)}, bf16[768,384]{1,0:T(8,128)(2,1)S(1)}, u32[]{:S(2)}, u32[]{:S(2)}) collective-permute-start(bf16[768,384]{1,0:T(8,128)(2,1)S(1)} %get-tuple-element.135), channel_id=1, source_target_pairs={{0,1},{1,0},{2,3},{3,2},{4,5},{5,4},{6,7},{7,6},{8,9},{9,8},{10,11... | collective-permute-start | bytes 1769480 | tf_op jit(solution)/shard_map/ppermute | solution.py:624
  221.6 19.7 %collective-permute-start.36 = (bf16[4,2,24,1536]{3,2,0,1:T(8,128)(2,1)S(1)}, bf16[4,2,24,1536]{3,2,0,1:T(8,128)(2,1)S(1)}, u32[]{:S(2)}, u32[]{:S(2)}) collective-permute-start(bf16[4,2,24,1536]{3,2,0,1:T(8,128)(2,1)S(1)} %fusion.15), channel_id=1, source_target_pairs={{0,4},{4,0},{8,12},{12,8},{16,20},{20,16},{24,28},{28,24},{1,5},{5... | collective-permute-start | bytes 1769480 | tf_op jit(solution)/shard_map/ppermute | solution.py:630
  222.5 15.0 %collective-permute-start.33 = (bf16[96,768]{1,0:T(8,128)(2,1)S(1)}, bf16[96,768]{1,0:T(8,128)(2,1)S(1)}, u32[]{:S(2)}, u32[]{:S(2)}) collective-permute-start(bf16[96,768]{1,0:T(8,128)(2,1)S(1)} %get-tuple-element.196), channel_id=1, source_target_pairs={{0,24},{4,28},{8,16},{12,20},{16,8},{20,12},{24,0},{28,4},{1,25},{... | collective-permute-start | bytes 442376 | tf_op jit(solution)/shard_map/ppermute | solution.py:633
  224.3 14.7 %collective-permute-start.31 = (bf16[96,768]{1,0:T(8,128)(2,1)S(1)}, bf16[96,768]{1,0:T(8,128)(2,1)S(1)}, u32[]{:S(2)}, u32[]{:S(2)}) collective-permute-start(bf16[96,768]{1,0:T(8,128)(2,1)S(1)} %get-tuple-element.197), channel_id=1, source_target_pairs={{0,8},{4,12},{8,0},{12,4},{16,24},{20,28},{24,16},{28,20},{1,9},{5... | collective-permute-start | bytes 442376 | tf_op jit(solution)/shard_map/ppermute | solution.py:633
  237.6 16.3 %collective-permute-start.35 = (bf16[4,2,24,1536]{3,2,0,1:T(8,128)(2,1)S(1)}, bf16[4,2,24,1536]{3,2,0,1:T(8,128)(2,1)S(1)}, u32[]{:S(2)}, u32[]{:S(2)}) collective-permute-start(bf16[4,2,24,1536]{3,2,0,1:T(8,128)(2,1)S(1)} %fusion.14), channel_id=1, source_target_pairs={{0,2},{1,3},{2,0},{3,1},{4,6},{5,7},{6,4},{7,5},{8,10},{9,11},{10,... | collective-permute-start | bytes 1769480 | tf_op jit(solution)/shard_map/ppermute | solution.py:627
  239.1 26.2 %collective-permute-start.41 = (bf16[768,384]{1,0:T(8,128)(2,1)S(1)}, bf16[768,384]{1,0:T(8,128)(2,1)S(1)}, u32[]{:S(2)}, u32[]{:S(2)}) collective-permute-start(bf16[768,384]{1,0:T(8,128)(2,1)S(1)} %get-tuple-element.169), channel_id=1, source_target_pairs={{0,1},{1,0},{2,3},{3,2},{4,5},{5,4},{6,7},{7,6},{8,9},{9,8},{10,11... | collective-permute-start | bytes 1769480 | tf_op jit(solution)/shard_map/ppermute | solution.py:624
  239.9 25.4 %collective-permute-start.40 = (bf16[768,384]{1,0:T(8,128)(2,1)S(1)}, bf16[768,384]{1,0:T(8,128)(2,1)S(1)}, u32[]{:S(2)}, u32[]{:S(2)}) collective-permute-start(bf16[768,384]{1,0:T(8,128)(2,1)S(1)} %get-tuple-element.170), channel_id=1, source_target_pairs={{0,1},{1,0},{2,3},{3,2},{4,5},{5,4},{6,7},{7,6},{8,9},{9,8},{10,11... | collective-permute-start | bytes 1769480 | tf_op jit(solution)/shard_map/ppermute | solution.py:624
  240.7 24.2 %collective-permute-start.39 = (bf16[768,384]{1,0:T(8,128)(2,1)S(1)}, bf16[768,384]{1,0:T(8,128)(2,1)S(1)}, u32[]{:S(2)}, u32[]{:S(2)}) collective-permute-start(bf16[768,384]{1,0:T(8,128)(2,1)S(1)} %get-tuple-element.171), channel_id=1, source_target_pairs={{0,1},{1,0},{2,3},{3,2},{4,5},{5,4},{6,7},{7,6},{8,9},{9,8},{10,11... | collective-permute-start | bytes 1769480 | tf_op jit(solution)/shard_map/ppermute | solution.py:624
  241.5 24.7 %collective-permute-start.38 = (bf16[4,24,1536]{2,1,0:T(8,128)(2,1)S(1)}, bf16[4,24,1536]{2,1,0:T(8,128)(2,1)S(1)}, u32[]{:S(2)}, u32[]{:S(2)}) collective-permute-start(bf16[4,24,1536]{2,1,0:T(8,128)(2,1)S(1)} %fusion.33), channel_id=1, source_target_pairs={{0,2},{1,3},{2,0},{3,1},{4,6},{5,7},{6,4},{7,5},{8,10},{9,11},{10,... | collective-permute-start | bytes 884744 | tf_op jit(solution)/shard_map/ppermute | solution.py:627
  279.5 16.5 %collective-permute-start.44 = (bf16[4,2,24,1664]{3,2,1,0:T(8,128)(2,1)S(1)}, bf16[4,2,24,1664]{3,2,1,0:T(8,128)(2,1)S(1)}, u32[]{:S(2)}, u32[]{:S(2)}) collective-permute-start(bf16[4,2,24,1664]{3,2,1,0:T(8,128)(2,1)S(1)} %constant_dynamic-update-slice_fusion.5), channel_id=1, source_target_pairs={{0,2},{1,3},{2,0},{3,1},{4,6},{5,7},{6,4},{7,5},{8,10},{9,11},{10,... | collective-permute-start | bytes 1916936 | tf_op jit(solution)/shard_map/ppermute | solution.py:627
  280.9 16.3 %collective-permute-start.46 = (bf16[4,2,24,1664]{3,2,1,0:T(8,128)(2,1)S(1)}, bf16[4,2,24,1664]{3,2,1,0:T(8,128)(2,1)S(1)}, u32[]{:S(2)}, u32[]{:S(2)}) collective-permute-start(bf16[4,2,24,1664]{3,2,1,0:T(8,128)(2,1)S(1)} %constant_dynamic-update-slice_fusion.6), channel_id=1, source_target_pairs={{0,4},{4,0},{8,12},{12,8},{16,20},{20,16},{24,28},{28,24},{1,5},{5... | collective-permute-start | bytes 1916936 | tf_op jit(solution)/shard_map/ppermute | solution.py:630
  (83 other events, 562.2 us)

commit v2 on v1

--- a/solution.py
+++ b/solution.py
@@ -618,127 +618,121 @@
 class Tree:
     def __init__(self):
         fsdp, rep = lax.axis_index("fsdp"), lax.axis_index("rep")
-        self.z, self.y, self.x, self.core = fsdp // 2, fsdp % 2, rep // 2, rep % 2
+        self.z, self.core = fsdp // 2, rep % 2
+        x, y = rep // 2, fsdp % 2
+        self.near = jnp.where(self.core == 0, x, y)
+        self.far = jnp.where(self.core == 0, y, x)
+        self.x, self.y = x, y
 
     def to_core(self, value):
         return lax.ppermute(value, "rep", [(i, i ^ 1) for i in range(4)])
 
-    def to_x(self, value):
-        return lax.ppermute(value, "rep", [(i, i ^ 2) for i in range(4)])
-
-    def to_y(self, value):
-        return lax.ppermute(value, "fsdp", [(i, i ^ 1) for i in range(8)])
+    def to_near(self, value):
+        return lax.ppermute(value, AXES, [(i, i ^ (4 if i % 2 else 2)) for i in range(32)])
+
+    def to_far(self, value):
+        return lax.ppermute(value, AXES, [(i, i ^ (2 if i % 2 else 4)) for i in range(32)])
 
     def to_z(self, value, step):
         return lax.ppermute(value, "fsdp", [(i, i ^ (2 * step)) for i in range(8)])
 
 
 class Gather:
-    def __init__(self, tree, first, second):
-        self.tree, self.cut = tree, first.shape[0]
-        self.own = jnp.concatenate([first, second], 0)
+    def __init__(self, tree, own):
+        self.tree, self.own = tree, own
 
     @staticmethod
     def columns(tree, shard):
         mine = pick(shard, tree.core, 1)
         got = tree.to_core(pick(shard, 1 - tree.core, 1))
-        return Gather(tree, jnp.where(tree.core == 0, mine, got), jnp.where(tree.core == 0, got, mine))
+        return Gather(tree, paired(tree.core, mine, got, 0).reshape(-1, mine.shape[1]))
 
     @staticmethod
     def rows(tree, shard):
-        cut = shard.shape[0] // 2
-        return Gather(tree, shard[:cut], shard[cut:])
+        return Gather(tree, shard)
 
     def along_z(self, *wait):
         tree = self.tree
         own = after(self.own, *wait)
         held = [own] + [tree.to_z(own, step) for step in (1, 2, 3)]
         low, high = tree.z % 2 == 1, tree.z // 2 == 1
-
-        def chosen(rows):
-            out = []
-            for place in range(4):
-                near = [jnp.where(low, held[(place ^ 1) ^ h], held[place ^ h]) for h in (0, 2)]
-                out.append(jnp.where(high, near[1], near[0])[rows])
-            return jnp.stack(out)
-
-        self.first, self.second = chosen(slice(0, self.cut)), chosen(slice(self.cut, None))
-        return self.first, self.second
+        out = []
+        for place in range(4):
+            near = [jnp.where(low, held[(place ^ 1) ^ h], held[place ^ h]) for h in (0, 2)]
+            out.append(jnp.where(high, near[1], near[0]))
+        self.held = jnp.stack(out)
+        return self.held
 
     def one(self, *wait):
         tree = self.tree
-        first, second = after((self.first, self.second), *wait)
-        self.first = paired(tree.x, first, tree.to_x(first), 1)
-        self.second = paired(tree.y, second, tree.to_y(second), 1)
-        return self.first, self.second
+        held = after(self.held, *wait)
+        self.held = paired(tree.near, held, tree.to_near(held), 1)
+        return self.held
 
     def two(self, *wait):
         tree = self.tree
-        first, second = after((self.first, self.second), *wait)
-        first = paired(tree.y, first, tree.to_y(first), 1)
-        second = paired(tree.x, second, tree.to_x(second), 2)
-        half = jnp.concatenate([first, second], 3)
-        self.half = half.reshape(-1, half.shape[-1])
+        held = after(self.held, *wait)
+        got = tree.to_far(held)
+        same, first = tree.far == 0, tree.core == 0
+        lower, upper = jnp.where(same, held, got), jnp.where(same, got, held)
+        blocks = [
+            lower[:, 0],
+            jnp.where(first, lower[:, 1], upper[:, 0]),
+            jnp.where(first, upper[:, 0], lower[:, 1]),
+            upper[:, 1],
+        ]
+        self.half = jnp.stack(blocks, 1).reshape(-1, held.shape[-1])
         return self.half
 
-    def halves(self):
-        return self.half, self.tree.to_core(self.half)
+    def halves(self, *wait):
+        return self.half, self.tree.to_core(after(self.half, *wait))
 
 
 class Reduce:
     def __init__(self, tree, rows):
         self.tree, self.rows = tree, rows
-        self.mine, self.got = [], []
+        self.terms = []
 
     def add(self, mine, other):
-        sent = other.astype(BF)
-        got = self.tree.to_core(sent)
-        self.mine.append(mine)
-        self.got.append(got)
+        got = self.tree.to_core(other.astype(BF))
+        self.terms.append([array.reshape(4, 4, self.rows, -1) for array in (mine, got)])
         return got
 
     def one(self):
         tree = self.tree
-        shaped = [
-            [array.reshape(4, 2, 2, self.rows, -1) for array in (mine, got)] for mine, got in zip(self.mine, self.got)
-        ]
-
-        def stage(rows, index, axis):
+
+        def stage(near):
+            places = [jnp.where(tree.core == 0, 2 * far + near, 2 * near + far) for far in (0, 1)]
             sums = [
-                pick(mine[:, :, :, rows], index, axis).astype(F32) + pick(got[:, :, :, rows], index, axis).astype(F32)
-                for mine, got in shaped
+                jnp.concatenate([sum(pick(term, place, 1).astype(F32) for term in pair) for pair in self.terms], -1)
+                for place in places
             ]
-            return jnp.concatenate(sums, -1)
-
-        upper, lower = slice(0, self.rows // 2), slice(self.rows // 2, None)
-        self.first_kept = stage(upper, tree.x, 2)
-        self.second_kept = stage(lower, tree.y, 1)
-        self.sent = (stage(upper, 1 - tree.x, 2).astype(BF), stage(lower, 1 - tree.y, 1).astype(BF))
-        self.got = (tree.to_x(self.sent[0]), tree.to_y(self.sent[1]))
+            return jnp.stack(sums, 1)
+
+        self.kept, self.sent = stage(tree.near), stage(1 - tree.near).astype(BF)
+        self.got = tree.to_near(self.sent)
 
     def two(self):
         tree = self.tree
-        first, second = self.first_kept + self.got[0], self.second_kept + self.got[1]
-        self.first_kept, self.second_kept = pick(first, tree.y, 1), pick(second, tree.x, 1)
-        self.sent = (pick(first, 1 - tree.y, 1).astype(BF), pick(second, 1 - tree.x, 1).astype(BF))
-        self.got = (tree.to_y(self.sent[0]), tree.to_x(self.sent[1]))
+        total = self.kept + self.got
+        self.kept, self.sent = pick(total, tree.far, 1), pick(total, 1 - tree.far, 1).astype(BF)
+        self.got = tree.to_far(self.sent)
 
     def along_z(self):
         tree = self.tree
-        both = jnp.concatenate([self.first_kept + self.got[0], self.second_kept + self.got[1]], 1)
-        self.first_kept = pick(both, tree.z, 0)
-        self.sent = tuple(pick(both, tree.z ^ step, 0).astype(BF) for step in (1, 2, 3))
+        total = self.kept + self.got
+        self.kept = pick(total, tree.z, 0)
+        self.sent = tuple(pick(total, tree.z ^ step, 0).astype(BF) for step in (1, 2, 3))
         self.got = tuple(tree.to_z(sent, step) for sent, step in zip(self.sent, (1, 2, 3)))
 
     def sums(self):
-        return self.first_kept + self.got[0] + self.got[1] + self.got[2]
+        return self.kept + self.got[0] + self.got[1] + self.got[2]
 
     def columns(self):
         tree, total = self.tree, self.sums()
-        first, second = total[: self.rows // 2], total[self.rows // 2 :]
-        keep = jnp.where(tree.core == 0, first, second)
-        got = tree.to_core(jnp.where(tree.core == 0, second, first))
-        return paired(tree.core, keep, got, 1)
+        rows = total.reshape(2, self.rows // 2, -1)
+        keep = pick(rows, tree.core, 0)
+        return paired(tree.core, keep, tree.to_core(pick(rows, 1 - tree.core, 0)), 1)
 
 
 class Whole:
@@ -772,7 +766,7 @@
     def two(self, *wait):
         return self.half
 
-    def halves(self):
+    def halves(self, *wait):
         return self.half, self.rest
 
     def add(self, mine, other):
@@ -854,13 +848,14 @@
         .reshape(part, 2, hidden_width // 2)
     )
     down_w = gather_rows(w_down.astype(BF))
-    attn_z = attn_w.along_z()
-    up_z = up_w.along_z(attn_z)
+    attn_w.along_z()
     attn_one = attn_w.one()
-    down_z = down_w.along_z(up_z)
-    attn_w.two()
-    up_one = up_w.one(attn_w.half)
-    attn_w = attn_w.halves()
+    up_z = up_w.along_z(attn_one)
+    attn_half = attn_w.two()
+    attn_w = attn_w.halves(up_z)
+    up_one = up_w.one(attn_half)
+    down_z = down_w.along_z(attn_half)
+
     place = jnp.concatenate([jnp.stack([jnp.int32(core), place]), timesteps])
     rows, start, normed_one, across_one, bias_mine, bias_other, bias_up = start_rows(
         place, tokens, absorbed, attn_w, fixed, up_cols, table_cols, small_cols, chips, hidden_part
@@ -869,20 +864,20 @@
     steps = steps.reshape(seq_cols, count, part).transpose(1, 0, 2).reshape(count, -1).astype(jnp.int32)
     steps = (steps[:, :seq_count] * 256 + steps[:, seq_count : 2 * seq_count]).reshape(-1)
 
-    qkv_mine, context_mine = attention(normed_one, attn_w[0], bias_mine, seq_length)
-    up_half = up_w.two(context_mine)
-    qkv_other, context_other = attention(after(normed_one, up_one), attn_w[1], bias_other, seq_length)
+    up_half = up_w.two(normed_one)
+    qkv_mine, context_mine = attention(after(normed_one, up_one, down_z), attn_w[0], bias_mine, seq_length)
+    down_one = down_w.one(up_half, context_mine)
+    up_w = up_w.halves(context_mine)
+    qkv_other, context_other = attention(after(normed_one, up_half), attn_w[1], bias_other, seq_length)
+    down_half = down_w.two(context_other)
+    down_w = down_w.halves()
     contexts = (context_mine, context_other)
-    middle, normed_two, across_two = middle_rows(place, contexts, attn_w, start, rows)
-    down_one = down_w.one(up_half, context_other)
-    up_w = up_w.halves()
-    down_w.two(normed_two)
+    middle, normed_two, across_two = middle_rows(place, contexts, attn_w, after(start, down_one), rows)
     hidden, slope = [None, None], [None, None]
     hidden[0], slope[0] = feed(normed_two, up_w[0], bias_up, 0)
-    hidden[1], slope[1] = feed(after(normed_two, down_one), up_w[1], bias_up, 1)
-    down_w = down_w.halves()
-
-    grad_branch = (cotangent * absorbed).astype(BF)
+    hidden[1], slope[1] = feed(normed_two, up_w[1], bias_up, 1)
+
+    grad_branch = after((cotangent * absorbed).astype(BF), down_half)
     down_sum = reduction(hidden_part)
     down_got = down_sum.add(left_product(hidden[0], grad_branch), left_product(hidden[1], grad_branch))
     up_sum = reduction(2 * part)
@@ -902,6 +897,7 @@
     )
 
     attn_sum = reduction(2 * part)
+    up_sum.add(grad_out_mine, grad_out_other)
     if fast:
         down_sum.along_z()
         up_sum.one()
@@ -917,7 +913,6 @@
     grad_qkv, grad_weights, sums = zip(*grads)
     for index in range(3):
         attn_sum.add(grad_weights[0][index], grad_weights[1][index])
-    attn_sum.add(grad_out_mine, grad_out_other)
     if fast:
         up_sum.along_z()
     grad_qkv = after(grad_qkv, up_sum.sent)
@@ -936,7 +931,7 @@
         attn_sum.two()
         attn_sum.along_z()
         attn_grad = attn_sum.columns()
-        small, seq_sums = attn_grad[:, 0, 4 * half :], attn_grad[:, 1, 4 * half :]
+        small, seq_sums = attn_grad[:, 0, 3 * half :], attn_grad[:, 1, 3 * half :]
     else:
         attn_grad = attn_sum.columns()
         small, seq_sums = [
@@ -947,9 +942,11 @@
     onehot = (steps[:, None] == lax.broadcasted_iota(jnp.int32, (seqs, table_cols), 1)).astype(F32)
     grad_time_table = jnp.dot(seq_sums, onehot, precision=lax.Precision.HIGHEST)
     grad_w_qkv = attn_grad[:, :, : 3 * half].reshape(part, 2, 3, half).transpose(0, 2, 1, 3).reshape(part, 3 * width)
-    grad_w_out = attn_grad[:, :, 3 * half : 4 * half].reshape(part, width)
-    grad_w_up = up_sum.columns().reshape(part, 2, chips, hidden_part).transpose(0, 2, 1, 3)
+    up_grad = up_sum.columns()
+    grad_w_out = up_grad[:, :, hidden_width // 2 :].reshape(part, width)
+    grad_w_up = up_grad[:, :, : hidden_width // 2].reshape(part, 2, chips, hidden_part).transpose(0, 2, 1, 3)
     grad_w_up = grad_w_up.reshape(part, hidden_width)
+    hidden = after(hidden, attn_sum.sent)
     output = middle + (product(hidden[0], down_w[0]) + product(hidden[1], down_w[1]) + rows[seq_count + 3])
     return (
         output,

time: 331 us -> 311 us (0.940)
  waiting for transfers between devices: 121 us -> 97.1 us
  starting transfers between devices: 61.7 us -> 44.6 us
  other arithmetic: 23.4 us -> 38 us
  local copies, waits for them, and re-layouts: 25.7 us -> 34 us
    ppermute x24 -> x12, waiting for transfers between devices: 75 us -> 44 us  [the longest x6 23.7 us: to_near(): lax.ppermute(value, AXES, [(i, i ^ (4 if i % 2 else 2)) for i in range(32)])]
    unnamed x107 -> x131, local copies, waits for them, and re-layouts: 2.83 us -> 24.1 us
    add x15 -> x18, other arithmetic: 4.73 us -> 20.4 us  [the longest x9 12.8 us: stage(): sum((pick(term, place, 1).astype(F32) for term in pair))]
    ppermute x24 -> x12, starting transfers between devices: 27.7 us -> 14.7 us  [the longest x6 7.62 us: to_near(): lax.ppermute(value, AXES, [(i, i ^ (4 if i % 2 else 2)) for i in range(32)])]
    ppermute x18, waiting for transfers between devices: 43.3 us -> 52.1 us  [to_z(): return lax.ppermute(value, 'fsdp', [(i, i ^ 2 * step) for i in range(8)])]
    dynamic_slice x9 -> x1, local copies, waits for them, and re-layouts: 6.98 us -> 0.41 us  [pick(): return lax.dynamic_index_in_dim(array, index, axis, keepdims=False)]
    another operation x9 -> x23, other arithmetic: 1.79 us -> 8.1 us  [the longest x11 3.03 us: stage(): return jnp.stack(sums, 1)]
    slice x14 -> x0, local copies, waits for them, and re-layouts: 5.75 us -> none  [the longest x7 3.39 us: stage(): mine[:, :, :, rows]]
  transfers between devices with their start and end apart: 56 -> 44, of which waited for: 25 -> 20; matrix products, arithmetic and copies ran while one was open for 15% -> 15% of each run, Pallas kernels for 21% -> 24%
where the time goes in v2:
time: 311 us; the launch traced here: 307 us
  waiting for transfers between devices  97.1 us (31%)
  Pallas kernels  77.9 us (25%)
  starting transfers between devices  44.6 us (14%)
  other arithmetic  38 us (12%)
  local copies, waits for them, and re-layouts  34 us (11%)
  matrix products  12.5 us (4%)
    ppermute x18, waiting for transfers between devices, to_z(): return lax.ppermute(value, 'fsdp', [(i, i ^ 2 * step) for i in range(8)])  52.1 us
    ppermute x18, starting transfers between devices, to_z(): return lax.ppermute(value, 'fsdp', [(i, i ^ 2 * step) for i in range(8)])  27.9 us
    unnamed x131, local copies, waits for them, and re-layouts  24.1 us
    ppermute x6, waiting for transfers between devices, to_near(): lax.ppermute(value, AXES, [(i, i ^ (4 if i % 2 else 2)) for i in range(32)])  23.7 us
    ppermute x6, waiting for transfers between devices, to_far(): lax.ppermute(value, AXES, [(i, i ^ (2 if i % 2 else 4)) for i in range(32)])  20.3 us
    pallas_call x2, Pallas kernels, attention_back(): pl.pallas_call(functools.partial(attention_back_kernel, length, 1.0 / mat...  18.8 us
    pallas_call x2, Pallas kernels, attention(): pl.pallas_call(functools.partial(attention_kernel, length, 1.0 / math.sqr...  15.9 us
    add x9, other arithmetic, stage(): sum((pick(term, place, 1).astype(F32) for term in pair))  12.8 us
  transfers between devices with their start and end apart: 44, of which 20 were waited for; matrix products, arithmetic and copies ran while one was open for 15% of the time, Pallas kernels for 24%

profile of v2, /device:TPU:0, one launch (start us, length us, event | category | flops | bytes accessed | tf_op | source)
XLA Modules:
  0.0 306.7 jit_solution(8845269966878177045)
XLA Ops:
  10.9 5.0 %collective-permute-start.1 = (bf16[48,2048]{1,0:T(8,128)(2,1)S(1)}, bf16[48,2048]{1,0:T(8,128)(2,1)S(1)}, u32[]{:S(2)}, u32[]{:S(2)}) collective-permute-start(bf16[48,2048]{1,0:T(8,128)(2,1)S(1)} %bitcast.452), channel_id=1, source_target_pairs={{0,24},{4,28},{8,16},{12,20},{16,8},{20,12},{24,0},{28,4},{1,25},{... | collective-permute-start | bytes 589832 | tf_op jit(solution)/shard_map/ppermute | solution.py:637
  16.6 5.2 %collective-permute-done.1 = bf16[48,2048]{1,0:T(8,128)(2,1)S(1)} collective-permute-done((bf16[48,2048]{1,0:T(8,128)(2,1)S(1)}, bf16[48,2048]{1,0:T(8,128)(2,1)S(1)}, u32[]{:S(2)}, u32[]{:S(2)}) %collective-permute-start.1) | collective-permute-done | bytes 196640 | tf_op jit(solution)/shard_map/ppermute | solution.py:637
  21.7 11.2 %collective-permute-done.2 = bf16[48,2048]{1,0:T(8,128)(2,1)S(1)} collective-permute-done((bf16[48,2048]{1,0:T(8,128)(2,1)S(1)}, bf16[48,2048]{1,0:T(8,128)(2,1)S(1)}, u32[]{:S(2)}, u32[]{:S(2)}) %collective-permute-start.2) | collective-permute-done | bytes 196640 | tf_op jit(solution)/shard_map/ppermute | solution.py:637
  35.3 9.9 %collective-permute-done.4 = bf16[4,48,2048]{2,1,0:T(8,128)(2,1)S(1)} collective-permute-done((bf16[4,48,2048]{2,1,0:T(8,128)(2,1)S(1)}, bf16[4,48,2048]{2,1,0:T(8,128)(2,1)S(1)}, u32[]{:S(2)}, u32[]{:S(2)}) %collective-permute-start.4) | collective-permute-done | bytes 786464 | tf_op jit(solution)/shard_map/ppermute | solution.py:631
  51.5 4.2 %collective-permute-done.7 = bf16[48,1536]{1,0:T(8,128)(2,1)S(1)} collective-permute-done((bf16[48,1536]{1,0:T(8,128)(2,1)S(1)}, bf16[48,1536]{1,0:T(8,128)(2,1)S(1)}, u32[]{:S(2)}, u32[]{:S(2)}) %collective-permute-start.7) | collective-permute-done | bytes 147488 | tf_op jit(solution)/shard_map/ppermute | solution.py:637
  55.7 5.1 %collective-permute-done.8 = bf16[48,1536]{1,0:T(8,128)(2,1)} collective-permute-done((bf16[48,1536]{1,0:T(8,128)(2,1)S(1)}, bf16[48,1536]{1,0:T(8,128)(2,1)}, u32[]{:S(2)}, u32[]{:S(2)}) %collective-permute-start.8) | collective-permute-done | bytes 147488 | tf_op jit(solution)/shard_map/ppermute | solution.py:637
  68.9 8.5 %collective-permute-done.11 = bf16[4,48,1536]{2,1,0:T(8,128)(2,1)} collective-permute-done((bf16[4,48,1536]{2,1,0:T(8,128)(2,1)}, bf16[4,48,1536]{2,1,0:T(8,128)(2,1)}, u32[]{:S(2)}, u32[]{:S(2)}) %collective-permute-start.11) | collective-permute-done | bytes 589856 | tf_op jit(solution)/shard_map/ppermute | solution.py:631
  90.0 4.2 %collective-permute-done.12 = bf16[96,768]{1,0:T(8,128)(2,1)S(1)} collective-permute-done((bf16[96,768]{1,0:T(8,128)(2,1)S(1)}, bf16[96,768]{1,0:T(8,128)(2,1)S(1)}, u32[]{:S(2)}, u32[]{:S(2)}) %collective-permute-start.12) | collective-permute-done | bytes 147488 | tf_op jit(solution)/shard_map/ppermute | solution.py:637
  94.2 5.1 %collective-permute-done.13 = bf16[96,768]{1,0:T(8,128)(2,1)S(1)} collective-permute-done((bf16[96,768]{1,0:T(8,128)(2,1)S(1)}, bf16[96,768]{1,0:T(8,128)(2,1)S(1)}, u32[]{:S(2)}, u32[]{:S(2)}) %collective-permute-start.13) | collective-permute-done | bytes 147488 | tf_op jit(solution)/shard_map/ppermute | solution.py:637
  99.5 7.6 %attention.2 = (bf16[3,512,384]{2,1,0:T(8,128)(2,1)S(1)}, bf16[512,384]{1,0:T(8,128)(2,1)S(1)}) custom-call(bf16[512,768]{1,0:T(8,128)(2,1)S(1)} %get-tuple-element.85.rows_ref, bf16[768,2048]{1,0:T(8,128)(2,1)S(1)} %bitcast.427, bf16[768,2048]{1,0:T(8,128)(2,1)S(1)} %bitcast.428, bf16[768,2048]{1,0:T(8,128)(2,1)S(1)} %bitcast.429, ...), custom_call_target="tpu_custom_call" | custom-call | flops 905969664 | bytes 4128768 | tf_op jit(solution)/shard_map/attention/pallas_call | solution.py:85
  110.2 8.3 %attention.3 = (bf16[3,512,384]{2,1,0:T(8,128)(2,1)S(1)}, bf16[512,384]{1,0:T(8,128)(2,1)S(1)}) custom-call(bf16[512,768]{1,0:T(8,128)(2,1)S(1)} %get-tuple-element.85.rows_ref, bf16[768,2048]{1,0:T(8,128)(2,1)} %collective-permute-done.10.table_other_ref.query_ref.key_ref.value_ref.out_other_ref.weight_other_ref, ...), custom_call_target="tpu_custom_call" | custom-call | flops 905969664 | bytes 4128768 | tf_op jit(solution)/shard_map/attention/pallas_call | solution.py:85
  124.2 11.5 %collective-permute-done.18 = bf16[4,2,96,768]{3,2,0,1:T(8,128)(2,1)S(1)} collective-permute-done((bf16[4,2,96,768]{3,2,0,1:T(8,128)(2,1)S(1)}, bf16[4,2,96,768]{3,2,0,1:T(8,128)(2,1)S(1)}, u32[]{:S(2)}, u32[]{:S(2)}) %collective-permute-start.18) | collective-permute-done | bytes 1179680 | tf_op jit(solution)/shard_map/ppermute | solution.py:634
  138.0 4.4 %feed.3 = (bf16[512,1536]{1,0:T(8,128)(2,1)S(1)}, f32[512,1536]{1,0:T(8,128)S(1)}) custom-call(bf16[512,768]{1,0:T(8,128)(2,1)S(1)} %get-tuple-element.93.rows_ref, bf16[768,1536]{1,0:T(8,128)(2,1)S(1)} %collective-permute-done.17.weight_ref.up_other_ref, f32[8,1536]{1,0:T(8,128)S(1)} %get-tuple-element.94.bias_ref), custom_call_target="tpu_custom_call" | custom-call | flops 1207959552 | bytes 7864320 | tf_op jit(solution)/shard_map/feed/pallas_call | solution.py:196
  149.3 4.4 %feed.2 = (bf16[512,1536]{1,0:T(8,128)(2,1)S(1)}, f32[512,1536]{1,0:T(8,128)S(1)}) custom-call(bf16[512,768]{1,0:T(8,128)(2,1)S(1)} %copy-done.39, bf16[768,1536]{1,0:T(8,128)(2,1)S(1)} %bitcast.434, f32[8,1536]{1,0:T(8,128)S(1)} %copy-done.45), custom_call_target="tpu_custom_call" | custom-call | flops 1207959552 | bytes 7864320 | tf_op jit(solution)/shard_map/feed/pallas_call | solution.py:196
  157.5 5.9 %feed_back.3 = (bf16[512,1536]{1,0:T(8,128)(2,1)S(1)}, f32[1,1536]{1,0:T(1,128)S(1)}, bf16[768,1536]{1,0:T(8,128)(2,1)}) custom-call(bf16[512,768]{1,0:T(8,128)(2,1)S(1)} %copy-done.9, bf16[1536,768]{1,0:T(8,128)(2,1)} %collective-permute-done.20.weight_ref, f32[512,1536]{1,0:T(8,128)S(1)} %copy-done.49, bf16[768,512]{1,0:T(8,128)(2,1)S(1)} %copy-done.36), custom_call_target="tpu_custom_call" | custom-call | flops 2415919104 | bytes 13369344 | tf_op jit(solution)/shard_map/feed_back/pallas_call | solution.py:232
  173.9 5.0 %feed_back.2 = (bf16[512,1536]{1,0:T(8,128)(2,1)S(1)}, f32[1,1536]{1,0:T(1,128)S(1)}, f32[768,1536]{1,0:T(8,128)S(1)}) custom-call(bf16[512,768]{1,0:T(8,128)(2,1)S(1)} %copy-done.10, bf16[1536,768]{1,0:T(8,128)(2,1)} %bitcast.48.weight_ref, f32[512,1536]{1,0:T(8,128)S(1)} %copy-done.47, bf16[768,512]{1,0:T(8,128)(2,1)S(1)} %copy-done.37), custom_call_target="tpu_custom_call" | custom-call | flops 2415919104 | bytes 13369344 | tf_op jit(solution)/shard_map/feed_back/pallas_call | solution.py:232
  189.7 9.4 %middle_back.1 = (f32[512,768]{1,0:T(8,128)S(1)}, bf16[512,384]{1,0:T(8,128)(2,1)S(1)}, bf16[512,384]{1,0:T(8,128)(2,1)S(1)}, f32[768,384]{1,0:T(8,128)S(1)}, bf...) custom-call(s32[6]{0:T(128)S(1)} %pad_add_fusion.place_ref, bf16[512,1536]{1,0:T(8,128)(2,1)S(1)} %get-tuple-element.107.pre_mine_ref, ...), custom_call_target="tpu_custom_call" | custom-call | flops 3623878656 | bytes 14155776 | tf_op jit(solution)/shard_map/middle_back/pallas_call | solution.py:487
  205.3 4.6 %fusion.8 = (bf16[4,48,1536]{2,1,0:T(8,128)(2,1)S(1)}, f32[4,48,1536]{2,1,0:T(8,128)}, f32[4,48,1536]{2,1,0:T(8,128)}) fusion(f32[4,4,48,1536]{3,2,1,0:T(8,128)} %bitcast.437, s32[]{:T(128)S(6)} %select_n.606, bf16[4,4,48,1536]{3,2,1,0:T(8,128)(2,1)} %bitcast.57, s32[]{:T(128)S(6)} %select_n.612, s32[]{:T(128)S(6)} %select_n.610), kind=kLoop, calls=%fused_computation.54 | loop fusion | flops 2064384 | bytes 8257548 | tf_op jit(solution)/shard_map/add | solution.py:707
  221.1 9.3 %attention_back.3 = (bf16[3,512,384]{2,1,0:T(8,128)(2,1)S(1)}, bf16[3,768,384]{2,1,0:T(8,128)(2,1)S(1)}, f32[3,384]{1,0:T(4,128)S(1)}) custom-call(bf16[3,512,384]{2,1,0:T(8,128)(2,1)S(1)} %copy-done.32, bf16[512,384]{1,0:T(8,128)(2,1)S(1)} %copy-done.43, bf16[768,512]{1,0:T(8,128)(2,1)S(1)} %copy-done.34), custom_call_target="tpu_custom_call" | custom-call | flops 905969664 | bytes 7077888 | tf_op jit(solution)/shard_map/attention_back/pallas_call | solution.py:145
  237.5 9.5 %attention_back.2 = (bf16[3,512,384]{2,1,0:T(8,128)(2,1)S(1)}, f32[3,768,384]{2,1,0:T(8,128)S(1)}, f32[3,384]{1,0:T(4,128)S(1)}) custom-call(bf16[3,512,384]{2,1,0:T(8,128)(2,1)S(1)} %copy-done.30, bf16[512,384]{1,0:T(8,128)(2,1)S(1)} %copy-done.41, bf16[768,512]{1,0:T(8,128)(2,1)S(1)} %copy-done.34), custom_call_target="tpu_custom_call" | custom-call | flops 905969664 | bytes 7077888 | tf_op jit(solution)/shard_map/attention_back/pallas_call | solution.py:145
  249.4 6.8 %start_back.1 = (f32[512,768]{1,0:T(8,128)}, f32[768,256]{1,0:T(8,128)S(1)}) custom-call(s32[6]{0:T(128)S(1)} %pad_add_fusion.place_ref, bf16[3,512,384]{2,1,0:T(8,128)(2,1)S(1)} %get-tuple-element.123.grads_mine_ref, bf16[3,512,384]{2,1,0:T(8,128)(2,1)S(1)} %get-tuple-element.124.grads_other_ref, bf16[768,2048]{1,0:T(8,128)(2,1)S(1)} %bitcast.432, ...), custom_call_target="tpu_custom_call" | custom-call | flops 1811939328 | bytes 10616832 | tf_op jit(solution)/shard_map/start_back/pallas_call | solution.py:585
  266.0 8.5 %collective-permute-done.41 = bf16[48,1920]{1,0:T(8,128)(2,1)S(1)} collective-permute-done((bf16[48,1920]{1,0:T(8,128)(2,1)S(1)}, bf16[48,1920]{1,0:T(8,128)(2,1)S(1)}, u32[]{:S(2)}, u32[]{:S(2)}) %collective-permute-start.41) | collective-permute-done | bytes 184352 | tf_op jit(solution)/shard_map/ppermute | solution.py:637
  279.1 5.6 %collective-permute-done.35 = bf16[4,48,1280]{2,1,0:T(8,128)(2,1)} collective-permute-done((bf16[4,48,1280]{2,1,0:T(8,128)(2,1)S(1)}, bf16[4,48,1280]{2,1,0:T(8,128)(2,1)}, u32[]{:S(2)}, u32[]{:S(2)}) %collective-permute-start.35) | collective-permute-done | bytes 491552 | tf_op jit(solution)/shard_map/ppermute | solution.py:634
  298.3 4.3 %add_add_fusion = f32[512,768]{1,0:T(8,128)} fusion(f32[512,768]{1,0:T(8,128)S(1)} %copy-done.18, f32[512,768]{1,0:T(8,128)S(1)} %fusion.64, f32[768]{0:T(1024)S(1)} %slice_reduce_fusion.9, bf16[512,1536]{1,0:T(8,128)(2,1)S(1)} %copy-done.51, bf16[1536,768]{1,0:T(8,128)(2,1)} %collective-permute-done.20.weight_ref), kind=kOutput, calls=%fused_computation.8 | convolution fusion | flops 1209139200 | bytes 8653824 | tf_op jit(solution)/shard_map/dot_general | solution.py:24
  (337 shorter events, 140.8 us)
Async XLA Ops:
  15.9 17.0 %collective-permute-start.2 = (bf16[48,2048]{1,0:T(8,128)(2,1)S(1)}, bf16[48,2048]{1,0:T(8,128)(2,1)S(1)}, u32[]{:S(2)}, u32[]{:S(2)}) collective-permute-start(bf16[48,2048]{1,0:T(8,128)(2,1)S(1)} %bitcast.453), channel_id=1, source_target_pairs={{0,16},{4,20},{8,24},{12,28},{16,0},{20,4},{24,8},{28,12},{1,17},{... | collective-permute-start | bytes 589832 | tf_op jit(solution)/shard_map/ppermute | solution.py:637
  15.9 17.0 %collective-permute-start.3 = (bf16[48,2048]{1,0:T(8,128)(2,1)S(1)}, bf16[48,2048]{1,0:T(8,128)(2,1)S(1)}, u32[]{:S(2)}, u32[]{:S(2)}) collective-permute-start(bf16[48,2048]{1,0:T(8,128)(2,1)S(1)} %bitcast.454), channel_id=1, source_target_pairs={{0,8},{4,12},{8,0},{12,4},{16,24},{20,28},{24,16},{28,20},{1,9},{5... | collective-permute-start | bytes 589832 | tf_op jit(solution)/shard_map/ppermute | solution.py:637
  33.1 12.1 %collective-permute-start.4 = (bf16[4,48,2048]{2,1,0:T(8,128)(2,1)S(1)}, bf16[4,48,2048]{2,1,0:T(8,128)(2,1)S(1)}, u32[]{:S(2)}, u32[]{:S(2)}) collective-permute-start(bf16[4,48,2048]{2,1,0:T(8,128)(2,1)S(1)} %pad_maximum_fusion.9), channel_id=1, source_target_pairs={{0,2},{1,5},{2,0},{3,7},{4,6},{5,1},{6,4},{7,3},{8,10},{9,13},{10,... | collective-permute-start | bytes 2359304 | tf_op jit(solution)/shard_map/ppermute | solution.py:631
  35.1 11.9 %collective-permute-start.6 = (bf16[24,1536]{1,0:T(8,128)(2,1)S(1)}, bf16[24,1536]{1,0:T(8,128)(2,1)S(1)}, u32[]{:S(2)}, u32[]{:S(2)}) collective-permute-start(bf16[24,1536]{1,0:T(8,128)(2,1)S(1)} %dynamic-slice_bitcast_fusion.2), channel_id=1, source_target_pairs={{0,1},{1,0},{2,3},{3,2},{4,5},{5,4},{6,7},{7,6},{8,9},{9,8},{10,11... | collective-permute-start | bytes 221192 | tf_op jit(solution)/shard_map/ppermute | solution.py:628
  45.4 20.5 %collective-permute-start.5 = (bf16[4,2,48,2048]{3,2,1,0:T(8,128)(2,1)S(1)}, bf16[4,2,48,2048]{3,2,1,0:T(8,128)(2,1)S(1)}, u32[]{:S(2)}, u32[]{:S(2)}) collective-permute-start(bf16[4,2,48,2048]{3,2,1,0:T(8,128)(2,1)S(1)} %pad_maximum_fusion.3), channel_id=1, source_target_pairs={{0,4},{1,3},{2,6},{3,1},{4,0},{5,7},{6,2},{7,5},{8,12},{9,11},{10,... | collective-permute-start | bytes 4718600 | tf_op jit(solution)/shard_map/ppermute | solution.py:634
  84.0 23.2 %collective-permute-start.15 = (bf16[4,2,48,1536]{3,2,1,0:T(8,128)(2,1)S(1)}, bf16[4,2,48,1536]{3,2,1,0:T(8,128)(2,1)S(1)}, u32[]{:S(2)}, u32[]{:S(2)}) collective-permute-start(bf16[4,2,48,1536]{3,2,1,0:T(8,128)(2,1)S(1)} %pad_maximum_fusion.5), channel_id=1, source_target_pairs={{0,4},{1,3},{2,6},{3,1},{4,0},{5,7},{6,2},{7,5},{8,12},{9,11},{10,... | collective-permute-start | bytes 3538952 | tf_op jit(solution)/shard_map/ppermute | solution.py:634
  110.2 27.7 %collective-permute-start.17 = (bf16[768,1536]{1,0:T(8,128)(2,1)S(1)}, bf16[768,1536]{1,0:T(8,128)(2,1)S(1)}, u32[]{:S(2)}, u32[]{:S(2)}) collective-permute-start(bf16[768,1536]{1,0:T(8,128)(2,1)S(1)} %bitcast.433), channel_id=1, source_target_pairs={{0,1},{1,0},{2,3},{3,2},{4,5},{5,4},{6,7},{7,6},{8,9},{9,8},{10,11... | collective-permute-start | bytes 7077896 | tf_op jit(solution)/shard_map/ppermute | solution.py:628
  119.6 16.2 %collective-permute-start.18 = (bf16[4,2,96,768]{3,2,0,1:T(8,128)(2,1)S(1)}, bf16[4,2,96,768]{3,2,0,1:T(8,128)(2,1)S(1)}, u32[]{:S(2)}, u32[]{:S(2)}) collective-permute-start(bf16[4,2,96,768]{3,2,0,1:T(8,128)(2,1)S(1)} %pad_maximum_fusion.6), channel_id=1, source_target_pairs={{0,4},{1,3},{2,6},{3,1},{4,0},{5,7},{6,2},{7,5},{8,12},{9,11},{10,... | collective-permute-start | bytes 3538952 | tf_op jit(solution)/shard_map/ppermute | solution.py:634
  137.9 18.1 %collective-permute-start.20 = (bf16[1536,768]{1,0:T(8,128)(2,1)}, bf16[1536,768]{1,0:T(8,128)(2,1)}, u32[]{:S(2)}, u32[]{:S(2)}) collective-permute-start(bf16[1536,768]{1,0:T(8,128)(2,1)} %bitcast.48.weight_ref), channel_id=1, source_target_pairs={{0,1},{1,0},{2,3},{3,2},{4,5},{5,4},{6,7},{7,6},{8,9},{9,8},{10,11... | collective-permute-start | bytes 7077896 | tf_op jit(solution)/shard_map/ppermute | solution.py:628
  145.2 18.3 %collective-permute-start.19 = (bf16[1536,768]{1,0:T(8,128)(2,1)}, bf16[1536,768]{1,0:T(8,128)(2,1)}, u32[]{:S(2)}, u32[]{:S(2)}) collective-permute-start(bf16[1536,768]{1,0:T(8,128)(2,1)} %convolution_convert_fusion), channel_id=1, source_target_pairs={{0,1},{1,0},{2,3},{3,2},{4,5},{5,4},{6,7},{7,6},{8,9},{9,8},{10,11... | collective-permute-start | bytes 7077896 | tf_op jit(solution)/shard_map/ppermute | solution.py:628
  163.5 40.3 %collective-permute-start.26 = (bf16[768,1536]{1,0:T(8,128)(2,1)}, bf16[768,1536]{1,0:T(8,128)(2,1)}, u32[]{:S(2)}, u32[]{:S(2)}) collective-permute-start(bf16[768,1536]{1,0:T(8,128)(2,1)} %get-tuple-element.111), channel_id=1, source_target_pairs={{0,1},{1,0},{2,3},{3,2},{4,5},{5,4},{6,7},{7,6},{8,9},{9,8},{10,11... | collective-permute-start | bytes 7077896 | tf_op jit(solution)/shard_map/ppermute | solution.py:628
  168.7 16.5 %collective-permute-start.21 = (bf16[4,2,96,768]{3,2,0,1:T(8,128)(2,1)}, bf16[4,2,96,768]{3,2,0,1:T(8,128)(2,1)}, u32[]{:S(2)}, u32[]{:S(2)}) collective-permute-start(bf16[4,2,96,768]{3,2,0,1:T(8,128)(2,1)} %pad_maximum_fusion.7), channel_id=1, source_target_pairs={{0,2},{1,5},{2,0},{3,7},{4,6},{5,1},{6,4},{7,3},{8,10},{9,13},{10,... | collective-permute-start | bytes 3538952 | tf_op jit(solution)/shard_map/ppermute | solution.py:631
  202.9 12.0 %collective-permute-start.22 = (bf16[4,96,768]{2,1,0:T(8,128)(2,1)}, bf16[4,96,768]{2,1,0:T(8,128)(2,1)}, u32[]{:S(2)}, u32[]{:S(2)}) collective-permute-start(bf16[4,96,768]{2,1,0:T(8,128)(2,1)} %fusion.6), channel_id=1, source_target_pairs={{0,4},{1,3},{2,6},{3,1},{4,0},{5,7},{6,2},{7,5},{8,12},{9,11},{10,... | collective-permute-start | bytes 1769480 | tf_op jit(solution)/shard_map/ppermute | solution.py:634
  213.4 19.7 %collective-permute-start.28 = (bf16[4,2,48,1920]{3,2,0,1:T(8,128)(2,1)}, bf16[4,2,48,1920]{3,2,0,1:T(8,128)(2,1)}, u32[]{:S(2)}, u32[]{:S(2)}) collective-permute-start(bf16[4,2,48,1920]{3,2,0,1:T(8,128)(2,1)} %pad_maximum_fusion.4), channel_id=1, source_target_pairs={{0,2},{1,5},{2,0},{3,7},{4,6},{5,1},{6,4},{7,3},{8,10},{9,13},{10,... | collective-permute-start | bytes 4423688 | tf_op jit(solution)/shard_map/ppermute | solution.py:631
  216.7 18.2 %collective-permute-start.23 = (bf16[96,768]{1,0:T(8,128)(2,1)S(1)}, bf16[96,768]{1,0:T(8,128)(2,1)S(1)}, u32[]{:S(2)}, u32[]{:S(2)}) collective-permute-start(bf16[96,768]{1,0:T(8,128)(2,1)S(1)} %get-tuple-element.197), channel_id=1, source_target_pairs={{0,8},{4,12},{8,0},{12,4},{16,24},{20,28},{24,16},{28,20},{1,9},{5... | collective-permute-start | bytes 442376 | tf_op jit(solution)/shard_map/ppermute | solution.py:637
  217.0 18.4 %collective-permute-start.24 = (bf16[96,768]{1,0:T(8,128)(2,1)S(1)}, bf16[96,768]{1,0:T(8,128)(2,1)S(1)}, u32[]{:S(2)}, u32[]{:S(2)}) collective-permute-start(bf16[96,768]{1,0:T(8,128)(2,1)S(1)} %get-tuple-element.196), channel_id=1, source_target_pairs={{0,16},{4,20},{8,24},{12,28},{16,0},{20,4},{24,8},{28,12},{1,17},{... | collective-permute-start | bytes 442376 | tf_op jit(solution)/shard_map/ppermute | solution.py:637
  219.3 17.4 %collective-permute-start.25 = (bf16[96,768]{1,0:T(8,128)(2,1)S(1)}, bf16[96,768]{1,0:T(8,128)(2,1)S(1)}, u32[]{:S(2)}, u32[]{:S(2)}) collective-permute-start(bf16[96,768]{1,0:T(8,128)(2,1)S(1)} %get-tuple-element.195), channel_id=1, source_target_pairs={{0,24},{4,28},{8,16},{12,20},{16,8},{20,12},{24,0},{28,4},{1,25},{... | collective-permute-start | bytes 442376 | tf_op jit(solution)/shard_map/ppermute | solution.py:637
  230.7 16.5 %collective-permute-start.31 = (bf16[768,384]{1,0:T(8,128)(2,1)S(1)}, bf16[768,384]{1,0:T(8,128)(2,1)S(1)}, u32[]{:S(2)}, u32[]{:S(2)}) collective-permute-start(bf16[768,384]{1,0:T(8,128)(2,1)S(1)} %get-tuple-element.180), channel_id=1, source_target_pairs={{0,1},{1,0},{2,3},{3,2},{4,5},{5,4},{6,7},{7,6},{8,9},{9,8},{10,11... | collective-permute-start | bytes 1769480 | tf_op jit(solution)/shard_map/ppermute | solution.py:628
  233.0 14.3 %collective-permute-start.30 = (bf16[768,384]{1,0:T(8,128)(2,1)S(1)}, bf16[768,384]{1,0:T(8,128)(2,1)S(1)}, u32[]{:S(2)}, u32[]{:S(2)}) collective-permute-start(bf16[768,384]{1,0:T(8,128)(2,1)S(1)} %get-tuple-element.181), channel_id=1, source_target_pairs={{0,1},{1,0},{2,3},{3,2},{4,5},{5,4},{6,7},{7,6},{8,9},{9,8},{10,11... | collective-permute-start | bytes 1769480 | tf_op jit(solution)/shard_map/ppermute | solution.py:628
  234.9 21.5 %collective-permute-start.29 = (bf16[768,384]{1,0:T(8,128)(2,1)S(1)}, bf16[768,384]{1,0:T(8,128)(2,1)S(1)}, u32[]{:S(2)}, u32[]{:S(2)}) collective-permute-start(bf16[768,384]{1,0:T(8,128)(2,1)S(1)} %get-tuple-element.179), channel_id=1, source_target_pairs={{0,1},{1,0},{2,3},{3,2},{4,5},{5,4},{6,7},{7,6},{8,9},{9,8},{10,11... | collective-permute-start | bytes 1769480 | tf_op jit(solution)/shard_map/ppermute | solution.py:628
  235.4 12.1 %collective-permute-start.32 = (bf16[4,48,1920]{2,1,0:T(8,128)(2,1)S(1)}, bf16[4,48,1920]{2,1,0:T(8,128)(2,1)S(1)}, u32[]{:S(2)}, u32[]{:S(2)}) collective-permute-start(bf16[4,48,1920]{2,1,0:T(8,128)(2,1)S(1)} %fusion.5), channel_id=1, source_target_pairs={{0,4},{1,3},{2,6},{3,1},{4,0},{5,7},{6,2},{7,5},{8,12},{9,11},{10,... | collective-permute-start | bytes 2211848 | tf_op jit(solution)/shard_map/ppermute | solution.py:634
  258.3 16.1 %collective-permute-start.41 = (bf16[48,1920]{1,0:T(8,128)(2,1)S(1)}, bf16[48,1920]{1,0:T(8,128)(2,1)S(1)}, u32[]{:S(2)}, u32[]{:S(2)}) collective-permute-start(bf16[48,1920]{1,0:T(8,128)(2,1)S(1)} %get-tuple-element.191), channel_id=1, source_target_pairs={{0,16},{4,20},{8,24},{12,28},{16,0},{20,4},{24,8},{28,12},{1,17},{... | collective-permute-start | bytes 552968 | tf_op jit(solution)/shard_map/ppermute | solution.py:637
  258.3 16.1 %collective-permute-start.40 = (bf16[48,1920]{1,0:T(8,128)(2,1)S(1)}, bf16[48,1920]{1,0:T(8,128)(2,1)S(1)}, u32[]{:S(2)}, u32[]{:S(2)}) collective-permute-start(bf16[48,1920]{1,0:T(8,128)(2,1)S(1)} %get-tuple-element.192), channel_id=1, source_target_pairs={{0,8},{4,12},{8,0},{12,4},{16,24},{20,28},{24,16},{28,20},{1,9},{5... | collective-permute-start | bytes 552968 | tf_op jit(solution)/shard_map/ppermute | solution.py:637
  261.2 14.2 %collective-permute-start.34 = (bf16[4,2,48,1280]{3,2,0,1:T(8,128)(2,1)S(1)}, bf16[4,2,48,1280]{3,2,0,1:T(8,128)(2,1)S(1)}, u32[]{:S(2)}, u32[]{:S(2)}) collective-permute-start(bf16[4,2,48,1280]{3,2,0,1:T(8,128)(2,1)S(1)} %pad_maximum_fusion.8), channel_id=1, source_target_pairs={{0,2},{1,5},{2,0},{3,7},{4,6},{5,1},{6,4},{7,3},{8,10},{9,13},{10,... | collective-permute-start | bytes 2949128 | tf_op jit(solution)/shard_map/ppermute | solution.py:631
  (83 other events, 592.0 us)

commit v3 on v2

--- a/solution.py
+++ b/solution.py
@@ -14,7 +14,7 @@
 BF = jnp.bfloat16
 F32 = jnp.float32
 LANES = 128
-VMEM_BYTES = 32 << 20
+VMEM_BYTES = 16 << 20
 GELU_OUTER = math.sqrt(2.0 / math.pi)
 GELU_INNER = 0.044715
 
@@ -519,7 +519,7 @@
             jax.ShapeDtypeStruct((8, width), F32),
         ],
         scratch_shapes=[pltpu.VMEM((block, width), F32), pltpu.VMEM((2, width, half), F32)],
-        compiler_params=pltpu.CompilerParams(vmem_limit_bytes=VMEM_BYTES),
+        compiler_params=pltpu.CompilerParams(vmem_limit_bytes=2 * VMEM_BYTES),
         cost_estimate=pl.CostEstimate(
             flops=4 * count * width * (hidden_half + width),
             bytes_accessed=4 * count * hidden_half + 4 * width * hidden_half + 16 * count * width,
@@ -530,9 +530,9 @@
 
 
 def start_back_kernel(
-    small, length, place_ref, grads_mine_ref, grads_other_ref, weight_mine_ref, weight_other_ref, start_ref, middle_ref,
-    mask_ref, rows_ref, sums_ref, sums_mine_ref, sums_other_ref,
-    tokens_ref, blocks_ref, lines_ref,
+    small, length, swap, place_ref, grads_mine_ref, grads_other_ref, weight_mine_ref, weight_other_ref, start_ref, middle_ref,
+    mask_ref, rows_ref, sums_ref, sums_mine_ref, sums_other_ref, bias_ref,
+    tokens_ref, mine_ref, other_ref, lines_ref,
 ):
     core, place = place_ref[0], place_ref[1]
     step = pl.program_id(0)
@@ -565,10 +565,16 @@
 
     @pl.when(step == pl.num_programs(0) - 1)
     def _():
-        blocks_ref[...] = lines_ref[...].T
-
-
-def start_back(place, grads, weights, start, middle, mask, rows, sums, side_sums, seqs, length, block=256):
+        blocks = (lines_ref[:LANES, :].T + bias_ref[...], lines_ref[LANES:, :].T)
+        if swap:
+            blocks = chosen_side(core, *blocks)
+        mine_ref[...] = blocks[0]
+        other_ref[...] = blocks[1].astype(other_ref.dtype)
+
+
+def start_back(
+    place, grads, weights, start, middle, mask, rows, sums, side_sums, bias, seqs, length, swap, block=256
+):
     count, width = start.shape
     half = width // 2
     small = place.shape[0] - 2
@@ -583,7 +589,7 @@
 
     grads_spec = pl.BlockSpec((3, block, half), lambda step: (0, step, 0))
     return pl.pallas_call(
-        functools.partial(start_back_kernel, small, length),
+        functools.partial(start_back_kernel, small, length, swap),
         grid=(count // block,),
         in_specs=[
             pl.BlockSpec(memory_space=pltpu.SMEM),
@@ -598,11 +604,13 @@
             whole(*sums.shape),
             whole(*side_sums[0].shape),
             whole(*side_sums[1].shape),
-        ],
-        out_specs=[over_rows(width), whole(width, lines)],
+            whole(width, LANES),
+        ],
+        out_specs=[over_rows(width), whole(width, LANES), whole(width, lines - LANES)],
         out_shape=[
             jax.ShapeDtypeStruct((count, width), F32),
-            jax.ShapeDtypeStruct((width, lines), F32),
+            jax.ShapeDtypeStruct((width, LANES), F32),
+            jax.ShapeDtypeStruct((width, lines - LANES), BF if swap else F32),
         ],
         scratch_shapes=[pltpu.VMEM((lines, width), F32)],
         compiler_params=pltpu.CompilerParams(vmem_limit_bytes=VMEM_BYTES),
@@ -612,7 +620,104 @@
             transcendentals=0,
         ),
         name="start_back",
-    )(place, *grads, *weights, start, middle, mask, rows, sums, *side_sums)
+    )(place, *grads, *weights, start, middle, mask, rows, sums, *side_sums, bias)
+
+
+def shards_kernel(fixed, seq_cols, place_ref, qkv_ref, out_ref, table_ref, *refs):
+    small_refs, (mine_ref, other_ref, full_ref) = refs[: fixed + 1], refs[fixed + 1 :]
+    core = place_ref[0]
+    part, table_cols = table_ref.shape
+    half = out_ref.shape[1] // 2
+    seq_count = place_ref.shape[0] - 2
+    lines = [ref[...] for ref in small_refs[:fixed]]
+    up = small_refs[fixed][...]
+    lines += [up[:, i : i + part] for i in range(0, up.shape[1], part)]
+    lane = lax.broadcasted_iota(jnp.int32, (1, part), 1)
+    for row in range(seq_cols):
+        line = jnp.zeros((1, part), jnp.int32)
+        for index in range(seq_count):
+            step = place_ref[2 + index]
+            line = jnp.where(lane + row * part == index, step // 256, line)
+            line = jnp.where(lane + row * part == seq_count + index, step % 256, line)
+        lines.append(line.astype(F32))
+    lines = jnp.concatenate(lines, 0).astype(BF)
+    square = (part, part)
+    unit = lax.broadcasted_iota(jnp.int32, square, 0) == lax.broadcasted_iota(jnp.int32, square, 1)
+    full_ref[...] = jnp.zeros_like(full_ref)
+    full_ref[:, :table_cols] = table_ref[...]
+    full_ref[:, table_cols : table_cols + lines.shape[0]] = right_product(jnp.where(unit, 1.0, 0.0).astype(BF), lines)
+    table_half = full_ref.shape[1] // 2
+
+    def halves(ref, top, wide):
+        return chosen_side(core, ref[:, top : top + wide], ref[:, top + wide : top + 2 * wide])
+
+    sources = [(qkv_ref, 2 * half * i, half) for i in range(3)] + [(out_ref, 0, half), (full_ref, 0, table_half)]
+    left = 0
+    for ref, top, wide in sources:
+        mine, other = halves(ref, top, wide)
+        mine_ref[:, left : left + wide] = mine.astype(BF)
+        other_ref[:, left : left + wide] = other.astype(BF)
+        left += wide
+
+
+def attention_shards(place, w_qkv, w_out, table, small, b_up, seq_cols, all_cols):
+    part = table.shape[0]
+    shape = jax.ShapeDtypeStruct((part, 2 * w_out.shape[1] + all_cols // 2), BF)
+    vmem = pl.BlockSpec(memory_space=pltpu.VMEM)
+    return pl.pallas_call(
+        functools.partial(shards_kernel, len(small), seq_cols),
+        in_specs=[pl.BlockSpec(memory_space=pltpu.SMEM)] + [vmem] * (4 + len(small)),
+        out_specs=[vmem, vmem],
+        out_shape=[shape, shape],
+        scratch_shapes=[pltpu.VMEM((part, all_cols), F32)],
+        compiler_params=pltpu.CompilerParams(vmem_limit_bytes=VMEM_BYTES),
+        cost_estimate=pl.CostEstimate(flops=0, bytes_accessed=24 * part * w_out.shape[1], transcendentals=0),
+        name="attention_shards",
+    )(place, w_qkv, w_out, table, *[item.reshape(1, -1) for item in small], b_up.reshape(1, -1))
+
+
+def route_kernel(rows, route_ref, *refs):
+    terms, (sent_ref, kept_ref) = refs[:-2], refs[-2:]
+    for index in range(2):
+        for out, place in ((sent_ref, route_ref[index]), (kept_ref, route_ref[2 + index])):
+            span = pl.ds(pl.multiple_of(place * rows, 8), rows)
+            left = 0
+            for mine, got in zip(terms[::2], terms[1::2]):
+                many = [(slice(None),)] if len(mine.shape) == 2 else [(i, slice(None)) for i in range(mine.shape[0])]
+                for at in many:
+                    where = (*at[:-1], span)
+                    total = mine[where].astype(F32) + got[where].astype(F32)
+                    out[0, index, :, left : left + total.shape[1]] = total.astype(out.dtype)
+                    left += total.shape[1]
+
+
+def routed(terms, rows, route):
+    specs, columns, bytes_read = [], 0, 0
+    for array in [item for pair in terms for item in pair]:
+        shape = (4 * rows, array.shape[-1])
+        if array.ndim == 2:
+            specs.append(pl.BlockSpec(shape, lambda z: (z, 0)))
+        else:
+            specs.append(pl.BlockSpec((array.shape[0], *shape), lambda z: (0, z, 0)))
+        bytes_read += array.size * array.dtype.itemsize
+        columns += array.size // (16 * rows)
+    columns //= 2
+    out = pl.BlockSpec((1, 2, rows, columns), lambda z: (z, 0, 0, 0))
+    return pl.pallas_call(
+        functools.partial(route_kernel, rows),
+        grid=(4,),
+        in_specs=[pl.BlockSpec(memory_space=pltpu.SMEM)] + specs,
+        out_specs=[out, out],
+        out_shape=[
+            jax.ShapeDtypeStruct((4, 2, rows, columns), BF),
+            jax.ShapeDtypeStruct((4, 2, rows, columns), F32),
+        ],
+        compiler_params=pltpu.CompilerParams(vmem_limit_bytes=VMEM_BYTES),
+        cost_estimate=pl.CostEstimate(
+            flops=0, bytes_accessed=bytes_read + 48 * rows * columns, transcendentals=0
+        ),
+        name="routed",
+    )(route, *[item for pair in terms for item in pair])
 
 
 class Tree:
@@ -622,7 +727,8 @@
         x, y = rep // 2, fsdp % 2
         self.near = jnp.where(self.core == 0, x, y)
         self.far = jnp.where(self.core == 0, y, x)
-        self.x, self.y = x, y
+        places = [jnp.where(self.core == 0, 2 * i + near, 2 * near + i) for near in (1 - self.near, self.near) for i in (0, 1)]
+        self.route = jnp.stack(places)
 
     def to_core(self, value):
         return lax.ppermute(value, "rep", [(i, i ^ 1) for i in range(4)])
@@ -642,9 +748,8 @@
         self.tree, self.own = tree, own
 
     @staticmethod
-    def columns(tree, shard):
-        mine = pick(shard, tree.core, 1)
-        got = tree.to_core(pick(shard, 1 - tree.core, 1))
+    def columns(tree, mine, other):
+        got = tree.to_core(other)
         return Gather(tree, paired(tree.core, mine, got, 0).reshape(-1, mine.shape[1]))
 
     @staticmethod
@@ -652,27 +757,33 @@
         return Gather(tree, shard)
 
     def along_z(self, *wait):
+        own = after(self.own, *wait)
+        self.got = [self.tree.to_z(own, step) for step in (1, 2, 3)]
+        self.held = own
+        return self.got
+
+    def one(self, *wait):
         tree = self.tree
-        own = after(self.own, *wait)
-        held = [own] + [tree.to_z(own, step) for step in (1, 2, 3)]
+        held = after([self.held, *self.got], *wait)
         low, high = tree.z % 2 == 1, tree.z // 2 == 1
         out = []
         for place in range(4):
             near = [jnp.where(low, held[(place ^ 1) ^ h], held[place ^ h]) for h in (0, 2)]
             out.append(jnp.where(high, near[1], near[0]))
         self.held = jnp.stack(out)
-        return self.held
-
-    def one(self, *wait):
-        tree = self.tree
-        held = after(self.held, *wait)
-        self.held = paired(tree.near, held, tree.to_near(held), 1)
-        return self.held
+        self.got = tree.to_near(self.held)
+        return self.got
 
     def two(self, *wait):
         tree = self.tree
-        held = after(self.held, *wait)
-        got = tree.to_far(held)
+        held, got = after((self.held, self.got), *wait)
+        self.held = paired(tree.near, held, got, 1)
+        self.got = tree.to_far(self.held)
+        return self.got
+
+    def halves(self, *wait):
+        tree = self.tree
+        held, got = after((self.held, self.got), *wait)
         same, first = tree.far == 0, tree.core == 0
         lower, upper = jnp.where(same, held, got), jnp.where(same, got, held)
         blocks = [
@@ -681,11 +792,8 @@
             jnp.where(first, upper[:, 0], lower[:, 1]),
             upper[:, 1],
         ]
-        self.half = jnp.stack(blocks, 1).reshape(-1, held.shape[-1])
-        return self.half
-
-    def halves(self, *wait):
-        return self.half, self.tree.to_core(after(self.half, *wait))
+        half = jnp.stack(blocks, 1).reshape(-1, held.shape[-1])
+        return half, tree.to_core(half)
 
 
 class Reduce:
@@ -695,41 +803,33 @@
 
     def add(self, mine, other):
         got = self.tree.to_core(other.astype(BF))
-        self.terms.append([array.reshape(4, 4, self.rows, -1) for array in (mine, got)])
+        self.terms.append((mine, got))
         return got
 
-    def one(self):
+    def one(self, *wait):
+        self.sent, self.kept = routed(after(self.terms, *wait), self.rows, self.tree.route)
+        self.got = self.tree.to_near(self.sent)
+
+    def two(self, *wait):
         tree = self.tree
-
-        def stage(near):
-            places = [jnp.where(tree.core == 0, 2 * far + near, 2 * near + far) for far in (0, 1)]
-            sums = [
-                jnp.concatenate([sum(pick(term, place, 1).astype(F32) for term in pair) for pair in self.terms], -1)
-                for place in places
-            ]
-            return jnp.stack(sums, 1)
-
-        self.kept, self.sent = stage(tree.near), stage(1 - tree.near).astype(BF)
-        self.got = tree.to_near(self.sent)
-
-    def two(self):
-        tree = self.tree
-        total = self.kept + self.got
+        kept, got = after((self.kept, self.got), *wait)
+        total = kept + got
         self.kept, self.sent = pick(total, tree.far, 1), pick(total, 1 - tree.far, 1).astype(BF)
         self.got = tree.to_far(self.sent)
 
-    def along_z(self):
+    def along_z(self, *others):
         tree = self.tree
-        total = self.kept + self.got
+        total = jnp.concatenate([item.kept + item.got for item in (self, *others)], -1)
         self.kept = pick(total, tree.z, 0)
         self.sent = tuple(pick(total, tree.z ^ step, 0).astype(BF) for step in (1, 2, 3))
         self.got = tuple(tree.to_z(sent, step) for sent, step in zip(self.sent, (1, 2, 3)))
 
-    def sums(self):
-        return self.kept + self.got[0] + self.got[1] + self.got[2]
-
-    def columns(self):
-        tree, total = self.tree, self.sums()
+    def sums(self, *wait):
+        kept, got = after((self.kept, self.got), *wait)
+        return kept + got[0] + got[1] + got[2]
+
+    def columns(self, *wait):
+        tree, total = self.tree, self.sums(*wait)
         rows = total.reshape(2, self.rows // 2, -1)
         keep = pick(rows, tree.core, 0)
         return paired(tree.core, keep, tree.to_core(pick(rows, 1 - tree.core, 0)), 1)
@@ -743,9 +843,9 @@
         self.got, self.sent = (), ()
 
     @staticmethod
-    def columns_of(shard):
+    def columns_of(mine, other):
         out = Whole()
-        whole = lax.all_gather(shard, AXES, axis=0, tiled=True)
+        whole = lax.all_gather(jnp.stack([mine, other], 1), AXES, axis=0, tiled=True)
         out.half, out.rest = whole[:, 0], whole[:, 1]
         return out
 
@@ -764,7 +864,7 @@
         return ()
 
     def two(self, *wait):
-        return self.half
+        return ()
 
     def halves(self, *wait):
         return self.half, self.rest
@@ -775,7 +875,10 @@
         return mine
 
     def columns(self):
-        parts = [jnp.concatenate(item, 1) for item in (self.mine, self.other)]
+        def flat(items):
+            return jnp.concatenate([part for item in items for part in (item if item.ndim == 3 else [item])], 1)
+
+        parts = [flat(item) for item in (self.mine, self.other)]
         return lax.psum_scatter(jnp.stack(parts, 1), AXES, scatter_dimension=0, tiled=True).astype(F32)
 
     def sums(self):
@@ -829,34 +932,23 @@
     fixed = len(small)
     up_cols = hidden_part // part
     seq_cols = -(-2 * seq_count // part)
-    steps = jnp.concatenate([timesteps // 256, timesteps % 256]).astype(F32)
-    steps = jnp.pad(steps, (0, seq_cols * part - 2 * seq_count)).reshape(seq_cols, part)
-    small = jnp.concatenate([jnp.stack(small), b_up.reshape(up_cols, part), steps], 0)
-    small_cols = small.shape[0]
+    small_cols = fixed + up_cols + seq_cols
     all_cols = -(-(table_cols + small_cols) // (2 * LANES)) * (2 * LANES)
-    table_half = all_cols // 2
-    small = jnp.pad(small, ((0, all_cols - table_cols - small_cols), (0, 0)))
-    table = jnp.concatenate([time_table, small.T], 1).astype(BF).reshape(part, 2, table_half)
-
-    qkv = w_qkv.astype(BF).reshape(part, 3, 2, half)
-    shard = [qkv[:, 0], qkv[:, 1], qkv[:, 2], w_out.astype(BF).reshape(part, 2, half), table]
-    attn_w = gather_columns(jnp.concatenate(shard, 2))
-    up_w = gather_columns(
-        w_up.astype(BF)
-        .reshape(part, chips, 2, hidden_part)
-        .transpose(0, 2, 1, 3)
-        .reshape(part, 2, hidden_width // 2)
-    )
+    place = jnp.concatenate([jnp.stack([jnp.int32(core), place]), timesteps])
+
+    attn_w = gather_columns(*attention_shards(place, w_qkv, w_out, time_table, small, b_up, seq_cols, all_cols))
+    up_shard = w_up.astype(BF).reshape(part, chips, 2, hidden_part).transpose(2, 0, 1, 3)
+    up_shard = up_shard.reshape(2, part, hidden_width // 2)
+    up_w = gather_columns(*[pick(up_shard, side, 0) for side in (core, 1 - core)])
     down_w = gather_rows(w_down.astype(BF))
     attn_w.along_z()
     attn_one = attn_w.one()
     up_z = up_w.along_z(attn_one)
-    attn_half = attn_w.two()
+    attn_two = attn_w.two()
+    up_one = up_w.one(attn_two)
     attn_w = attn_w.halves(up_z)
-    up_one = up_w.one(attn_half)
-    down_z = down_w.along_z(attn_half)
-
-    place = jnp.concatenate([jnp.stack([jnp.int32(core), place]), timesteps])
+    down_z = down_w.along_z(attn_two)
+
     rows, start, normed_one, across_one, bias_mine, bias_other, bias_up = start_rows(
         place, tokens, absorbed, attn_w, fixed, up_cols, table_cols, small_cols, chips, hidden_part
     )
@@ -864,33 +956,33 @@
     steps = steps.reshape(seq_cols, count, part).transpose(1, 0, 2).reshape(count, -1).astype(jnp.int32)
     steps = (steps[:, :seq_count] * 256 + steps[:, seq_count : 2 * seq_count]).reshape(-1)
 
-    up_half = up_w.two(normed_one)
-    qkv_mine, context_mine = attention(after(normed_one, up_one, down_z), attn_w[0], bias_mine, seq_length)
-    down_one = down_w.one(up_half, context_mine)
+    up_two = up_w.two(normed_one)
+    qkv_mine, context_mine = attention(after(normed_one, up_one), attn_w[0], bias_mine, seq_length)
+    down_one = down_w.one(up_two, context_mine)
     up_w = up_w.halves(context_mine)
-    qkv_other, context_other = attention(after(normed_one, up_half), attn_w[1], bias_other, seq_length)
-    down_half = down_w.two(context_other)
-    down_w = down_w.halves()
+    qkv_other, context_other = attention(after(normed_one, up_two), attn_w[1], bias_other, seq_length)
+    down_two = down_w.two(context_other)
     contexts = (context_mine, context_other)
     middle, normed_two, across_two = middle_rows(place, contexts, attn_w, after(start, down_one), rows)
     hidden, slope = [None, None], [None, None]
     hidden[0], slope[0] = feed(normed_two, up_w[0], bias_up, 0)
-    hidden[1], slope[1] = feed(normed_two, up_w[1], bias_up, 1)
-
-    grad_branch = after((cotangent * absorbed).astype(BF), down_half)
+    down_w = down_w.halves(hidden[0])
+    hidden[1], slope[1] = feed(after(normed_two, down_two), up_w[1], bias_up, 1)
+
+    grad_branch = (cotangent * absorbed).astype(BF)
     down_sum = reduction(hidden_part)
-    down_got = down_sum.add(left_product(hidden[0], grad_branch), left_product(hidden[1], grad_branch))
+    down_sum.add(left_product(hidden[0], grad_branch), left_product(hidden[1], grad_branch))
     up_sum = reduction(2 * part)
     grad_pre, grad_b_up, grad_up = [None, None], [None, None], [None, None]
-    grad_pre[1], grad_b_up[1], grad_up[1] = feed_back(grad_branch, down_w[1], slope[1], across_two, BF)
     if fast:
         down_sum.one()
-    grad_pre[0], grad_b_up[0], grad_up[0] = feed_back(
-        after(grad_branch, down_sum.sent), down_w[0], slope[0], across_two, F32
+    grad_pre[1], grad_b_up[1], grad_up[1] = feed_back(
+        after(grad_branch, down_sum.sent), down_w[1], slope[1], across_two, BF
     )
+    grad_pre[0], grad_b_up[0], grad_up[0] = feed_back(grad_branch, down_w[0], slope[0], across_two, F32)
     up_sum.add(grad_up[0], grad_up[1])
     if fast:
-        down_sum.two()
+        down_sum.two(grad_pre[0])
     grad_pre = after(grad_pre, down_sum.sent)
     grad_middle, *grad_context, grad_out_mine, grad_out_other, middle_sums = middle_back(
         place, grad_pre, up_w, middle, cotangent, absorbed, rows, contexts, attn_w
@@ -899,38 +991,39 @@
     attn_sum = reduction(2 * part)
     up_sum.add(grad_out_mine, grad_out_other)
     if fast:
+        up_sum.one(down_sum.got)
         down_sum.along_z()
-        up_sum.one()
     grads = [None, None]
     grads[1] = attention_back(
         qkv_other, after(grad_context[1], down_sum.sent, up_sum.sent), across_one, seq_length, BF
     )
     if fast:
-        up_sum.two()
-    grads[0] = attention_back(
-        qkv_mine, after(grad_context[0], down_sum.got, up_sum.sent), across_one, seq_length, F32
-    )
+        up_sum.two(down_sum.got, grads[1])
+    grads[0] = attention_back(qkv_mine, after(grad_context[0], up_sum.sent), across_one, seq_length, F32)
     grad_qkv, grad_weights, sums = zip(*grads)
-    for index in range(3):
-        attn_sum.add(grad_weights[0][index], grad_weights[1][index])
+    attn_sum.add(grad_weights[0], grad_weights[1])
     if fast:
+        attn_sum.one(up_sum.got)
         up_sum.along_z()
-    grad_qkv = after(grad_qkv, up_sum.sent)
-    seqs = count * seq_count
-    grad_tokens, blocks = start_back(
-        place, grad_qkv, attn_w, start, grad_middle, absorbed, rows, middle_sums, sums, seqs, seq_length
-    )
-
+    grad_qkv = after(grad_qkv, up_sum.sent, attn_sum.sent)
     grad_b_up = paired(core, *[item.reshape(chips, hidden_part) for item in grad_b_up], 1).reshape(count, hidden_part)
     grad_b_up = jnp.pad(grad_b_up[:, None], ((0, 0), (0, part - 1), (LANES - hidden_part, 0)))
-    grad_b_up = grad_b_up.reshape(width, LANES)
-    blocks = [blocks[:, :LANES] + grad_b_up, blocks[:, LANES:]]
+    seqs = count * seq_count
+    grad_tokens, *blocks = start_back(
+        place, grad_qkv, attn_w, start, grad_middle, absorbed, rows, middle_sums, sums,
+        grad_b_up.reshape(width, LANES), seqs, seq_length, fast,
+    )
     if fast:
-        attn_sum.add(jnp.where(core == 0, *blocks), jnp.where(core == 0, *blocks[::-1]))
-        attn_sum.one()
-        attn_sum.two()
-        attn_sum.along_z()
-        attn_grad = attn_sum.columns()
+        attn_sum.two(grad_tokens)
+        extra_sum = reduction(2 * part)
+        extra_sum.add(*blocks)
+        extra_sum.one()
+        extra_sum.two(attn_sum.sent)
+        attn_sum.along_z(extra_sum)
+        hidden = after(hidden, attn_sum.sent)
+    output = middle + (product(hidden[0], down_w[0]) + product(hidden[1], down_w[1]) + rows[seq_count + 3])
+    if fast:
+        attn_grad = attn_sum.columns(output)
         small, seq_sums = attn_grad[:, 0, 3 * half :], attn_grad[:, 1, 3 * half :]
     else:
         attn_grad = attn_sum.columns()
@@ -946,8 +1039,6 @@
     grad_w_out = up_grad[:, :, hidden_width // 2 :].reshape(part, width)
     grad_w_up = up_grad[:, :, : hidden_width // 2].reshape(part, 2, chips, hidden_part).transpose(0, 2, 1, 3)
     grad_w_up = grad_w_up.reshape(part, hidden_width)
-    hidden = after(hidden, attn_sum.sent)
-    output = middle + (product(hidden[0], down_w[0]) + product(hidden[1], down_w[1]) + rows[seq_count + 3])
     return (
         output,
         grad_tokens,

time: 311 us -> 285 us (0.916)
  waiting for transfers between devices: 97.1 us -> 65.9 us
  other arithmetic: 38 us -> 17.9 us
  Pallas kernels: 77.9 us -> 90.8 us
  local copies, waits for them, and re-layouts: 34 us -> 43.4 us
  starting transfers between devices: 44.6 us -> 49.4 us
    ppermute x6 -> x7, waiting for transfers between devices: 20.3 us -> 6.31 us  [to_far(): lax.ppermute(value, AXES, [(i, i ^ (2 if i % 2 else 4)) for i in range(32)])]
    ppermute x18, waiting for transfers between devices: 52.1 us -> 38.8 us  [to_z(): return lax.ppermute(value, 'fsdp', [(i, i ^ 2 * step) for i in range(8)])]
    pallas_call x1 -> x6, Pallas kernels: 6.75 us -> 19.3 us  [the longest x4 11.6 us: routed(): pl.pallas_call(functools.partial(route_kernel, rows), grid=(4,), in_specs...]
    add x18 -> x11, other arithmetic: 20.4 us -> 8.6 us  [the longest x4 3.54 us: two(): total = kept + got]
    ppermute x6 -> x7, waiting for transfers between devices: 23.7 us -> 14.7 us  [to_near(): lax.ppermute(value, AXES, [(i, i ^ (4 if i % 2 else 2)) for i in range(32)])]
    unnamed x131 -> x154, local copies, waits for them, and re-layouts: 24.1 us -> 32.5 us
    another operation x28 -> x10, other arithmetic: 11.5 us -> 3.53 us  [the longest x6 2.24 us: one(): self.held = jnp.stack(out)]
    ppermute x14 -> x12, waiting for transfers between devices: 0.98 us -> 6.05 us  [to_core(): return lax.ppermute(value, 'rep', [(i, i ^ 1) for i in range(4)])]
  transfers between devices with their start and end apart: 44 -> 44, of which waited for: 20 -> 16; matrix products, arithmetic and copies ran while one was open for 15% -> 11% of each run, Pallas kernels for 24% -> 28%
where the time goes in v3:
time: 285 us; the launch traced here: 283 us
  Pallas kernels  90.8 us (32%)
  waiting for transfers between devices  65.9 us (23%)
  starting transfers between devices  49.4 us (17%)
  local copies, waits for them, and re-layouts  43.4 us (15%)
  other arithmetic  17.9 us (6%)
  matrix products  14.1 us (5%)
    ppermute x18, waiting for transfers between devices, to_z(): return lax.ppermute(value, 'fsdp', [(i, i ^ 2 * step) for i in range(8)])  38.8 us
    unnamed x154, local copies, waits for them, and re-layouts  32.5 us
    ppermute x18, starting transfers between devices, to_z(): return lax.ppermute(value, 'fsdp', [(i, i ^ 2 * step) for i in range(8)])  32.1 us
    pallas_call x2, Pallas kernels, attention_back(): pl.pallas_call(functools.partial(attention_back_kernel, length, 1.0 / mat...  19.4 us
    pallas_call x2, Pallas kernels, attention(): pl.pallas_call(functools.partial(attention_kernel, length, 1.0 / math.sqr...  16.7 us
    ppermute x7, waiting for transfers between devices, to_near(): lax.ppermute(value, AXES, [(i, i ^ (4 if i % 2 else 2)) for i in range(32)])  14.7 us
    dot_general x4, matrix products, contract(): return lax.dot_general(left, right, dims, preferred_element_type=F32)  13.1 us
    pallas_call x4, Pallas kernels, routed(): pl.pallas_call(functools.partial(route_kernel, rows), grid=(4,), in_specs...  11.6 us
  transfers between devices with their start and end apart: 44, of which 16 were waited for; matrix products, arithmetic and copies ran while one was open for 11% of the time, Pallas kernels for 28%

profile of v3, /device:TPU:0, one launch (start us, length us, event | category | flops | bytes accessed | tf_op | source)
XLA Modules:
  0.0 283.4 jit_solution(8909563284172639654)
XLA Ops:
  18.5 6.3 %collective-permute-done.1 = bf16[48,2048]{1,0:T(8,128)(2,1)S(1)} collective-permute-done((bf16[48,2048]{1,0:T(8,128)(2,1)S(1)}, bf16[48,2048]{1,0:T(8,128)(2,1)S(1)}, u32[]{:S(2)}, u32[]{:S(2)}) %collective-permute-start.1) | collective-permute-done | bytes 196640 | tf_op jit(solution)/shard_map/ppermute | solution.py:743
  24.8 8.3 %collective-permute-done.2 = bf16[48,2048]{1,0:T(8,128)(2,1)S(1)} collective-permute-done((bf16[48,2048]{1,0:T(8,128)(2,1)S(1)}, bf16[48,2048]{1,0:T(8,128)(2,1)S(1)}, u32[]{:S(2)}, u32[]{:S(2)}) %collective-permute-start.2) | collective-permute-done | bytes 196640 | tf_op jit(solution)/shard_map/ppermute | solution.py:743
  34.8 10.5 %collective-permute-done.4 = bf16[4,48,2048]{2,1,0:T(8,128)(2,1)S(1)} collective-permute-done((bf16[4,48,2048]{2,1,0:T(8,128)(2,1)S(1)}, bf16[4,48,2048]{2,1,0:T(8,128)(2,1)S(1)}, u32[]{:S(2)}, u32[]{:S(2)}) %collective-permute-start.4) | collective-permute-done | bytes 786464 | tf_op jit(solution)/shard_map/ppermute | solution.py:737
  50.0 3.8 %collective-permute-start.7 = (bf16[48,1536]{1,0:T(8,128)(2,1)S(1)}, bf16[48,1536]{1,0:T(8,128)(2,1)S(1)}, u32[]{:S(2)}, u32[]{:S(2)}) collective-permute-start(bf16[48,1536]{1,0:T(8,128)(2,1)S(1)} %bitcast.213), channel_id=1, source_target_pairs={{0,8},{4,12},{8,0},{12,4},{16,24},{20,28},{24,16},{28,20},{1,9},{5... | collective-permute-start | bytes 442376 | tf_op jit(solution)/shard_map/ppermute | solution.py:743
  56.2 4.1 %collective-permute-done.7 = bf16[48,1536]{1,0:T(8,128)(2,1)S(1)} collective-permute-done((bf16[48,1536]{1,0:T(8,128)(2,1)S(1)}, bf16[48,1536]{1,0:T(8,128)(2,1)S(1)}, u32[]{:S(2)}, u32[]{:S(2)}) %collective-permute-start.7) | collective-permute-done | bytes 147488 | tf_op jit(solution)/shard_map/ppermute | solution.py:743
  60.3 7.5 %collective-permute-done.8 = bf16[48,1536]{1,0:T(8,128)(2,1)} collective-permute-done((bf16[48,1536]{1,0:T(8,128)(2,1)S(1)}, bf16[48,1536]{1,0:T(8,128)(2,1)}, u32[]{:S(2)}, u32[]{:S(2)}) %collective-permute-start.8) | collective-permute-done | bytes 147488 | tf_op jit(solution)/shard_map/ppermute | solution.py:743
  76.2 3.9 %start_rows.1 = (f32[24,768]{1,0:T(8,128)S(1)}, f32[512,768]{1,0:T(8,128)S(1)}, bf16[512,768]{1,0:T(8,128)(2,1)S(1)}, bf16[768,512]{1,0:T(8,128)(2,1)S(1)}, f32[...) custom-call(s32[6]{0:T(128)S(1)} %pad_add_fusion.place_ref, f32[512,768]{1,0:T(8,128)S(1)} %copy-done.17, ...), custom_call_target="tpu_custom_call" | custom-call | flops 37748736 | bytes 5505024 | tf_op jit(solution)/shard_map/start_rows/pallas_call | solution.py:332
  88.7 7.7 %attention.2 = (bf16[3,512,384]{2,1,0:T(8,128)(2,1)S(1)}, bf16[512,384]{1,0:T(8,128)(2,1)S(1)}) custom-call(bf16[512,768]{1,0:T(8,128)(2,1)S(1)} %get-tuple-element.156.rows_ref, bf16[768,2048]{1,0:T(8,128)(2,1)S(1)} %bitcast.182, bf16[768,2048]{1,0:T(8,128)(2,1)S(1)} %bitcast.183, bf16[768,2048]{1,0:T(8,128)(2,1)S(1)} %bitcast.184, ...), custom_call_target="tpu_custom_call" | custom-call | flops 905969664 | bytes 4128768 | tf_op jit(solution)/shard_map/attention/pallas_call | solution.py:85
  96.4 3.8 %collective-permute-done.14 = bf16[96,768]{1,0:T(8,128)(2,1)S(1)} collective-permute-done((bf16[96,768]{1,0:T(8,128)(2,1)S(1)}, bf16[96,768]{1,0:T(8,128)(2,1)S(1)}, u32[]{:S(2)}, u32[]{:S(2)}) %collective-permute-start.14) | collective-permute-done | bytes 147488 | tf_op jit(solution)/shard_map/ppermute | solution.py:743
  102.6 9.1 %attention.3 = (bf16[3,512,384]{2,1,0:T(8,128)(2,1)S(1)}, bf16[512,384]{1,0:T(8,128)(2,1)S(1)}) custom-call(bf16[512,768]{1,0:T(8,128)(2,1)S(1)} %get-tuple-element.156.rows_ref, bf16[768,2048]{1,0:T(8,128)(2,1)} %collective-permute-done.10.table_other_ref.query_ref.key_ref.value_ref.out_other_ref.weight_other_ref, ...), custom_call_target="tpu_custom_call" | custom-call | flops 905969664 | bytes 4128768 | tf_op jit(solution)/shard_map/attention/pallas_call | solution.py:85
  113.9 3.4 %middle_rows.1 = (f32[512,768]{1,0:T(8,128)S(1)}, bf16[512,768]{1,0:T(8,128)(2,1)S(1)}, bf16[768,512]{1,0:T(8,128)(2,1)S(1)}) custom-call(s32[6]{0:T(128)S(1)} %pad_add_fusion.place_ref, bf16[512,384]{1,0:T(8,128)(2,1)S(1)} %get-tuple-element.153.context_mine_ref, bf16[512,384]{1,0:T(8,128)(2,1)S(1)} %get-tuple-element.158.context_other_ref, ...), custom_call_target="tpu_custom_call" | custom-call | flops 603979776 | bytes 6684672 | tf_op jit(solution)/shard_map/middle_rows/pallas_call | solution.py:396
  119.4 4.4 %feed.2 = (bf16[512,1536]{1,0:T(8,128)(2,1)S(1)}, f32[512,1536]{1,0:T(8,128)S(1)}) custom-call(bf16[512,768]{1,0:T(8,128)(2,1)S(1)} %get-tuple-element.175.rows_ref, bf16[768,1536]{1,0:T(8,128)(2,1)S(1)} %bitcast.189, f32[8,1536]{1,0:T(8,128)S(1)} %get-tuple-element.171.bias_ref), custom_call_target="tpu_custom_call" | custom-call | flops 1207959552 | bytes 7864320 | tf_op jit(solution)/shard_map/feed/pallas_call | solution.py:196
  129.3 4.4 %feed.3 = (bf16[512,1536]{1,0:T(8,128)(2,1)S(1)}, f32[512,1536]{1,0:T(8,128)S(1)}) custom-call(bf16[512,768]{1,0:T(8,128)(2,1)S(1)} %get-tuple-element.175.rows_ref, bf16[768,1536]{1,0:T(8,128)(2,1)S(1)} %collective-permute-done.18.weight_ref.up_other_ref, f32[8,1536]{1,0:T(8,128)S(1)} %get-tuple-element.171.bias_ref), custom_call_target="tpu_custom_call" | custom-call | flops 1207959552 | bytes 7864320 | tf_op jit(solution)/shard_map/feed/pallas_call | solution.py:196
  143.7 4.2 %routed.4 = (bf16[4,2,96,768]{3,2,1,0:T(8,128)(2,1)}, f32[4,2,96,768]{3,2,1,0:T(8,128)S(1)}) custom-call(s32[4]{0:T(128)S(1)} %pad_add_fusion.1.route_ref, f32[1536,768]{1,0:T(8,128)S(1)} %fusion.31.refs_0_, bf16[1536,768]{1,0:T(8,128)(2,1)} %collective-permute-done.19.refs_1_), custom_call_target="tpu_custom_call" | custom-call | bytes 10616832 | tf_op jit(solution)/shard_map/routed/pallas_call | solution.py:706
  149.8 5.7 %feed_back.3 = (bf16[512,1536]{1,0:T(8,128)(2,1)S(1)}, f32[1,1536]{1,0:T(1,128)S(1)}, bf16[768,1536]{1,0:T(8,128)(2,1)}) custom-call(bf16[512,768]{1,0:T(8,128)(2,1)S(1)} %copy-done.7, bf16[1536,768]{1,0:T(8,128)(2,1)} %collective-permute-done.20.weight_ref, f32[512,1536]{1,0:T(8,128)S(1)} %copy-done.61, bf16[768,512]{1,0:T(8,128)(2,1)S(1)} %copy-done.52), custom_call_target="tpu_custom_call" | custom-call | flops 2415919104 | bytes 13369344 | tf_op jit(solution)/shard_map/feed_back/pallas_call | solution.py:232
  161.0 5.0 %feed_back.2 = (bf16[512,1536]{1,0:T(8,128)(2,1)S(1)}, f32[1,1536]{1,0:T(1,128)S(1)}, f32[768,1536]{1,0:T(8,128)S(1)}) custom-call(bf16[512,768]{1,0:T(8,128)(2,1)S(1)} %copy-done.8, bf16[1536,768]{1,0:T(8,128)(2,1)} %bitcast.48.weight_ref, f32[512,1536]{1,0:T(8,128)S(1)} %copy-done.59, bf16[768,512]{1,0:T(8,128)(2,1)S(1)} %copy-done.53), custom_call_target="tpu_custom_call" | custom-call | flops 2415919104 | bytes 13369344 | tf_op jit(solution)/shard_map/feed_back/pallas_call | solution.py:232
  170.3 8.6 %middle_back.1 = (f32[512,768]{1,0:T(8,128)S(1)}, bf16[512,384]{1,0:T(8,128)(2,1)S(1)}, bf16[512,384]{1,0:T(8,128)(2,1)S(1)}, f32[768,384]{1,0:T(8,128)S(1)}, bf...) custom-call(s32[6]{0:T(128)S(1)} %pad_add_fusion.place_ref, bf16[512,1536]{1,0:T(8,128)(2,1)S(1)} %get-tuple-element.192.pre_mine_ref, ...), custom_call_target="tpu_custom_call" | custom-call | flops 3623878656 | bytes 14155776 | tf_op jit(solution)/shard_map/middle_back/pallas_call | solution.py:487
  181.0 3.9 %routed.5 = (bf16[4,2,48,1920]{3,2,1,0:T(8,128)(2,1)}, f32[4,2,48,1920]{3,2,1,0:T(8,128)S(1)}) custom-call(s32[4]{0:T(128)S(1)} %pad_add_fusion.1.route_ref, f32[768,1536]{1,0:T(8,128)S(1)} %get-tuple-element.199.refs_0_, bf16[768,1536]{1,0:T(8,128)(2,1)} %collective-permute-done.22.refs_1_, f32[768,384]{1,0:T(8,128)S(1)} %get-tuple-element.201.refs_2_, ...), custom_call_target="tpu_custom_call" | custom-call | bytes 13271040 | tf_op jit(solution)/shard_map/routed/pallas_call | solution.py:706
  194.8 9.9 %attention_back.2 = (bf16[3,512,384]{2,1,0:T(8,128)(2,1)S(1)}, bf16[3,768,384]{2,1,0:T(8,128)(2,1)}, f32[3,384]{1,0:T(4,128)S(1)}) custom-call(bf16[3,512,384]{2,1,0:T(8,128)(2,1)S(1)} %copy-done.47, bf16[512,384]{1,0:T(8,128)(2,1)S(1)} %copy-done.57, bf16[768,512]{1,0:T(8,128)(2,1)S(1)} %copy-done.49), custom_call_target="tpu_custom_call" | custom-call | flops 905969664 | bytes 7077888 | tf_op jit(solution)/shard_map/attention_back/pallas_call | solution.py:145
  217.8 9.5 %attention_back.3 = (bf16[3,512,384]{2,1,0:T(8,128)(2,1)S(1)}, f32[3,768,384]{2,1,0:T(8,128)S(1)}, f32[3,384]{1,0:T(4,128)S(1)}) custom-call(bf16[3,512,384]{2,1,0:T(8,128)(2,1)S(1)} %copy-done.45, bf16[512,384]{1,0:T(8,128)(2,1)S(1)} %copy-done.55, bf16[768,512]{1,0:T(8,128)(2,1)S(1)} %copy-done.50), custom_call_target="tpu_custom_call" | custom-call | flops 905969664 | bytes 7077888 | tf_op jit(solution)/shard_map/attention_back/pallas_call | solution.py:145
  237.7 6.9 %start_back.1 = (f32[512,768]{1,0:T(8,128)}, f32[768,128]{1,0:T(8,128)S(1)}, bf16[768,128]{1,0:T(8,128)(2,1)S(1)}) custom-call(s32[6]{0:T(128)S(1)} %pad_add_fusion.place_ref, bf16[3,512,384]{2,1,0:T(8,128)(2,1)S(1)} %get-tuple-element.221.grads_mine_ref, bf16[3,512,384]{2,1,0:T(8,128)(2,1)S(1)} %copy-done.30, bf16[768,2048]{1,0:T(8,128)(2,1)S(1)} %bitcast.187, ...), custom_call_target="tpu_custom_call" | custom-call | flops 1811939328 | bytes 10616832 | tf_op jit(solution)/shard_map/start_back/pallas_call | solution.py:591
  244.6 6.5 %collective-permute-done.41 = bf16[48,1920]{1,0:T(8,128)(2,1)S(1)} collective-permute-done((bf16[48,1920]{1,0:T(8,128)(2,1)S(1)}, bf16[48,1920]{1,0:T(8,128)(2,1)S(1)}, u32[]{:S(2)}, u32[]{:S(2)}) %collective-permute-start.41) | collective-permute-done | bytes 184352 | tf_op jit(solution)/shard_map/ppermute | solution.py:743
  258.1 4.0 %collective-permute-done.35 = bf16[4,48,128]{2,1,0:T(8,128)(2,1)S(1)} collective-permute-done((bf16[4,48,128]{2,1,0:T(8,128)(2,1)S(1)}, bf16[4,48,128]{2,1,0:T(8,128)(2,1)S(1)}, u32[]{:S(2)}, u32[]{:S(2)}) %collective-permute-start.35) | collective-permute-done | bytes 49184 | tf_op jit(solution)/shard_map/ppermute | solution.py:740
  270.6 4.2 %add_add_fusion = f32[512,768]{1,0:T(8,128)} fusion(f32[512,768]{1,0:T(8,128)S(1)} %copy-done.20, f32[512,768]{1,0:T(8,128)S(1)} %fusion.32, f32[768]{0:T(1024)S(1)} %copy-done.74, bf16[512,1536]{1,0:T(8,128)(2,1)S(1)} %copy-done.63, bf16[1536,768]{1,0:T(8,128)(2,1)} %collective-permute-done.20.weight_ref), kind=kOutput, calls=%fused_computation.12 | convolution fusion | flops 1209139200 | bytes 8653824 | tf_op jit(solution)/shard_map/dot_general | solution.py:24
  (327 shorter events, 136.2 us)
Async XLA Ops:
  15.9 17.1 %collective-permute-start.2 = (bf16[48,2048]{1,0:T(8,128)(2,1)S(1)}, bf16[48,2048]{1,0:T(8,128)(2,1)S(1)}, u32[]{:S(2)}, u32[]{:S(2)}) collective-permute-start(bf16[48,2048]{1,0:T(8,128)(2,1)S(1)} %bitcast.210), channel_id=1, source_target_pairs={{0,16},{4,20},{8,24},{12,28},{16,0},{20,4},{24,8},{28,12},{1,17},{... | collective-permute-start | bytes 589832 | tf_op jit(solution)/shard_map/ppermute | solution.py:743
  18.5 14.5 %collective-permute-start.3 = (bf16[48,2048]{1,0:T(8,128)(2,1)S(1)}, bf16[48,2048]{1,0:T(8,128)(2,1)S(1)}, u32[]{:S(2)}, u32[]{:S(2)}) collective-permute-start(bf16[48,2048]{1,0:T(8,128)(2,1)S(1)} %bitcast.211), channel_id=1, source_target_pairs={{0,24},{4,28},{8,16},{12,20},{16,8},{20,12},{24,0},{28,4},{1,25},{... | collective-permute-start | bytes 589832 | tf_op jit(solution)/shard_map/ppermute | solution.py:743
  45.6 22.2 %collective-permute-start.5 = (bf16[4,2,48,2048]{3,2,1,0:T(8,128)(2,1)S(1)}, bf16[4,2,48,2048]{3,2,1,0:T(8,128)(2,1)S(1)}, u32[]{:S(2)}, u32[]{:S(2)}) collective-permute-start(bf16[4,2,48,2048]{3,2,1,0:T(8,128)(2,1)S(1)} %pad_maximum_fusion.3), channel_id=1, source_target_pairs={{0,4},{1,3},{2,6},{3,1},{4,0},{5,7},{6,2},{7,5},{8,12},{9,11},{10,... | collective-permute-start | bytes 4718600 | tf_op jit(solution)/shard_map/ppermute | solution.py:740
  53.8 14.1 %collective-permute-start.8 = (bf16[48,1536]{1,0:T(8,128)(2,1)S(1)}, bf16[48,1536]{1,0:T(8,128)(2,1)}, u32[]{:S(2)}, u32[]{:S(2)}) collective-permute-start(bf16[48,1536]{1,0:T(8,128)(2,1)S(1)} %bitcast.214), channel_id=1, source_target_pairs={{0,16},{4,20},{8,24},{12,28},{16,0},{20,4},{24,8},{28,12},{1,17},{... | collective-permute-start | bytes 442376 | tf_op jit(solution)/shard_map/ppermute | solution.py:743
  54.8 13.0 %collective-permute-start.9 = (bf16[48,1536]{1,0:T(8,128)(2,1)S(1)}, bf16[48,1536]{1,0:T(8,128)(2,1)}, u32[]{:S(2)}, u32[]{:S(2)}) collective-permute-start(bf16[48,1536]{1,0:T(8,128)(2,1)S(1)} %bitcast.215), channel_id=1, source_target_pairs={{0,24},{4,28},{8,16},{12,20},{16,8},{20,12},{24,0},{28,4},{1,25},{... | collective-permute-start | bytes 442376 | tf_op jit(solution)/shard_map/ppermute | solution.py:743
  82.6 17.6 %collective-permute-start.12 = (bf16[4,2,48,1536]{3,2,1,0:T(8,128)(2,1)S(1)}, bf16[4,2,48,1536]{3,2,1,0:T(8,128)(2,1)S(1)}, u32[]{:S(2)}, u32[]{:S(2)}) collective-permute-start(bf16[4,2,48,1536]{3,2,1,0:T(8,128)(2,1)S(1)} %pad_maximum_fusion.4), channel_id=1, source_target_pairs={{0,4},{1,3},{2,6},{3,1},{4,0},{5,7},{6,2},{7,5},{8,12},{9,11},{10,... | collective-permute-start | bytes 3538952 | tf_op jit(solution)/shard_map/ppermute | solution.py:740
  83.4 12.9 %collective-permute-start.13 = (bf16[96,768]{1,0:T(8,128)(2,1)S(1)}, bf16[96,768]{1,0:T(8,128)(2,1)S(1)}, u32[]{:S(2)}, u32[]{:S(2)}) collective-permute-start(bf16[96,768]{1,0:T(8,128)(2,1)S(1)} %convert_element_type.155), channel_id=1, source_target_pairs={{0,8},{4,12},{8,0},{12,4},{16,24},{20,28},{24,16},{28,20},{1,9},{5... | collective-permute-start | bytes 442376 | tf_op jit(solution)/shard_map/ppermute | solution.py:743
  86.2 14.0 %collective-permute-start.14 = (bf16[96,768]{1,0:T(8,128)(2,1)S(1)}, bf16[96,768]{1,0:T(8,128)(2,1)S(1)}, u32[]{:S(2)}, u32[]{:S(2)}) collective-permute-start(bf16[96,768]{1,0:T(8,128)(2,1)S(1)} %convert_element_type.155), channel_id=1, source_target_pairs={{0,16},{4,20},{8,24},{12,28},{16,0},{20,4},{24,8},{28,12},{1,17},{... | collective-permute-start | bytes 442376 | tf_op jit(solution)/shard_map/ppermute | solution.py:743
  87.3 12.9 %collective-permute-start.15 = (bf16[96,768]{1,0:T(8,128)(2,1)S(1)}, bf16[96,768]{1,0:T(8,128)(2,1)S(1)}, u32[]{:S(2)}, u32[]{:S(2)}) collective-permute-start(bf16[96,768]{1,0:T(8,128)(2,1)S(1)} %convert_element_type.155), channel_id=1, source_target_pairs={{0,24},{4,28},{8,16},{12,20},{16,8},{20,12},{24,0},{28,4},{1,25},{... | collective-permute-start | bytes 442376 | tf_op jit(solution)/shard_map/ppermute | solution.py:743
  102.5 26.7 %collective-permute-start.18 = (bf16[768,1536]{1,0:T(8,128)(2,1)S(1)}, bf16[768,1536]{1,0:T(8,128)(2,1)S(1)}, u32[]{:S(2)}, u32[]{:S(2)}) collective-permute-start(bf16[768,1536]{1,0:T(8,128)(2,1)S(1)} %bitcast.188), channel_id=1, source_target_pairs={{0,1},{1,0},{2,3},{3,2},{4,5},{5,4},{6,7},{7,6},{8,9},{9,8},{10,11... | collective-permute-start | bytes 7077896 | tf_op jit(solution)/shard_map/ppermute | solution.py:734
  112.7 16.2 %collective-permute-start.17 = (bf16[4,2,96,768]{3,2,0,1:T(8,128)(2,1)S(1)}, bf16[4,2,96,768]{3,2,0,1:T(8,128)(2,1)S(1)}, u32[]{:S(2)}, u32[]{:S(2)}) collective-permute-start(bf16[4,2,96,768]{3,2,0,1:T(8,128)(2,1)S(1)} %pad_maximum_fusion.5), channel_id=1, source_target_pairs={{0,4},{1,3},{2,6},{3,1},{4,0},{5,7},{6,2},{7,5},{8,12},{9,11},{10,... | collective-permute-start | bytes 3538952 | tf_op jit(solution)/shard_map/ppermute | solution.py:740
  149.3 16.7 %collective-permute-start.21 = (bf16[4,2,96,768]{3,2,1,0:T(8,128)(2,1)}, bf16[4,2,96,768]{3,2,1,0:T(8,128)(2,1)}, u32[]{:S(2)}, u32[]{:S(2)}) collective-permute-start(bf16[4,2,96,768]{3,2,1,0:T(8,128)(2,1)} %get-tuple-element.185), channel_id=1, source_target_pairs={{0,2},{1,5},{2,0},{3,7},{4,6},{5,1},{6,4},{7,3},{8,10},{9,13},{10,... | collective-permute-start | bytes 3538952 | tf_op jit(solution)/shard_map/ppermute | solution.py:737
  156.7 24.3 %collective-permute-start.22 = (bf16[768,1536]{1,0:T(8,128)(2,1)}, bf16[768,1536]{1,0:T(8,128)(2,1)}, u32[]{:S(2)}, u32[]{:S(2)}) collective-permute-start(bf16[768,1536]{1,0:T(8,128)(2,1)} %get-tuple-element.196), channel_id=1, source_target_pairs={{0,1},{1,0},{2,3},{3,2},{4,5},{5,4},{6,7},{7,6},{8,9},{9,8},{10,11... | collective-permute-start | bytes 7077896 | tf_op jit(solution)/shard_map/ppermute | solution.py:734
  186.6 19.9 %collective-permute-start.25 = (bf16[4,2,48,1920]{3,2,1,0:T(8,128)(2,1)}, bf16[4,2,48,1920]{3,2,1,0:T(8,128)(2,1)}, u32[]{:S(2)}, u32[]{:S(2)}) collective-permute-start(bf16[4,2,48,1920]{3,2,1,0:T(8,128)(2,1)} %get-tuple-element.204), channel_id=1, source_target_pairs={{0,2},{1,5},{2,0},{3,7},{4,6},{5,1},{6,4},{7,3},{8,10},{9,13},{10,... | collective-permute-start | bytes 4423688 | tf_op jit(solution)/shard_map/ppermute | solution.py:737
  190.0 16.5 %collective-permute-start.26 = (bf16[96,768]{1,0:T(8,128)(2,1)S(1)}, bf16[96,768]{1,0:T(8,128)(2,1)S(1)}, u32[]{:S(2)}, u32[]{:S(2)}) collective-permute-start(bf16[96,768]{1,0:T(8,128)(2,1)S(1)} %get-tuple-element.285), channel_id=1, source_target_pairs={{0,8},{4,12},{8,0},{12,4},{16,24},{20,28},{24,16},{28,20},{1,9},{5... | collective-permute-start | bytes 442376 | tf_op jit(solution)/shard_map/ppermute | solution.py:743
  192.4 14.1 %collective-permute-start.27 = (bf16[96,768]{1,0:T(8,128)(2,1)S(1)}, bf16[96,768]{1,0:T(8,128)(2,1)S(1)}, u32[]{:S(2)}, u32[]{:S(2)}) collective-permute-start(bf16[96,768]{1,0:T(8,128)(2,1)S(1)} %get-tuple-element.284), channel_id=1, source_target_pairs={{0,16},{4,20},{8,24},{12,28},{16,0},{20,4},{24,8},{28,12},{1,17},{... | collective-permute-start | bytes 442376 | tf_op jit(solution)/shard_map/ppermute | solution.py:743
  193.4 13.1 %collective-permute-start.28 = (bf16[96,768]{1,0:T(8,128)(2,1)S(1)}, bf16[96,768]{1,0:T(8,128)(2,1)S(1)}, u32[]{:S(2)}, u32[]{:S(2)}) collective-permute-start(bf16[96,768]{1,0:T(8,128)(2,1)S(1)} %get-tuple-element.283), channel_id=1, source_target_pairs={{0,24},{4,28},{8,16},{12,20},{16,8},{20,12},{24,0},{28,4},{1,25},{... | collective-permute-start | bytes 442376 | tf_op jit(solution)/shard_map/ppermute | solution.py:743
  205.8 21.6 %collective-permute-start.29 = (bf16[3,768,384]{2,1,0:T(8,128)(2,1)}, bf16[3,768,384]{2,1,0:T(8,128)(2,1)}, u32[]{:S(2)}, u32[]{:S(2)}) collective-permute-start(bf16[3,768,384]{2,1,0:T(8,128)(2,1)} %get-tuple-element.210), channel_id=1, source_target_pairs={{0,1},{1,0},{2,3},{3,2},{4,5},{5,4},{6,7},{7,6},{8,9},{9,8},{10,11... | collective-permute-start | bytes 5308424 | tf_op jit(solution)/shard_map/ppermute | solution.py:734
  211.5 15.8 %collective-permute-start.30 = (bf16[4,48,1920]{2,1,0:T(8,128)(2,1)}, bf16[4,48,1920]{2,1,0:T(8,128)(2,1)}, u32[]{:S(2)}, u32[]{:S(2)}) collective-permute-start(bf16[4,48,1920]{2,1,0:T(8,128)(2,1)} %fusion), channel_id=1, source_target_pairs={{0,4},{1,3},{2,6},{3,1},{4,0},{5,7},{6,2},{7,5},{8,12},{9,11},{10,... | collective-permute-start | bytes 2211848 | tf_op jit(solution)/shard_map/ppermute | solution.py:740
  231.6 21.4 %collective-permute-start.31 = (bf16[4,2,48,1152]{3,2,1,0:T(8,128)(2,1)S(1)}, bf16[4,2,48,1152]{3,2,1,0:T(8,128)(2,1)S(1)}, u32[]{:S(2)}, u32[]{:S(2)}) collective-permute-start(bf16[4,2,48,1152]{3,2,1,0:T(8,128)(2,1)S(1)} %get-tuple-element.219), channel_id=1, source_target_pairs={{0,2},{1,5},{2,0},{3,7},{4,6},{5,1},{6,4},{7,3},{8,10},{9,13},{10,... | collective-permute-start | bytes 2654216 | tf_op jit(solution)/shard_map/ppermute | solution.py:737
  235.2 15.8 %collective-permute-start.41 = (bf16[48,1920]{1,0:T(8,128)(2,1)S(1)}, bf16[48,1920]{1,0:T(8,128)(2,1)S(1)}, u32[]{:S(2)}, u32[]{:S(2)}) collective-permute-start(bf16[48,1920]{1,0:T(8,128)(2,1)S(1)} %get-tuple-element.281), channel_id=1, source_target_pairs={{0,16},{4,20},{8,24},{12,28},{16,0},{20,4},{24,8},{28,12},{1,17},{... | collective-permute-start | bytes 552968 | tf_op jit(solution)/shard_map/ppermute | solution.py:743
  236.2 14.9 %collective-permute-start.42 = (bf16[48,1920]{1,0:T(8,128)(2,1)S(1)}, bf16[48,1920]{1,0:T(8,128)(2,1)S(1)}, u32[]{:S(2)}, u32[]{:S(2)}) collective-permute-start(bf16[48,1920]{1,0:T(8,128)(2,1)S(1)} %get-tuple-element.280), channel_id=1, source_target_pairs={{0,24},{4,28},{8,16},{12,20},{16,8},{20,12},{24,0},{28,4},{1,25},{... | collective-permute-start | bytes 552968 | tf_op jit(solution)/shard_map/ppermute | solution.py:743
  262.3 12.5 %collective-permute-start.36 = (bf16[48,1280]{1,0:T(8,128)(2,1)S(1)}, bf16[48,1280]{1,0:T(8,128)(2,1)S(1)}, u32[]{:S(2)}, u32[]{:S(2)}) collective-permute-start(bf16[48,1280]{1,0:T(8,128)(2,1)S(1)} %get-tuple-element.295), channel_id=1, source_target_pairs={{0,8},{4,12},{8,0},{12,4},{16,24},{20,28},{24,16},{28,20},{1,9},{5... | collective-permute-start | bytes 368648 | tf_op jit(solution)/shard_map/ppermute | solution.py:743
  264.9 12.3 %collective-permute-start.37 = (bf16[48,1280]{1,0:T(8,128)(2,1)S(1)}, bf16[48,1280]{1,0:T(8,128)(2,1)S(1)}, u32[]{:S(2)}, u32[]{:S(2)}) collective-permute-start(bf16[48,1280]{1,0:T(8,128)(2,1)S(1)} %get-tuple-element.296), channel_id=1, source_target_pairs={{0,16},{4,20},{8,24},{12,28},{16,0},{20,4},{24,8},{28,12},{1,17},{... | collective-permute-start | bytes 368648 | tf_op jit(solution)/shard_map/ppermute | solution.py:743
  (97 other events, 488.6 us)

commit v4 on v3

--- a/solution.py
+++ b/solution.py
@@ -44,6 +44,10 @@
     return jnp.stack([jnp.where(bit == 0, mine, other), jnp.where(bit == 0, other, mine)], axis)
 
 
+def in_hbm(value):
+    return pltpu.with_memory_space_constraint(value, pltpu.HBM)
+
+
 def after(value, *others):
     return lax.optimization_barrier((value, others))[0]
 
@@ -97,7 +101,7 @@
             pl.BlockSpec((tokens, LANES), lambda pair: (0, pair)),
         ],
         out_shape=[
-            jax.ShapeDtypeStruct((3, tokens, half), BF),
+            pltpu.HBM((3, tokens, half), BF),
             jax.ShapeDtypeStruct((tokens, half), BF),
         ],
         compiler_params=pltpu.CompilerParams(vmem_limit_bytes=VMEM_BYTES),
@@ -156,7 +160,7 @@
             pl.BlockSpec((3, LANES), lambda pair: (0, pair)),
         ],
         out_shape=[
-            jax.ShapeDtypeStruct((3, tokens, half), BF),
+            pltpu.HBM((3, tokens, half), BF),
             jax.ShapeDtypeStruct((3, width, half), dtype),
             jax.ShapeDtypeStruct((3, half), F32),
         ],
@@ -167,7 +171,7 @@
             transcendentals=2 * tokens * length * pairs,
         ),
         name="attention_back",
-    )(qkv, grad, rows_across)
+    )(in_hbm(qkv), in_hbm(grad), in_hbm(rows_across))
 
 
 def feed_kernel(side, rows_ref, weight_ref, bias_ref, hidden_ref, slope_ref, pre_ref):
@@ -203,8 +207,8 @@
         ],
         out_specs=[out, out],
         out_shape=[
-            jax.ShapeDtypeStruct((tokens, columns), BF),
-            jax.ShapeDtypeStruct((tokens, columns), F32),
+            pltpu.HBM((tokens, columns), BF),
+            pltpu.HBM((tokens, columns), F32),
         ],
         scratch_shapes=[pltpu.VMEM((tokens, block), F32)],
         compiler_params=pltpu.CompilerParams(vmem_limit_bytes=VMEM_BYTES),
@@ -244,7 +248,7 @@
             pl.BlockSpec((width, block), lambda step: (0, step)),
         ],
         out_shape=[
-            jax.ShapeDtypeStruct((tokens, columns), BF),
+            pltpu.HBM((tokens, columns), BF),
             jax.ShapeDtypeStruct((1, columns), F32),
             jax.ShapeDtypeStruct((width, columns), dtype),
         ],
@@ -255,7 +259,7 @@
             transcendentals=0,
         ),
         name="feed_back",
-    )(grad, weight, slope, rows_across)
+    )(in_hbm(grad), in_hbm(weight), in_hbm(slope), in_hbm(rows_across))
 
 
 def chosen_side(core, mine, other):
@@ -352,9 +356,9 @@
         ],
         out_shape=[
             jax.ShapeDtypeStruct((row_count, width), F32),
-            jax.ShapeDtypeStruct((count, width), F32),
+            pltpu.HBM((count, width), F32),
             jax.ShapeDtypeStruct((count, width), BF),
-            jax.ShapeDtypeStruct((width, count), BF),
+            pltpu.HBM((width, count), BF),
             jax.ShapeDtypeStruct((8, half), F32),
             jax.ShapeDtypeStruct((8, half), F32),
             jax.ShapeDtypeStruct((8, chips * hidden_part), F32),
@@ -364,7 +368,7 @@
             flops=4 * row_count * width * table_half, bytes_accessed=14 * count * width, transcendentals=0
         ),
         name="start_rows",
-    )(place, tokens, mask, *weights)
+    )(place, in_hbm(tokens), mask, *weights)
 
 
 def middle_kernel(
@@ -407,9 +411,9 @@
         ],
         out_specs=[rows_spec, rows_spec, pl.BlockSpec((width, block), lambda step: (0, step))],
         out_shape=[
-            jax.ShapeDtypeStruct((count, width), F32),
+            pltpu.HBM((count, width), F32),
             jax.ShapeDtypeStruct((count, width), BF),
-            jax.ShapeDtypeStruct((width, count), BF),
+            pltpu.HBM((width, count), BF),
         ],
         compiler_params=pltpu.CompilerParams(vmem_limit_bytes=VMEM_BYTES),
         cost_estimate=pl.CostEstimate(
@@ -615,9 +619,7 @@
         scratch_shapes=[pltpu.VMEM((lines, width), F32)],
         compiler_params=pltpu.CompilerParams(vmem_limit_bytes=VMEM_BYTES),
         cost_estimate=pl.CostEstimate(
-            flops=4 * count * width * 3 * half,
-            bytes_accessed=12 * count * half + 12 * width * half + 12 * count * width,
-            transcendentals=0,
+            flops=0, bytes_accessed=1024, transcendentals=0
         ),
         name="start_back",
     )(place, *grads, *weights, start, middle, mask, rows, sums, *side_sums, bias)
@@ -670,7 +672,7 @@
         out_specs=[vmem, vmem],
         out_shape=[shape, shape],
         scratch_shapes=[pltpu.VMEM((part, all_cols), F32)],
-        compiler_params=pltpu.CompilerParams(vmem_limit_bytes=VMEM_BYTES),
+        compiler_params=pltpu.CompilerParams(vmem_limit_bytes=60 << 20),
         cost_estimate=pl.CostEstimate(flops=0, bytes_accessed=24 * part * w_out.shape[1], transcendentals=0),
         name="attention_shards",
     )(place, w_qkv, w_out, table, *[item.reshape(1, -1) for item in small], b_up.reshape(1, -1))
@@ -710,7 +712,7 @@
         out_specs=[out, out],
         out_shape=[
             jax.ShapeDtypeStruct((4, 2, rows, columns), BF),
-            jax.ShapeDtypeStruct((4, 2, rows, columns), F32),
+            pltpu.HBM((4, 2, rows, columns), F32),
         ],
         compiler_params=pltpu.CompilerParams(vmem_limit_bytes=VMEM_BYTES),
         cost_estimate=pl.CostEstimate(
@@ -758,8 +760,8 @@
 
     def along_z(self, *wait):
         own = after(self.own, *wait)
-        self.got = [self.tree.to_z(own, step) for step in (1, 2, 3)]
-        self.held = own
+        one, three, two = [self.tree.to_z(own, step) for step in (1, 3, 2)]
+        self.held, self.got = own, [one, two, three]
         return self.got
 
     def one(self, *wait):
@@ -858,7 +860,7 @@
         return out
 
     def along_z(self, *wait):
-        return ()
+        return []
 
     def one(self, *wait):
         return ()
@@ -874,14 +876,14 @@
         self.other.append(other.astype(BF))
         return mine
 
-    def columns(self):
+    def columns(self, *wait):
         def flat(items):
             return jnp.concatenate([part for item in items for part in (item if item.ndim == 3 else [item])], 1)
 
         parts = [flat(item) for item in (self.mine, self.other)]
         return lax.psum_scatter(jnp.stack(parts, 1), AXES, scatter_dimension=0, tiled=True).astype(F32)
 
-    def sums(self):
+    def sums(self, *wait):
         count = lax.axis_size(AXES)
         mine, other = [item[0].reshape(count // 2, -1, item[0].shape[1]) for item in (self.mine, self.other)]
         sums = jnp.stack([mine, other], 1).reshape(-1, mine.shape[-1])
@@ -942,9 +944,9 @@
     up_w = gather_columns(*[pick(up_shard, side, 0) for side in (core, 1 - core)])
     down_w = gather_rows(w_down.astype(BF))
     attn_w.along_z()
+    up_z = up_w.along_z()
     attn_one = attn_w.one()
-    up_z = up_w.along_z(attn_one)
-    attn_two = attn_w.two()
+    attn_two = attn_w.two(up_z[::2])
     up_one = up_w.one(attn_two)
     attn_w = attn_w.halves(up_z)
     down_z = down_w.along_z(attn_two)
@@ -952,10 +954,6 @@
     rows, start, normed_one, across_one, bias_mine, bias_other, bias_up = start_rows(
         place, tokens, absorbed, attn_w, fixed, up_cols, table_cols, small_cols, chips, hidden_part
     )
-    steps = rows[seq_count + fixed + up_cols : seq_count + small_cols]
-    steps = steps.reshape(seq_cols, count, part).transpose(1, 0, 2).reshape(count, -1).astype(jnp.int32)
-    steps = (steps[:, :seq_count] * 256 + steps[:, seq_count : 2 * seq_count]).reshape(-1)
-
     up_two = up_w.two(normed_one)
     qkv_mine, context_mine = attention(after(normed_one, up_one), attn_w[0], bias_mine, seq_length)
     down_one = down_w.one(up_two, context_mine)
@@ -1018,9 +1016,9 @@
         extra_sum = reduction(2 * part)
         extra_sum.add(*blocks)
         extra_sum.one()
-        extra_sum.two(attn_sum.sent)
+        extra_sum.two(attn_sum.sent, up_sum.got)
         attn_sum.along_z(extra_sum)
-        hidden = after(hidden, attn_sum.sent)
+        hidden, rows = after((hidden, rows), attn_sum.sent)
     output = middle + (product(hidden[0], down_w[0]) + product(hidden[1], down_w[1]) + rows[seq_count + 3])
     if fast:
         attn_grad = attn_sum.columns(output)
@@ -1030,12 +1028,15 @@
         small, seq_sums = [
             lax.psum_scatter(item.astype(BF), AXES, scatter_dimension=0, tiled=True).astype(F32) for item in blocks
         ]
+    steps = rows[seq_count + fixed + up_cols : seq_count + small_cols]
+    steps = steps.reshape(seq_cols, count, part).transpose(1, 0, 2).reshape(count, -1).astype(jnp.int32)
+    steps = (steps[:, :seq_count] * 256 + steps[:, seq_count : 2 * seq_count]).reshape(-1)
     grad_b_up = small[0, LANES - hidden_part :]
     small = small[:, :fixed].T
     onehot = (steps[:, None] == lax.broadcasted_iota(jnp.int32, (seqs, table_cols), 1)).astype(F32)
     grad_time_table = jnp.dot(seq_sums, onehot, precision=lax.Precision.HIGHEST)
     grad_w_qkv = attn_grad[:, :, : 3 * half].reshape(part, 2, 3, half).transpose(0, 2, 1, 3).reshape(part, 3 * width)
-    up_grad = up_sum.columns()
+    up_grad = up_sum.columns(extra_sum.sent if fast else ())
     grad_w_out = up_grad[:, :, hidden_width // 2 :].reshape(part, width)
     grad_w_up = up_grad[:, :, : hidden_width // 2].reshape(part, 2, chips, hidden_part).transpose(0, 2, 1, 3)
     grad_w_up = grad_w_up.reshape(part, hidden_width)
@@ -1045,7 +1046,7 @@
         grad_w_qkv,
         grad_w_out,
         grad_w_up,
-        down_sum.sums(),
+        down_sum.sums(extra_sum.sent if fast else ()),
         grad_time_table,
         small[0],
         small[1],

time: 285 us -> 270 us (0.947)
  local copies, waits for them, and re-layouts: 43.4 us -> 15.7 us
  Pallas kernels: 90.8 us -> 104 us
  waiting for transfers between devices: 65.9 us -> 62 us
  matrix products: 14.1 us -> 17.7 us
    unnamed x154 -> x90, local copies, waits for them, and re-layouts: 32.5 us -> 5.17 us
    ppermute x7, waiting for transfers between devices: 6.31 us -> 19.5 us  [to_far(): lax.ppermute(value, AXES, [(i, i ^ (2 if i % 2 else 4)) for i in range(32)])]
    ppermute x7, waiting for transfers between devices: 14.7 us -> 5.28 us  [to_near(): lax.ppermute(value, AXES, [(i, i ^ (4 if i % 2 else 2)) for i in range(32)])]
    ppermute x18, waiting for transfers between devices: 38.8 us -> 30.6 us  [to_z(): return lax.ppermute(value, 'fsdp', [(i, i ^ 2 * step) for i in range(8)])]
    dot_general x4, matrix products: 13.1 us -> 16.7 us  [contract(): return lax.dot_general(left, right, dims, preferred_element_type=F32)]
    pallas_call x4, Pallas kernels: 11.6 us -> 14.6 us  [routed(): pl.pallas_call(functools.partial(route_kernel, rows), grid=(4,), in_specs...]
    pallas_call x2, Pallas kernels: 10.7 us -> 13.6 us  [feed_back(): pl.pallas_call(feed_back_kernel, grid=(columns // block,), in_specs=[pl.B...]
  transfers between devices with their start and end apart: 44 -> 44, of which waited for: 16 -> 18; matrix products, arithmetic and copies ran while one was open for 11% -> 12% of each run, Pallas kernels for 28% -> 33%
where the time goes in v4:
time: 270 us; the launch traced here: 269 us
  Pallas kernels  104 us (39%)
  waiting for transfers between devices  62 us (23%)
  starting transfers between devices  50.9 us (19%)
  matrix products  17.7 us (7%)
  other arithmetic  17 us (6%)
  local copies, waits for them, and re-layouts  15.7 us (6%)
    ppermute x18, starting transfers between devices, to_z(): return lax.ppermute(value, 'fsdp', [(i, i ^ 2 * step) for i in range(8)])  33.8 us
    ppermute x18, waiting for transfers between devices, to_z(): return lax.ppermute(value, 'fsdp', [(i, i ^ 2 * step) for i in range(8)])  30.6 us
    pallas_call x2, Pallas kernels, attention_back(): pl.pallas_call(functools.partial(attention_back_kernel, length, 1.0 / mat...  21.2 us
    ppermute x7, waiting for transfers between devices, to_far(): lax.ppermute(value, AXES, [(i, i ^ (2 if i % 2 else 4)) for i in range(32)])  19.5 us
    dot_general x4, matrix products, contract(): return lax.dot_general(left, right, dims, preferred_element_type=F32)  16.7 us
    pallas_call x2, Pallas kernels, attention(): pl.pallas_call(functools.partial(attention_kernel, length, 1.0 / math.sqr...  16.6 us
    pallas_call x4, Pallas kernels, routed(): pl.pallas_call(functools.partial(route_kernel, rows), grid=(4,), in_specs...  14.6 us
    pallas_call x2, Pallas kernels, feed_back(): pl.pallas_call(feed_back_kernel, grid=(columns // block,), in_specs=[pl.B...  13.6 us
  transfers between devices with their start and end apart: 44, of which 18 were waited for; matrix products, arithmetic and copies ran while one was open for 12% of the time, Pallas kernels for 33%

profile of v4, /device:TPU:0, one launch (start us, length us, event | category | flops | bytes accessed | tf_op | source)
XLA Modules:
  0.0 269.2 jit_solution(79001046254416077)
XLA Ops:
  11.4 6.5 %collective-permute-done.1 = bf16[48,2048]{1,0:T(8,128)(2,1)S(1)} collective-permute-done((bf16[48,2048]{1,0:T(8,128)(2,1)S(1)}, bf16[48,2048]{1,0:T(8,128)(2,1)S(1)}, u32[]{:S(2)}, u32[]{:S(2)}) %collective-permute-start.1) | collective-permute-done | bytes 196640 | tf_op jit(solution)/shard_map/ppermute | solution.py:745
  18.0 7.8 %collective-permute-done.2 = bf16[48,2048]{1,0:T(8,128)(2,1)S(1)} collective-permute-done((bf16[48,2048]{1,0:T(8,128)(2,1)S(1)}, bf16[48,2048]{1,0:T(8,128)(2,1)S(1)}, u32[]{:S(2)}, u32[]{:S(2)}) %collective-permute-start.2) | collective-permute-done | bytes 196640 | tf_op jit(solution)/shard_map/ppermute | solution.py:745
  35.6 4.5 %collective-permute-done.7 = bf16[48,1536]{1,0:T(8,128)(2,1)S(1)} collective-permute-done((bf16[48,1536]{1,0:T(8,128)(2,1)S(1)}, bf16[48,1536]{1,0:T(8,128)(2,1)S(1)}, u32[]{:S(2)}, u32[]{:S(2)}) %collective-permute-start.7) | collective-permute-done | bytes 147488 | tf_op jit(solution)/shard_map/ppermute | solution.py:745
  44.9 6.4 %collective-permute-done.9 = bf16[48,1536]{1,0:T(8,128)(2,1)} collective-permute-done((bf16[48,1536]{1,0:T(8,128)(2,1)S(1)}, bf16[48,1536]{1,0:T(8,128)(2,1)}, u32[]{:S(2)}, u32[]{:S(2)}) %collective-permute-start.9) | collective-permute-done | bytes 147488 | tf_op jit(solution)/shard_map/ppermute | solution.py:745
  51.3 10.1 %collective-permute-done.8 = bf16[4,2,48,2048]{3,2,1,0:T(8,128)(2,1)S(1)} collective-permute-done((bf16[4,2,48,2048]{3,2,1,0:T(8,128)(2,1)S(1)}, bf16[4,2,48,2048]{3,2,1,0:T(8,128)(2,1)S(1)}, u32[]{:S(2)}, u32[]{:S(2)}) %collective-permute-start.8) | collective-permute-done | bytes 1572896 | tf_op jit(solution)/shard_map/ppermute | solution.py:742
  68.4 5.5 %start_rows.1 = (f32[24,768]{1,0:T(8,128)S(1)}, f32[512,768]{1,0:T(8,128)}, bf16[512,768]{1,0:T(8,128)(2,1)S(1)}, bf16[768,512]{1,0:T(8,128)(2,1)}, f32[8,384]{1...) custom-call(s32[6]{0:T(128)S(1)} %copy-done.20, f32[512,768]{1,0:T(8,128)} %tokens_ref.1, ...), custom_call_target="tpu_custom_call" | custom-call | flops 37748736 | bytes 5505024 | tf_op jit(solution)/shard_map/start_rows/pallas_call | solution.py:336
  81.8 7.6 %attention.2 = (bf16[3,512,384]{2,1,0:T(8,128)(2,1)}, bf16[512,384]{1,0:T(8,128)(2,1)S(1)}) custom-call(bf16[512,768]{1,0:T(8,128)(2,1)S(1)} %get-tuple-element.155.rows_ref, bf16[768,2048]{1,0:T(8,128)(2,1)S(1)} %bitcast.182, bf16[768,2048]{1,0:T(8,128)(2,1)S(1)} %bitcast.183, bf16[768,2048]{1,0:T(8,128)(2,1)S(1)} %bitcast.184, ...), custom_call_target="tpu_custom_call" | custom-call | flops 905969664 | bytes 4128768 | tf_op jit(solution)/shard_map/attention/pallas_call | solution.py:89
  95.0 9.0 %attention.3 = (bf16[3,512,384]{2,1,0:T(8,128)(2,1)}, bf16[512,384]{1,0:T(8,128)(2,1)S(1)}) custom-call(bf16[512,768]{1,0:T(8,128)(2,1)S(1)} %get-tuple-element.155.rows_ref, bf16[768,2048]{1,0:T(8,128)(2,1)} %collective-permute-done.10.table_other_ref.query_ref.key_ref.value_ref.out_other_ref.weight_other_ref, ...), custom_call_target="tpu_custom_call" | custom-call | flops 905969664 | bytes 4128768 | tf_op jit(solution)/shard_map/attention/pallas_call | solution.py:89
  110.0 5.3 %feed.2 = (bf16[512,1536]{1,0:T(8,128)(2,1)}, f32[512,1536]{1,0:T(8,128)}) custom-call(bf16[512,768]{1,0:T(8,128)(2,1)S(1)} %get-tuple-element.174.rows_ref, bf16[768,1536]{1,0:T(8,128)(2,1)S(1)} %bitcast.189, f32[8,1536]{1,0:T(8,128)S(1)} %get-tuple-element.170.bias_ref), custom_call_target="tpu_custom_call" | custom-call | flops 1207959552 | bytes 7864320 | tf_op jit(solution)/shard_map/feed/pallas_call | solution.py:200
  115.3 5.2 %collective-permute-done.17 = bf16[4,2,96,768]{3,2,0,1:T(8,128)(2,1)S(1)} collective-permute-done((bf16[4,2,96,768]{3,2,0,1:T(8,128)(2,1)S(1)}, bf16[4,2,96,768]{3,2,0,1:T(8,128)(2,1)S(1)}, u32[]{:S(2)}, u32[]{:S(2)}) %collective-permute-start.17) | collective-permute-done | bytes 1179680 | tf_op jit(solution)/shard_map/ppermute | solution.py:742
  120.8 5.3 %feed.3 = (bf16[512,1536]{1,0:T(8,128)(2,1)}, f32[512,1536]{1,0:T(8,128)}) custom-call(bf16[512,768]{1,0:T(8,128)(2,1)S(1)} %get-tuple-element.174.rows_ref, bf16[768,1536]{1,0:T(8,128)(2,1)S(1)} %collective-permute-done.18.weight_ref.up_other_ref, f32[8,1536]{1,0:T(8,128)S(1)} %get-tuple-element.170.bias_ref), custom_call_target="tpu_custom_call" | custom-call | flops 1207959552 | bytes 7864320 | tf_op jit(solution)/shard_map/feed/pallas_call | solution.py:200
  126.2 4.2 %convolution_convert_fusion = bf16[1536,768]{1,0:T(8,128)(2,1)} fusion(bf16[512,1536]{1,0:T(8,128)(2,1)} %get-tuple-element.239, bf16[512,768]{1,0:T(8,128)(2,1)S(1)} %multiply_convert_fusion.grad_ref), kind=kOutput, calls=%fused_computation | convolution fusion | flops 1209139200 | bytes 4718592 | tf_op jit(solution)/shard_map/dot_general | solution.py:24
  135.9 4.3 %routed.4 = (bf16[4,2,96,768]{3,2,1,0:T(8,128)(2,1)}, f32[4,2,96,768]{3,2,1,0:T(8,128)}) custom-call(s32[4]{0:T(128)S(1)} %pad_add_fusion.1.route_ref, f32[1536,768]{1,0:T(8,128)S(1)} %fusion.31.refs_0_, bf16[1536,768]{1,0:T(8,128)(2,1)} %collective-permute-done.19.refs_1_), custom_call_target="tpu_custom_call" | custom-call | bytes 10616832 | tf_op jit(solution)/shard_map/routed/pallas_call | solution.py:708
  141.0 7.3 %feed_back.3 = (bf16[512,1536]{1,0:T(8,128)(2,1)}, f32[1,1536]{1,0:T(1,128)S(1)}, bf16[768,1536]{1,0:T(8,128)(2,1)}) custom-call(bf16[512,768]{1,0:T(8,128)(2,1)} %copy-done.26, bf16[1536,768]{1,0:T(8,128)(2,1)} %collective-permute-done.20.weight_ref, f32[512,1536]{1,0:T(8,128)} %get-tuple-element.186.slope_ref, bf16[768,512]{1,0:T(8,128)(2,1)} %get-tuple-element.180.rows_ref), custom_call_target="tpu_custom_call" | custom-call | flops 2415919104 | bytes 13369344 | tf_op jit(solution)/shard_map/feed_back/pallas_call | solution.py:236
  148.5 6.4 %feed_back.2 = (bf16[512,1536]{1,0:T(8,128)(2,1)}, f32[1,1536]{1,0:T(1,128)S(1)}, f32[768,1536]{1,0:T(8,128)S(1)}) custom-call(bf16[512,768]{1,0:T(8,128)(2,1)} %copy-done.26, bf16[1536,768]{1,0:T(8,128)(2,1)} %bitcast.48.weight_ref, f32[512,1536]{1,0:T(8,128)} %get-tuple-element.179.slope_ref, bf16[768,512]{1,0:T(8,128)(2,1)} %get-tuple-element.180.rows_ref), custom_call_target="tpu_custom_call" | custom-call | flops 2415919104 | bytes 13369344 | tf_op jit(solution)/shard_map/feed_back/pallas_call | solution.py:236
  162.2 8.6 %middle_back.1 = (f32[512,768]{1,0:T(8,128)S(1)}, bf16[512,384]{1,0:T(8,128)(2,1)S(1)}, bf16[512,384]{1,0:T(8,128)(2,1)S(1)}, f32[768,384]{1,0:T(8,128)S(1)}, bf...) custom-call(s32[6]{0:T(128)S(1)} %copy-done.20, bf16[512,1536]{1,0:T(8,128)(2,1)S(1)} %copy-done.13, ...), custom_call_target="tpu_custom_call" | custom-call | flops 3623878656 | bytes 14155776 | tf_op jit(solution)/shard_map/middle_back/pallas_call | solution.py:491
  173.0 4.4 %routed.5 = (bf16[4,2,48,1920]{3,2,1,0:T(8,128)(2,1)}, f32[4,2,48,1920]{3,2,1,0:T(8,128)}) custom-call(s32[4]{0:T(128)S(1)} %pad_add_fusion.1.route_ref, f32[768,1536]{1,0:T(8,128)S(1)} %get-tuple-element.198.refs_0_, bf16[768,1536]{1,0:T(8,128)(2,1)} %collective-permute-done.22.refs_1_, f32[768,384]{1,0:T(8,128)S(1)} %get-tuple-element.200.refs_2_, ...), custom_call_target="tpu_custom_call" | custom-call | bytes 13271040 | tf_op jit(solution)/shard_map/routed/pallas_call | solution.py:708
  184.6 11.1 %attention_back.2 = (bf16[3,512,384]{2,1,0:T(8,128)(2,1)}, bf16[3,768,384]{2,1,0:T(8,128)(2,1)}, f32[3,384]{1,0:T(4,128)S(1)}) custom-call(bf16[3,512,384]{2,1,0:T(8,128)(2,1)} %get-tuple-element.204.qkv_ref, bf16[512,384]{1,0:T(8,128)(2,1)} %copy-done.22, bf16[768,512]{1,0:T(8,128)(2,1)} %get-tuple-element.207.rows_ref), custom_call_target="tpu_custom_call" | custom-call | flops 905969664 | bytes 7077888 | tf_op jit(solution)/shard_map/attention_back/pallas_call | solution.py:149
  204.2 10.2 %attention_back.3 = (bf16[3,512,384]{2,1,0:T(8,128)(2,1)}, f32[3,768,384]{2,1,0:T(8,128)S(1)}, f32[3,384]{1,0:T(4,128)S(1)}) custom-call(bf16[3,512,384]{2,1,0:T(8,128)(2,1)} %get-tuple-element.176.qkv_ref, bf16[512,384]{1,0:T(8,128)(2,1)} %copy-done.21, bf16[768,512]{1,0:T(8,128)(2,1)} %get-tuple-element.207.rows_ref), custom_call_target="tpu_custom_call" | custom-call | flops 905969664 | bytes 7077888 | tf_op jit(solution)/shard_map/attention_back/pallas_call | solution.py:149
  214.4 4.1 %routed.6 = (bf16[4,2,48,1152]{3,2,1,0:T(8,128)(2,1)S(1)}, f32[4,2,48,1152]{3,2,1,0:T(8,128)}) custom-call(s32[4]{0:T(128)S(1)} %pad_add_fusion.1.route_ref, f32[3,768,384]{2,1,0:T(8,128)S(1)} %get-tuple-element.215.refs_0_, bf16[3,768,384]{2,1,0:T(8,128)(2,1)} %collective-permute-done.29.refs_1_), custom_call_target="tpu_custom_call" | custom-call | bytes 7962624 | tf_op jit(solution)/shard_map/routed/pallas_call | solution.py:708
  225.8 7.2 %start_back.1 = (f32[512,768]{1,0:T(8,128)}, f32[768,128]{1,0:T(8,128)S(1)}, bf16[768,128]{1,0:T(8,128)(2,1)S(1)}) custom-call(s32[6]{0:T(128)S(1)} %copy-done.20, bf16[3,512,384]{2,1,0:T(8,128)(2,1)S(1)} %copy-done.19, bf16[3,512,384]{2,1,0:T(8,128)(2,1)S(1)} %copy-done.18, bf16[768,2048]{1,0:T(8,128)(2,1)S(1)} %bitcast.187, ...), custom_call_target="tpu_custom_call" | custom-call | bytes 1024 | tf_op jit(solution)/shard_map/start_back/pallas_call | solution.py:595
  243.1 4.3 %collective-permute-done.38 = bf16[4,48,128]{2,1,0:T(8,128)(2,1)S(1)} collective-permute-done((bf16[4,48,128]{2,1,0:T(8,128)(2,1)S(1)}, bf16[4,48,128]{2,1,0:T(8,128)(2,1)S(1)}, u32[]{:S(2)}, u32[]{:S(2)}) %collective-permute-start.38) | collective-permute-done | bytes 49184 | tf_op jit(solution)/shard_map/ppermute | solution.py:742
  254.5 4.3 %fusion.32 = f32[512,768]{1,0:T(8,128)} fusion(bf16[512,1536]{1,0:T(8,128)(2,1)S(1)} %copy-done.30, bf16[1536,768]{1,0:T(8,128)(2,1)} %bitcast.48.weight_ref), kind=kOutput, calls=%fused_computation.157 | convolution fusion | flops 1207959552 | bytes 5505024 | tf_op jit(solution)/shard_map/dot_general | solution.py:24
  258.9 5.1 %add_add_fusion = f32[512,768]{1,0:T(8,128)} fusion(f32[512,768]{1,0:T(8,128)S(1)} %copy-done.9, f32[512,768]{1,0:T(8,128)} %fusion.32, bf16[512,1536]{1,0:T(8,128)(2,1)} %get-tuple-element.239, bf16[1536,768]{1,0:T(8,128)(2,1)} %collective-permute-done.20.weight_ref, f32[768]{0:T(1024)S(1)} %slice_reduce_fusion.9), kind=kOutput, calls=%fused_computation.12 | convolution fusion | flops 1209139200 | bytes 8653824 | tf_op jit(solution)/shard_map/dot_general | solution.py:24
  (263 shorter events, 112.9 us)
Async XLA Ops:
  8.7 17.1 %collective-permute-start.2 = (bf16[48,2048]{1,0:T(8,128)(2,1)S(1)}, bf16[48,2048]{1,0:T(8,128)(2,1)S(1)}, u32[]{:S(2)}, u32[]{:S(2)}) collective-permute-start(bf16[48,2048]{1,0:T(8,128)(2,1)S(1)} %bitcast.200), channel_id=1, source_target_pairs={{0,16},{4,20},{8,24},{12,28},{16,0},{20,4},{24,8},{28,12},{1,17},{... | collective-permute-start | bytes 589832 | tf_op jit(solution)/shard_map/ppermute | solution.py:745
  11.3 14.5 %collective-permute-start.3 = (bf16[48,2048]{1,0:T(8,128)(2,1)S(1)}, bf16[48,2048]{1,0:T(8,128)(2,1)S(1)}, u32[]{:S(2)}, u32[]{:S(2)}) collective-permute-start(bf16[48,2048]{1,0:T(8,128)(2,1)S(1)} %bitcast.201), channel_id=1, source_target_pairs={{0,24},{4,28},{8,16},{12,20},{16,8},{20,12},{24,0},{28,4},{1,25},{... | collective-permute-start | bytes 589832 | tf_op jit(solution)/shard_map/ppermute | solution.py:745
  11.3 16.3 %collective-permute-start.5 = (bf16[24,1536]{1,0:T(8,128)(2,1)S(1)}, bf16[24,1536]{1,0:T(8,128)(2,1)S(1)}, u32[]{:S(2)}, u32[]{:S(2)}) collective-permute-start(bf16[24,1536]{1,0:T(8,128)(2,1)S(1)} %dynamic-slice_bitcast_fusion.4), channel_id=1, source_target_pairs={{0,1},{1,0},{2,3},{3,2},{4,5},{5,4},{6,7},{7,6},{8,9},{9,8},{10,11... | collective-permute-start | bytes 221192 | tf_op jit(solution)/shard_map/ppermute | solution.py:736
  26.0 14.1 %collective-permute-start.4 = (bf16[4,48,2048]{2,1,0:T(8,128)(2,1)S(1)}, bf16[4,48,2048]{2,1,0:T(8,128)(2,1)S(1)}, u32[]{:S(2)}, u32[]{:S(2)}) collective-permute-start(bf16[4,48,2048]{2,1,0:T(8,128)(2,1)S(1)} %pad_maximum_fusion.6), channel_id=1, source_target_pairs={{0,2},{1,5},{2,0},{3,7},{4,6},{5,1},{6,4},{7,3},{8,10},{9,13},{10,... | collective-permute-start | bytes 2359304 | tf_op jit(solution)/shard_map/ppermute | solution.py:739
  40.9 20.5 %collective-permute-start.8 = (bf16[4,2,48,2048]{3,2,1,0:T(8,128)(2,1)S(1)}, bf16[4,2,48,2048]{3,2,1,0:T(8,128)(2,1)S(1)}, u32[]{:S(2)}, u32[]{:S(2)}) collective-permute-start(bf16[4,2,48,2048]{3,2,1,0:T(8,128)(2,1)S(1)} %pad_maximum_fusion.3), channel_id=1, source_target_pairs={{0,4},{1,3},{2,6},{3,1},{4,0},{5,7},{6,2},{7,5},{8,12},{9,11},{10,... | collective-permute-start | bytes 4718600 | tf_op jit(solution)/shard_map/ppermute | solution.py:742
  76.3 16.6 %collective-permute-start.12 = (bf16[4,2,48,1536]{3,2,1,0:T(8,128)(2,1)S(1)}, bf16[4,2,48,1536]{3,2,1,0:T(8,128)(2,1)S(1)}, u32[]{:S(2)}, u32[]{:S(2)}) collective-permute-start(bf16[4,2,48,1536]{3,2,1,0:T(8,128)(2,1)S(1)} %pad_maximum_fusion.4), channel_id=1, source_target_pairs={{0,4},{1,3},{2,6},{3,1},{4,0},{5,7},{6,2},{7,5},{8,12},{9,11},{10,... | collective-permute-start | bytes 3538952 | tf_op jit(solution)/shard_map/ppermute | solution.py:742
  79.4 13.5 %collective-permute-start.14 = (bf16[96,768]{1,0:T(8,128)(2,1)S(1)}, bf16[96,768]{1,0:T(8,128)(2,1)S(1)}, u32[]{:S(2)}, u32[]{:S(2)}) collective-permute-start(bf16[96,768]{1,0:T(8,128)(2,1)S(1)} %convert_element_type.155), channel_id=1, source_target_pairs={{0,16},{4,20},{8,24},{12,28},{16,0},{20,4},{24,8},{28,12},{1,17},{... | collective-permute-start | bytes 442376 | tf_op jit(solution)/shard_map/ppermute | solution.py:745
  94.9 25.9 %collective-permute-start.18 = (bf16[768,1536]{1,0:T(8,128)(2,1)S(1)}, bf16[768,1536]{1,0:T(8,128)(2,1)S(1)}, u32[]{:S(2)}, u32[]{:S(2)}) collective-permute-start(bf16[768,1536]{1,0:T(8,128)(2,1)S(1)} %bitcast.188), channel_id=1, source_target_pairs={{0,1},{1,0},{2,3},{3,2},{4,5},{5,4},{6,7},{7,6},{8,9},{9,8},{10,11... | collective-permute-start | bytes 7077896 | tf_op jit(solution)/shard_map/ppermute | solution.py:736
  104.2 16.3 %collective-permute-start.17 = (bf16[4,2,96,768]{3,2,0,1:T(8,128)(2,1)S(1)}, bf16[4,2,96,768]{3,2,0,1:T(8,128)(2,1)S(1)}, u32[]{:S(2)}, u32[]{:S(2)}) collective-permute-start(bf16[4,2,96,768]{3,2,0,1:T(8,128)(2,1)S(1)} %pad_maximum_fusion.5), channel_id=1, source_target_pairs={{0,4},{1,3},{2,6},{3,1},{4,0},{5,7},{6,2},{7,5},{8,12},{9,11},{10,... | collective-permute-start | bytes 3538952 | tf_op jit(solution)/shard_map/ppermute | solution.py:742
  140.1 16.5 %collective-permute-start.21 = (bf16[4,2,96,768]{3,2,1,0:T(8,128)(2,1)}, bf16[4,2,96,768]{3,2,1,0:T(8,128)(2,1)}, u32[]{:S(2)}, u32[]{:S(2)}) collective-permute-start(bf16[4,2,96,768]{3,2,1,0:T(8,128)(2,1)} %get-tuple-element.184), channel_id=1, source_target_pairs={{0,2},{1,5},{2,0},{3,7},{4,6},{5,1},{6,4},{7,3},{8,10},{9,13},{10,... | collective-permute-start | bytes 3538952 | tf_op jit(solution)/shard_map/ppermute | solution.py:739
  148.2 24.7 %collective-permute-start.22 = (bf16[768,1536]{1,0:T(8,128)(2,1)}, bf16[768,1536]{1,0:T(8,128)(2,1)}, u32[]{:S(2)}, u32[]{:S(2)}) collective-permute-start(bf16[768,1536]{1,0:T(8,128)(2,1)} %get-tuple-element.195), channel_id=1, source_target_pairs={{0,1},{1,0},{2,3},{3,2},{4,5},{5,4},{6,7},{7,6},{8,9},{9,8},{10,11... | collective-permute-start | bytes 7077896 | tf_op jit(solution)/shard_map/ppermute | solution.py:736
  158.5 12.5 %collective-permute-start.24 = (bf16[4,96,768]{2,1,0:T(8,128)(2,1)S(1)}, bf16[4,96,768]{2,1,0:T(8,128)(2,1)S(1)}, u32[]{:S(2)}, u32[]{:S(2)}) collective-permute-start(bf16[4,96,768]{2,1,0:T(8,128)(2,1)S(1)} %fusion.1), channel_id=1, source_target_pairs={{0,4},{1,3},{2,6},{3,1},{4,0},{5,7},{6,2},{7,5},{8,12},{9,11},{10,... | collective-permute-start | bytes 1769480 | tf_op jit(solution)/shard_map/ppermute | solution.py:742
  177.4 19.7 %collective-permute-start.25 = (bf16[4,2,48,1920]{3,2,1,0:T(8,128)(2,1)}, bf16[4,2,48,1920]{3,2,1,0:T(8,128)(2,1)}, u32[]{:S(2)}, u32[]{:S(2)}) collective-permute-start(bf16[4,2,48,1920]{3,2,1,0:T(8,128)(2,1)} %get-tuple-element.203), channel_id=1, source_target_pairs={{0,2},{1,5},{2,0},{3,7},{4,6},{5,1},{6,4},{7,3},{8,10},{9,13},{10,... | collective-permute-start | bytes 4423688 | tf_op jit(solution)/shard_map/ppermute | solution.py:739
  180.0 15.7 %collective-permute-start.26 = (bf16[96,768]{1,0:T(8,128)(2,1)S(1)}, bf16[96,768]{1,0:T(8,128)(2,1)S(1)}, u32[]{:S(2)}, u32[]{:S(2)}) collective-permute-start(bf16[96,768]{1,0:T(8,128)(2,1)S(1)} %get-tuple-element.285), channel_id=1, source_target_pairs={{0,8},{4,12},{8,0},{12,4},{16,24},{20,28},{24,16},{28,20},{1,9},{5... | collective-permute-start | bytes 442376 | tf_op jit(solution)/shard_map/ppermute | solution.py:745
  182.2 14.0 %collective-permute-start.27 = (bf16[96,768]{1,0:T(8,128)(2,1)S(1)}, bf16[96,768]{1,0:T(8,128)(2,1)S(1)}, u32[]{:S(2)}, u32[]{:S(2)}) collective-permute-start(bf16[96,768]{1,0:T(8,128)(2,1)S(1)} %get-tuple-element.284), channel_id=1, source_target_pairs={{0,16},{4,20},{8,24},{12,28},{16,0},{20,4},{24,8},{28,12},{1,17},{... | collective-permute-start | bytes 442376 | tf_op jit(solution)/shard_map/ppermute | solution.py:745
  183.2 12.9 %collective-permute-start.28 = (bf16[96,768]{1,0:T(8,128)(2,1)S(1)}, bf16[96,768]{1,0:T(8,128)(2,1)S(1)}, u32[]{:S(2)}, u32[]{:S(2)}) collective-permute-start(bf16[96,768]{1,0:T(8,128)(2,1)S(1)} %get-tuple-element.283), channel_id=1, source_target_pairs={{0,24},{4,28},{8,16},{12,20},{16,8},{20,12},{24,0},{28,4},{1,25},{... | collective-permute-start | bytes 442376 | tf_op jit(solution)/shard_map/ppermute | solution.py:745
  195.7 18.7 %collective-permute-start.29 = (bf16[3,768,384]{2,1,0:T(8,128)(2,1)}, bf16[3,768,384]{2,1,0:T(8,128)(2,1)}, u32[]{:S(2)}, u32[]{:S(2)}) collective-permute-start(bf16[3,768,384]{2,1,0:T(8,128)(2,1)} %get-tuple-element.209), channel_id=1, source_target_pairs={{0,1},{1,0},{2,3},{3,2},{4,5},{5,4},{6,7},{7,6},{8,9},{9,8},{10,11... | collective-permute-start | bytes 5308424 | tf_op jit(solution)/shard_map/ppermute | solution.py:736
  201.5 12.9 %collective-permute-start.30 = (bf16[4,48,1920]{2,1,0:T(8,128)(2,1)}, bf16[4,48,1920]{2,1,0:T(8,128)(2,1)}, u32[]{:S(2)}, u32[]{:S(2)}) collective-permute-start(bf16[4,48,1920]{2,1,0:T(8,128)(2,1)} %fusion), channel_id=1, source_target_pairs={{0,4},{1,3},{2,6},{3,1},{4,0},{5,7},{6,2},{7,5},{8,12},{9,11},{10,... | collective-permute-start | bytes 2211848 | tf_op jit(solution)/shard_map/ppermute | solution.py:742
  218.5 18.8 %collective-permute-start.31 = (bf16[4,2,48,1152]{3,2,1,0:T(8,128)(2,1)S(1)}, bf16[4,2,48,1152]{3,2,1,0:T(8,128)(2,1)S(1)}, u32[]{:S(2)}, u32[]{:S(2)}) collective-permute-start(bf16[4,2,48,1152]{3,2,1,0:T(8,128)(2,1)S(1)} %get-tuple-element.218), channel_id=1, source_target_pairs={{0,2},{1,5},{2,0},{3,7},{4,6},{5,1},{6,4},{7,3},{8,10},{9,13},{10,... | collective-permute-start | bytes 2654216 | tf_op jit(solution)/shard_map/ppermute | solution.py:739
  221.0 18.3 %collective-permute-start.35 = (bf16[48,1920]{1,0:T(8,128)(2,1)S(1)}, bf16[48,1920]{1,0:T(8,128)(2,1)S(1)}, u32[]{:S(2)}, u32[]{:S(2)}) collective-permute-start(bf16[48,1920]{1,0:T(8,128)(2,1)S(1)} %get-tuple-element.282), channel_id=1, source_target_pairs={{0,8},{4,12},{8,0},{12,4},{16,24},{20,28},{24,16},{28,20},{1,9},{5... | collective-permute-start | bytes 552968 | tf_op jit(solution)/shard_map/ppermute | solution.py:745
  223.4 16.0 %collective-permute-start.36 = (bf16[48,1920]{1,0:T(8,128)(2,1)S(1)}, bf16[48,1920]{1,0:T(8,128)(2,1)S(1)}, u32[]{:S(2)}, u32[]{:S(2)}) collective-permute-start(bf16[48,1920]{1,0:T(8,128)(2,1)S(1)} %get-tuple-element.281), channel_id=1, source_target_pairs={{0,16},{4,20},{8,24},{12,28},{16,0},{20,4},{24,8},{28,12},{1,17},{... | collective-permute-start | bytes 552968 | tf_op jit(solution)/shard_map/ppermute | solution.py:745
  224.4 14.9 %collective-permute-start.37 = (bf16[48,1920]{1,0:T(8,128)(2,1)S(1)}, bf16[48,1920]{1,0:T(8,128)(2,1)S(1)}, u32[]{:S(2)}, u32[]{:S(2)}) collective-permute-start(bf16[48,1920]{1,0:T(8,128)(2,1)S(1)} %get-tuple-element.280), channel_id=1, source_target_pairs={{0,24},{4,28},{8,16},{12,20},{16,8},{20,12},{24,0},{28,4},{1,25},{... | collective-permute-start | bytes 552968 | tf_op jit(solution)/shard_map/ppermute | solution.py:745
  249.9 14.1 %collective-permute-start.39 = (bf16[48,1280]{1,0:T(8,128)(2,1)S(1)}, bf16[48,1280]{1,0:T(8,128)(2,1)S(1)}, u32[]{:S(2)}, u32[]{:S(2)}) collective-permute-start(bf16[48,1280]{1,0:T(8,128)(2,1)S(1)} %get-tuple-element.295), channel_id=1, source_target_pairs={{0,8},{4,12},{8,0},{12,4},{16,24},{20,28},{24,16},{28,20},{1,9},{5... | collective-permute-start | bytes 368648 | tf_op jit(solution)/shard_map/ppermute | solution.py:745
  251.1 13.0 %collective-permute-start.40 = (bf16[48,1280]{1,0:T(8,128)(2,1)S(1)}, bf16[48,1280]{1,0:T(8,128)(2,1)S(1)}, u32[]{:S(2)}, u32[]{:S(2)}) collective-permute-start(bf16[48,1280]{1,0:T(8,128)(2,1)S(1)} %get-tuple-element.296), channel_id=1, source_target_pairs={{0,16},{4,20},{8,24},{12,28},{16,0},{20,4},{24,8},{28,12},{1,17},{... | collective-permute-start | bytes 368648 | tf_op jit(solution)/shard_map/ppermute | solution.py:745
  (65 other events, 404.6 us)

commit v5 on v4

--- a/solution.py
+++ b/solution.py
@@ -57,25 +57,34 @@
     return [jnp.where((lane < HDIM) == (head == 0), factor, 0.0).astype(BF) for head in (0, 1)]
 
 
-def softmax(scores):
-    powers = jnp.exp(scores - jnp.max(scores, -1, keepdims=True))
-    return powers * (1.0 / jnp.sum(powers, -1, keepdims=True))
+def stacked(values, masks):
+    return jnp.concatenate([values * masks[0], values * masks[1]], 0)
+
+
+def unstacked(values):
+    rows = values.shape[0] // 2
+    lane = lax.broadcasted_iota(jnp.int32, (1, LANES), 1)
+    return jnp.where(lane < HDIM, values[:rows], values[rows:])
+
+
+def softmax_down(scores):
+    powers = jnp.exp(scores - jnp.max(scores, 0, keepdims=True))
+    return powers * (1.0 / jnp.sum(powers, 0, keepdims=True))
 
 
 def attention_kernel(length, scale, rows_ref, query_ref, key_ref, value_ref, bias_ref, qkv_ref, context_ref):
-    rows = rows_ref[...]
-    for index, weight in enumerate((query_ref, key_ref, value_ref)):
-        qkv_ref[index] = (product(rows, weight[...]) + bias_ref[index : index + 1, :]).astype(BF)
-    ones, scaled = lane_masks(1.0), lane_masks(scale)
-
-    for sequence in range(rows.shape[0] // length):
+    weight = jnp.concatenate([query_ref[...], key_ref[...], value_ref[...]], 1)
+    projected = product(rows_ref[...], weight)
+    for index in range(3):
+        part = projected[:, index * LANES : (index + 1) * LANES]
+        qkv_ref[index] = (part + bias_ref[index : index + 1, :]).astype(BF)
+    scaled = lane_masks(scale)
+
+    for sequence in range(rows_ref.shape[0] // length):
         span = slice(sequence * length, (sequence + 1) * length)
         queries, key_rows, value_rows = [qkv_ref[index, span, :] for index in range(3)]
-        total = 0.0
-        for head in (0, 1):
-            probs = softmax(right_product(queries * scaled[head], key_rows)).astype(BF)
-            total = total + product(probs, value_rows * ones[head])
-        context_ref[span, :] = total.astype(BF)
+        probs = softmax_down(right_product(key_rows, stacked(queries, scaled))).astype(BF)
+        context_ref[span, :] = unstacked(left_product(probs, value_rows)).astype(BF)
 
 
 def attention(rows, weight, bias, length):
@@ -120,26 +129,21 @@
     for sequence in range(grad_ref.shape[0] // length):
         span = slice(sequence * length, (sequence + 1) * length)
         queries, key_rows, value_rows = [qkv_ref[index, span, :] for index in range(3)]
-        grad = grad_ref[span, :]
-        grad_queries, grad_keys, grad_values = 0.0, 0.0, 0.0
-        for head in (0, 1):
-            probs = softmax(right_product(queries * scaled[head], key_rows))
-            grad_head = grad * ones[head]
-            grad_probs = right_product(grad_head, value_rows)
-            grad_scores = probs * (grad_probs - jnp.sum(grad_probs * probs, -1, keepdims=True))
-            grad_scores = grad_scores.astype(BF)
-            grad_values = grad_values + left_product(probs.astype(BF), grad_head)
-            grad_queries = grad_queries + product(grad_scores, key_rows * ones[head])
-            grad_keys = grad_keys + left_product(grad_scores, queries * ones[head])
-        grads_ref[0, span, :] = (grad_queries * scale).astype(BF)
-        grads_ref[1, span, :] = (grad_keys * scale).astype(BF)
-        grads_ref[2, span, :] = grad_values.astype(BF)
-
-    rows = rows_ref[...]
+        queries, grad = stacked(queries, scaled), stacked(grad_ref[span, :], ones)
+        probs = softmax_down(right_product(key_rows, queries))
+        grad_probs = right_product(value_rows, grad)
+        grad_scores = probs * (grad_probs - jnp.sum(grad_probs * probs, 0, keepdims=True))
+        grad_scores = grad_scores.astype(BF)
+        grad_queries = unstacked(left_product(grad_scores, key_rows)) * scale
+        grads_ref[0, span, :] = grad_queries.astype(BF)
+        grads_ref[1, span, :] = product(grad_scores, queries).astype(BF)
+        grads_ref[2, span, :] = product(probs.astype(BF), grad).astype(BF)
+
+    grads = jnp.concatenate([grads_ref[index] for index in range(3)], 1)
+    weight = product(rows_ref[...], grads)
     for index in range(3):
-        grads = grads_ref[index]
-        weight_ref[index] = product(rows, grads).astype(weight_ref.dtype)
-        sums_ref[index : index + 1, :] = jnp.sum(grads.astype(F32), 0, keepdims=True)
+        weight_ref[index] = weight[:, index * LANES : (index + 1) * LANES].astype(weight_ref.dtype)
+        sums_ref[index : index + 1, :] = jnp.sum(grads_ref[index].astype(F32), 0, keepdims=True)
 
 
 def attention_back(qkv, grad, rows_across, length, dtype):
@@ -228,7 +232,7 @@
     up_ref[...] = product(rows_ref[...], grad).astype(up_ref.dtype)
 
 
-def feed_back(grad, weight, slope, rows_across, dtype, block=512):
+def feed_back(grad, weight, slope, rows_across, dtype, block=768):
     tokens, width = grad.shape
     columns = weight.shape[0]
     block = math.gcd(block, columns)
@@ -474,7 +478,7 @@
         out_grad_other_ref[...] = total_ref[1].astype(BF)
 
 
-def middle_back(place, grads, ups, middle, cotangent, mask, rows, contexts, weights, block=256):
+def middle_back(place, grads, ups, middle, cotangent, mask, rows, contexts, weights, block=512):
     count, width = middle.shape
     half = width // 2
     hidden_half = ups[0].shape[1]

time: 270 us -> 268 us (level)
  Pallas kernels: 104 us -> 89.2 us
  waiting for transfers between devices: 62 us -> 74 us
    pallas_call x2, Pallas kernels: 16.6 us -> 9.66 us  [attention(): pl.pallas_call(functools.partial(attention_kernel, length, 1.0 / math.sqr...]
    ppermute x18, waiting for transfers between devices: 30.6 us -> 37.3 us  [to_z(): return lax.ppermute(value, 'fsdp', [(i, i ^ 2 * step) for i in range(8)])]
    pallas_call x2, Pallas kernels: 21.2 us -> 15.3 us  [attention_back(): pl.pallas_call(functools.partial(attention_back_kernel, length, 1.0 / mat...]
    ppermute x7, waiting for transfers between devices: 5.28 us -> 8.56 us  [to_near(): lax.ppermute(value, AXES, [(i, i ^ (4 if i % 2 else 2)) for i in range(32)])]
  transfers between devices with their start and end apart: 44 -> 44, of which waited for: 18 -> 20; matrix products, arithmetic and copies ran while one was open for 12% -> 12% of each run, Pallas kernels for 33% -> 27%
where the time goes in v5:
time: 268 us; the launch traced here: 267 us
  Pallas kernels  89.2 us (33%)
  waiting for transfers between devices  74 us (28%)
  starting transfers between devices  51.7 us (19%)
  matrix products  17.7 us (7%)
  other arithmetic  16.7 us (6%)
  local copies, waits for them, and re-layouts  15.9 us (6%)
    ppermute x18, waiting for transfers between devices, to_z(): return lax.ppermute(value, 'fsdp', [(i, i ^ 2 * step) for i in range(8)])  37.3 us
    ppermute x18, starting transfers between devices, to_z(): return lax.ppermute(value, 'fsdp', [(i, i ^ 2 * step) for i in range(8)])  34.1 us
    ppermute x7, waiting for transfers between devices, to_far(): lax.ppermute(value, AXES, [(i, i ^ (2 if i % 2 else 4)) for i in range(32)])  21.4 us
    dot_general x4, matrix products, contract(): return lax.dot_general(left, right, dims, preferred_element_type=F32)  16.7 us
    pallas_call x2, Pallas kernels, attention_back(): pl.pallas_call(functools.partial(attention_back_kernel, length, 1.0 / mat...  15.3 us
    pallas_call x4, Pallas kernels, routed(): pl.pallas_call(functools.partial(route_kernel, rows), grid=(4,), in_specs...  14.6 us
    pallas_call x2, Pallas kernels, feed_back(): pl.pallas_call(feed_back_kernel, grid=(columns // block,), in_specs=[pl.B...  12.4 us
    pallas_call x2, Pallas kernels, feed(): pl.pallas_call(functools.partial(feed_kernel, side), grid=(columns // blo...  10.6 us
  transfers between devices with their start and end apart: 44, of which 20 were waited for; matrix products, arithmetic and copies ran while one was open for 12% of the time, Pallas kernels for 27%

profile of v5, /device:TPU:0, one launch (start us, length us, event | category | flops | bytes accessed | tf_op | source)
XLA Modules:
  0.0 266.7 jit_solution(11614720423721974703)
XLA Ops:
  11.4 6.5 %collective-permute-done.1 = bf16[48,2048]{1,0:T(8,128)(2,1)S(1)} collective-permute-done((bf16[48,2048]{1,0:T(8,128)(2,1)S(1)}, bf16[48,2048]{1,0:T(8,128)(2,1)S(1)}, u32[]{:S(2)}, u32[]{:S(2)}) %collective-permute-start.1) | collective-permute-done | bytes 196640 | tf_op jit(solution)/shard_map/ppermute | solution.py:749
  18.0 7.8 %collective-permute-done.2 = bf16[48,2048]{1,0:T(8,128)(2,1)S(1)} collective-permute-done((bf16[48,2048]{1,0:T(8,128)(2,1)S(1)}, bf16[48,2048]{1,0:T(8,128)(2,1)S(1)}, u32[]{:S(2)}, u32[]{:S(2)}) %collective-permute-start.2) | collective-permute-done | bytes 196640 | tf_op jit(solution)/shard_map/ppermute | solution.py:749
  35.6 4.5 %collective-permute-done.7 = bf16[48,1536]{1,0:T(8,128)(2,1)S(1)} collective-permute-done((bf16[48,1536]{1,0:T(8,128)(2,1)S(1)}, bf16[48,1536]{1,0:T(8,128)(2,1)S(1)}, u32[]{:S(2)}, u32[]{:S(2)}) %collective-permute-start.7) | collective-permute-done | bytes 147488 | tf_op jit(solution)/shard_map/ppermute | solution.py:749
  44.9 6.4 %collective-permute-done.9 = bf16[48,1536]{1,0:T(8,128)(2,1)} collective-permute-done((bf16[48,1536]{1,0:T(8,128)(2,1)S(1)}, bf16[48,1536]{1,0:T(8,128)(2,1)}, u32[]{:S(2)}, u32[]{:S(2)}) %collective-permute-start.9) | collective-permute-done | bytes 147488 | tf_op jit(solution)/shard_map/ppermute | solution.py:749
  51.3 10.1 %collective-permute-done.8 = bf16[4,2,48,2048]{3,2,1,0:T(8,128)(2,1)S(1)} collective-permute-done((bf16[4,2,48,2048]{3,2,1,0:T(8,128)(2,1)S(1)}, bf16[4,2,48,2048]{3,2,1,0:T(8,128)(2,1)S(1)}, u32[]{:S(2)}, u32[]{:S(2)}) %collective-permute-start.8) | collective-permute-done | bytes 1572896 | tf_op jit(solution)/shard_map/ppermute | solution.py:746
  68.4 5.5 %start_rows.1 = (f32[24,768]{1,0:T(8,128)S(1)}, f32[512,768]{1,0:T(8,128)}, bf16[512,768]{1,0:T(8,128)(2,1)S(1)}, bf16[768,512]{1,0:T(8,128)(2,1)}, f32[8,384]{1...) custom-call(s32[6]{0:T(128)S(1)} %copy-done.20, f32[512,768]{1,0:T(8,128)} %tokens_ref.1, ...), custom_call_target="tpu_custom_call" | custom-call | flops 37748736 | bytes 5505024 | tf_op jit(solution)/shard_map/start_rows/pallas_call | solution.py:340
  81.8 4.1 %attention.2 = (bf16[3,512,384]{2,1,0:T(8,128)(2,1)}, bf16[512,384]{1,0:T(8,128)(2,1)S(1)}) custom-call(bf16[512,768]{1,0:T(8,128)(2,1)S(1)} %get-tuple-element.155.rows_ref, bf16[768,2048]{1,0:T(8,128)(2,1)S(1)} %bitcast.182, bf16[768,2048]{1,0:T(8,128)(2,1)S(1)} %bitcast.183, bf16[768,2048]{1,0:T(8,128)(2,1)S(1)} %bitcast.184, ...), custom_call_target="tpu_custom_call" | custom-call | flops 905969664 | bytes 4128768 | tf_op jit(solution)/shard_map/attention/pallas_call | solution.py:98
  85.9 6.9 %collective-permute-done.14 = bf16[96,768]{1,0:T(8,128)(2,1)S(1)} collective-permute-done((bf16[96,768]{1,0:T(8,128)(2,1)S(1)}, bf16[96,768]{1,0:T(8,128)(2,1)S(1)}, u32[]{:S(2)}, u32[]{:S(2)}) %collective-permute-start.14) | collective-permute-done | bytes 147488 | tf_op jit(solution)/shard_map/ppermute | solution.py:749
  95.0 5.6 %attention.3 = (bf16[3,512,384]{2,1,0:T(8,128)(2,1)}, bf16[512,384]{1,0:T(8,128)(2,1)S(1)}) custom-call(bf16[512,768]{1,0:T(8,128)(2,1)S(1)} %get-tuple-element.155.rows_ref, bf16[768,2048]{1,0:T(8,128)(2,1)} %collective-permute-done.10.table_other_ref.query_ref.key_ref.value_ref.out_other_ref.weight_other_ref, ...), custom_call_target="tpu_custom_call" | custom-call | flops 905969664 | bytes 4128768 | tf_op jit(solution)/shard_map/attention/pallas_call | solution.py:98
  109.0 5.3 %feed.2 = (bf16[512,1536]{1,0:T(8,128)(2,1)}, f32[512,1536]{1,0:T(8,128)}) custom-call(bf16[512,768]{1,0:T(8,128)(2,1)S(1)} %get-tuple-element.174.rows_ref, bf16[768,1536]{1,0:T(8,128)(2,1)S(1)} %bitcast.189, f32[8,1536]{1,0:T(8,128)S(1)} %get-tuple-element.170.bias_ref), custom_call_target="tpu_custom_call" | custom-call | flops 1207959552 | bytes 7864320 | tf_op jit(solution)/shard_map/feed/pallas_call | solution.py:204
  114.2 5.2 %collective-permute-done.17 = bf16[4,2,96,768]{3,2,0,1:T(8,128)(2,1)S(1)} collective-permute-done((bf16[4,2,96,768]{3,2,0,1:T(8,128)(2,1)S(1)}, bf16[4,2,96,768]{3,2,0,1:T(8,128)(2,1)S(1)}, u32[]{:S(2)}, u32[]{:S(2)}) %collective-permute-start.17) | collective-permute-done | bytes 1179680 | tf_op jit(solution)/shard_map/ppermute | solution.py:746
  119.8 5.3 %feed.3 = (bf16[512,1536]{1,0:T(8,128)(2,1)}, f32[512,1536]{1,0:T(8,128)}) custom-call(bf16[512,768]{1,0:T(8,128)(2,1)S(1)} %get-tuple-element.174.rows_ref, bf16[768,1536]{1,0:T(8,128)(2,1)S(1)} %collective-permute-done.18.weight_ref.up_other_ref, f32[8,1536]{1,0:T(8,128)S(1)} %get-tuple-element.170.bias_ref), custom_call_target="tpu_custom_call" | custom-call | flops 1207959552 | bytes 7864320 | tf_op jit(solution)/shard_map/feed/pallas_call | solution.py:204
  125.1 4.2 %convolution_convert_fusion = bf16[1536,768]{1,0:T(8,128)(2,1)} fusion(bf16[512,1536]{1,0:T(8,128)(2,1)} %get-tuple-element.239, bf16[512,768]{1,0:T(8,128)(2,1)S(1)} %multiply_convert_fusion.grad_ref), kind=kOutput, calls=%fused_computation | convolution fusion | flops 1209139200 | bytes 4718592 | tf_op jit(solution)/shard_map/dot_general | solution.py:24
  134.8 4.3 %routed.4 = (bf16[4,2,96,768]{3,2,1,0:T(8,128)(2,1)}, f32[4,2,96,768]{3,2,1,0:T(8,128)}) custom-call(s32[4]{0:T(128)S(1)} %pad_add_fusion.1.route_ref, f32[1536,768]{1,0:T(8,128)S(1)} %fusion.31.refs_0_, bf16[1536,768]{1,0:T(8,128)(2,1)} %collective-permute-done.19.refs_1_), custom_call_target="tpu_custom_call" | custom-call | bytes 10616832 | tf_op jit(solution)/shard_map/routed/pallas_call | solution.py:712
  140.3 6.5 %feed_back.3 = (bf16[512,1536]{1,0:T(8,128)(2,1)}, f32[1,1536]{1,0:T(1,128)S(1)}, bf16[768,1536]{1,0:T(8,128)(2,1)}) custom-call(bf16[512,768]{1,0:T(8,128)(2,1)} %copy-done.26, bf16[1536,768]{1,0:T(8,128)(2,1)} %collective-permute-done.20.weight_ref, f32[512,1536]{1,0:T(8,128)} %get-tuple-element.186.slope_ref, bf16[768,512]{1,0:T(8,128)(2,1)} %get-tuple-element.180.rows_ref), custom_call_target="tpu_custom_call" | custom-call | flops 2415919104 | bytes 13369344 | tf_op jit(solution)/shard_map/feed_back/pallas_call | solution.py:240
  146.8 5.9 %feed_back.2 = (bf16[512,1536]{1,0:T(8,128)(2,1)}, f32[1,1536]{1,0:T(1,128)S(1)}, f32[768,1536]{1,0:T(8,128)S(1)}) custom-call(bf16[512,768]{1,0:T(8,128)(2,1)} %copy-done.26, bf16[1536,768]{1,0:T(8,128)(2,1)} %bitcast.48.weight_ref, f32[512,1536]{1,0:T(8,128)} %get-tuple-element.179.slope_ref, bf16[768,512]{1,0:T(8,128)(2,1)} %get-tuple-element.180.rows_ref), custom_call_target="tpu_custom_call" | custom-call | flops 2415919104 | bytes 13369344 | tf_op jit(solution)/shard_map/feed_back/pallas_call | solution.py:240
  161.2 7.9 %middle_back.1 = (f32[512,768]{1,0:T(8,128)S(1)}, bf16[512,384]{1,0:T(8,128)(2,1)S(1)}, bf16[512,384]{1,0:T(8,128)(2,1)S(1)}, f32[768,384]{1,0:T(8,128)S(1)}, bf...) custom-call(s32[6]{0:T(128)S(1)} %copy-done.20, bf16[512,1536]{1,0:T(8,128)(2,1)S(1)} %copy-done.13, ...), custom_call_target="tpu_custom_call" | custom-call | flops 3623878656 | bytes 14155776 | tf_op jit(solution)/shard_map/middle_back/pallas_call | solution.py:495
  171.2 4.4 %routed.5 = (bf16[4,2,48,1920]{3,2,1,0:T(8,128)(2,1)}, f32[4,2,48,1920]{3,2,1,0:T(8,128)}) custom-call(s32[4]{0:T(128)S(1)} %pad_add_fusion.1.route_ref, f32[768,1536]{1,0:T(8,128)S(1)} %get-tuple-element.198.refs_0_, bf16[768,1536]{1,0:T(8,128)(2,1)} %collective-permute-done.22.refs_1_, f32[768,384]{1,0:T(8,128)S(1)} %get-tuple-element.200.refs_2_, ...), custom_call_target="tpu_custom_call" | custom-call | bytes 13271040 | tf_op jit(solution)/shard_map/routed/pallas_call | solution.py:712
  183.0 7.9 %attention_back.2 = (bf16[3,512,384]{2,1,0:T(8,128)(2,1)}, bf16[3,768,384]{2,1,0:T(8,128)(2,1)}, f32[3,384]{1,0:T(4,128)S(1)}) custom-call(bf16[3,512,384]{2,1,0:T(8,128)(2,1)} %get-tuple-element.204.qkv_ref, bf16[512,384]{1,0:T(8,128)(2,1)} %copy-done.22, bf16[768,512]{1,0:T(8,128)(2,1)} %get-tuple-element.207.rows_ref), custom_call_target="tpu_custom_call" | custom-call | flops 905969664 | bytes 7077888 | tf_op jit(solution)/shard_map/attention_back/pallas_call | solution.py:153
  202.2 7.5 %attention_back.3 = (bf16[3,512,384]{2,1,0:T(8,128)(2,1)}, f32[3,768,384]{2,1,0:T(8,128)S(1)}, f32[3,384]{1,0:T(4,128)S(1)}) custom-call(bf16[3,512,384]{2,1,0:T(8,128)(2,1)} %get-tuple-element.176.qkv_ref, bf16[512,384]{1,0:T(8,128)(2,1)} %copy-done.21, bf16[768,512]{1,0:T(8,128)(2,1)} %get-tuple-element.207.rows_ref), custom_call_target="tpu_custom_call" | custom-call | flops 905969664 | bytes 7077888 | tf_op jit(solution)/shard_map/attention_back/pallas_call | solution.py:153
  223.4 7.1 %start_back.1 = (f32[512,768]{1,0:T(8,128)}, f32[768,128]{1,0:T(8,128)S(1)}, bf16[768,128]{1,0:T(8,128)(2,1)S(1)}) custom-call(s32[6]{0:T(128)S(1)} %copy-done.20, bf16[3,512,384]{2,1,0:T(8,128)(2,1)S(1)} %copy-done.19, bf16[3,512,384]{2,1,0:T(8,128)(2,1)S(1)} %copy-done.18, bf16[768,2048]{1,0:T(8,128)(2,1)S(1)} %bitcast.187, ...), custom_call_target="tpu_custom_call" | custom-call | bytes 1024 | tf_op jit(solution)/shard_map/start_back/pallas_call | solution.py:599
  240.5 4.4 %collective-permute-done.38 = bf16[4,48,128]{2,1,0:T(8,128)(2,1)S(1)} collective-permute-done((bf16[4,48,128]{2,1,0:T(8,128)(2,1)S(1)}, bf16[4,48,128]{2,1,0:T(8,128)(2,1)S(1)}, u32[]{:S(2)}, u32[]{:S(2)}) %collective-permute-start.38) | collective-permute-done | bytes 49184 | tf_op jit(solution)/shard_map/ppermute | solution.py:746
  252.0 4.3 %fusion.32 = f32[512,768]{1,0:T(8,128)} fusion(bf16[512,1536]{1,0:T(8,128)(2,1)S(1)} %copy-done.30, bf16[1536,768]{1,0:T(8,128)(2,1)} %bitcast.48.weight_ref), kind=kOutput, calls=%fused_computation.157 | convolution fusion | flops 1207959552 | bytes 5505024 | tf_op jit(solution)/shard_map/dot_general | solution.py:24
  256.4 5.1 %add_add_fusion = f32[512,768]{1,0:T(8,128)} fusion(f32[512,768]{1,0:T(8,128)S(1)} %copy-done.9, f32[512,768]{1,0:T(8,128)} %fusion.32, bf16[512,1536]{1,0:T(8,128)(2,1)} %get-tuple-element.239, bf16[1536,768]{1,0:T(8,128)(2,1)} %collective-permute-done.20.weight_ref, f32[768]{0:T(1024)S(1)} %slice_reduce_fusion.9), kind=kOutput, calls=%fused_computation.12 | convolution fusion | flops 1209139200 | bytes 8653824 | tf_op jit(solution)/shard_map/dot_general | solution.py:24
  (263 shorter events, 122.5 us)
Async XLA Ops:
  6.0 12.0 %collective-permute-start.1 = (bf16[48,2048]{1,0:T(8,128)(2,1)S(1)}, bf16[48,2048]{1,0:T(8,128)(2,1)S(1)}, u32[]{:S(2)}, u32[]{:S(2)}) collective-permute-start(bf16[48,2048]{1,0:T(8,128)(2,1)S(1)} %bitcast.199), channel_id=1, source_target_pairs={{0,8},{4,12},{8,0},{12,4},{16,24},{20,28},{24,16},{28,20},{1,9},{5... | collective-permute-start | bytes 589832 | tf_op jit(solution)/shard_map/ppermute | solution.py:749
  8.7 17.1 %collective-permute-start.2 = (bf16[48,2048]{1,0:T(8,128)(2,1)S(1)}, bf16[48,2048]{1,0:T(8,128)(2,1)S(1)}, u32[]{:S(2)}, u32[]{:S(2)}) collective-permute-start(bf16[48,2048]{1,0:T(8,128)(2,1)S(1)} %bitcast.200), channel_id=1, source_target_pairs={{0,16},{4,20},{8,24},{12,28},{16,0},{20,4},{24,8},{28,12},{1,17},{... | collective-permute-start | bytes 589832 | tf_op jit(solution)/shard_map/ppermute | solution.py:749
  11.3 14.5 %collective-permute-start.3 = (bf16[48,2048]{1,0:T(8,128)(2,1)S(1)}, bf16[48,2048]{1,0:T(8,128)(2,1)S(1)}, u32[]{:S(2)}, u32[]{:S(2)}) collective-permute-start(bf16[48,2048]{1,0:T(8,128)(2,1)S(1)} %bitcast.201), channel_id=1, source_target_pairs={{0,24},{4,28},{8,16},{12,20},{16,8},{20,12},{24,0},{28,4},{1,25},{... | collective-permute-start | bytes 589832 | tf_op jit(solution)/shard_map/ppermute | solution.py:749
  11.3 16.3 %collective-permute-start.5 = (bf16[24,1536]{1,0:T(8,128)(2,1)S(1)}, bf16[24,1536]{1,0:T(8,128)(2,1)S(1)}, u32[]{:S(2)}, u32[]{:S(2)}) collective-permute-start(bf16[24,1536]{1,0:T(8,128)(2,1)S(1)} %dynamic-slice_bitcast_fusion.4), channel_id=1, source_target_pairs={{0,1},{1,0},{2,3},{3,2},{4,5},{5,4},{6,7},{7,6},{8,9},{9,8},{10,11... | collective-permute-start | bytes 221192 | tf_op jit(solution)/shard_map/ppermute | solution.py:740
  26.0 14.1 %collective-permute-start.4 = (bf16[4,48,2048]{2,1,0:T(8,128)(2,1)S(1)}, bf16[4,48,2048]{2,1,0:T(8,128)(2,1)S(1)}, u32[]{:S(2)}, u32[]{:S(2)}) collective-permute-start(bf16[4,48,2048]{2,1,0:T(8,128)(2,1)S(1)} %pad_maximum_fusion.6), channel_id=1, source_target_pairs={{0,2},{1,5},{2,0},{3,7},{4,6},{5,1},{6,4},{7,3},{8,10},{9,13},{10,... | collective-permute-start | bytes 2359304 | tf_op jit(solution)/shard_map/ppermute | solution.py:743
  40.9 20.5 %collective-permute-start.8 = (bf16[4,2,48,2048]{3,2,1,0:T(8,128)(2,1)S(1)}, bf16[4,2,48,2048]{3,2,1,0:T(8,128)(2,1)S(1)}, u32[]{:S(2)}, u32[]{:S(2)}) collective-permute-start(bf16[4,2,48,2048]{3,2,1,0:T(8,128)(2,1)S(1)} %pad_maximum_fusion.3), channel_id=1, source_target_pairs={{0,4},{1,3},{2,6},{3,1},{4,0},{5,7},{6,2},{7,5},{8,12},{9,11},{10,... | collective-permute-start | bytes 4718600 | tf_op jit(solution)/shard_map/ppermute | solution.py:746
  76.3 16.6 %collective-permute-start.12 = (bf16[4,2,48,1536]{3,2,1,0:T(8,128)(2,1)S(1)}, bf16[4,2,48,1536]{3,2,1,0:T(8,128)(2,1)S(1)}, u32[]{:S(2)}, u32[]{:S(2)}) collective-permute-start(bf16[4,2,48,1536]{3,2,1,0:T(8,128)(2,1)S(1)} %pad_maximum_fusion.4), channel_id=1, source_target_pairs={{0,4},{1,3},{2,6},{3,1},{4,0},{5,7},{6,2},{7,5},{8,12},{9,11},{10,... | collective-permute-start | bytes 3538952 | tf_op jit(solution)/shard_map/ppermute | solution.py:746
  79.4 13.5 %collective-permute-start.14 = (bf16[96,768]{1,0:T(8,128)(2,1)S(1)}, bf16[96,768]{1,0:T(8,128)(2,1)S(1)}, u32[]{:S(2)}, u32[]{:S(2)}) collective-permute-start(bf16[96,768]{1,0:T(8,128)(2,1)S(1)} %convert_element_type.155), channel_id=1, source_target_pairs={{0,16},{4,20},{8,24},{12,28},{16,0},{20,4},{24,8},{28,12},{1,17},{... | collective-permute-start | bytes 442376 | tf_op jit(solution)/shard_map/ppermute | solution.py:749
  80.4 12.4 %collective-permute-start.15 = (bf16[96,768]{1,0:T(8,128)(2,1)S(1)}, bf16[96,768]{1,0:T(8,128)(2,1)S(1)}, u32[]{:S(2)}, u32[]{:S(2)}) collective-permute-start(bf16[96,768]{1,0:T(8,128)(2,1)S(1)} %convert_element_type.155), channel_id=1, source_target_pairs={{0,24},{4,28},{8,16},{12,20},{16,8},{20,12},{24,0},{28,4},{1,25},{... | collective-permute-start | bytes 442376 | tf_op jit(solution)/shard_map/ppermute | solution.py:749
  94.9 24.9 %collective-permute-start.18 = (bf16[768,1536]{1,0:T(8,128)(2,1)S(1)}, bf16[768,1536]{1,0:T(8,128)(2,1)S(1)}, u32[]{:S(2)}, u32[]{:S(2)}) collective-permute-start(bf16[768,1536]{1,0:T(8,128)(2,1)S(1)} %bitcast.188), channel_id=1, source_target_pairs={{0,1},{1,0},{2,3},{3,2},{4,5},{5,4},{6,7},{7,6},{8,9},{9,8},{10,11... | collective-permute-start | bytes 7077896 | tf_op jit(solution)/shard_map/ppermute | solution.py:740
  103.2 16.3 %collective-permute-start.17 = (bf16[4,2,96,768]{3,2,0,1:T(8,128)(2,1)S(1)}, bf16[4,2,96,768]{3,2,0,1:T(8,128)(2,1)S(1)}, u32[]{:S(2)}, u32[]{:S(2)}) collective-permute-start(bf16[4,2,96,768]{3,2,0,1:T(8,128)(2,1)S(1)} %pad_maximum_fusion.5), channel_id=1, source_target_pairs={{0,4},{1,3},{2,6},{3,1},{4,0},{5,7},{6,2},{7,5},{8,12},{9,11},{10,... | collective-permute-start | bytes 3538952 | tf_op jit(solution)/shard_map/ppermute | solution.py:746
  139.1 16.5 %collective-permute-start.21 = (bf16[4,2,96,768]{3,2,1,0:T(8,128)(2,1)}, bf16[4,2,96,768]{3,2,1,0:T(8,128)(2,1)}, u32[]{:S(2)}, u32[]{:S(2)}) collective-permute-start(bf16[4,2,96,768]{3,2,1,0:T(8,128)(2,1)} %get-tuple-element.184), channel_id=1, source_target_pairs={{0,2},{1,5},{2,0},{3,7},{4,6},{5,1},{6,4},{7,3},{8,10},{9,13},{10,... | collective-permute-start | bytes 3538952 | tf_op jit(solution)/shard_map/ppermute | solution.py:743
  146.8 24.4 %collective-permute-start.22 = (bf16[768,1536]{1,0:T(8,128)(2,1)}, bf16[768,1536]{1,0:T(8,128)(2,1)}, u32[]{:S(2)}, u32[]{:S(2)}) collective-permute-start(bf16[768,1536]{1,0:T(8,128)(2,1)} %get-tuple-element.195), channel_id=1, source_target_pairs={{0,1},{1,0},{2,3},{3,2},{4,5},{5,4},{6,7},{7,6},{8,9},{9,8},{10,11... | collective-permute-start | bytes 7077896 | tf_op jit(solution)/shard_map/ppermute | solution.py:740
  175.6 19.7 %collective-permute-start.25 = (bf16[4,2,48,1920]{3,2,1,0:T(8,128)(2,1)}, bf16[4,2,48,1920]{3,2,1,0:T(8,128)(2,1)}, u32[]{:S(2)}, u32[]{:S(2)}) collective-permute-start(bf16[4,2,48,1920]{3,2,1,0:T(8,128)(2,1)} %get-tuple-element.203), channel_id=1, source_target_pairs={{0,2},{1,5},{2,0},{3,7},{4,6},{5,1},{6,4},{7,3},{8,10},{9,13},{10,... | collective-permute-start | bytes 4423688 | tf_op jit(solution)/shard_map/ppermute | solution.py:743
  178.5 12.4 %collective-permute-start.26 = (bf16[96,768]{1,0:T(8,128)(2,1)S(1)}, bf16[96,768]{1,0:T(8,128)(2,1)S(1)}, u32[]{:S(2)}, u32[]{:S(2)}) collective-permute-start(bf16[96,768]{1,0:T(8,128)(2,1)S(1)} %get-tuple-element.285), channel_id=1, source_target_pairs={{0,8},{4,12},{8,0},{12,4},{16,24},{20,28},{24,16},{28,20},{1,9},{5... | collective-permute-start | bytes 442376 | tf_op jit(solution)/shard_map/ppermute | solution.py:749
  180.6 14.0 %collective-permute-start.27 = (bf16[96,768]{1,0:T(8,128)(2,1)S(1)}, bf16[96,768]{1,0:T(8,128)(2,1)S(1)}, u32[]{:S(2)}, u32[]{:S(2)}) collective-permute-start(bf16[96,768]{1,0:T(8,128)(2,1)S(1)} %get-tuple-element.284), channel_id=1, source_target_pairs={{0,16},{4,20},{8,24},{12,28},{16,0},{20,4},{24,8},{28,12},{1,17},{... | collective-permute-start | bytes 442376 | tf_op jit(solution)/shard_map/ppermute | solution.py:749
  181.6 12.9 %collective-permute-start.28 = (bf16[96,768]{1,0:T(8,128)(2,1)S(1)}, bf16[96,768]{1,0:T(8,128)(2,1)S(1)}, u32[]{:S(2)}, u32[]{:S(2)}) collective-permute-start(bf16[96,768]{1,0:T(8,128)(2,1)S(1)} %get-tuple-element.283), channel_id=1, source_target_pairs={{0,24},{4,28},{8,16},{12,20},{16,8},{20,12},{24,0},{28,4},{1,25},{... | collective-permute-start | bytes 442376 | tf_op jit(solution)/shard_map/ppermute | solution.py:749
  190.9 18.9 %collective-permute-start.29 = (bf16[3,768,384]{2,1,0:T(8,128)(2,1)}, bf16[3,768,384]{2,1,0:T(8,128)(2,1)}, u32[]{:S(2)}, u32[]{:S(2)}) collective-permute-start(bf16[3,768,384]{2,1,0:T(8,128)(2,1)} %get-tuple-element.209), channel_id=1, source_target_pairs={{0,1},{1,0},{2,3},{3,2},{4,5},{5,4},{6,7},{7,6},{8,9},{9,8},{10,11... | collective-permute-start | bytes 5308424 | tf_op jit(solution)/shard_map/ppermute | solution.py:740
  215.6 19.3 %collective-permute-start.31 = (bf16[4,2,48,1152]{3,2,1,0:T(8,128)(2,1)S(1)}, bf16[4,2,48,1152]{3,2,1,0:T(8,128)(2,1)S(1)}, u32[]{:S(2)}, u32[]{:S(2)}) collective-permute-start(bf16[4,2,48,1152]{3,2,1,0:T(8,128)(2,1)S(1)} %get-tuple-element.218), channel_id=1, source_target_pairs={{0,2},{1,5},{2,0},{3,7},{4,6},{5,1},{6,4},{7,3},{8,10},{9,13},{10,... | collective-permute-start | bytes 2654216 | tf_op jit(solution)/shard_map/ppermute | solution.py:743
  218.2 18.6 %collective-permute-start.35 = (bf16[48,1920]{1,0:T(8,128)(2,1)S(1)}, bf16[48,1920]{1,0:T(8,128)(2,1)S(1)}, u32[]{:S(2)}, u32[]{:S(2)}) collective-permute-start(bf16[48,1920]{1,0:T(8,128)(2,1)S(1)} %get-tuple-element.282), channel_id=1, source_target_pairs={{0,8},{4,12},{8,0},{12,4},{16,24},{20,28},{24,16},{28,20},{1,9},{5... | collective-permute-start | bytes 552968 | tf_op jit(solution)/shard_map/ppermute | solution.py:749
  220.9 15.9 %collective-permute-start.36 = (bf16[48,1920]{1,0:T(8,128)(2,1)S(1)}, bf16[48,1920]{1,0:T(8,128)(2,1)S(1)}, u32[]{:S(2)}, u32[]{:S(2)}) collective-permute-start(bf16[48,1920]{1,0:T(8,128)(2,1)S(1)} %get-tuple-element.281), channel_id=1, source_target_pairs={{0,16},{4,20},{8,24},{12,28},{16,0},{20,4},{24,8},{28,12},{1,17},{... | collective-permute-start | bytes 552968 | tf_op jit(solution)/shard_map/ppermute | solution.py:749
  222.0 14.9 %collective-permute-start.37 = (bf16[48,1920]{1,0:T(8,128)(2,1)S(1)}, bf16[48,1920]{1,0:T(8,128)(2,1)S(1)}, u32[]{:S(2)}, u32[]{:S(2)}) collective-permute-start(bf16[48,1920]{1,0:T(8,128)(2,1)S(1)} %get-tuple-element.280), channel_id=1, source_target_pairs={{0,24},{4,28},{8,16},{12,20},{16,8},{20,12},{24,0},{28,4},{1,25},{... | collective-permute-start | bytes 552968 | tf_op jit(solution)/shard_map/ppermute | solution.py:749
  247.5 14.1 %collective-permute-start.39 = (bf16[48,1280]{1,0:T(8,128)(2,1)S(1)}, bf16[48,1280]{1,0:T(8,128)(2,1)S(1)}, u32[]{:S(2)}, u32[]{:S(2)}) collective-permute-start(bf16[48,1280]{1,0:T(8,128)(2,1)S(1)} %get-tuple-element.295), channel_id=1, source_target_pairs={{0,8},{4,12},{8,0},{12,4},{16,24},{20,28},{24,16},{28,20},{1,9},{5... | collective-permute-start | bytes 368648 | tf_op jit(solution)/shard_map/ppermute | solution.py:749
  248.6 13.0 %collective-permute-start.40 = (bf16[48,1280]{1,0:T(8,128)(2,1)S(1)}, bf16[48,1280]{1,0:T(8,128)(2,1)S(1)}, u32[]{:S(2)}, u32[]{:S(2)}) collective-permute-start(bf16[48,1280]{1,0:T(8,128)(2,1)S(1)} %get-tuple-element.296), channel_id=1, source_target_pairs={{0,16},{4,20},{8,24},{12,28},{16,0},{20,4},{24,8},{28,12},{1,17},{... | collective-permute-start | bytes 368648 | tf_op jit(solution)/shard_map/ppermute | solution.py:749
  (65 other events, 408.9 us)

commit v6 on v5

--- a/solution.py
+++ b/solution.py
@@ -14,7 +14,7 @@
 BF = jnp.bfloat16
 F32 = jnp.float32
 LANES = 128
-VMEM_BYTES = 16 << 20
+VMEM_BYTES = 18 << 20
 GELU_OUTER = math.sqrt(2.0 / math.pi)
 GELU_INNER = 0.044715
 
@@ -629,12 +629,12 @@
     )(place, *grads, *weights, start, middle, mask, rows, sums, *side_sums, bias)
 
 
-def shards_kernel(fixed, seq_cols, place_ref, qkv_ref, out_ref, table_ref, *refs):
+def shards_kernel(fixed, seq_cols, core_ref, steps_ref, qkv_ref, out_ref, table_ref, *refs):
     small_refs, (mine_ref, other_ref, full_ref) = refs[: fixed + 1], refs[fixed + 1 :]
-    core = place_ref[0]
+    core = core_ref[0]
     part, table_cols = table_ref.shape
     half = out_ref.shape[1] // 2
-    seq_count = place_ref.shape[0] - 2
+    seq_count = steps_ref.shape[0]
     lines = [ref[...] for ref in small_refs[:fixed]]
     up = small_refs[fixed][...]
     lines += [up[:, i : i + part] for i in range(0, up.shape[1], part)]
@@ -642,7 +642,7 @@
     for row in range(seq_cols):
         line = jnp.zeros((1, part), jnp.int32)
         for index in range(seq_count):
-            step = place_ref[2 + index]
+            step = steps_ref[index]
             line = jnp.where(lane + row * part == index, step // 256, line)
             line = jnp.where(lane + row * part == seq_count + index, step % 256, line)
         lines.append(line.astype(F32))
@@ -666,20 +666,20 @@
         left += wide
 
 
-def attention_shards(place, w_qkv, w_out, table, small, b_up, seq_cols, all_cols):
+def attention_shards(core, timesteps, w_qkv, w_out, table, small, b_up, seq_cols, all_cols):
     part = table.shape[0]
     shape = jax.ShapeDtypeStruct((part, 2 * w_out.shape[1] + all_cols // 2), BF)
     vmem = pl.BlockSpec(memory_space=pltpu.VMEM)
     return pl.pallas_call(
         functools.partial(shards_kernel, len(small), seq_cols),
-        in_specs=[pl.BlockSpec(memory_space=pltpu.SMEM)] + [vmem] * (4 + len(small)),
+        in_specs=[pl.BlockSpec(memory_space=pltpu.SMEM)] * 2 + [vmem] * (4 + len(small)),
         out_specs=[vmem, vmem],
         out_shape=[shape, shape],
         scratch_shapes=[pltpu.VMEM((part, all_cols), F32)],
         compiler_params=pltpu.CompilerParams(vmem_limit_bytes=60 << 20),
         cost_estimate=pl.CostEstimate(flops=0, bytes_accessed=24 * part * w_out.shape[1], transcendentals=0),
         name="attention_shards",
-    )(place, w_qkv, w_out, table, *[item.reshape(1, -1) for item in small], b_up.reshape(1, -1))
+    )(core, timesteps, w_qkv, w_out, table, *[item.reshape(1, -1) for item in small], b_up.reshape(1, -1))
 
 
 def route_kernel(rows, route_ref, *refs):
@@ -816,9 +816,14 @@
         self.sent, self.kept = routed(after(self.terms, *wait), self.rows, self.tree.route)
         self.got = self.tree.to_near(self.sent)
 
-    def two(self, *wait):
+    def two(self, *wait, apart=False):
         tree = self.tree
         kept, got = after((self.kept, self.got), *wait)
+        if apart:
+            self.sent = (pick(kept, 1 - tree.far, 1) + pick(got, 1 - tree.far, 1)).astype(BF)
+            self.kept = pick(kept, tree.far, 1) + pick(got, tree.far, 1)
+            self.got = tree.to_far(self.sent)
+            return
         total = kept + got
         self.kept, self.sent = pick(total, tree.far, 1), pick(total, 1 - tree.far, 1).astype(BF)
         self.got = tree.to_far(self.sent)
@@ -942,7 +947,10 @@
     all_cols = -(-(table_cols + small_cols) // (2 * LANES)) * (2 * LANES)
     place = jnp.concatenate([jnp.stack([jnp.int32(core), place]), timesteps])
 
-    attn_w = gather_columns(*attention_shards(place, w_qkv, w_out, time_table, small, b_up, seq_cols, all_cols))
+    shards = attention_shards(
+        jnp.full((1,), core, jnp.int32), timesteps, w_qkv, w_out, time_table, small, b_up, seq_cols, all_cols
+    )
+    attn_w = gather_columns(*shards)
     up_shard = w_up.astype(BF).reshape(part, chips, 2, hidden_part).transpose(2, 0, 1, 3)
     up_shard = up_shard.reshape(2, part, hidden_width // 2)
     up_w = gather_columns(*[pick(up_shard, side, 0) for side in (core, 1 - core)])
@@ -963,7 +971,7 @@
     down_one = down_w.one(up_two, context_mine)
     up_w = up_w.halves(context_mine)
     qkv_other, context_other = attention(after(normed_one, up_two), attn_w[1], bias_other, seq_length)
-    down_two = down_w.two(context_other)
+    down_two = down_w.two()
     contexts = (context_mine, context_other)
     middle, normed_two, across_two = middle_rows(place, contexts, attn_w, after(start, down_one), rows)
     hidden, slope = [None, None], [None, None]
@@ -979,12 +987,12 @@
     if fast:
         down_sum.one()
     grad_pre[1], grad_b_up[1], grad_up[1] = feed_back(
-        after(grad_branch, down_sum.sent), down_w[1], slope[1], across_two, BF
+        grad_branch, down_w[1], slope[1], across_two, BF
     )
     grad_pre[0], grad_b_up[0], grad_up[0] = feed_back(grad_branch, down_w[0], slope[0], across_two, F32)
     up_sum.add(grad_up[0], grad_up[1])
     if fast:
-        down_sum.two(grad_pre[0])
+        down_sum.two(grad_pre[1])
     grad_pre = after(grad_pre, down_sum.sent)
     grad_middle, *grad_context, grad_out_mine, grad_out_other, middle_sums = middle_back(
         place, grad_pre, up_w, middle, cotangent, absorbed, rows, contexts, attn_w
@@ -1005,7 +1013,7 @@
     grad_qkv, grad_weights, sums = zip(*grads)
     attn_sum.add(grad_weights[0], grad_weights[1])
     if fast:
-        attn_sum.one(up_sum.got)
+        attn_sum.one()
         up_sum.along_z()
     grad_qkv = after(grad_qkv, up_sum.sent, attn_sum.sent)
     grad_b_up = paired(core, *[item.reshape(chips, hidden_part) for item in grad_b_up], 1).reshape(count, hidden_part)
@@ -1016,7 +1024,7 @@
         grad_b_up.reshape(width, LANES), seqs, seq_length, fast,
     )
     if fast:
-        attn_sum.two(grad_tokens)
+        attn_sum.two()
         extra_sum = reduction(2 * part)
         extra_sum.add(*blocks)
         extra_sum.one()

time: 268 us -> 259 us (0.966)
  Pallas kernels: 89.2 us -> 84.8 us
    ppermute x7, waiting for transfers between devices: 21.4 us -> 14.9 us  [to_far(): lax.ppermute(value, AXES, [(i, i ^ (2 if i % 2 else 4)) for i in range(32)])]
    ppermute x7, waiting for transfers between devices: 8.56 us -> 14.1 us  [to_near(): lax.ppermute(value, AXES, [(i, i ^ (4 if i % 2 else 2)) for i in range(32)])]
    pallas_call x4, Pallas kernels: 14.6 us -> 10.7 us  [routed(): pl.pallas_call(functools.partial(route_kernel, rows), grid=(4,), in_specs...]
    unnamed x90 -> x104, local copies, waits for them, and re-layouts: 5.39 us -> 5.37 us
  transfers between devices with their start and end apart: 44 -> 44, of which waited for: 20 -> 20; matrix products, arithmetic and copies ran while one was open for 12% -> 12% of each run, Pallas kernels for 27% -> 29%
where the time goes in v6:
time: 259 us; the launch traced here: 258 us
  Pallas kernels  84.8 us (33%)
  waiting for transfers between devices  73.4 us (28%)
  starting transfers between devices  51.4 us (20%)
  matrix products  17.6 us (7%)
  local copies, waits for them, and re-layouts  14.9 us (6%)
  other arithmetic  14.7 us (6%)
    ppermute x18, waiting for transfers between devices, to_z(): return lax.ppermute(value, 'fsdp', [(i, i ^ 2 * step) for i in range(8)])  37.4 us
    ppermute x18, starting transfers between devices, to_z(): return lax.ppermute(value, 'fsdp', [(i, i ^ 2 * step) for i in range(8)])  33.7 us
    dot_general x4, matrix products, contract(): return lax.dot_general(left, right, dims, preferred_element_type=F32)  16.6 us
    pallas_call x2, Pallas kernels, attention_back(): pl.pallas_call(functools.partial(attention_back_kernel, length, 1.0 / mat...  15.4 us
    ppermute x7, waiting for transfers between devices, to_far(): lax.ppermute(value, AXES, [(i, i ^ (2 if i % 2 else 4)) for i in range(32)])  14.9 us
    ppermute x7, waiting for transfers between devices, to_near(): lax.ppermute(value, AXES, [(i, i ^ (4 if i % 2 else 2)) for i in range(32)])  14.1 us
    pallas_call x2, Pallas kernels, feed_back(): pl.pallas_call(feed_back_kernel, grid=(columns // block,), in_specs=[pl.B...  12.4 us
    pallas_call x4, Pallas kernels, routed(): pl.pallas_call(functools.partial(route_kernel, rows), grid=(4,), in_specs...  10.7 us
  transfers between devices with their start and end apart: 44, of which 20 were waited for; matrix products, arithmetic and copies ran while one was open for 12% of the time, Pallas kernels for 29%

profile of v6, /device:TPU:0, one launch (start us, length us, event | category | flops | bytes accessed | tf_op | source)
XLA Modules:
  0.0 258.5 jit_solution(11310682853482697503)
XLA Ops:
  10.2 6.5 %collective-permute-done.1 = bf16[48,2048]{1,0:T(8,128)(2,1)S(1)} collective-permute-done((bf16[48,2048]{1,0:T(8,128)(2,1)S(1)}, bf16[48,2048]{1,0:T(8,128)(2,1)S(1)}, u32[]{:S(2)}, u32[]{:S(2)}) %collective-permute-start.1) | collective-permute-done | bytes 196640 | tf_op jit(solution)/shard_map/ppermute | solution.py:749
  16.7 7.8 %collective-permute-done.2 = bf16[48,2048]{1,0:T(8,128)(2,1)S(1)} collective-permute-done((bf16[48,2048]{1,0:T(8,128)(2,1)S(1)}, bf16[48,2048]{1,0:T(8,128)(2,1)S(1)}, u32[]{:S(2)}, u32[]{:S(2)}) %collective-permute-start.2) | collective-permute-done | bytes 196640 | tf_op jit(solution)/shard_map/ppermute | solution.py:749
  26.4 4.1 %collective-permute-start.6 = (bf16[48,1536]{1,0:T(8,128)(2,1)S(1)}, bf16[48,1536]{1,0:T(8,128)(2,1)S(1)}, u32[]{:S(2)}, u32[]{:S(2)}) collective-permute-start(bf16[48,1536]{1,0:T(8,128)(2,1)S(1)} %bitcast.203), channel_id=1, source_target_pairs={{0,8},{4,12},{8,0},{12,4},{16,24},{20,28},{24,16},{28,20},{1,9},{5... | collective-permute-start | bytes 442376 | tf_op jit(solution)/shard_map/ppermute | solution.py:749
  34.4 4.5 %collective-permute-done.7 = bf16[48,1536]{1,0:T(8,128)(2,1)S(1)} collective-permute-done((bf16[48,1536]{1,0:T(8,128)(2,1)S(1)}, bf16[48,1536]{1,0:T(8,128)(2,1)S(1)}, u32[]{:S(2)}, u32[]{:S(2)}) %collective-permute-start.7) | collective-permute-done | bytes 147488 | tf_op jit(solution)/shard_map/ppermute | solution.py:749
  43.7 6.3 %collective-permute-done.9 = bf16[48,1536]{1,0:T(8,128)(2,1)S(1)} collective-permute-done((bf16[48,1536]{1,0:T(8,128)(2,1)S(1)}, bf16[48,1536]{1,0:T(8,128)(2,1)S(1)}, u32[]{:S(2)}, u32[]{:S(2)}) %collective-permute-start.9) | collective-permute-done | bytes 147488 | tf_op jit(solution)/shard_map/ppermute | solution.py:749
  50.0 10.2 %collective-permute-done.8 = bf16[4,2,48,2048]{3,2,1,0:T(8,128)(2,1)S(1)} collective-permute-done((bf16[4,2,48,2048]{3,2,1,0:T(8,128)(2,1)S(1)}, bf16[4,2,48,2048]{3,2,1,0:T(8,128)(2,1)S(1)}, u32[]{:S(2)}, u32[]{:S(2)}) %collective-permute-start.8) | collective-permute-done | bytes 1572896 | tf_op jit(solution)/shard_map/ppermute | solution.py:746
  67.2 5.5 %start_rows.1 = (f32[24,768]{1,0:T(8,128)S(1)}, f32[512,768]{1,0:T(8,128)}, bf16[512,768]{1,0:T(8,128)(2,1)S(1)}, bf16[768,512]{1,0:T(8,128)(2,1)}, f32[8,384]{1...) custom-call(s32[6]{0:T(128)S(1)} %pad_add_fusion.place_ref, f32[512,768]{1,0:T(8,128)} %tokens_ref.1, ...), custom_call_target="tpu_custom_call" | custom-call | flops 37748736 | bytes 5505024 | tf_op jit(solution)/shard_map/start_rows/pallas_call | solution.py:340
  80.3 4.1 %attention.2 = (bf16[3,512,384]{2,1,0:T(8,128)(2,1)}, bf16[512,384]{1,0:T(8,128)(2,1)S(1)}) custom-call(bf16[512,768]{1,0:T(8,128)(2,1)S(1)} %get-tuple-element.154.rows_ref, bf16[768,2048]{1,0:T(8,128)(2,1)S(1)} %bitcast.182, bf16[768,2048]{1,0:T(8,128)(2,1)S(1)} %bitcast.183, bf16[768,2048]{1,0:T(8,128)(2,1)S(1)} %bitcast.184, ...), custom_call_target="tpu_custom_call" | custom-call | flops 905969664 | bytes 4128768 | tf_op jit(solution)/shard_map/attention/pallas_call | solution.py:98
  84.4 7.0 %collective-permute-done.14 = bf16[96,768]{1,0:T(8,128)(2,1)S(1)} collective-permute-done((bf16[96,768]{1,0:T(8,128)(2,1)S(1)}, bf16[96,768]{1,0:T(8,128)(2,1)S(1)}, u32[]{:S(2)}, u32[]{:S(2)}) %collective-permute-start.14) | collective-permute-done | bytes 147488 | tf_op jit(solution)/shard_map/ppermute | solution.py:749
  93.5 8.0 %collective-permute-done.16 = bf16[4,96,768]{2,1,0:T(8,128)(2,1)S(1)} collective-permute-done((bf16[4,96,768]{2,1,0:T(8,128)(2,1)S(1)}, bf16[4,96,768]{2,1,0:T(8,128)(2,1)S(1)}, u32[]{:S(2)}, u32[]{:S(2)}) %collective-permute-start.16) | collective-permute-done | bytes 589856 | tf_op jit(solution)/shard_map/ppermute | solution.py:743
  103.3 5.1 %attention.3 = (bf16[3,512,384]{2,1,0:T(8,128)(2,1)}, bf16[512,384]{1,0:T(8,128)(2,1)S(1)}) custom-call(bf16[512,768]{1,0:T(8,128)(2,1)S(1)} %get-tuple-element.154.rows_ref, bf16[768,2048]{1,0:T(8,128)(2,1)} %collective-permute-done.10.table_other_ref.query_ref.key_ref.value_ref.out_other_ref.weight_other_ref, ...), custom_call_target="tpu_custom_call" | custom-call | flops 905969664 | bytes 4128768 | tf_op jit(solution)/shard_map/attention/pallas_call | solution.py:98
  108.4 4.1 %middle_rows.1 = (f32[512,768]{1,0:T(8,128)}, bf16[512,768]{1,0:T(8,128)(2,1)S(1)}, bf16[768,512]{1,0:T(8,128)(2,1)}) custom-call(s32[6]{0:T(128)S(1)} %pad_add_fusion.place_ref, bf16[512,384]{1,0:T(8,128)(2,1)S(1)} %get-tuple-element.151.context_mine_ref, bf16[512,384]{1,0:T(8,128)(2,1)S(1)} %get-tuple-element.156.context_other_ref, ...), custom_call_target="tpu_custom_call" | custom-call | flops 603979776 | bytes 6684672 | tf_op jit(solution)/shard_map/middle_rows/pallas_call | solution.py:404
  112.5 5.3 %feed.2 = (bf16[512,1536]{1,0:T(8,128)(2,1)}, f32[512,1536]{1,0:T(8,128)}) custom-call(bf16[512,768]{1,0:T(8,128)(2,1)S(1)} %get-tuple-element.173.rows_ref, bf16[768,1536]{1,0:T(8,128)(2,1)S(1)} %bitcast.189, f32[8,1536]{1,0:T(8,128)S(1)} %get-tuple-element.169.bias_ref), custom_call_target="tpu_custom_call" | custom-call | flops 1207959552 | bytes 7864320 | tf_op jit(solution)/shard_map/feed/pallas_call | solution.py:204
  118.3 5.3 %feed.3 = (bf16[512,1536]{1,0:T(8,128)(2,1)}, f32[512,1536]{1,0:T(8,128)}) custom-call(bf16[512,768]{1,0:T(8,128)(2,1)S(1)} %get-tuple-element.173.rows_ref, bf16[768,1536]{1,0:T(8,128)(2,1)S(1)} %collective-permute-done.18.weight_ref.up_other_ref, f32[8,1536]{1,0:T(8,128)S(1)} %get-tuple-element.169.bias_ref), custom_call_target="tpu_custom_call" | custom-call | flops 1207959552 | bytes 7864320 | tf_op jit(solution)/shard_map/feed/pallas_call | solution.py:204
  123.6 4.3 %convolution_convert_fusion = bf16[1536,768]{1,0:T(8,128)(2,1)} fusion(bf16[512,1536]{1,0:T(8,128)(2,1)} %get-tuple-element.236, bf16[512,768]{1,0:T(8,128)(2,1)S(1)} %multiply_convert_fusion.grad_ref), kind=kOutput, calls=%fused_computation | convolution fusion | flops 1209139200 | bytes 4718592 | tf_op jit(solution)/shard_map/dot_general | solution.py:24
  137.3 6.5 %feed_back.3 = (bf16[512,1536]{1,0:T(8,128)(2,1)}, f32[1,1536]{1,0:T(1,128)S(1)}, bf16[768,1536]{1,0:T(8,128)(2,1)}) custom-call(bf16[512,768]{1,0:T(8,128)(2,1)} %copy-done.27, bf16[1536,768]{1,0:T(8,128)(2,1)} %collective-permute-done.19.weight_ref, f32[512,1536]{1,0:T(8,128)} %get-tuple-element.181.slope_ref, bf16[768,512]{1,0:T(8,128)(2,1)} %get-tuple-element.179.rows_ref), custom_call_target="tpu_custom_call" | custom-call | flops 2415919104 | bytes 13369344 | tf_op jit(solution)/shard_map/feed_back/pallas_call | solution.py:240
  143.8 5.9 %feed_back.2 = (bf16[512,1536]{1,0:T(8,128)(2,1)}, f32[1,1536]{1,0:T(1,128)S(1)}, f32[768,1536]{1,0:T(8,128)S(1)}) custom-call(bf16[512,768]{1,0:T(8,128)(2,1)} %copy-done.27, bf16[1536,768]{1,0:T(8,128)(2,1)} %bitcast.48.weight_ref, f32[512,1536]{1,0:T(8,128)} %get-tuple-element.178.slope_ref, bf16[768,512]{1,0:T(8,128)(2,1)} %get-tuple-element.179.rows_ref), custom_call_target="tpu_custom_call" | custom-call | flops 2415919104 | bytes 13369344 | tf_op jit(solution)/shard_map/feed_back/pallas_call | solution.py:240
  158.2 8.0 %middle_back.1 = (f32[512,768]{1,0:T(8,128)S(1)}, bf16[512,384]{1,0:T(8,128)(2,1)S(1)}, bf16[512,384]{1,0:T(8,128)(2,1)S(1)}, f32[768,384]{1,0:T(8,128)S(1)}, bf...) custom-call(s32[6]{0:T(128)S(1)} %pad_add_fusion.place_ref, bf16[512,1536]{1,0:T(8,128)(2,1)S(1)} %copy-done.15, ...), custom_call_target="tpu_custom_call" | custom-call | flops 3623878656 | bytes 14155776 | tf_op jit(solution)/shard_map/middle_back/pallas_call | solution.py:495
  178.8 7.8 %attention_back.2 = (bf16[3,512,384]{2,1,0:T(8,128)(2,1)}, bf16[3,768,384]{2,1,0:T(8,128)(2,1)}, f32[3,384]{1,0:T(4,128)S(1)}) custom-call(bf16[3,512,384]{2,1,0:T(8,128)(2,1)} %get-tuple-element.202.qkv_ref, bf16[512,384]{1,0:T(8,128)(2,1)} %copy-done.23, bf16[768,512]{1,0:T(8,128)(2,1)} %get-tuple-element.205.rows_ref), custom_call_target="tpu_custom_call" | custom-call | flops 905969664 | bytes 7077888 | tf_op jit(solution)/shard_map/attention_back/pallas_call | solution.py:153
  197.4 7.6 %attention_back.3 = (bf16[3,512,384]{2,1,0:T(8,128)(2,1)}, f32[3,768,384]{2,1,0:T(8,128)S(1)}, f32[3,384]{1,0:T(4,128)S(1)}) custom-call(bf16[3,512,384]{2,1,0:T(8,128)(2,1)} %get-tuple-element.175.qkv_ref, bf16[512,384]{1,0:T(8,128)(2,1)} %copy-done.22, bf16[768,512]{1,0:T(8,128)(2,1)} %get-tuple-element.205.rows_ref), custom_call_target="tpu_custom_call" | custom-call | flops 905969664 | bytes 7077888 | tf_op jit(solution)/shard_map/attention_back/pallas_call | solution.py:153
  215.3 7.0 %start_back.1 = (f32[512,768]{1,0:T(8,128)}, f32[768,128]{1,0:T(8,128)S(1)}, bf16[768,128]{1,0:T(8,128)(2,1)S(1)}) custom-call(s32[6]{0:T(128)S(1)} %pad_add_fusion.place_ref, bf16[3,512,384]{2,1,0:T(8,128)(2,1)S(1)} %copy-done.21, bf16[3,512,384]{2,1,0:T(8,128)(2,1)S(1)} %copy-done.20, bf16[768,2048]{1,0:T(8,128)(2,1)S(1)} %bitcast.187, ...), custom_call_target="tpu_custom_call" | custom-call | bytes 1024 | tf_op jit(solution)/shard_map/start_back/pallas_call | solution.py:599
  232.1 4.5 %collective-permute-done.38 = bf16[4,48,128]{2,1,0:T(8,128)(2,1)S(1)} collective-permute-done((bf16[4,48,128]{2,1,0:T(8,128)(2,1)S(1)}, bf16[4,48,128]{2,1,0:T(8,128)(2,1)S(1)}, u32[]{:S(2)}, u32[]{:S(2)}) %collective-permute-start.38) | collective-permute-done | bytes 49184 | tf_op jit(solution)/shard_map/ppermute | solution.py:746
  243.8 4.3 %fusion.32 = f32[512,768]{1,0:T(8,128)} fusion(bf16[512,1536]{1,0:T(8,128)(2,1)S(1)} %copy-done.31, bf16[1536,768]{1,0:T(8,128)(2,1)} %bitcast.48.weight_ref), kind=kOutput, calls=%fused_computation.157 | convolution fusion | flops 1207959552 | bytes 5505024 | tf_op jit(solution)/shard_map/dot_general | solution.py:24
  248.2 5.1 %add_add_fusion = f32[512,768]{1,0:T(8,128)} fusion(f32[512,768]{1,0:T(8,128)S(1)} %copy-done.11, f32[512,768]{1,0:T(8,128)} %fusion.32, bf16[512,1536]{1,0:T(8,128)(2,1)} %get-tuple-element.236, bf16[1536,768]{1,0:T(8,128)(2,1)} %collective-permute-done.19.weight_ref, f32[768]{0:T(1024)S(1)} %slice_reduce_fusion.9), kind=kOutput, calls=%fused_computation.12 | convolution fusion | flops 1209139200 | bytes 8653824 | tf_op jit(solution)/shard_map/dot_general | solution.py:24
  (277 shorter events, 112.1 us)
Async XLA Ops:
  7.5 17.1 %collective-permute-start.2 = (bf16[48,2048]{1,0:T(8,128)(2,1)S(1)}, bf16[48,2048]{1,0:T(8,128)(2,1)S(1)}, u32[]{:S(2)}, u32[]{:S(2)}) collective-permute-start(bf16[48,2048]{1,0:T(8,128)(2,1)S(1)} %bitcast.200), channel_id=1, source_target_pairs={{0,16},{4,20},{8,24},{12,28},{16,0},{20,4},{24,8},{28,12},{1,17},{... | collective-permute-start | bytes 589832 | tf_op jit(solution)/shard_map/ppermute | solution.py:749
  10.0 14.5 %collective-permute-start.3 = (bf16[48,2048]{1,0:T(8,128)(2,1)S(1)}, bf16[48,2048]{1,0:T(8,128)(2,1)S(1)}, u32[]{:S(2)}, u32[]{:S(2)}) collective-permute-start(bf16[48,2048]{1,0:T(8,128)(2,1)S(1)} %bitcast.201), channel_id=1, source_target_pairs={{0,24},{4,28},{8,16},{12,20},{16,8},{20,12},{24,0},{28,4},{1,25},{... | collective-permute-start | bytes 589832 | tf_op jit(solution)/shard_map/ppermute | solution.py:749
  10.1 16.3 %collective-permute-start.5 = (bf16[24,1536]{1,0:T(8,128)(2,1)S(1)}, bf16[24,1536]{1,0:T(8,128)(2,1)S(1)}, u32[]{:S(2)}, u32[]{:S(2)}) collective-permute-start(bf16[24,1536]{1,0:T(8,128)(2,1)S(1)} %dynamic-slice_bitcast_fusion.4), channel_id=1, source_target_pairs={{0,1},{1,0},{2,3},{3,2},{4,5},{5,4},{6,7},{7,6},{8,9},{9,8},{10,11... | collective-permute-start | bytes 221192 | tf_op jit(solution)/shard_map/ppermute | solution.py:740
  24.8 14.1 %collective-permute-start.4 = (bf16[4,48,2048]{2,1,0:T(8,128)(2,1)S(1)}, bf16[4,48,2048]{2,1,0:T(8,128)(2,1)S(1)}, u32[]{:S(2)}, u32[]{:S(2)}) collective-permute-start(bf16[4,48,2048]{2,1,0:T(8,128)(2,1)S(1)} %pad_maximum_fusion.6), channel_id=1, source_target_pairs={{0,2},{1,5},{2,0},{3,7},{4,6},{5,1},{6,4},{7,3},{8,10},{9,13},{10,... | collective-permute-start | bytes 2359304 | tf_op jit(solution)/shard_map/ppermute | solution.py:743
  39.7 20.5 %collective-permute-start.8 = (bf16[4,2,48,2048]{3,2,1,0:T(8,128)(2,1)S(1)}, bf16[4,2,48,2048]{3,2,1,0:T(8,128)(2,1)S(1)}, u32[]{:S(2)}, u32[]{:S(2)}) collective-permute-start(bf16[4,2,48,2048]{3,2,1,0:T(8,128)(2,1)S(1)} %pad_maximum_fusion.3), channel_id=1, source_target_pairs={{0,4},{1,3},{2,6},{3,1},{4,0},{5,7},{6,2},{7,5},{8,12},{9,11},{10,... | collective-permute-start | bytes 4718600 | tf_op jit(solution)/shard_map/ppermute | solution.py:746
  74.8 16.6 %collective-permute-start.12 = (bf16[4,2,48,1536]{3,2,1,0:T(8,128)(2,1)S(1)}, bf16[4,2,48,1536]{3,2,1,0:T(8,128)(2,1)S(1)}, u32[]{:S(2)}, u32[]{:S(2)}) collective-permute-start(bf16[4,2,48,1536]{3,2,1,0:T(8,128)(2,1)S(1)} %pad_maximum_fusion.4), channel_id=1, source_target_pairs={{0,4},{1,3},{2,6},{3,1},{4,0},{5,7},{6,2},{7,5},{8,12},{9,11},{10,... | collective-permute-start | bytes 3538952 | tf_op jit(solution)/shard_map/ppermute | solution.py:746
  77.9 13.5 %collective-permute-start.14 = (bf16[96,768]{1,0:T(8,128)(2,1)S(1)}, bf16[96,768]{1,0:T(8,128)(2,1)S(1)}, u32[]{:S(2)}, u32[]{:S(2)}) collective-permute-start(bf16[96,768]{1,0:T(8,128)(2,1)S(1)} %convert_element_type.155), channel_id=1, source_target_pairs={{0,16},{4,20},{8,24},{12,28},{16,0},{20,4},{24,8},{28,12},{1,17},{... | collective-permute-start | bytes 442376 | tf_op jit(solution)/shard_map/ppermute | solution.py:749
  78.9 12.5 %collective-permute-start.15 = (bf16[96,768]{1,0:T(8,128)(2,1)S(1)}, bf16[96,768]{1,0:T(8,128)(2,1)S(1)}, u32[]{:S(2)}, u32[]{:S(2)}) collective-permute-start(bf16[96,768]{1,0:T(8,128)(2,1)S(1)} %convert_element_type.155), channel_id=1, source_target_pairs={{0,24},{4,28},{8,16},{12,20},{16,8},{20,12},{24,0},{28,4},{1,25},{... | collective-permute-start | bytes 442376 | tf_op jit(solution)/shard_map/ppermute | solution.py:749
  93.4 24.9 %collective-permute-start.18 = (bf16[768,1536]{1,0:T(8,128)(2,1)S(1)}, bf16[768,1536]{1,0:T(8,128)(2,1)S(1)}, u32[]{:S(2)}, u32[]{:S(2)}) collective-permute-start(bf16[768,1536]{1,0:T(8,128)(2,1)S(1)} %bitcast.188), channel_id=1, source_target_pairs={{0,1},{1,0},{2,3},{3,2},{4,5},{5,4},{6,7},{7,6},{8,9},{9,8},{10,11... | collective-permute-start | bytes 7077896 | tf_op jit(solution)/shard_map/ppermute | solution.py:740
  101.7 16.3 %collective-permute-start.17 = (bf16[4,2,96,768]{3,2,0,1:T(8,128)(2,1)S(1)}, bf16[4,2,96,768]{3,2,0,1:T(8,128)(2,1)S(1)}, u32[]{:S(2)}, u32[]{:S(2)}) collective-permute-start(bf16[4,2,96,768]{3,2,0,1:T(8,128)(2,1)S(1)} %pad_maximum_fusion.5), channel_id=1, source_target_pairs={{0,4},{1,3},{2,6},{3,1},{4,0},{5,7},{6,2},{7,5},{8,12},{9,11},{10,... | collective-permute-start | bytes 3538952 | tf_op jit(solution)/shard_map/ppermute | solution.py:746
  136.1 16.5 %collective-permute-start.21 = (bf16[4,2,96,768]{3,2,1,0:T(8,128)(2,1)}, bf16[4,2,96,768]{3,2,1,0:T(8,128)(2,1)}, u32[]{:S(2)}, u32[]{:S(2)}) collective-permute-start(bf16[4,2,96,768]{3,2,1,0:T(8,128)(2,1)} %get-tuple-element.186), channel_id=1, source_target_pairs={{0,2},{1,5},{2,0},{3,7},{4,6},{5,1},{6,4},{7,3},{8,10},{9,13},{10,... | collective-permute-start | bytes 3538952 | tf_op jit(solution)/shard_map/ppermute | solution.py:743
  143.8 24.5 %collective-permute-start.22 = (bf16[768,1536]{1,0:T(8,128)(2,1)}, bf16[768,1536]{1,0:T(8,128)(2,1)S(1)}, u32[]{:S(2)}, u32[]{:S(2)}) collective-permute-start(bf16[768,1536]{1,0:T(8,128)(2,1)} %get-tuple-element.193), channel_id=1, source_target_pairs={{0,1},{1,0},{2,3},{3,2},{4,5},{5,4},{6,7},{7,6},{8,9},{9,8},{10,11... | collective-permute-start | bytes 7077896 | tf_op jit(solution)/shard_map/ppermute | solution.py:740
  171.6 19.7 %collective-permute-start.25 = (bf16[4,2,48,1920]{3,2,1,0:T(8,128)(2,1)}, bf16[4,2,48,1920]{3,2,1,0:T(8,128)(2,1)}, u32[]{:S(2)}, u32[]{:S(2)}) collective-permute-start(bf16[4,2,48,1920]{3,2,1,0:T(8,128)(2,1)} %get-tuple-element.201), channel_id=1, source_target_pairs={{0,2},{1,5},{2,0},{3,7},{4,6},{5,1},{6,4},{7,3},{8,10},{9,13},{10,... | collective-permute-start | bytes 4423688 | tf_op jit(solution)/shard_map/ppermute | solution.py:743
  174.3 12.4 %collective-permute-start.26 = (bf16[96,768]{1,0:T(8,128)(2,1)S(1)}, bf16[96,768]{1,0:T(8,128)(2,1)S(1)}, u32[]{:S(2)}, u32[]{:S(2)}) collective-permute-start(bf16[96,768]{1,0:T(8,128)(2,1)S(1)} %get-tuple-element.283), channel_id=1, source_target_pairs={{0,8},{4,12},{8,0},{12,4},{16,24},{20,28},{24,16},{28,20},{1,9},{5... | collective-permute-start | bytes 442376 | tf_op jit(solution)/shard_map/ppermute | solution.py:749
  176.4 14.0 %collective-permute-start.27 = (bf16[96,768]{1,0:T(8,128)(2,1)S(1)}, bf16[96,768]{1,0:T(8,128)(2,1)S(1)}, u32[]{:S(2)}, u32[]{:S(2)}) collective-permute-start(bf16[96,768]{1,0:T(8,128)(2,1)S(1)} %get-tuple-element.282), channel_id=1, source_target_pairs={{0,16},{4,20},{8,24},{12,28},{16,0},{20,4},{24,8},{28,12},{1,17},{... | collective-permute-start | bytes 442376 | tf_op jit(solution)/shard_map/ppermute | solution.py:749
  177.4 12.9 %collective-permute-start.28 = (bf16[96,768]{1,0:T(8,128)(2,1)S(1)}, bf16[96,768]{1,0:T(8,128)(2,1)S(1)}, u32[]{:S(2)}, u32[]{:S(2)}) collective-permute-start(bf16[96,768]{1,0:T(8,128)(2,1)S(1)} %get-tuple-element.281), channel_id=1, source_target_pairs={{0,24},{4,28},{8,16},{12,20},{16,8},{20,12},{24,0},{28,4},{1,25},{... | collective-permute-start | bytes 442376 | tf_op jit(solution)/shard_map/ppermute | solution.py:749
  186.6 18.4 %collective-permute-start.29 = (bf16[3,768,384]{2,1,0:T(8,128)(2,1)}, bf16[3,768,384]{2,1,0:T(8,128)(2,1)S(1)}, u32[]{:S(2)}, u32[]{:S(2)}) collective-permute-start(bf16[3,768,384]{2,1,0:T(8,128)(2,1)} %get-tuple-element.207), channel_id=1, source_target_pairs={{0,1},{1,0},{2,3},{3,2},{4,5},{5,4},{6,7},{7,6},{8,9},{9,8},{10,11... | collective-permute-start | bytes 5308424 | tf_op jit(solution)/shard_map/ppermute | solution.py:740
  195.7 13.3 %collective-permute-start.32 = (bf16[4,48,1920]{2,1,0:T(8,128)(2,1)}, bf16[4,48,1920]{2,1,0:T(8,128)(2,1)}, u32[]{:S(2)}, u32[]{:S(2)}) collective-permute-start(bf16[4,48,1920]{2,1,0:T(8,128)(2,1)} %fusion), channel_id=1, source_target_pairs={{0,4},{1,3},{2,6},{3,1},{4,0},{5,7},{6,2},{7,5},{8,12},{9,11},{10,... | collective-permute-start | bytes 2211848 | tf_op jit(solution)/shard_map/ppermute | solution.py:746
  207.7 18.9 %collective-permute-start.30 = (bf16[4,2,48,1152]{3,2,1,0:T(8,128)(2,1)S(1)}, bf16[4,2,48,1152]{3,2,1,0:T(8,128)(2,1)S(1)}, u32[]{:S(2)}, u32[]{:S(2)}) collective-permute-start(bf16[4,2,48,1152]{3,2,1,0:T(8,128)(2,1)S(1)} %get-tuple-element.216), channel_id=1, source_target_pairs={{0,2},{1,5},{2,0},{3,7},{4,6},{5,1},{6,4},{7,3},{8,10},{9,13},{10,... | collective-permute-start | bytes 2654216 | tf_op jit(solution)/shard_map/ppermute | solution.py:743
  210.4 18.1 %collective-permute-start.35 = (bf16[48,1920]{1,0:T(8,128)(2,1)S(1)}, bf16[48,1920]{1,0:T(8,128)(2,1)S(1)}, u32[]{:S(2)}, u32[]{:S(2)}) collective-permute-start(bf16[48,1920]{1,0:T(8,128)(2,1)S(1)} %get-tuple-element.280), channel_id=1, source_target_pairs={{0,8},{4,12},{8,0},{12,4},{16,24},{20,28},{24,16},{28,20},{1,9},{5... | collective-permute-start | bytes 552968 | tf_op jit(solution)/shard_map/ppermute | solution.py:749
  212.8 15.8 %collective-permute-start.36 = (bf16[48,1920]{1,0:T(8,128)(2,1)S(1)}, bf16[48,1920]{1,0:T(8,128)(2,1)S(1)}, u32[]{:S(2)}, u32[]{:S(2)}) collective-permute-start(bf16[48,1920]{1,0:T(8,128)(2,1)S(1)} %get-tuple-element.279), channel_id=1, source_target_pairs={{0,16},{4,20},{8,24},{12,28},{16,0},{20,4},{24,8},{28,12},{1,17},{... | collective-permute-start | bytes 552968 | tf_op jit(solution)/shard_map/ppermute | solution.py:749
  213.8 14.8 %collective-permute-start.37 = (bf16[48,1920]{1,0:T(8,128)(2,1)S(1)}, bf16[48,1920]{1,0:T(8,128)(2,1)S(1)}, u32[]{:S(2)}, u32[]{:S(2)}) collective-permute-start(bf16[48,1920]{1,0:T(8,128)(2,1)S(1)} %get-tuple-element.278), channel_id=1, source_target_pairs={{0,24},{4,28},{8,16},{12,20},{16,8},{20,12},{24,0},{28,4},{1,25},{... | collective-permute-start | bytes 552968 | tf_op jit(solution)/shard_map/ppermute | solution.py:749
  239.3 14.1 %collective-permute-start.39 = (bf16[48,1280]{1,0:T(8,128)(2,1)S(1)}, bf16[48,1280]{1,0:T(8,128)(2,1)S(1)}, u32[]{:S(2)}, u32[]{:S(2)}) collective-permute-start(bf16[48,1280]{1,0:T(8,128)(2,1)S(1)} %get-tuple-element.293), channel_id=1, source_target_pairs={{0,8},{4,12},{8,0},{12,4},{16,24},{20,28},{24,16},{28,20},{1,9},{5... | collective-permute-start | bytes 368648 | tf_op jit(solution)/shard_map/ppermute | solution.py:749
  240.4 13.0 %collective-permute-start.40 = (bf16[48,1280]{1,0:T(8,128)(2,1)S(1)}, bf16[48,1280]{1,0:T(8,128)(2,1)S(1)}, u32[]{:S(2)}, u32[]{:S(2)}) collective-permute-start(bf16[48,1280]{1,0:T(8,128)(2,1)S(1)} %get-tuple-element.294), channel_id=1, source_target_pairs={{0,16},{4,20},{8,24},{12,28},{16,0},{20,4},{24,8},{28,12},{1,17},{... | collective-permute-start | bytes 368648 | tf_op jit(solution)/shard_map/ppermute | solution.py:749
  (72 other events, 502.3 us)

commit v7 on v6

--- a/solution.py
+++ b/solution.py
@@ -1028,7 +1028,7 @@
         extra_sum = reduction(2 * part)
         extra_sum.add(*blocks)
         extra_sum.one()
-        extra_sum.two(attn_sum.sent, up_sum.got)
+        extra_sum.two(attn_sum.sent)
         attn_sum.along_z(extra_sum)
         hidden, rows = after((hidden, rows), attn_sum.sent)
     output = middle + (product(hidden[0], down_w[0]) + product(hidden[1], down_w[1]) + rows[seq_count + 3])

time: 259 us -> 259 us (level)
  transfers between devices with their start and end apart: 44 -> 44, of which waited for: 20 -> 19; matrix products, arithmetic and copies ran while one was open for 12% -> 12% of each run, Pallas kernels for 29% -> 29%
where the time goes in v7:
time: 259 us; the launch traced here: 258 us
  Pallas kernels  84.8 us (33%)
  waiting for transfers between devices  73.3 us (28%)
  starting transfers between devices  51.4 us (20%)
  matrix products  17.6 us (7%)
  local copies, waits for them, and re-layouts  14.9 us (6%)
  other arithmetic  14.8 us (6%)
    ppermute x18, waiting for transfers between devices, to_z(): return lax.ppermute(value, 'fsdp', [(i, i ^ 2 * step) for i in range(8)])  37.4 us
    ppermute x18, starting transfers between devices, to_z(): return lax.ppermute(value, 'fsdp', [(i, i ^ 2 * step) for i in range(8)])  33.7 us
    dot_general x4, matrix products, contract(): return lax.dot_general(left, right, dims, preferred_element_type=F32)  16.6 us
    pallas_call x2, Pallas kernels, attention_back(): pl.pallas_call(functools.partial(attention_back_kernel, length, 1.0 / mat...  15.4 us
    ppermute x7, waiting for transfers between devices, to_far(): lax.ppermute(value, AXES, [(i, i ^ (2 if i % 2 else 4)) for i in range(32)])  14.9 us
    ppermute x7, waiting for transfers between devices, to_near(): lax.ppermute(value, AXES, [(i, i ^ (4 if i % 2 else 2)) for i in range(32)])  14.2 us
    pallas_call x2, Pallas kernels, feed_back(): pl.pallas_call(feed_back_kernel, grid=(columns // block,), in_specs=[pl.B...  12.4 us
    pallas_call x4, Pallas kernels, routed(): pl.pallas_call(functools.partial(route_kernel, rows), grid=(4,), in_specs...  10.7 us
  transfers between devices with their start and end apart: 44, of which 19 were waited for; matrix products, arithmetic and copies ran while one was open for 12% of the time, Pallas kernels for 29%

profile of v7, /device:TPU:0, one launch (start us, length us, event | category | flops | bytes accessed | tf_op | source)
XLA Modules:
  0.0 258.5 jit_solution(13925083054065505517)
XLA Ops:
  10.2 6.5 %collective-permute-done.1 = bf16[48,2048]{1,0:T(8,128)(2,1)S(1)} collective-permute-done((bf16[48,2048]{1,0:T(8,128)(2,1)S(1)}, bf16[48,2048]{1,0:T(8,128)(2,1)S(1)}, u32[]{:S(2)}, u32[]{:S(2)}) %collective-permute-start.1) | collective-permute-done | bytes 196640 | tf_op jit(solution)/shard_map/ppermute | solution.py:749
  16.7 7.8 %collective-permute-done.2 = bf16[48,2048]{1,0:T(8,128)(2,1)S(1)} collective-permute-done((bf16[48,2048]{1,0:T(8,128)(2,1)S(1)}, bf16[48,2048]{1,0:T(8,128)(2,1)S(1)}, u32[]{:S(2)}, u32[]{:S(2)}) %collective-permute-start.2) | collective-permute-done | bytes 196640 | tf_op jit(solution)/shard_map/ppermute | solution.py:749
  26.4 4.1 %collective-permute-start.6 = (bf16[48,1536]{1,0:T(8,128)(2,1)S(1)}, bf16[48,1536]{1,0:T(8,128)(2,1)S(1)}, u32[]{:S(2)}, u32[]{:S(2)}) collective-permute-start(bf16[48,1536]{1,0:T(8,128)(2,1)S(1)} %bitcast.203), channel_id=1, source_target_pairs={{0,8},{4,12},{8,0},{12,4},{16,24},{20,28},{24,16},{28,20},{1,9},{5... | collective-permute-start | bytes 442376 | tf_op jit(solution)/shard_map/ppermute | solution.py:749
  34.4 4.5 %collective-permute-done.7 = bf16[48,1536]{1,0:T(8,128)(2,1)S(1)} collective-permute-done((bf16[48,1536]{1,0:T(8,128)(2,1)S(1)}, bf16[48,1536]{1,0:T(8,128)(2,1)S(1)}, u32[]{:S(2)}, u32[]{:S(2)}) %collective-permute-start.7) | collective-permute-done | bytes 147488 | tf_op jit(solution)/shard_map/ppermute | solution.py:749
  43.7 6.3 %collective-permute-done.9 = bf16[48,1536]{1,0:T(8,128)(2,1)S(1)} collective-permute-done((bf16[48,1536]{1,0:T(8,128)(2,1)S(1)}, bf16[48,1536]{1,0:T(8,128)(2,1)S(1)}, u32[]{:S(2)}, u32[]{:S(2)}) %collective-permute-start.9) | collective-permute-done | bytes 147488 | tf_op jit(solution)/shard_map/ppermute | solution.py:749
  50.0 10.2 %collective-permute-done.8 = bf16[4,2,48,2048]{3,2,1,0:T(8,128)(2,1)S(1)} collective-permute-done((bf16[4,2,48,2048]{3,2,1,0:T(8,128)(2,1)S(1)}, bf16[4,2,48,2048]{3,2,1,0:T(8,128)(2,1)S(1)}, u32[]{:S(2)}, u32[]{:S(2)}) %collective-permute-start.8) | collective-permute-done | bytes 1572896 | tf_op jit(solution)/shard_map/ppermute | solution.py:746
  67.2 5.5 %start_rows.1 = (f32[24,768]{1,0:T(8,128)S(1)}, f32[512,768]{1,0:T(8,128)}, bf16[512,768]{1,0:T(8,128)(2,1)S(1)}, bf16[768,512]{1,0:T(8,128)(2,1)}, f32[8,384]{1...) custom-call(s32[6]{0:T(128)S(1)} %pad_add_fusion.place_ref, f32[512,768]{1,0:T(8,128)} %tokens_ref.1, ...), custom_call_target="tpu_custom_call" | custom-call | flops 37748736 | bytes 5505024 | tf_op jit(solution)/shard_map/start_rows/pallas_call | solution.py:340
  80.3 4.1 %attention.2 = (bf16[3,512,384]{2,1,0:T(8,128)(2,1)}, bf16[512,384]{1,0:T(8,128)(2,1)S(1)}) custom-call(bf16[512,768]{1,0:T(8,128)(2,1)S(1)} %get-tuple-element.154.rows_ref, bf16[768,2048]{1,0:T(8,128)(2,1)S(1)} %bitcast.182, bf16[768,2048]{1,0:T(8,128)(2,1)S(1)} %bitcast.183, bf16[768,2048]{1,0:T(8,128)(2,1)S(1)} %bitcast.184, ...), custom_call_target="tpu_custom_call" | custom-call | flops 905969664 | bytes 4128768 | tf_op jit(solution)/shard_map/attention/pallas_call | solution.py:98
  84.4 7.0 %collective-permute-done.14 = bf16[96,768]{1,0:T(8,128)(2,1)S(1)} collective-permute-done((bf16[96,768]{1,0:T(8,128)(2,1)S(1)}, bf16[96,768]{1,0:T(8,128)(2,1)S(1)}, u32[]{:S(2)}, u32[]{:S(2)}) %collective-permute-start.14) | collective-permute-done | bytes 147488 | tf_op jit(solution)/shard_map/ppermute | solution.py:749
  93.5 8.0 %collective-permute-done.16 = bf16[4,96,768]{2,1,0:T(8,128)(2,1)S(1)} collective-permute-done((bf16[4,96,768]{2,1,0:T(8,128)(2,1)S(1)}, bf16[4,96,768]{2,1,0:T(8,128)(2,1)S(1)}, u32[]{:S(2)}, u32[]{:S(2)}) %collective-permute-start.16) | collective-permute-done | bytes 589856 | tf_op jit(solution)/shard_map/ppermute | solution.py:743
  103.3 5.1 %attention.3 = (bf16[3,512,384]{2,1,0:T(8,128)(2,1)}, bf16[512,384]{1,0:T(8,128)(2,1)S(1)}) custom-call(bf16[512,768]{1,0:T(8,128)(2,1)S(1)} %get-tuple-element.154.rows_ref, bf16[768,2048]{1,0:T(8,128)(2,1)} %collective-permute-done.10.table_other_ref.query_ref.key_ref.value_ref.out_other_ref.weight_other_ref, ...), custom_call_target="tpu_custom_call" | custom-call | flops 905969664 | bytes 4128768 | tf_op jit(solution)/shard_map/attention/pallas_call | solution.py:98
  108.4 4.1 %middle_rows.1 = (f32[512,768]{1,0:T(8,128)}, bf16[512,768]{1,0:T(8,128)(2,1)S(1)}, bf16[768,512]{1,0:T(8,128)(2,1)}) custom-call(s32[6]{0:T(128)S(1)} %pad_add_fusion.place_ref, bf16[512,384]{1,0:T(8,128)(2,1)S(1)} %get-tuple-element.151.context_mine_ref, bf16[512,384]{1,0:T(8,128)(2,1)S(1)} %get-tuple-element.156.context_other_ref, ...), custom_call_target="tpu_custom_call" | custom-call | flops 603979776 | bytes 6684672 | tf_op jit(solution)/shard_map/middle_rows/pallas_call | solution.py:404
  112.5 5.3 %feed.2 = (bf16[512,1536]{1,0:T(8,128)(2,1)}, f32[512,1536]{1,0:T(8,128)}) custom-call(bf16[512,768]{1,0:T(8,128)(2,1)S(1)} %get-tuple-element.173.rows_ref, bf16[768,1536]{1,0:T(8,128)(2,1)S(1)} %bitcast.189, f32[8,1536]{1,0:T(8,128)S(1)} %get-tuple-element.169.bias_ref), custom_call_target="tpu_custom_call" | custom-call | flops 1207959552 | bytes 7864320 | tf_op jit(solution)/shard_map/feed/pallas_call | solution.py:204
  118.3 5.3 %feed.3 = (bf16[512,1536]{1,0:T(8,128)(2,1)}, f32[512,1536]{1,0:T(8,128)}) custom-call(bf16[512,768]{1,0:T(8,128)(2,1)S(1)} %get-tuple-element.173.rows_ref, bf16[768,1536]{1,0:T(8,128)(2,1)S(1)} %collective-permute-done.18.weight_ref.up_other_ref, f32[8,1536]{1,0:T(8,128)S(1)} %get-tuple-element.169.bias_ref), custom_call_target="tpu_custom_call" | custom-call | flops 1207959552 | bytes 7864320 | tf_op jit(solution)/shard_map/feed/pallas_call | solution.py:204
  123.6 4.3 %convolution_convert_fusion = bf16[1536,768]{1,0:T(8,128)(2,1)} fusion(bf16[512,1536]{1,0:T(8,128)(2,1)} %get-tuple-element.236, bf16[512,768]{1,0:T(8,128)(2,1)S(1)} %multiply_convert_fusion.grad_ref), kind=kOutput, calls=%fused_computation | convolution fusion | flops 1209139200 | bytes 4718592 | tf_op jit(solution)/shard_map/dot_general | solution.py:24
  137.3 6.5 %feed_back.3 = (bf16[512,1536]{1,0:T(8,128)(2,1)}, f32[1,1536]{1,0:T(1,128)S(1)}, bf16[768,1536]{1,0:T(8,128)(2,1)}) custom-call(bf16[512,768]{1,0:T(8,128)(2,1)} %copy-done.27, bf16[1536,768]{1,0:T(8,128)(2,1)} %collective-permute-done.19.weight_ref, f32[512,1536]{1,0:T(8,128)} %get-tuple-element.181.slope_ref, bf16[768,512]{1,0:T(8,128)(2,1)} %get-tuple-element.179.rows_ref), custom_call_target="tpu_custom_call" | custom-call | flops 2415919104 | bytes 13369344 | tf_op jit(solution)/shard_map/feed_back/pallas_call | solution.py:240
  143.8 5.9 %feed_back.2 = (bf16[512,1536]{1,0:T(8,128)(2,1)}, f32[1,1536]{1,0:T(1,128)S(1)}, f32[768,1536]{1,0:T(8,128)S(1)}) custom-call(bf16[512,768]{1,0:T(8,128)(2,1)} %copy-done.27, bf16[1536,768]{1,0:T(8,128)(2,1)} %bitcast.48.weight_ref, f32[512,1536]{1,0:T(8,128)} %get-tuple-element.178.slope_ref, bf16[768,512]{1,0:T(8,128)(2,1)} %get-tuple-element.179.rows_ref), custom_call_target="tpu_custom_call" | custom-call | flops 2415919104 | bytes 13369344 | tf_op jit(solution)/shard_map/feed_back/pallas_call | solution.py:240
  158.2 8.0 %middle_back.1 = (f32[512,768]{1,0:T(8,128)S(1)}, bf16[512,384]{1,0:T(8,128)(2,1)S(1)}, bf16[512,384]{1,0:T(8,128)(2,1)S(1)}, f32[768,384]{1,0:T(8,128)S(1)}, bf...) custom-call(s32[6]{0:T(128)S(1)} %pad_add_fusion.place_ref, bf16[512,1536]{1,0:T(8,128)(2,1)S(1)} %copy-done.15, ...), custom_call_target="tpu_custom_call" | custom-call | flops 3623878656 | bytes 14155776 | tf_op jit(solution)/shard_map/middle_back/pallas_call | solution.py:495
  178.8 7.8 %attention_back.2 = (bf16[3,512,384]{2,1,0:T(8,128)(2,1)}, bf16[3,768,384]{2,1,0:T(8,128)(2,1)}, f32[3,384]{1,0:T(4,128)S(1)}) custom-call(bf16[3,512,384]{2,1,0:T(8,128)(2,1)} %get-tuple-element.202.qkv_ref, bf16[512,384]{1,0:T(8,128)(2,1)} %copy-done.23, bf16[768,512]{1,0:T(8,128)(2,1)} %get-tuple-element.205.rows_ref), custom_call_target="tpu_custom_call" | custom-call | flops 905969664 | bytes 7077888 | tf_op jit(solution)/shard_map/attention_back/pallas_call | solution.py:153
  197.4 7.6 %attention_back.3 = (bf16[3,512,384]{2,1,0:T(8,128)(2,1)}, f32[3,768,384]{2,1,0:T(8,128)S(1)}, f32[3,384]{1,0:T(4,128)S(1)}) custom-call(bf16[3,512,384]{2,1,0:T(8,128)(2,1)} %get-tuple-element.175.qkv_ref, bf16[512,384]{1,0:T(8,128)(2,1)} %copy-done.22, bf16[768,512]{1,0:T(8,128)(2,1)} %get-tuple-element.205.rows_ref), custom_call_target="tpu_custom_call" | custom-call | flops 905969664 | bytes 7077888 | tf_op jit(solution)/shard_map/attention_back/pallas_call | solution.py:153
  215.3 7.0 %start_back.1 = (f32[512,768]{1,0:T(8,128)}, f32[768,128]{1,0:T(8,128)S(1)}, bf16[768,128]{1,0:T(8,128)(2,1)S(1)}) custom-call(s32[6]{0:T(128)S(1)} %pad_add_fusion.place_ref, bf16[3,512,384]{2,1,0:T(8,128)(2,1)S(1)} %copy-done.21, bf16[3,512,384]{2,1,0:T(8,128)(2,1)S(1)} %copy-done.20, bf16[768,2048]{1,0:T(8,128)(2,1)S(1)} %bitcast.187, ...), custom_call_target="tpu_custom_call" | custom-call | bytes 1024 | tf_op jit(solution)/shard_map/start_back/pallas_call | solution.py:599
  232.2 4.5 %collective-permute-done.35 = bf16[4,48,128]{2,1,0:T(8,128)(2,1)S(1)} collective-permute-done((bf16[4,48,128]{2,1,0:T(8,128)(2,1)S(1)}, bf16[4,48,128]{2,1,0:T(8,128)(2,1)S(1)}, u32[]{:S(2)}, u32[]{:S(2)}) %collective-permute-start.35) | collective-permute-done | bytes 49184 | tf_op jit(solution)/shard_map/ppermute | solution.py:746
  243.8 4.3 %fusion.32 = f32[512,768]{1,0:T(8,128)} fusion(bf16[512,1536]{1,0:T(8,128)(2,1)S(1)} %copy-done.31, bf16[1536,768]{1,0:T(8,128)(2,1)} %bitcast.48.weight_ref), kind=kOutput, calls=%fused_computation.157 | convolution fusion | flops 1207959552 | bytes 5505024 | tf_op jit(solution)/shard_map/dot_general | solution.py:24
  248.2 5.1 %add_add_fusion = f32[512,768]{1,0:T(8,128)} fusion(f32[512,768]{1,0:T(8,128)S(1)} %copy-done.11, f32[512,768]{1,0:T(8,128)} %fusion.32, bf16[512,1536]{1,0:T(8,128)(2,1)} %get-tuple-element.236, bf16[1536,768]{1,0:T(8,128)(2,1)} %collective-permute-done.19.weight_ref, f32[768]{0:T(1024)S(1)} %slice_reduce_fusion.9), kind=kOutput, calls=%fused_computation.12 | convolution fusion | flops 1209139200 | bytes 8653824 | tf_op jit(solution)/shard_map/dot_general | solution.py:24
  (277 shorter events, 112.1 us)
Async XLA Ops:
  7.5 17.1 %collective-permute-start.2 = (bf16[48,2048]{1,0:T(8,128)(2,1)S(1)}, bf16[48,2048]{1,0:T(8,128)(2,1)S(1)}, u32[]{:S(2)}, u32[]{:S(2)}) collective-permute-start(bf16[48,2048]{1,0:T(8,128)(2,1)S(1)} %bitcast.200), channel_id=1, source_target_pairs={{0,16},{4,20},{8,24},{12,28},{16,0},{20,4},{24,8},{28,12},{1,17},{... | collective-permute-start | bytes 589832 | tf_op jit(solution)/shard_map/ppermute | solution.py:749
  10.0 14.5 %collective-permute-start.3 = (bf16[48,2048]{1,0:T(8,128)(2,1)S(1)}, bf16[48,2048]{1,0:T(8,128)(2,1)S(1)}, u32[]{:S(2)}, u32[]{:S(2)}) collective-permute-start(bf16[48,2048]{1,0:T(8,128)(2,1)S(1)} %bitcast.201), channel_id=1, source_target_pairs={{0,24},{4,28},{8,16},{12,20},{16,8},{20,12},{24,0},{28,4},{1,25},{... | collective-permute-start | bytes 589832 | tf_op jit(solution)/shard_map/ppermute | solution.py:749
  10.1 16.3 %collective-permute-start.5 = (bf16[24,1536]{1,0:T(8,128)(2,1)S(1)}, bf16[24,1536]{1,0:T(8,128)(2,1)S(1)}, u32[]{:S(2)}, u32[]{:S(2)}) collective-permute-start(bf16[24,1536]{1,0:T(8,128)(2,1)S(1)} %dynamic-slice_bitcast_fusion.4), channel_id=1, source_target_pairs={{0,1},{1,0},{2,3},{3,2},{4,5},{5,4},{6,7},{7,6},{8,9},{9,8},{10,11... | collective-permute-start | bytes 221192 | tf_op jit(solution)/shard_map/ppermute | solution.py:740
  24.8 14.1 %collective-permute-start.4 = (bf16[4,48,2048]{2,1,0:T(8,128)(2,1)S(1)}, bf16[4,48,2048]{2,1,0:T(8,128)(2,1)S(1)}, u32[]{:S(2)}, u32[]{:S(2)}) collective-permute-start(bf16[4,48,2048]{2,1,0:T(8,128)(2,1)S(1)} %pad_maximum_fusion.6), channel_id=1, source_target_pairs={{0,2},{1,5},{2,0},{3,7},{4,6},{5,1},{6,4},{7,3},{8,10},{9,13},{10,... | collective-permute-start | bytes 2359304 | tf_op jit(solution)/shard_map/ppermute | solution.py:743
  39.7 20.5 %collective-permute-start.8 = (bf16[4,2,48,2048]{3,2,1,0:T(8,128)(2,1)S(1)}, bf16[4,2,48,2048]{3,2,1,0:T(8,128)(2,1)S(1)}, u32[]{:S(2)}, u32[]{:S(2)}) collective-permute-start(bf16[4,2,48,2048]{3,2,1,0:T(8,128)(2,1)S(1)} %pad_maximum_fusion.3), channel_id=1, source_target_pairs={{0,4},{1,3},{2,6},{3,1},{4,0},{5,7},{6,2},{7,5},{8,12},{9,11},{10,... | collective-permute-start | bytes 4718600 | tf_op jit(solution)/shard_map/ppermute | solution.py:746
  74.8 16.6 %collective-permute-start.12 = (bf16[4,2,48,1536]{3,2,1,0:T(8,128)(2,1)S(1)}, bf16[4,2,48,1536]{3,2,1,0:T(8,128)(2,1)S(1)}, u32[]{:S(2)}, u32[]{:S(2)}) collective-permute-start(bf16[4,2,48,1536]{3,2,1,0:T(8,128)(2,1)S(1)} %pad_maximum_fusion.4), channel_id=1, source_target_pairs={{0,4},{1,3},{2,6},{3,1},{4,0},{5,7},{6,2},{7,5},{8,12},{9,11},{10,... | collective-permute-start | bytes 3538952 | tf_op jit(solution)/shard_map/ppermute | solution.py:746
  77.9 13.5 %collective-permute-start.14 = (bf16[96,768]{1,0:T(8,128)(2,1)S(1)}, bf16[96,768]{1,0:T(8,128)(2,1)S(1)}, u32[]{:S(2)}, u32[]{:S(2)}) collective-permute-start(bf16[96,768]{1,0:T(8,128)(2,1)S(1)} %convert_element_type.155), channel_id=1, source_target_pairs={{0,16},{4,20},{8,24},{12,28},{16,0},{20,4},{24,8},{28,12},{1,17},{... | collective-permute-start | bytes 442376 | tf_op jit(solution)/shard_map/ppermute | solution.py:749
  78.9 12.5 %collective-permute-start.15 = (bf16[96,768]{1,0:T(8,128)(2,1)S(1)}, bf16[96,768]{1,0:T(8,128)(2,1)S(1)}, u32[]{:S(2)}, u32[]{:S(2)}) collective-permute-start(bf16[96,768]{1,0:T(8,128)(2,1)S(1)} %convert_element_type.155), channel_id=1, source_target_pairs={{0,24},{4,28},{8,16},{12,20},{16,8},{20,12},{24,0},{28,4},{1,25},{... | collective-permute-start | bytes 442376 | tf_op jit(solution)/shard_map/ppermute | solution.py:749
  93.4 24.9 %collective-permute-start.18 = (bf16[768,1536]{1,0:T(8,128)(2,1)S(1)}, bf16[768,1536]{1,0:T(8,128)(2,1)S(1)}, u32[]{:S(2)}, u32[]{:S(2)}) collective-permute-start(bf16[768,1536]{1,0:T(8,128)(2,1)S(1)} %bitcast.188), channel_id=1, source_target_pairs={{0,1},{1,0},{2,3},{3,2},{4,5},{5,4},{6,7},{7,6},{8,9},{9,8},{10,11... | collective-permute-start | bytes 7077896 | tf_op jit(solution)/shard_map/ppermute | solution.py:740
  101.7 16.3 %collective-permute-start.17 = (bf16[4,2,96,768]{3,2,0,1:T(8,128)(2,1)S(1)}, bf16[4,2,96,768]{3,2,0,1:T(8,128)(2,1)S(1)}, u32[]{:S(2)}, u32[]{:S(2)}) collective-permute-start(bf16[4,2,96,768]{3,2,0,1:T(8,128)(2,1)S(1)} %pad_maximum_fusion.5), channel_id=1, source_target_pairs={{0,4},{1,3},{2,6},{3,1},{4,0},{5,7},{6,2},{7,5},{8,12},{9,11},{10,... | collective-permute-start | bytes 3538952 | tf_op jit(solution)/shard_map/ppermute | solution.py:746
  136.1 16.5 %collective-permute-start.21 = (bf16[4,2,96,768]{3,2,1,0:T(8,128)(2,1)}, bf16[4,2,96,768]{3,2,1,0:T(8,128)(2,1)}, u32[]{:S(2)}, u32[]{:S(2)}) collective-permute-start(bf16[4,2,96,768]{3,2,1,0:T(8,128)(2,1)} %get-tuple-element.186), channel_id=1, source_target_pairs={{0,2},{1,5},{2,0},{3,7},{4,6},{5,1},{6,4},{7,3},{8,10},{9,13},{10,... | collective-permute-start | bytes 3538952 | tf_op jit(solution)/shard_map/ppermute | solution.py:743
  143.8 24.5 %collective-permute-start.22 = (bf16[768,1536]{1,0:T(8,128)(2,1)}, bf16[768,1536]{1,0:T(8,128)(2,1)S(1)}, u32[]{:S(2)}, u32[]{:S(2)}) collective-permute-start(bf16[768,1536]{1,0:T(8,128)(2,1)} %get-tuple-element.193), channel_id=1, source_target_pairs={{0,1},{1,0},{2,3},{3,2},{4,5},{5,4},{6,7},{7,6},{8,9},{9,8},{10,11... | collective-permute-start | bytes 7077896 | tf_op jit(solution)/shard_map/ppermute | solution.py:740
  171.6 19.7 %collective-permute-start.25 = (bf16[4,2,48,1920]{3,2,1,0:T(8,128)(2,1)}, bf16[4,2,48,1920]{3,2,1,0:T(8,128)(2,1)}, u32[]{:S(2)}, u32[]{:S(2)}) collective-permute-start(bf16[4,2,48,1920]{3,2,1,0:T(8,128)(2,1)} %get-tuple-element.201), channel_id=1, source_target_pairs={{0,2},{1,5},{2,0},{3,7},{4,6},{5,1},{6,4},{7,3},{8,10},{9,13},{10,... | collective-permute-start | bytes 4423688 | tf_op jit(solution)/shard_map/ppermute | solution.py:743
  174.3 12.4 %collective-permute-start.26 = (bf16[96,768]{1,0:T(8,128)(2,1)S(1)}, bf16[96,768]{1,0:T(8,128)(2,1)S(1)}, u32[]{:S(2)}, u32[]{:S(2)}) collective-permute-start(bf16[96,768]{1,0:T(8,128)(2,1)S(1)} %get-tuple-element.283), channel_id=1, source_target_pairs={{0,8},{4,12},{8,0},{12,4},{16,24},{20,28},{24,16},{28,20},{1,9},{5... | collective-permute-start | bytes 442376 | tf_op jit(solution)/shard_map/ppermute | solution.py:749
  176.4 14.0 %collective-permute-start.27 = (bf16[96,768]{1,0:T(8,128)(2,1)S(1)}, bf16[96,768]{1,0:T(8,128)(2,1)S(1)}, u32[]{:S(2)}, u32[]{:S(2)}) collective-permute-start(bf16[96,768]{1,0:T(8,128)(2,1)S(1)} %get-tuple-element.282), channel_id=1, source_target_pairs={{0,16},{4,20},{8,24},{12,28},{16,0},{20,4},{24,8},{28,12},{1,17},{... | collective-permute-start | bytes 442376 | tf_op jit(solution)/shard_map/ppermute | solution.py:749
  177.4 12.9 %collective-permute-start.28 = (bf16[96,768]{1,0:T(8,128)(2,1)S(1)}, bf16[96,768]{1,0:T(8,128)(2,1)S(1)}, u32[]{:S(2)}, u32[]{:S(2)}) collective-permute-start(bf16[96,768]{1,0:T(8,128)(2,1)S(1)} %get-tuple-element.281), channel_id=1, source_target_pairs={{0,24},{4,28},{8,16},{12,20},{16,8},{20,12},{24,0},{28,4},{1,25},{... | collective-permute-start | bytes 442376 | tf_op jit(solution)/shard_map/ppermute | solution.py:749
  186.6 18.4 %collective-permute-start.29 = (bf16[3,768,384]{2,1,0:T(8,128)(2,1)}, bf16[3,768,384]{2,1,0:T(8,128)(2,1)S(1)}, u32[]{:S(2)}, u32[]{:S(2)}) collective-permute-start(bf16[3,768,384]{2,1,0:T(8,128)(2,1)} %get-tuple-element.207), channel_id=1, source_target_pairs={{0,1},{1,0},{2,3},{3,2},{4,5},{5,4},{6,7},{7,6},{8,9},{9,8},{10,11... | collective-permute-start | bytes 5308424 | tf_op jit(solution)/shard_map/ppermute | solution.py:740
  195.7 13.3 %collective-permute-start.32 = (bf16[4,48,1920]{2,1,0:T(8,128)(2,1)}, bf16[4,48,1920]{2,1,0:T(8,128)(2,1)}, u32[]{:S(2)}, u32[]{:S(2)}) collective-permute-start(bf16[4,48,1920]{2,1,0:T(8,128)(2,1)} %fusion), channel_id=1, source_target_pairs={{0,4},{1,3},{2,6},{3,1},{4,0},{5,7},{6,2},{7,5},{8,12},{9,11},{10,... | collective-permute-start | bytes 2211848 | tf_op jit(solution)/shard_map/ppermute | solution.py:746
  207.7 18.9 %collective-permute-start.30 = (bf16[4,2,48,1152]{3,2,1,0:T(8,128)(2,1)S(1)}, bf16[4,2,48,1152]{3,2,1,0:T(8,128)(2,1)S(1)}, u32[]{:S(2)}, u32[]{:S(2)}) collective-permute-start(bf16[4,2,48,1152]{3,2,1,0:T(8,128)(2,1)S(1)} %get-tuple-element.216), channel_id=1, source_target_pairs={{0,2},{1,5},{2,0},{3,7},{4,6},{5,1},{6,4},{7,3},{8,10},{9,13},{10,... | collective-permute-start | bytes 2654216 | tf_op jit(solution)/shard_map/ppermute | solution.py:743
  210.4 20.7 %collective-permute-start.40 = (bf16[48,1920]{1,0:T(8,128)(2,1)S(1)}, bf16[48,1920]{1,0:T(8,128)(2,1)S(1)}, u32[]{:S(2)}, u32[]{:S(2)}) collective-permute-start(bf16[48,1920]{1,0:T(8,128)(2,1)S(1)} %get-tuple-element.280), channel_id=1, source_target_pairs={{0,8},{4,12},{8,0},{12,4},{16,24},{20,28},{24,16},{28,20},{1,9},{5... | collective-permute-start | bytes 552968 | tf_op jit(solution)/shard_map/ppermute | solution.py:749
  212.8 18.4 %collective-permute-start.41 = (bf16[48,1920]{1,0:T(8,128)(2,1)S(1)}, bf16[48,1920]{1,0:T(8,128)(2,1)S(1)}, u32[]{:S(2)}, u32[]{:S(2)}) collective-permute-start(bf16[48,1920]{1,0:T(8,128)(2,1)S(1)} %get-tuple-element.279), channel_id=1, source_target_pairs={{0,16},{4,20},{8,24},{12,28},{16,0},{20,4},{24,8},{28,12},{1,17},{... | collective-permute-start | bytes 552968 | tf_op jit(solution)/shard_map/ppermute | solution.py:749
  213.8 17.3 %collective-permute-start.42 = (bf16[48,1920]{1,0:T(8,128)(2,1)S(1)}, bf16[48,1920]{1,0:T(8,128)(2,1)S(1)}, u32[]{:S(2)}, u32[]{:S(2)}) collective-permute-start(bf16[48,1920]{1,0:T(8,128)(2,1)S(1)} %get-tuple-element.278), channel_id=1, source_target_pairs={{0,24},{4,28},{8,16},{12,20},{16,8},{20,12},{24,0},{28,4},{1,25},{... | collective-permute-start | bytes 552968 | tf_op jit(solution)/shard_map/ppermute | solution.py:749
  239.3 14.1 %collective-permute-start.36 = (bf16[48,1280]{1,0:T(8,128)(2,1)S(1)}, bf16[48,1280]{1,0:T(8,128)(2,1)S(1)}, u32[]{:S(2)}, u32[]{:S(2)}) collective-permute-start(bf16[48,1280]{1,0:T(8,128)(2,1)S(1)} %get-tuple-element.293), channel_id=1, source_target_pairs={{0,8},{4,12},{8,0},{12,4},{16,24},{20,28},{24,16},{28,20},{1,9},{5... | collective-permute-start | bytes 368648 | tf_op jit(solution)/shard_map/ppermute | solution.py:749
  240.4 13.0 %collective-permute-start.37 = (bf16[48,1280]{1,0:T(8,128)(2,1)S(1)}, bf16[48,1280]{1,0:T(8,128)(2,1)S(1)}, u32[]{:S(2)}, u32[]{:S(2)}) collective-permute-start(bf16[48,1280]{1,0:T(8,128)(2,1)S(1)} %get-tuple-element.294), channel_id=1, source_target_pairs={{0,16},{4,20},{8,24},{12,28},{16,0},{20,4},{24,8},{28,12},{1,17},{... | collective-permute-start | bytes 368648 | tf_op jit(solution)/shard_map/ppermute | solution.py:749
  (72 other events, 502.4 us)

commit v8 on v6

--- a/solution.py
+++ b/solution.py
@@ -977,7 +977,7 @@
     hidden, slope = [None, None], [None, None]
     hidden[0], slope[0] = feed(normed_two, up_w[0], bias_up, 0)
     down_w = down_w.halves(hidden[0])
-    hidden[1], slope[1] = feed(after(normed_two, down_two), up_w[1], bias_up, 1)
+    hidden[1], slope[1] = feed(normed_two, up_w[1], bias_up, 1)
 
     grad_branch = (cotangent * absorbed).astype(BF)
     down_sum = reduction(hidden_part)

time: 259 us -> 259 us (level)
    ppermute x18, waiting for transfers between devices: 37.4 us -> 30.8 us  [to_z(): return lax.ppermute(value, 'fsdp', [(i, i ^ 2 * step) for i in range(8)])]
    ppermute x7, waiting for transfers between devices: 14.9 us -> 21.5 us  [to_far(): lax.ppermute(value, AXES, [(i, i ^ (2 if i % 2 else 4)) for i in range(32)])]
  transfers between devices with their start and end apart: 44 -> 44, of which waited for: 20 -> 21; matrix products, arithmetic and copies ran while one was open for 12% -> 12% of each run, Pallas kernels for 29% -> 29%
where the time goes in v8:
time: 259 us; the launch traced here: 258 us
  Pallas kernels  84.8 us (33%)
  waiting for transfers between devices  73.3 us (28%)
  starting transfers between devices  51.4 us (20%)
  matrix products  17.6 us (7%)
  local copies, waits for them, and re-layouts  14.9 us (6%)
  other arithmetic  14.8 us (6%)
    ppermute x18, starting transfers between devices, to_z(): return lax.ppermute(value, 'fsdp', [(i, i ^ 2 * step) for i in range(8)])  33.7 us
    ppermute x18, waiting for transfers between devices, to_z(): return lax.ppermute(value, 'fsdp', [(i, i ^ 2 * step) for i in range(8)])  30.8 us
    ppermute x7, waiting for transfers between devices, to_far(): lax.ppermute(value, AXES, [(i, i ^ (2 if i % 2 else 4)) for i in range(32)])  21.5 us
    dot_general x4, matrix products, contract(): return lax.dot_general(left, right, dims, preferred_element_type=F32)  16.6 us
    pallas_call x2, Pallas kernels, attention_back(): pl.pallas_call(functools.partial(attention_back_kernel, length, 1.0 / mat...  15.4 us
    ppermute x7, waiting for transfers between devices, to_near(): lax.ppermute(value, AXES, [(i, i ^ (4 if i % 2 else 2)) for i in range(32)])  14.1 us
    pallas_call x2, Pallas kernels, feed_back(): pl.pallas_call(feed_back_kernel, grid=(columns // block,), in_specs=[pl.B...  12.4 us
    pallas_call x4, Pallas kernels, routed(): pl.pallas_call(functools.partial(route_kernel, rows), grid=(4,), in_specs...  10.7 us
  transfers between devices with their start and end apart: 44, of which 21 were waited for; matrix products, arithmetic and copies ran while one was open for 12% of the time, Pallas kernels for 29%

profile of v8, /device:TPU:0, one launch (start us, length us, event | category | flops | bytes accessed | tf_op | source)
XLA Modules:
  0.0 258.5 jit_solution(17336194194134974473)
XLA Ops:
  10.2 6.5 %collective-permute-done.1 = bf16[48,2048]{1,0:T(8,128)(2,1)S(1)} collective-permute-done((bf16[48,2048]{1,0:T(8,128)(2,1)S(1)}, bf16[48,2048]{1,0:T(8,128)(2,1)S(1)}, u32[]{:S(2)}, u32[]{:S(2)}) %collective-permute-start.1) | collective-permute-done | bytes 196640 | tf_op jit(solution)/shard_map/ppermute | solution.py:749
  16.7 7.8 %collective-permute-done.2 = bf16[48,2048]{1,0:T(8,128)(2,1)S(1)} collective-permute-done((bf16[48,2048]{1,0:T(8,128)(2,1)S(1)}, bf16[48,2048]{1,0:T(8,128)(2,1)S(1)}, u32[]{:S(2)}, u32[]{:S(2)}) %collective-permute-start.2) | collective-permute-done | bytes 196640 | tf_op jit(solution)/shard_map/ppermute | solution.py:749
  26.4 4.1 %collective-permute-start.6 = (bf16[48,1536]{1,0:T(8,128)(2,1)S(1)}, bf16[48,1536]{1,0:T(8,128)(2,1)S(1)}, u32[]{:S(2)}, u32[]{:S(2)}) collective-permute-start(bf16[48,1536]{1,0:T(8,128)(2,1)S(1)} %bitcast.203), channel_id=1, source_target_pairs={{0,8},{4,12},{8,0},{12,4},{16,24},{20,28},{24,16},{28,20},{1,9},{5... | collective-permute-start | bytes 442376 | tf_op jit(solution)/shard_map/ppermute | solution.py:749
  34.4 4.5 %collective-permute-done.7 = bf16[48,1536]{1,0:T(8,128)(2,1)S(1)} collective-permute-done((bf16[48,1536]{1,0:T(8,128)(2,1)S(1)}, bf16[48,1536]{1,0:T(8,128)(2,1)S(1)}, u32[]{:S(2)}, u32[]{:S(2)}) %collective-permute-start.7) | collective-permute-done | bytes 147488 | tf_op jit(solution)/shard_map/ppermute | solution.py:749
  43.7 6.3 %collective-permute-done.9 = bf16[48,1536]{1,0:T(8,128)(2,1)S(1)} collective-permute-done((bf16[48,1536]{1,0:T(8,128)(2,1)S(1)}, bf16[48,1536]{1,0:T(8,128)(2,1)S(1)}, u32[]{:S(2)}, u32[]{:S(2)}) %collective-permute-start.9) | collective-permute-done | bytes 147488 | tf_op jit(solution)/shard_map/ppermute | solution.py:749
  50.0 10.2 %collective-permute-done.8 = bf16[4,2,48,2048]{3,2,1,0:T(8,128)(2,1)S(1)} collective-permute-done((bf16[4,2,48,2048]{3,2,1,0:T(8,128)(2,1)S(1)}, bf16[4,2,48,2048]{3,2,1,0:T(8,128)(2,1)S(1)}, u32[]{:S(2)}, u32[]{:S(2)}) %collective-permute-start.8) | collective-permute-done | bytes 1572896 | tf_op jit(solution)/shard_map/ppermute | solution.py:746
  67.2 5.5 %start_rows.1 = (f32[24,768]{1,0:T(8,128)S(1)}, f32[512,768]{1,0:T(8,128)}, bf16[512,768]{1,0:T(8,128)(2,1)S(1)}, bf16[768,512]{1,0:T(8,128)(2,1)}, f32[8,384]{1...) custom-call(s32[6]{0:T(128)S(1)} %pad_add_fusion.place_ref, f32[512,768]{1,0:T(8,128)} %tokens_ref.1, ...), custom_call_target="tpu_custom_call" | custom-call | flops 37748736 | bytes 5505024 | tf_op jit(solution)/shard_map/start_rows/pallas_call | solution.py:340
  80.3 4.1 %attention.2 = (bf16[3,512,384]{2,1,0:T(8,128)(2,1)}, bf16[512,384]{1,0:T(8,128)(2,1)S(1)}) custom-call(bf16[512,768]{1,0:T(8,128)(2,1)S(1)} %get-tuple-element.153.rows_ref, bf16[768,2048]{1,0:T(8,128)(2,1)S(1)} %bitcast.182, bf16[768,2048]{1,0:T(8,128)(2,1)S(1)} %bitcast.183, bf16[768,2048]{1,0:T(8,128)(2,1)S(1)} %bitcast.184, ...), custom_call_target="tpu_custom_call" | custom-call | flops 905969664 | bytes 4128768 | tf_op jit(solution)/shard_map/attention/pallas_call | solution.py:98
  84.4 6.6 %collective-permute-done.12 = bf16[4,2,48,1536]{3,2,1,0:T(8,128)(2,1)S(1)} collective-permute-done((bf16[4,2,48,1536]{3,2,1,0:T(8,128)(2,1)S(1)}, bf16[4,2,48,1536]{3,2,1,0:T(8,128)(2,1)S(1)}, u32[]{:S(2)}, u32[]{:S(2)}) %collective-permute-start.12) | collective-permute-done | bytes 1179680 | tf_op jit(solution)/shard_map/ppermute | solution.py:746
  93.5 8.0 %collective-permute-done.16 = bf16[4,96,768]{2,1,0:T(8,128)(2,1)S(1)} collective-permute-done((bf16[4,96,768]{2,1,0:T(8,128)(2,1)S(1)}, bf16[4,96,768]{2,1,0:T(8,128)(2,1)S(1)}, u32[]{:S(2)}, u32[]{:S(2)}) %collective-permute-start.16) | collective-permute-done | bytes 589856 | tf_op jit(solution)/shard_map/ppermute | solution.py:743
  103.3 5.1 %attention.3 = (bf16[3,512,384]{2,1,0:T(8,128)(2,1)}, bf16[512,384]{1,0:T(8,128)(2,1)S(1)}) custom-call(bf16[512,768]{1,0:T(8,128)(2,1)S(1)} %get-tuple-element.153.rows_ref, bf16[768,2048]{1,0:T(8,128)(2,1)} %collective-permute-done.10.table_other_ref.query_ref.key_ref.value_ref.out_other_ref.weight_other_ref, ...), custom_call_target="tpu_custom_call" | custom-call | flops 905969664 | bytes 4128768 | tf_op jit(solution)/shard_map/attention/pallas_call | solution.py:98
  108.4 4.1 %middle_rows.1 = (f32[512,768]{1,0:T(8,128)}, bf16[512,768]{1,0:T(8,128)(2,1)S(1)}, bf16[768,512]{1,0:T(8,128)(2,1)}) custom-call(s32[6]{0:T(128)S(1)} %pad_add_fusion.place_ref, bf16[512,384]{1,0:T(8,128)(2,1)S(1)} %get-tuple-element.150.context_mine_ref, bf16[512,384]{1,0:T(8,128)(2,1)S(1)} %get-tuple-element.155.context_other_ref, ...), custom_call_target="tpu_custom_call" | custom-call | flops 603979776 | bytes 6684672 | tf_op jit(solution)/shard_map/middle_rows/pallas_call | solution.py:404
  112.5 5.3 %feed.2 = (bf16[512,1536]{1,0:T(8,128)(2,1)}, f32[512,1536]{1,0:T(8,128)}) custom-call(bf16[512,768]{1,0:T(8,128)(2,1)S(1)} %get-tuple-element.165.rows_ref, bf16[768,1536]{1,0:T(8,128)(2,1)S(1)} %bitcast.189, f32[8,1536]{1,0:T(8,128)S(1)} %get-tuple-element.168.bias_ref), custom_call_target="tpu_custom_call" | custom-call | flops 1207959552 | bytes 7864320 | tf_op jit(solution)/shard_map/feed/pallas_call | solution.py:204
  118.3 5.3 %feed.3 = (bf16[512,1536]{1,0:T(8,128)(2,1)}, f32[512,1536]{1,0:T(8,128)}) custom-call(bf16[512,768]{1,0:T(8,128)(2,1)S(1)} %get-tuple-element.165.rows_ref, bf16[768,1536]{1,0:T(8,128)(2,1)S(1)} %collective-permute-done.17.weight_ref.up_other_ref, f32[8,1536]{1,0:T(8,128)S(1)} %get-tuple-element.168.bias_ref), custom_call_target="tpu_custom_call" | custom-call | flops 1207959552 | bytes 7864320 | tf_op jit(solution)/shard_map/feed/pallas_call | solution.py:204
  123.6 4.3 %convolution_convert_fusion = bf16[1536,768]{1,0:T(8,128)(2,1)} fusion(bf16[512,1536]{1,0:T(8,128)(2,1)} %get-tuple-element.234, bf16[512,768]{1,0:T(8,128)(2,1)S(1)} %multiply_convert_fusion.grad_ref), kind=kOutput, calls=%fused_computation | convolution fusion | flops 1209139200 | bytes 4718592 | tf_op jit(solution)/shard_map/dot_general | solution.py:24
  137.3 6.5 %feed_back.3 = (bf16[512,1536]{1,0:T(8,128)(2,1)}, f32[1,1536]{1,0:T(1,128)S(1)}, bf16[768,1536]{1,0:T(8,128)(2,1)}) custom-call(bf16[512,768]{1,0:T(8,128)(2,1)} %copy-done.27, bf16[1536,768]{1,0:T(8,128)(2,1)} %collective-permute-done.19.weight_ref, f32[512,1536]{1,0:T(8,128)} %get-tuple-element.179.slope_ref, bf16[768,512]{1,0:T(8,128)(2,1)} %get-tuple-element.177.rows_ref), custom_call_target="tpu_custom_call" | custom-call | flops 2415919104 | bytes 13369344 | tf_op jit(solution)/shard_map/feed_back/pallas_call | solution.py:240
  143.8 5.9 %feed_back.2 = (bf16[512,1536]{1,0:T(8,128)(2,1)}, f32[1,1536]{1,0:T(1,128)S(1)}, f32[768,1536]{1,0:T(8,128)S(1)}) custom-call(bf16[512,768]{1,0:T(8,128)(2,1)} %copy-done.27, bf16[1536,768]{1,0:T(8,128)(2,1)} %bitcast.48.weight_ref, f32[512,1536]{1,0:T(8,128)} %get-tuple-element.176.slope_ref, bf16[768,512]{1,0:T(8,128)(2,1)} %get-tuple-element.177.rows_ref), custom_call_target="tpu_custom_call" | custom-call | flops 2415919104 | bytes 13369344 | tf_op jit(solution)/shard_map/feed_back/pallas_call | solution.py:240
  158.2 8.0 %middle_back.1 = (f32[512,768]{1,0:T(8,128)S(1)}, bf16[512,384]{1,0:T(8,128)(2,1)S(1)}, bf16[512,384]{1,0:T(8,128)(2,1)S(1)}, f32[768,384]{1,0:T(8,128)S(1)}, bf...) custom-call(s32[6]{0:T(128)S(1)} %pad_add_fusion.place_ref, bf16[512,1536]{1,0:T(8,128)(2,1)S(1)} %copy-done.15, ...), custom_call_target="tpu_custom_call" | custom-call | flops 3623878656 | bytes 14155776 | tf_op jit(solution)/shard_map/middle_back/pallas_call | solution.py:495
  178.8 7.8 %attention_back.2 = (bf16[3,512,384]{2,1,0:T(8,128)(2,1)}, bf16[3,768,384]{2,1,0:T(8,128)(2,1)}, f32[3,384]{1,0:T(4,128)S(1)}) custom-call(bf16[3,512,384]{2,1,0:T(8,128)(2,1)} %get-tuple-element.200.qkv_ref, bf16[512,384]{1,0:T(8,128)(2,1)} %copy-done.23, bf16[768,512]{1,0:T(8,128)(2,1)} %get-tuple-element.203.rows_ref), custom_call_target="tpu_custom_call" | custom-call | flops 905969664 | bytes 7077888 | tf_op jit(solution)/shard_map/attention_back/pallas_call | solution.py:153
  197.4 7.6 %attention_back.3 = (bf16[3,512,384]{2,1,0:T(8,128)(2,1)}, f32[3,768,384]{2,1,0:T(8,128)S(1)}, f32[3,384]{1,0:T(4,128)S(1)}) custom-call(bf16[3,512,384]{2,1,0:T(8,128)(2,1)} %get-tuple-element.171.qkv_ref, bf16[512,384]{1,0:T(8,128)(2,1)} %copy-done.22, bf16[768,512]{1,0:T(8,128)(2,1)} %get-tuple-element.203.rows_ref), custom_call_target="tpu_custom_call" | custom-call | flops 905969664 | bytes 7077888 | tf_op jit(solution)/shard_map/attention_back/pallas_call | solution.py:153
  215.3 7.0 %start_back.1 = (f32[512,768]{1,0:T(8,128)}, f32[768,128]{1,0:T(8,128)S(1)}, bf16[768,128]{1,0:T(8,128)(2,1)S(1)}) custom-call(s32[6]{0:T(128)S(1)} %pad_add_fusion.place_ref, bf16[3,512,384]{2,1,0:T(8,128)(2,1)S(1)} %copy-done.21, bf16[3,512,384]{2,1,0:T(8,128)(2,1)S(1)} %copy-done.20, bf16[768,2048]{1,0:T(8,128)(2,1)S(1)} %bitcast.187, ...), custom_call_target="tpu_custom_call" | custom-call | bytes 1024 | tf_op jit(solution)/shard_map/start_back/pallas_call | solution.py:599
  232.1 4.5 %collective-permute-done.38 = bf16[4,48,128]{2,1,0:T(8,128)(2,1)S(1)} collective-permute-done((bf16[4,48,128]{2,1,0:T(8,128)(2,1)S(1)}, bf16[4,48,128]{2,1,0:T(8,128)(2,1)S(1)}, u32[]{:S(2)}, u32[]{:S(2)}) %collective-permute-start.38) | collective-permute-done | bytes 49184 | tf_op jit(solution)/shard_map/ppermute | solution.py:746
  243.8 4.3 %fusion.32 = f32[512,768]{1,0:T(8,128)} fusion(bf16[512,1536]{1,0:T(8,128)(2,1)S(1)} %copy-done.31, bf16[1536,768]{1,0:T(8,128)(2,1)} %bitcast.48.weight_ref), kind=kOutput, calls=%fused_computation.157 | convolution fusion | flops 1207959552 | bytes 5505024 | tf_op jit(solution)/shard_map/dot_general | solution.py:24
  248.2 5.1 %add_add_fusion = f32[512,768]{1,0:T(8,128)} fusion(f32[512,768]{1,0:T(8,128)S(1)} %copy-done.11, f32[512,768]{1,0:T(8,128)} %fusion.32, bf16[512,1536]{1,0:T(8,128)(2,1)} %get-tuple-element.234, bf16[1536,768]{1,0:T(8,128)(2,1)} %collective-permute-done.19.weight_ref, f32[768]{0:T(1024)S(1)} %slice_reduce_fusion.9), kind=kOutput, calls=%fused_computation.12 | convolution fusion | flops 1209139200 | bytes 8653824 | tf_op jit(solution)/shard_map/dot_general | solution.py:24
  (277 shorter events, 112.4 us)
Async XLA Ops:
  7.5 17.1 %collective-permute-start.2 = (bf16[48,2048]{1,0:T(8,128)(2,1)S(1)}, bf16[48,2048]{1,0:T(8,128)(2,1)S(1)}, u32[]{:S(2)}, u32[]{:S(2)}) collective-permute-start(bf16[48,2048]{1,0:T(8,128)(2,1)S(1)} %bitcast.200), channel_id=1, source_target_pairs={{0,16},{4,20},{8,24},{12,28},{16,0},{20,4},{24,8},{28,12},{1,17},{... | collective-permute-start | bytes 589832 | tf_op jit(solution)/shard_map/ppermute | solution.py:749
  10.0 14.5 %collective-permute-start.3 = (bf16[48,2048]{1,0:T(8,128)(2,1)S(1)}, bf16[48,2048]{1,0:T(8,128)(2,1)S(1)}, u32[]{:S(2)}, u32[]{:S(2)}) collective-permute-start(bf16[48,2048]{1,0:T(8,128)(2,1)S(1)} %bitcast.201), channel_id=1, source_target_pairs={{0,24},{4,28},{8,16},{12,20},{16,8},{20,12},{24,0},{28,4},{1,25},{... | collective-permute-start | bytes 589832 | tf_op jit(solution)/shard_map/ppermute | solution.py:749
  10.1 16.3 %collective-permute-start.5 = (bf16[24,1536]{1,0:T(8,128)(2,1)S(1)}, bf16[24,1536]{1,0:T(8,128)(2,1)S(1)}, u32[]{:S(2)}, u32[]{:S(2)}) collective-permute-start(bf16[24,1536]{1,0:T(8,128)(2,1)S(1)} %dynamic-slice_bitcast_fusion.4), channel_id=1, source_target_pairs={{0,1},{1,0},{2,3},{3,2},{4,5},{5,4},{6,7},{7,6},{8,9},{9,8},{10,11... | collective-permute-start | bytes 221192 | tf_op jit(solution)/shard_map/ppermute | solution.py:740
  24.8 14.1 %collective-permute-start.4 = (bf16[4,48,2048]{2,1,0:T(8,128)(2,1)S(1)}, bf16[4,48,2048]{2,1,0:T(8,128)(2,1)S(1)}, u32[]{:S(2)}, u32[]{:S(2)}) collective-permute-start(bf16[4,48,2048]{2,1,0:T(8,128)(2,1)S(1)} %pad_maximum_fusion.6), channel_id=1, source_target_pairs={{0,2},{1,5},{2,0},{3,7},{4,6},{5,1},{6,4},{7,3},{8,10},{9,13},{10,... | collective-permute-start | bytes 2359304 | tf_op jit(solution)/shard_map/ppermute | solution.py:743
  39.7 20.5 %collective-permute-start.8 = (bf16[4,2,48,2048]{3,2,1,0:T(8,128)(2,1)S(1)}, bf16[4,2,48,2048]{3,2,1,0:T(8,128)(2,1)S(1)}, u32[]{:S(2)}, u32[]{:S(2)}) collective-permute-start(bf16[4,2,48,2048]{3,2,1,0:T(8,128)(2,1)S(1)} %pad_maximum_fusion.3), channel_id=1, source_target_pairs={{0,4},{1,3},{2,6},{3,1},{4,0},{5,7},{6,2},{7,5},{8,12},{9,11},{10,... | collective-permute-start | bytes 4718600 | tf_op jit(solution)/shard_map/ppermute | solution.py:746
  74.8 16.3 %collective-permute-start.12 = (bf16[4,2,48,1536]{3,2,1,0:T(8,128)(2,1)S(1)}, bf16[4,2,48,1536]{3,2,1,0:T(8,128)(2,1)S(1)}, u32[]{:S(2)}, u32[]{:S(2)}) collective-permute-start(bf16[4,2,48,1536]{3,2,1,0:T(8,128)(2,1)S(1)} %pad_maximum_fusion.4), channel_id=1, source_target_pairs={{0,4},{1,3},{2,6},{3,1},{4,0},{5,7},{6,2},{7,5},{8,12},{9,11},{10,... | collective-permute-start | bytes 3538952 | tf_op jit(solution)/shard_map/ppermute | solution.py:746
  75.6 15.4 %collective-permute-start.13 = (bf16[96,768]{1,0:T(8,128)(2,1)S(1)}, bf16[96,768]{1,0:T(8,128)(2,1)S(1)}, u32[]{:S(2)}, u32[]{:S(2)}) collective-permute-start(bf16[96,768]{1,0:T(8,128)(2,1)S(1)} %convert_element_type.155), channel_id=1, source_target_pairs={{0,8},{4,12},{8,0},{12,4},{16,24},{20,28},{24,16},{28,20},{1,9},{5... | collective-permute-start | bytes 442376 | tf_op jit(solution)/shard_map/ppermute | solution.py:749
  77.9 13.5 %collective-permute-start.14 = (bf16[96,768]{1,0:T(8,128)(2,1)S(1)}, bf16[96,768]{1,0:T(8,128)(2,1)S(1)}, u32[]{:S(2)}, u32[]{:S(2)}) collective-permute-start(bf16[96,768]{1,0:T(8,128)(2,1)S(1)} %convert_element_type.155), channel_id=1, source_target_pairs={{0,16},{4,20},{8,24},{12,28},{16,0},{20,4},{24,8},{28,12},{1,17},{... | collective-permute-start | bytes 442376 | tf_op jit(solution)/shard_map/ppermute | solution.py:749
  78.9 12.5 %collective-permute-start.15 = (bf16[96,768]{1,0:T(8,128)(2,1)S(1)}, bf16[96,768]{1,0:T(8,128)(2,1)S(1)}, u32[]{:S(2)}, u32[]{:S(2)}) collective-permute-start(bf16[96,768]{1,0:T(8,128)(2,1)S(1)} %convert_element_type.155), channel_id=1, source_target_pairs={{0,24},{4,28},{8,16},{12,20},{16,8},{20,12},{24,0},{28,4},{1,25},{... | collective-permute-start | bytes 442376 | tf_op jit(solution)/shard_map/ppermute | solution.py:749
  93.4 24.9 %collective-permute-start.17 = (bf16[768,1536]{1,0:T(8,128)(2,1)S(1)}, bf16[768,1536]{1,0:T(8,128)(2,1)S(1)}, u32[]{:S(2)}, u32[]{:S(2)}) collective-permute-start(bf16[768,1536]{1,0:T(8,128)(2,1)S(1)} %bitcast.188), channel_id=1, source_target_pairs={{0,1},{1,0},{2,3},{3,2},{4,5},{5,4},{6,7},{7,6},{8,9},{9,8},{10,11... | collective-permute-start | bytes 7077896 | tf_op jit(solution)/shard_map/ppermute | solution.py:740
  101.7 16.3 %collective-permute-start.18 = (bf16[4,2,96,768]{3,2,0,1:T(8,128)(2,1)S(1)}, bf16[4,2,96,768]{3,2,0,1:T(8,128)(2,1)S(1)}, u32[]{:S(2)}, u32[]{:S(2)}) collective-permute-start(bf16[4,2,96,768]{3,2,0,1:T(8,128)(2,1)S(1)} %pad_maximum_fusion.5), channel_id=1, source_target_pairs={{0,4},{1,3},{2,6},{3,1},{4,0},{5,7},{6,2},{7,5},{8,12},{9,11},{10,... | collective-permute-start | bytes 3538952 | tf_op jit(solution)/shard_map/ppermute | solution.py:746
  136.1 16.5 %collective-permute-start.21 = (bf16[4,2,96,768]{3,2,1,0:T(8,128)(2,1)}, bf16[4,2,96,768]{3,2,1,0:T(8,128)(2,1)}, u32[]{:S(2)}, u32[]{:S(2)}) collective-permute-start(bf16[4,2,96,768]{3,2,1,0:T(8,128)(2,1)} %get-tuple-element.184), channel_id=1, source_target_pairs={{0,2},{1,5},{2,0},{3,7},{4,6},{5,1},{6,4},{7,3},{8,10},{9,13},{10,... | collective-permute-start | bytes 3538952 | tf_op jit(solution)/shard_map/ppermute | solution.py:743
  143.8 24.5 %collective-permute-start.22 = (bf16[768,1536]{1,0:T(8,128)(2,1)}, bf16[768,1536]{1,0:T(8,128)(2,1)S(1)}, u32[]{:S(2)}, u32[]{:S(2)}) collective-permute-start(bf16[768,1536]{1,0:T(8,128)(2,1)} %get-tuple-element.191), channel_id=1, source_target_pairs={{0,1},{1,0},{2,3},{3,2},{4,5},{5,4},{6,7},{7,6},{8,9},{9,8},{10,11... | collective-permute-start | bytes 7077896 | tf_op jit(solution)/shard_map/ppermute | solution.py:740
  171.6 19.7 %collective-permute-start.25 = (bf16[4,2,48,1920]{3,2,1,0:T(8,128)(2,1)}, bf16[4,2,48,1920]{3,2,1,0:T(8,128)(2,1)}, u32[]{:S(2)}, u32[]{:S(2)}) collective-permute-start(bf16[4,2,48,1920]{3,2,1,0:T(8,128)(2,1)} %get-tuple-element.199), channel_id=1, source_target_pairs={{0,2},{1,5},{2,0},{3,7},{4,6},{5,1},{6,4},{7,3},{8,10},{9,13},{10,... | collective-permute-start | bytes 4423688 | tf_op jit(solution)/shard_map/ppermute | solution.py:743
  176.4 14.0 %collective-permute-start.27 = (bf16[96,768]{1,0:T(8,128)(2,1)S(1)}, bf16[96,768]{1,0:T(8,128)(2,1)S(1)}, u32[]{:S(2)}, u32[]{:S(2)}) collective-permute-start(bf16[96,768]{1,0:T(8,128)(2,1)S(1)} %get-tuple-element.280), channel_id=1, source_target_pairs={{0,16},{4,20},{8,24},{12,28},{16,0},{20,4},{24,8},{28,12},{1,17},{... | collective-permute-start | bytes 442376 | tf_op jit(solution)/shard_map/ppermute | solution.py:749
  177.4 12.9 %collective-permute-start.28 = (bf16[96,768]{1,0:T(8,128)(2,1)S(1)}, bf16[96,768]{1,0:T(8,128)(2,1)S(1)}, u32[]{:S(2)}, u32[]{:S(2)}) collective-permute-start(bf16[96,768]{1,0:T(8,128)(2,1)S(1)} %get-tuple-element.279), channel_id=1, source_target_pairs={{0,24},{4,28},{8,16},{12,20},{16,8},{20,12},{24,0},{28,4},{1,25},{... | collective-permute-start | bytes 442376 | tf_op jit(solution)/shard_map/ppermute | solution.py:749
  186.6 18.4 %collective-permute-start.29 = (bf16[3,768,384]{2,1,0:T(8,128)(2,1)}, bf16[3,768,384]{2,1,0:T(8,128)(2,1)S(1)}, u32[]{:S(2)}, u32[]{:S(2)}) collective-permute-start(bf16[3,768,384]{2,1,0:T(8,128)(2,1)} %get-tuple-element.205), channel_id=1, source_target_pairs={{0,1},{1,0},{2,3},{3,2},{4,5},{5,4},{6,7},{7,6},{8,9},{9,8},{10,11... | collective-permute-start | bytes 5308424 | tf_op jit(solution)/shard_map/ppermute | solution.py:740
  195.7 13.3 %collective-permute-start.32 = (bf16[4,48,1920]{2,1,0:T(8,128)(2,1)}, bf16[4,48,1920]{2,1,0:T(8,128)(2,1)}, u32[]{:S(2)}, u32[]{:S(2)}) collective-permute-start(bf16[4,48,1920]{2,1,0:T(8,128)(2,1)} %fusion), channel_id=1, source_target_pairs={{0,4},{1,3},{2,6},{3,1},{4,0},{5,7},{6,2},{7,5},{8,12},{9,11},{10,... | collective-permute-start | bytes 2211848 | tf_op jit(solution)/shard_map/ppermute | solution.py:746
  207.7 18.9 %collective-permute-start.30 = (bf16[4,2,48,1152]{3,2,1,0:T(8,128)(2,1)S(1)}, bf16[4,2,48,1152]{3,2,1,0:T(8,128)(2,1)S(1)}, u32[]{:S(2)}, u32[]{:S(2)}) collective-permute-start(bf16[4,2,48,1152]{3,2,1,0:T(8,128)(2,1)S(1)} %get-tuple-element.214), channel_id=1, source_target_pairs={{0,2},{1,5},{2,0},{3,7},{4,6},{5,1},{6,4},{7,3},{8,10},{9,13},{10,... | collective-permute-start | bytes 2654216 | tf_op jit(solution)/shard_map/ppermute | solution.py:743
  210.4 18.1 %collective-permute-start.35 = (bf16[48,1920]{1,0:T(8,128)(2,1)S(1)}, bf16[48,1920]{1,0:T(8,128)(2,1)S(1)}, u32[]{:S(2)}, u32[]{:S(2)}) collective-permute-start(bf16[48,1920]{1,0:T(8,128)(2,1)S(1)} %get-tuple-element.278), channel_id=1, source_target_pairs={{0,8},{4,12},{8,0},{12,4},{16,24},{20,28},{24,16},{28,20},{1,9},{5... | collective-permute-start | bytes 552968 | tf_op jit(solution)/shard_map/ppermute | solution.py:749
  212.8 15.8 %collective-permute-start.36 = (bf16[48,1920]{1,0:T(8,128)(2,1)S(1)}, bf16[48,1920]{1,0:T(8,128)(2,1)S(1)}, u32[]{:S(2)}, u32[]{:S(2)}) collective-permute-start(bf16[48,1920]{1,0:T(8,128)(2,1)S(1)} %get-tuple-element.277), channel_id=1, source_target_pairs={{0,16},{4,20},{8,24},{12,28},{16,0},{20,4},{24,8},{28,12},{1,17},{... | collective-permute-start | bytes 552968 | tf_op jit(solution)/shard_map/ppermute | solution.py:749
  213.8 14.8 %collective-permute-start.37 = (bf16[48,1920]{1,0:T(8,128)(2,1)S(1)}, bf16[48,1920]{1,0:T(8,128)(2,1)S(1)}, u32[]{:S(2)}, u32[]{:S(2)}) collective-permute-start(bf16[48,1920]{1,0:T(8,128)(2,1)S(1)} %get-tuple-element.276), channel_id=1, source_target_pairs={{0,24},{4,28},{8,16},{12,20},{16,8},{20,12},{24,0},{28,4},{1,25},{... | collective-permute-start | bytes 552968 | tf_op jit(solution)/shard_map/ppermute | solution.py:749
  239.3 14.1 %collective-permute-start.39 = (bf16[48,1280]{1,0:T(8,128)(2,1)S(1)}, bf16[48,1280]{1,0:T(8,128)(2,1)S(1)}, u32[]{:S(2)}, u32[]{:S(2)}) collective-permute-start(bf16[48,1280]{1,0:T(8,128)(2,1)S(1)} %get-tuple-element.291), channel_id=1, source_target_pairs={{0,8},{4,12},{8,0},{12,4},{16,24},{20,28},{24,16},{28,20},{1,9},{5... | collective-permute-start | bytes 368648 | tf_op jit(solution)/shard_map/ppermute | solution.py:749
  240.4 13.0 %collective-permute-start.40 = (bf16[48,1280]{1,0:T(8,128)(2,1)S(1)}, bf16[48,1280]{1,0:T(8,128)(2,1)S(1)}, u32[]{:S(2)}, u32[]{:S(2)}) collective-permute-start(bf16[48,1280]{1,0:T(8,128)(2,1)S(1)} %get-tuple-element.292), channel_id=1, source_target_pairs={{0,16},{4,20},{8,24},{12,28},{16,0},{20,4},{24,8},{28,12},{1,17},{... | collective-permute-start | bytes 368648 | tf_op jit(solution)/shard_map/ppermute | solution.py:749
  (72 other events, 505.8 us)
